TPU v7x, 32 devices: a whole 2x2x4 slice. The times are simulated.
32 devices in a mesh: ctx: 16 (over z, y, core), head: 2 (over x).
Axes of the slice: x: 2, y: 2, z: 4, core: 2. Of those that a mesh axis runs over, the one named last changes fastest.
Arguments:
- query_in: bfloat16 [2048, 2048], P('ctx', 'head'), may hold values from -6 to 6
- key_in: bfloat16 [2048, 2, 2048], P('ctx', None, 'head'), may hold values from -6 to 6
- value_in: bfloat16 [2048, 2, 2048], P('ctx', None, 'head'), may hold values from -6 to 6
- beta_logit: float32 [2048, 2, 16], P('ctx', None, 'head'), may hold values from -6 to 8
- query_conv: float32 [4, 2048], P(None, 'head'), may hold values from -2.5 to 2.5
- key_conv: float32 [4, 2, 2048], P(None, None, 'head'), may hold values from -2.5 to 2.5
- value_conv: float32 [4, 2, 2048], P(None, None, 'head'), may hold values from -2.5 to 2.5
- norm_gain: float32 [2048], P('head'), may hold values from 0.1 to 1.9
- out_weight: bfloat16 [2048, 2048], P('head'), may hold values from -0.125 to 0.125
- grad_out: bfloat16 [2048, 2048], P('ctx'), may hold values from -6 to 6
Outputs:
- layer_out: bfloat16 [2048, 2048], P(('ctx', 'head'))
- grad_query: float32 [2048, 2048], P('ctx', 'head')
- grad_key: float32 [2048, 2, 2048], P('ctx', None, 'head')
- grad_value: float32 [2048, 2, 2048], P('ctx', None, 'head')
- grad_beta: float32 [2048, 2, 16], P('ctx', None, 'head')
All inputs are finite; a program needn't handle non-finite values.
Results may differ from a plain program's by a relative error of at most 0.014.
Values may be sent and summed in bfloat16 or wider, within the bound.
No kernel may reach another device: no remote copies, remote signals or barrier semaphores. Data moves between devices by JAX's collectives and lax.ppermute only.
A program may use at most 128 MiB of HBM per device.

v0:
```python
import jax
import jax.numpy as jnp
from jax import lax
from jax.sharding import PartitionSpec as P

DK = 128
DV = 128
GROUP = 64


highest = lax.Precision.HIGHEST
epsilon = 1e-06


def passed_along(value, axis, steps):
    count = lax.axis_size(axis)
    leading, last = (max(0, -steps), min(count, count - steps))
    return lax.ppermute(value, axis, [(source, source + steps) for source in range(leading, last)])


def prefix_2(part, axis, combine, identity, reverse):
    count = lax.axis_size(axis)
    place = lax.axis_index(axis)
    ahead = count - 1 - place if reverse else place
    gathered = jax.tree.map(lambda a: lax.all_gather(a, axis), part)
    state = jax.tree.map(lambda a, e: jnp.zeros_like(a) + jnp.asarray(e, a.dtype), part, identity)

    def one(step, state):
        source = count - 1 - step if reverse else step
        return combine(
            state, jax.tree.map(lambda a: lax.dynamic_index_in_dim(a, source, 0, False), gathered)
        )

    return lax.fori_loop(0, ahead, one, state)


def causal_conv(raw_rows, edge_rows, kernel):
    padded = jnp.concatenate([edge_rows, raw_rows], axis=0)
    length = raw_rows.shape[0]
    summed = sum(
        (kernel[offset] * padded[offset : offset + length] for offset in range(kernel.shape[0]))
    )
    return jax.nn.silu(summed)


def unit_norm(values):
    return values * lax.rsqrt(jnp.sum(values * values, axis=-1, keepdims=True) + epsilon)


def prepare(
    query_raw,
    key_raw,
    value_raw,
    beta_raw,
    edge_query,
    edge_key,
    edge_value,
    query_conv,
    key_conv,
    value_conv,
):
    token_count = query_raw.shape[0]
    slot_count = key_raw.shape[1]
    head_count = query_raw.shape[1] // DK
    blocks = token_count // GROUP
    block_rows = GROUP * slot_count
    queries = unit_norm(
        causal_conv(query_raw, edge_query, query_conv).reshape(token_count, head_count, DK)
    )
    key_all = unit_norm(
        causal_conv(key_raw, edge_key, key_conv).reshape(token_count, slot_count, head_count, DK)
    )
    value_all = causal_conv(value_raw, edge_value, value_conv).reshape(
        token_count, slot_count, head_count, DV
    )
    strength = 2.0 * jax.nn.sigmoid(beta_raw)
    queries = queries.reshape(blocks, GROUP, head_count, DK).transpose(0, 2, 1, 3)
    key_rows = key_all.reshape(blocks, block_rows, head_count, DK).transpose(0, 2, 1, 3)
    value_rows = value_all.reshape(blocks, block_rows, head_count, DV).transpose(0, 2, 1, 3)
    strength = strength.reshape(blocks, block_rows, head_count).transpose(0, 2, 1)
    gram = jnp.einsum("nhcd,nhed->nhce", key_rows, key_rows, precision=highest)
    system = jnp.eye(block_rows, dtype=gram.dtype) + jnp.tril(gram * strength[..., :, None], -1)
    right_side = strength[..., None] * jnp.concatenate([key_rows, value_rows], axis=-1)
    solved = lax.linalg.triangular_solve(
        system, right_side, left_side=True, lower=True, unit_diagonal=True
    )
    w_rows = solved[..., :DK]
    u_rows = solved[..., DK:]
    token_pos = jnp.arange(GROUP)[:, None]
    row_pos = jnp.arange(block_rows)[None, :]
    visible = (row_pos <= slot_count * token_pos + slot_count - 1).astype(gram.dtype)
    scores = jnp.einsum("nhtd,nhcd->nhtc", queries, key_rows, precision=highest) * visible
    mapped_query = queries - jnp.einsum("nhtc,nhcd->nhtd", scores, w_rows, precision=highest)
    local_out = jnp.einsum("nhtc,nhce->nhte", scores, u_rows, precision=highest)
    transition = jnp.eye(DK, dtype=gram.dtype) - jnp.einsum(
        "nhcd,nhce->nhde", key_rows, w_rows, precision=highest
    )
    written = jnp.einsum("nhcd,nhce->nhde", key_rows, u_rows, precision=highest)
    return (mapped_query, local_out, transition, written)


def product(left_maps, right_maps):
    return jnp.einsum("hij,hjk->hik", left_maps, right_maps, precision=highest)


def compose(earlier, later):
    return (product(later[0], earlier[0]), product(later[0], earlier[1]) + later[1])


def identity_of(matrix, offset):
    return (
        jnp.broadcast_to(jnp.eye(matrix.shape[1], dtype=matrix.dtype), matrix.shape),
        jnp.zeros_like(offset),
    )


def state_pass(terms, start_state):

    def state_advance(current, block_terms):
        mapped_query, local_out, transition, written = block_terms
        out_rows = jnp.einsum("htd,hde->hte", mapped_query, current, precision=highest) + local_out
        return (
            jnp.einsum("hde,hef->hdf", transition, current, precision=highest) + written,
            out_rows,
        )

    return lax.scan(state_advance, start_state, terms)


def track(terms):
    transition_all = terms[2]
    head_count = transition_all.shape[1]
    start_matrix = jnp.broadcast_to(jnp.eye(DK, dtype=transition_all.dtype), (head_count, DK, DK))
    start_offset = jnp.zeros((head_count, DK, DV), transition_all.dtype)

    def track_advance(carried, block_terms):
        matrix, offset = carried
        transition, written = block_terms
        return ((product(transition, matrix), product(transition, offset) + written), None)

    carried, unused = lax.scan(track_advance, (start_matrix, start_offset), (terms[2], terms[3]))
    return carried


def finish(outs, gain):
    block_count, head_count, group_len, value_size = outs.shape
    merged = outs.transpose(0, 2, 1, 3).reshape(block_count * group_len, head_count, value_size)
    scale = lax.rsqrt(jnp.mean(merged * merged, axis=-1, keepdims=True) + epsilon)
    normed = merged * scale * gain.reshape(head_count, value_size)
    return normed.reshape(block_count * group_len, head_count * value_size)


def shards(
    query_in,
    key_in,
    value_in,
    beta_logit,
    query_conv,
    key_conv,
    value_conv,
    norm_gain,
    out_weight,
    grad_out,
):
    rim_len = query_conv.shape[0] - 1
    slot_count = key_in.shape[1]
    query_width = query_in.shape[1]
    key_width = key_in.shape[1] * key_in.shape[2]
    tail_rows = jnp.concatenate(
        [
            query_in[-rim_len:],
            key_in[-rim_len:].reshape(rim_len, key_width),
            value_in[-rim_len:].reshape(rim_len, -1),
        ],
        axis=1,
    )
    edges = passed_along(tail_rows, "ctx", 1).astype(jnp.float32)
    edge_query = edges[:, :query_width]
    edge_key = edges[:, query_width : query_width + key_width].reshape(rim_len, slot_count, -1)
    edge_value = edges[:, query_width + key_width :].reshape(rim_len, slot_count, -1)
    inputs = (
        query_in.astype(jnp.float32),
        key_in.astype(jnp.float32),
        value_in.astype(jnp.float32),
        beta_logit,
        edge_query,
        edge_key,
        edge_value,
    )
    grad_normed = jnp.dot(grad_out, out_weight.T, preferred_element_type=jnp.float32).astype(
        jnp.bfloat16
    )
    grad_normed = lax.optimization_barrier(grad_normed).astype(jnp.float32)

    def terms_of(query_raw, key_raw, value_raw, beta_raw, rim_query, rim_key, rim_value):
        return prepare(
            query_raw,
            key_raw,
            value_raw,
            beta_raw,
            rim_query,
            rim_key,
            rim_value,
            query_conv,
            key_conv,
            value_conv,
        )

    def whole(query_raw, key_raw, value_raw, beta_raw, rim_query, rim_key, rim_value, state_start):
        terms = terms_of(query_raw, key_raw, value_raw, beta_raw, rim_query, rim_key, rim_value)
        final, outs = state_pass(terms, state_start)
        return (finish(outs, norm_gain), final)

    matrix, offset = track(terms_of(*inputs))
    prefix = prefix_2((matrix, offset), "ctx", compose, identity_of(matrix, offset), False)
    state_in = prefix[1]
    forward_out, pull = jax.vjp(whole, *inputs, state_in)
    normed = forward_out[0]
    final = forward_out[1]
    first_pull = pull((grad_normed, jnp.zeros_like(final)))
    local_term = first_pull[-1]
    flipped = jnp.swapaxes(matrix, 1, 2)
    suffix = prefix_2((flipped, local_term), "ctx", compose, identity_of(flipped, local_term), True)
    second_pull = pull((grad_normed, suffix[1]))
    grads = second_pull[:7]
    rim_grads = jnp.concatenate(
        [grads[4], grads[5].reshape(rim_len, -1), grads[6].reshape(rim_len, -1)], axis=1
    )
    returned = passed_along(rim_grads, "ctx", -1)
    grad_query = grads[0].at[-rim_len:].add(returned[:, :query_width])
    grad_key = (
        grads[1]
        .at[-rim_len:]
        .add(returned[:, query_width : query_width + key_width].reshape(rim_len, slot_count, -1))
    )
    grad_value = (
        grads[2]
        .at[-rim_len:]
        .add(returned[:, query_width + key_width :].reshape(rim_len, slot_count, -1))
    )
    grad_beta = grads[3]
    normed_bf = normed.astype(jnp.bfloat16)
    layer_out = lax.psum_scatter(
        jnp.dot(normed_bf, out_weight, preferred_element_type=jnp.float32).astype(jnp.bfloat16),
        "head",
        scatter_dimension=0,
        tiled=True,
    )
    return (layer_out, grad_query, grad_key, grad_value, grad_beta)


def solution(mesh):
    placed = (
        P("ctx", "head"),
        P("ctx", None, "head"),
        P("ctx", None, "head"),
        P("ctx", None, "head"),
        P(None, "head"),
        P(None, None, "head"),
        P(None, None, "head"),
        P("head"),
        P("head", None),
        P("ctx", None),
    )
    return jax.shard_map(
        shards,
        mesh=mesh,
        in_specs=placed,
        out_specs=(
            P(("ctx", "head"), None),
            P("ctx", "head"),
            P("ctx", None, "head"),
            P("ctx", None, "head"),
            P("ctx", None, "head"),
        ),
        check_vma=False,
    )
```

profile of v0, /device:TPU:1, one launch (start us, length us, event | category | flops | bytes accessed | tf_op | source)
XLA Modules:
  0.0 648.0 jit_solution(7689422049410818755)
XLA Ops:
  9.6 4.5 collective-permute-start
  16.8 2.4 convert_element_type.51
  20.2 3.3 fusion.144
  26.3 5.0 fusion.145
  33.7 3.0 copy_bitcast_fusion
  36.7 2.3 fusion.155
  41.3 158.2 %custom-call.11 = f32[2,8,1,128,128]{3,4,2,1,0:T(8,128)S(1)} custom-call(f32[2,8,1,128,128]{4,3,2,1,0:T(8,128)} %add_bitcast_fusion), custom_call_target="InvertDiagBlocksLowerTriangular" | custom-call | tf_op jit(solution)/shard_map/triangular_solve/custom-call.1 | solution.py:84
  200.4 3.5 fusion.57
  204.0 1.9 convolution_subtract_fusion
  205.9 2.9 fusion.103
  209.6 10.2 %while.97 = (s32[]{:T(128)}, f32[8,128,128]{2,1,0:T(8,128)}, f32[8,128,128]{2,1,0:T(8,128)}, f32[2,8,128,128]{3,2,1,0:T(8,128)S(1)}, f32[2,8,128,128]{3,2,1,0:T(8,128)}, /*index=5*/s32[]{:T(128)}, s32[]{:T(128)}) while((s32[]{:T(128)}, f32[8,128,128]{2,1,0:T(8,128)}, f32[8,128,128]{2,1,0:T(8,128)}, ...), condition=%wide.region_2.4_spmd.clone, body=%wide.region_1.3_spmd.clone.sunk | while | flops 402915328 | bytes 7865982 | solution.py:141
  212.1 2.5 convolution_add_fusion.25
  217.2 2.5 convolution_add_fusion.25
  220.5 2.0 copy.120
  223.9 3.7 convolution_convert_fusion.1
  233.8 3.1 convolution_multiply_fusion
  236.9 1.9 fusion.101
  238.7 1.9 convolution_subtract_fusion.1
  240.6 54.4 %all-gather.9.cloned.1.call-done = f32[128,128,128]{2,1,0:T(8,128)} async-done(((f32[8,128,128]{2,1,0:T(8,128)}), f32[128,128,128]{2,1,0:T(8,128)}) %all-gather.9.cloned.1.call-update) | async-done | bytes 8388624 | tf_op jit(solution)/shard_map/all_gather | solution.py:25
  295.0 75.3 %all-gather.11.cloned.1.call-done = f32[128,128,128]{2,1,0:T(8,128)} async-done(((f32[8,128,128]{2,1,0:T(8,128)}), f32[128,128,128]{2,1,0:T(8,128)}) %all-gather.11.cloned.1.call-update) | async-done | bytes 8388624 | tf_op jit(solution)/shard_map/all_gather | solution.py:25
  370.4 1.9 while.93
  374.2 7.6 %while.94 = (s32[]{:T(128)}, f32[8,128,128]{2,1,0:T(8,128)S(1)}, f32[2,8,64,128]{3,2,1,0:T(8,128)}, f32[2,8,128,128]{3,2,1,0:T(8,128)}, f32[2,8,128,128]{3,2,1,0...) while((s32[]{:T(128)}, f32[8,128,128]{2,1,0:T(8,128)S(1)}, ...), condition=%wide.region_7.9_spmd, body=%wide.region_6.8_spmd.sunk | while | flops 302186496 | bytes 15993049 | solution.py:127
  385.0 9.1 %while.98 = (s32[]{:T(128)}, f32[8,128,128]{2,1,0:T(8,128)}, f32[2,8,128,128]{2,3,1,0:T(8,128)}, f32[2,8,64,128]{3,2,1,0:T(8,128)S(1)}, f32[2,8,64,128]{3,2,1,0:T(8,128)S(1)}, /*index=5*/s32[]{:T(128)}, s32[]{:T(128)}) while((s32[]{:T(128)}, f32[8,128,128]{2,1,0:T(8,128)}, f32[2,8,128,128]{2,3,1,0:T(8,128)}, ...), condition=%wide.region_12.14_spmd.clone, body=%wide.region_11.13_spmd.clone.sunk | while | flops 302252032 | bytes 4195439 | solution.py:127
  387.1 2.5 convolution_add_fusion.26
  391.7 2.5 convolution_add_fusion.26
  397.4 2.7 mul.630
  400.7 3.8 convolution_convert_fusion
  404.6 41.1 %all-gather.13.cloned.1.call-done = f32[128,128,128]{2,1,0:T(8,128)} async-done(((f32[8,128,128]{2,1,0:T(8,128)}), f32[128,128,128]{2,1,0:T(8,128)}) %all-gather.13.cloned.1.call-update) | async-done | bytes 8388624 | tf_op jit(solution)/shard_map/all_gather | solution.py:25
  445.7 75.2 %all-gather.15.cloned.1.call-done = f32[128,128,128]{2,1,0:T(8,128)} async-done(((f32[8,128,128]{2,1,0:T(8,128)}), f32[128,128,128]{2,1,0:T(8,128)}) %all-gather.15.cloned.1.call-update) | async-done | bytes 8388624 | tf_op jit(solution)/shard_map/all_gather | solution.py:25
  520.9 27.0 %while.95 = (s32[]{:T(128)}, f32[8,128,128]{2,1,0:T(8,128)S(1)}, s32[]{:T(128)}, f32[16,8,128,128]{3,2,1,0:T(8,128)}, f32[16,8,128,128]{3,2,1,0:T(8,128)}, /*index=5*/s32[]{:T(128)}, s32[]{:T(128)}, s32[]{:T(128)}, s32[]{:T(128)}) while((s32[]{:T(128)}, f32[8,128,128]{2,1,0:T(8,128)S(1)}, s32[]{:T(128)}, f32[16,8,128,128]{3,2,1,0:T(8,128)}, ...), condition=%wide.region_14.16_spmd, body=%wide.region_13.15_spmd.sunk | while | flops 201457664 | bytes 3146899 | solution.py:34
  526.8 1.9 convolution_add_fusion.23
  551.0 13.4 %while.96 = (s32[]{:T(128)}, f32[8,128,128]{2,1,0:T(8,128)S(1)}, f32[2,8,64,128]{3,2,1,0:T(8,128)S(1)}, f32[2,8,64,128]{3,2,1,0:T(8,128)}, f32[2,8,128,128]{2,3,...) while((s32[]{:T(128)}, f32[8,128,128]{2,1,0:T(8,128)S(1)}, ...), condition=%wide.region_16.18_spmd, body=%wide.region_15.17_spmd.sunk | while | flops 604110848 | bytes 29364020 | solution.py:127
  564.4 2.5 fusion.156
  567.0 2.3 fusion.97
  569.3 2.1 fusion.99
  571.5 2.3 fusion.94
  577.5 2.9 multiply_reduce_fusion
  580.4 2.5 fusion.59
  582.9 2.1 fusion.66
  589.2 2.1 fusion.62
  591.3 2.4 multiply_reduce_fusion.1
  593.8 2.2 convolution_add_fusion.8
  602.3 3.8 broadcast_multiply_fusion.5
  607.9 2.0 pad_add_fusion.4
  611.5 2.7 reshape.328
  614.2 2.9 broadcast_multiply_fusion.1
  619.4 2.1 pad_add_fusion.3
  626.0 4.1 collective-permute-start.1
  (378 shorter events, 126.7 us)
Async XLA Ops:
  7.2 216.7 %copy-start = (bf16[128,2048]{1,0:T(8,128)(2,1)S(1)}, bf16[128,2048]{1,0:T(8,128)(2,1)}, u32[]{:S(2)}) copy-start(bf16[128,2048]{1,0:T(8,128)(2,1)} %param.39) | copy-start | bytes 1572868
  7.2 12.0 %copy-start.49 = (bf16[128,2,1024]{2,1,0:T(2,128)(2,1)S(1)}, bf16[128,2,1024]{2,1,0:T(2,128)(2,1)}, u32[]{:S(2)}) copy-start(bf16[128,2,1024]{2,1,0:T(2,128)(2,1)} %param.31) | copy-start | bytes 1572868
  7.2 287.8 %all-gather.9.cloned.1.call-start = ((), (), s32[]{:S(2)}) async-start(), calls=%async_computation.2 | async-start | bytes 8912896 | tf_op jit(solution)/shard_map/all_gather | solution.py:25
  9.6 10.0 %collective-permute-start = (bf16[3,5120]{1,0:T(4,128)(2,1)S(1)}, bf16[3,5120]{1,0:T(4,128)(2,1)S(1)}, u32[]{:S(2)}, u32[]{:S(2)}) collective-permute-start(bf16[3,5120]{1,0:T(4,128)(2,1)S(1)} %pad_maximum_fusion.6), channel_id=1, source_target_pairs={{0,2},{2,4},{4,6},{6,8},{8,10},{10,12},{12,14},{14,16},{16,18},{18... | collective-permute-start | bytes 92168 | tf_op jit(solution)/shard_map/ppermute | solution.py:18
  14.2 24.8 %copy-start.53 = (pred[128,128]{1,0:T(8,128)(4,1)}, pred[128,128]{1,0:T(8,128)(4,1)S(1)}, u32[]{:S(2)}) copy-start(pred[128,128]{1,0:T(8,128)(4,1)S(1)} %get-tuple-element.800) | copy-start | bytes 49156
  15.0 11.3 %copy-start.55 = (f32[2,1024]{1,0:T(2,128)}, f32[2,1024]{1,0:T(2,128)S(1)}, u32[]{:S(2)}) copy-start(f32[2,1024]{1,0:T(2,128)S(1)} %get-tuple-element.786) | copy-start | bytes 24580
  15.0 11.3 %copy-start.61 = (f32[2,1024]{1,0:T(2,128)}, f32[2,1024]{1,0:T(2,128)S(1)}, u32[]{:S(2)}) copy-start(f32[2,1024]{1,0:T(2,128)S(1)} %get-tuple-element.784) | copy-start | bytes 24580
  15.0 11.3 %copy-start.63 = (f32[2,1024]{1,0:T(2,128)}, f32[2,1024]{1,0:T(2,128)S(1)}, u32[]{:S(2)}) copy-start(f32[2,1024]{1,0:T(2,128)S(1)} %get-tuple-element.785) | copy-start | bytes 24580
  15.0 11.3 %copy-start.65 = (f32[2,1024]{1,0:T(2,128)}, f32[2,1024]{1,0:T(2,128)S(1)}, u32[]{:S(2)}) copy-start(f32[2,1024]{1,0:T(2,128)S(1)} %get-tuple-element.787) | copy-start | bytes 24580
  15.8 7.8 %copy-start.57 = (f32[2,1024]{1,0:T(2,128)}, f32[2,1024]{1,0:T(2,128)S(1)}, u32[]{:S(2)}) copy-start(f32[2,1024]{1,0:T(2,128)S(1)} %get-tuple-element.790) | copy-start | bytes 24580
  15.8 7.8 %copy-start.67 = (f32[2,1024]{1,0:T(2,128)}, f32[2,1024]{1,0:T(2,128)S(1)}, u32[]{:S(2)}) copy-start(f32[2,1024]{1,0:T(2,128)S(1)} %get-tuple-element.788) | copy-start | bytes 24580
  15.8 7.8 %copy-start.69 = (f32[2,1024]{1,0:T(2,128)}, f32[2,1024]{1,0:T(2,128)S(1)}, u32[]{:S(2)}) copy-start(f32[2,1024]{1,0:T(2,128)S(1)} %get-tuple-element.789) | copy-start | bytes 24580
  15.8 7.8 %copy-start.71 = (f32[2,1024]{1,0:T(2,128)}, f32[2,1024]{1,0:T(2,128)S(1)}, u32[]{:S(2)}) copy-start(f32[2,1024]{1,0:T(2,128)S(1)} %get-tuple-element.791) | copy-start | bytes 24580
  24.4 8.7 %copy-start.29 = (f32[128,2,8,128]{3,2,1,0:T(8,128)}, f32[128,2,8,128]{3,2,1,0:T(8,128)S(1)}, u32[]{:S(2)}) copy-start(f32[128,2,8,128]{3,2,1,0:T(8,128)S(1)} %reshape.315) | copy-start | bytes 3145732
  204.0 4.8 copy-start.2
  219.7 150.6 %all-gather.11.cloned.1.call-start = ((), (), s32[]{:S(2)}) async-start(), calls=%async_computation.3 | async-start | bytes 8912896 | tf_op jit(solution)/shard_map/all_gather | solution.py:25
  220.5 225.2 %all-gather.13.cloned.1.call-start = ((), (), s32[]{:S(2)}) async-start(), calls=%async_computation.4 | async-start | bytes 8912896 | tf_op jit(solution)/shard_map/all_gather | solution.py:25
  222.6 298.3 %all-gather.15.cloned.1.call-start = ((), (), s32[]{:S(2)}) async-start(), calls=%async_computation.5 | async-start | bytes 8912896 | tf_op jit(solution)/shard_map/all_gather | solution.py:25
  229.4 3.8 copy-start.74
  229.4 3.8 copy-start.76
  229.4 3.8 copy-start.78
  229.5 3.8 copy-start.80
  233.4 5.3 copy-start.11
  233.7 5.1 copy-start.82
  233.7 5.1 copy-start.84
  233.8 3.1 copy-start.3
  374.2 2.9 copy-start.9
  378.0 3.1 copy-start.9
  381.8 3.2 copy-start.6
  394.2 5.9 copy-start.60
  394.2 6.0 copy-start.38
  394.2 247.2 %reduce-scatter.2.cloned.1.call-start = ((), (), s32[]{:S(2)}) async-start(), calls=%async_computation.1 | async-start | bytes 786432 | tf_op jit(solution)/shard_map/reduce_scatter | solution.py:243
  397.4 3.4 copy-start.73
  551.1 3.9 copy-start.7
  554.0 2.8 copy-start.34
  554.0 2.8 copy-start.41
  557.7 3.9 copy-start.7
  560.6 2.8 copy-start.41
  567.0 4.5 copy-start.35
  602.3 3.9 copy-start.72
  602.3 3.9 copy-start.70
  602.3 3.9 copy-start.68
  609.9 4.3 copy-start.56
  614.2 3.0 copy-start.66
  614.2 3.0 copy-start.64
  614.2 3.0 copy-start.62
  624.2 5.9 copy-start.85
  626.0 9.5 %collective-permute-start.1 = (f32[3,5120]{1,0:T(4,128)}, f32[3,5120]{1,0:T(4,128)}, u32[]{:S(2)}, u32[]{:S(2)}) collective-permute-start(f32[3,5120]{1,0:T(4,128)} %pad_maximum_fusion.5), channel_id=1, source_target_pairs={{2,0},{4,2},{6,4},{8,6},{10,8},{12,10},{14,12},{16,14},{18,16},{20... | collective-permute-start | bytes 184328 | tf_op jit(solution)/shard_map/ppermute | solution.py:18
  (56 other events, 92.6 us)
Sparse Core Ops, SparseCore 0:
  219.9 75.0 all-gather.8
  297.2 73.1 all-gather.10
  372.5 73.1 all-gather.12
  447.7 73.1 all-gather.14
  523.5 12.3 reduce-scatter.1
where the time goes:
time: 658 us; the launch traced here: 648 us
  waiting for transfers between devices  247 us (38%)
  other arithmetic  200 us (30%)
  matrix products  112 us (17%)
  local copies, waits for them, and re-layouts  64 us (10%)
  between operations  15.2 us (2%)
  starting transfers between devices  9.45 us (1%)
    all_gather x4, waiting for transfers between devices, prefix_2(): gathered = jax.tree.map(lambda a: lax.all_gather(a, axis), part)  246 us
    another operation x5, other arithmetic, prepare(): lax.linalg.triangular_solve(system, right_side, left_side=True, lower=Tru...  160 us
    dot_general x19, matrix products, product(): return jnp.einsum('hij,hjk->hik', left_maps, right_maps, precision=highest)  35.7 us
  transfers between devices with their start and end apart: 7, of which 4 were waited for; matrix products, arithmetic and copies ran while one was open for 25% of the time, Pallas kernels for 0%

commit v1 on v0

v1 whole, which is shorter than its diff:
```python
import functools

import jax
import jax.numpy as jnp
from jax import lax
from jax.experimental import pallas as pl
from jax.experimental.pallas import tpu as pltpu
from jax.sharding import PartitionSpec as P

HEAD = 128
TAPS = 4
RIM = TAPS - 1
EPS = 1e-06
F32 = jnp.float32
BF16 = jnp.bfloat16

ROWS_COLS = (((1,), (0,)), ((), ()))
ROWS_ROWS = (((1,), (1,)), ((), ()))
COLS_COLS = (((0,), (0,)), ((), ()))


def two(x):
    high = x.astype(BF16)
    return high, (x - high.astype(F32)).astype(BF16)


def one(x):
    return (x.astype(BF16),)


def mm(left, right, dims=ROWS_COLS):
    total = None
    for i, a in enumerate(left):
        for j, b in enumerate(right):
            if i + j < 2:
                part = lax.dot_general(a, b, dims, preferred_element_type=F32)
                total = part if total is None else total + part
    return total


def token_order(rows, cols):
    tokens = rows[0]
    r = lax.broadcasted_iota(jnp.int32, (rows[1], cols), 0)
    c = lax.broadcasted_iota(jnp.int32, (rows[1], cols), 1)
    return r % tokens, r // tokens, c % tokens, c // tokens


def before(tokens, slots):
    rt, rj, ct, cj = token_order((tokens, tokens * slots), tokens * slots)
    return slots * ct + cj < slots * rt + rj


def level_pairs(tokens, slots, level):
    rt, rj, ct, cj = token_order((tokens, tokens * slots), tokens * slots)
    if level < 0:
        return (rt == ct) & (cj < rj)
    return ((rt >> (level + 1)) == (ct >> (level + 1))) & (((rt >> level) & 1) == 1) & (((ct >> level) & 1) == 0)


def visible(tokens, slots):
    rt, _, ct, _ = token_order((tokens, tokens), tokens * slots)
    return ct <= rt


def conv_rows(x, tail, weight, pad):
    tokens = x.shape[0]
    pad[pl.ds(8 - RIM, RIM), :] = tail
    pad[pl.ds(8, tokens), :] = x
    total = None
    for i in range(TAPS):
        part = weight[i : i + 1] * pad[pl.ds(8 - RIM + i, tokens), :]
        total = part if total is None else total + part
    return total


def conv_back(grad, weight, pad):
    tokens = grad.shape[0]
    pad[pl.ds(0, 8), :] = jnp.zeros((8, HEAD), F32)
    pad[pl.ds(8, tokens), :] = grad
    pad[pl.ds(8 + tokens, 8), :] = jnp.zeros((8, HEAD), F32)
    inner, rim = None, None
    for i in range(TAPS):
        part = weight[i : i + 1] * pad[pl.ds(8 + RIM - i, tokens), :]
        edge = weight[i : i + 1] * pad[pl.ds(RIM - i, 8), :]
        inner = part if inner is None else inner + part
        rim = edge if rim is None else rim + edge
    return inner, rim


def sigmoid(x):
    return 1.0 / (1.0 + jnp.exp(-x))


def unit(values):
    scale = lax.rsqrt(jnp.sum(values * values, axis=-1, keepdims=True) + EPS)
    return values * scale, scale


def beta_rows(tile, slots):
    return [tile[3 * j : 3 * j + 1] + tile[3 * j + 1 : 3 * j + 2] + tile[3 * j + 2 : 3 * j + 3] for j in range(slots)]


def column(rows):
    tokens = rows[0].shape[1]
    eye = (
        lax.broadcasted_iota(jnp.int32, (tokens, tokens), 0) == lax.broadcasted_iota(jnp.int32, (tokens, tokens), 1)
    )
    return jnp.concatenate([jnp.sum(jnp.where(eye, row, 0.0), axis=1, keepdims=True) for row in rows], axis=0)


def load_kv(ref, n, tokens, slots):
    xs = [ref[n, pl.ds(a * tokens, tokens), :].astype(F32) for a in range(2 * slots)]
    base = 2 * slots * tokens
    betas = beta_rows(ref[n, pl.ds(base, 16), :].astype(F32), slots)
    tails = ref[n, pl.ds(base + 16, 16), :].astype(F32)
    return xs, betas, [tails[4 * a + 1 : 4 * a + 4] for a in range(2 * slots)]


def tap_rows(wts, slots, kind, slot):
    if kind == 0:
        return wts[0:TAPS]
    first = TAPS + (kind - 1) * TAPS * slots
    return jnp.concatenate([wts[first + i * slots + slot : first + i * slots + slot + 1] for i in range(TAPS)], axis=0)


def keys_kernel(per, tokens, slots, hid, kv_ref, wts_ref, kn_ref, wu_ref, ti_ref, a_ref, mc_ref, end_ref, pad, carry):
    step = pl.program_id(0)
    rows = tokens * slots
    wts = wts_ref[...]
    ir = lax.broadcasted_iota(jnp.int32, (HEAD, 2 * HEAD), 0)
    ic = lax.broadcasted_iota(jnp.int32, (HEAD, 2 * HEAD), 1)

    @pl.when(step == 0)
    def _():
        carry[...] = (ir == ic).astype(F32)

    keys, rights, systems = [], [], []
    order = before(tokens, slots)
    for n in range(per):
        xs, betas, tails = load_kv(kv_ref, n, tokens, slots)
        parts = []
        for a in range(2 * slots):
            kind, slot = 1 + a // slots, a % slots
            s = conv_rows(xs[a], tails[a], tap_rows(wts, slots, kind, slot), pad.at[n * 2 * slots + a])
            c = s * sigmoid(s)
            parts.append(unit(c)[0] if kind == 1 else c)
        k = jnp.concatenate(parts[:slots], axis=0)
        v = jnp.concatenate(parts[slots:], axis=0)
        strength = 2.0 * sigmoid(column(betas))
        kn_ref[n] = k
        k2 = two(k)
        gram = mm(k2, k2, ROWS_ROWS)
        systems.append(two(jnp.where(order, gram * strength, 0.0)))
        rights.append(two(strength * jnp.concatenate([k, v], axis=1)))
        keys.append(k2)
    eye = (
        lax.broadcasted_iota(jnp.int32, (rows, rows), 0) == lax.broadcasted_iota(jnp.int32, (rows, rows), 1)
    ).astype(F32)
    zero = jnp.zeros((rows, rows), BF16)
    pairs = level_pairs(tokens, slots, -1)
    inverse = [
        eye - jnp.where(pairs, system[0].astype(F32) + system[1].astype(F32), 0.0) for system in systems
    ]
    level = 0
    while (1 << level) < tokens:
        pairs = level_pairs(tokens, slots, level)
        split = [two(x) for x in inverse]
        crossed = [
            mm(tuple(jnp.where(pairs, part, zero) for part in system), x) for system, x in zip(systems, split)
        ]
        inverse = [x - mm(s, two(y)) for x, s, y in zip(inverse, split, crossed)]
        level += 1
    wus = []
    for n in range(per):
        ti_ref[n] = inverse[n]
        wus.append(mm(two(inverse[n]), rights[n]))
        wu_ref[n] = wus[n]
    maps = [mm(keys[n], two(wus[n]), COLS_COLS) for n in range(per)]
    state = carry[...]
    for n in range(per):
        mc_ref[n] = state
        a = (ir == ic)[:, :HEAD].astype(F32) - maps[n][:, :HEAD]
        a_ref[n] = a
        moved = mm(two(a), two(state))
        state = jnp.where(ic < HEAD, moved, moved + maps[n])
    carry[...] = state
    end_ref[...] = state


def queries_kernel(per, tokens, slots, hid, qg_ref, wts_ref, kn_ref, wu_ref, q_ref, sc_ref, qm_ref, ol_ref, pad):
    wts = wts_ref[...]
    seen = visible(tokens, slots)
    for n in range(per):
        x = qg_ref[n, pl.ds(0, tokens), :].astype(F32)
        tail = qg_ref[n, pl.ds(2 * tokens, 16), :].astype(F32)[1:4]
        s = conv_rows(x, tail, tap_rows(wts, slots, 0, 0), pad.at[n])
        q = unit(s * sigmoid(s))[0]
        scores = jnp.where(seen, mm(two(q), two(kn_ref[n]), ROWS_ROWS), 0.0)
        mapped = mm(two(scores), two(wu_ref[n]))
        q_ref[n] = q
        sc_ref[n] = scores
        qm_ref[n] = q - mapped[:, :HEAD]
        ol_ref[n] = mapped[:, HEAD:]


def outs_kernel(
    count, tokens, slots, hid, qg_ref, wts_ref, start_ref, mc_ref, qm_ref, ol_ref, a_ref,
    nm_ref, dr_ref, st_ref, mb_ref, end_ref,
):
    gain = wts_ref[...][TAPS + 2 * TAPS * slots : TAPS + 2 * TAPS * slots + 1]
    start = two(start_ref[...])
    states = [
        mm(two(mc_ref[n, :, pl.ds(0, HEAD)]), start) + mc_ref[n, :, pl.ds(HEAD, HEAD)] for n in range(count)
    ]
    mapped = [two(qm_ref[n]) for n in range(count)]
    raws = [mm(mapped[n], two(states[n])) + ol_ref[n] for n in range(count)]
    local = []
    for n in range(count):
        st_ref[n] = states[n]
        raw = raws[n]
        scale = lax.rsqrt(jnp.mean(raw * raw, axis=-1, keepdims=True) + EPS)
        hat = raw * scale
        nm_ref[n] = (hat * gain).astype(BF16)
        dn = qg_ref[n, pl.ds(tokens, tokens), :].astype(F32) * gain
        dr = scale * (dn - hat * jnp.mean(dn * hat, axis=-1, keepdims=True))
        dr_ref[n] = dr
        local.append(mm(mapped[n], two(dr), COLS_COLS))
    ir = lax.broadcasted_iota(jnp.int32, (HEAD, 2 * HEAD), 0)
    ic = lax.broadcasted_iota(jnp.int32, (HEAD, 2 * HEAD), 1)
    state = (ir == ic).astype(F32)
    for n in range(count - 1, -1, -1):
        mb_ref[n] = state
        moved = mm(two(a_ref[n]), two(state), COLS_COLS)
        state = moved + jnp.concatenate([jnp.zeros((HEAD, HEAD), F32), local[n]], axis=1)
    end_ref[...] = state


def query_grads_kernel(
    per, tokens, slots, hid, qg_ref, wts_ref, kn_ref, wu_ref, q_ref, sc_ref, dr_ref, st_ref,
    d_ref, dk_ref, dd_ref, gq_ref, pad,
):
    wts = wts_ref[...]
    seen = visible(tokens, slots)
    for n in range(per):
        state, dr, k2 = two(st_ref[n]), two(dr_ref[n]), two(kn_ref[n])
        d = wu_ref[n, :, pl.ds(HEAD, HEAD)] - mm(two(wu_ref[n, :, pl.ds(0, HEAD)]), state)
        d_ref[n] = d
        ds = two(jnp.where(seen, mm(dr, two(d), ROWS_ROWS), 0.0))
        dq = mm(dr, state, ROWS_ROWS) + mm(ds, k2)
        dk_ref[n] = mm(ds, two(q_ref[n]), COLS_COLS)
        dd_ref[n] = mm(two(sc_ref[n]), dr, COLS_COLS)
        x = qg_ref[n, pl.ds(0, tokens), :].astype(F32)
        tail = qg_ref[n, pl.ds(2 * tokens, 16), :].astype(F32)[1:4]
        taps = tap_rows(wts, slots, 0, 0)
        s = conv_rows(x, tail, taps, pad.at[n])
        sg = sigmoid(s)
        q, scale = unit(s * sg)
        dc = scale * (dq - q * jnp.sum(q * dq, axis=-1, keepdims=True))
        inner, rim = conv_back(dc * sg * (1.0 + s * (1.0 - sg)), taps, pad.at[n])
        gq_ref[n, pl.ds(0, tokens), :] = inner.astype(BF16)
        gq_ref[n, pl.ds(tokens, 16), :] = jnp.concatenate([rim, jnp.zeros((8, HEAD), F32)], axis=0).astype(BF16)


def key_grads_kernel(
    per, tokens, slots, hid, kv_ref, wts_ref, end_ref, mb_ref, kn_ref, ti_ref, d_ref, dk_ref, dd_ref, st_ref,
    out_ref, pad,
):
    wts = wts_ref[...]
    order = before(tokens, slots)
    end = two(end_ref[...])
    rows = tokens * slots
    for n in range(per):
        g = mm(two(mb_ref[n, :, pl.ds(0, HEAD)]), end) + mb_ref[n, :, pl.ds(HEAD, HEAD)]
        g2, k, d = two(g), kn_ref[n], d_ref[n]
        k2, d2 = two(k), two(d)
        dd = dd_ref[n] + mm(k2, g2)
        y = mm(two(ti_ref[n]), two(dd), COLS_COLS)
        xs, betas, tails = load_kv(kv_ref, n, tokens, slots)
        strength = 2.0 * sigmoid(column(betas))
        de = strength * y
        de2 = two(de)
        dgram = jnp.where(order, mm(de2, d2, ROWS_ROWS), 0.0)
        dk = dk_ref[n] + mm(d2, g2, ROWS_ROWS) - mm(de2, two(st_ref[n]), ROWS_ROWS)
        dk = dk - mm(two(dgram + dgram.T), k2)
        ones = (jnp.ones((8, HEAD), BF16),)
        dot = mm(ones, two(y * d), ROWS_ROWS)
        base = 2 * slots * tokens
        marks = []
        for j in range(slots):
            gb = dot[0:1, j * tokens : (j + 1) * tokens] * sigmoid(-betas[j])
            high = gb.astype(BF16).astype(F32)
            marks += [high, gb - high]
        marks.append(jnp.zeros((16 - 2 * slots, tokens), F32))
        out_ref[n, pl.ds(base, 16), :] = jnp.concatenate(marks, axis=0).astype(BF16)
        rims = []
        for a in range(2 * slots):
            kind, slot = 1 + a // slots, a % slots
            taps = tap_rows(wts, slots, kind, slot)
            s = conv_rows(xs[a], tails[a], taps, pad.at[n])
            sg = sigmoid(s)
            if kind == 1:
                mine = k[slot * tokens : (slot + 1) * tokens]
                c = s * sg
                scale = lax.rsqrt(jnp.sum(c * c, axis=-1, keepdims=True) + EPS)
                part = dk[slot * tokens : (slot + 1) * tokens]
                dc = scale * (part - mine * jnp.sum(mine * part, axis=-1, keepdims=True))
            else:
                dc = de[slot * tokens : (slot + 1) * tokens]
            inner, rim = conv_back(dc * sg * (1.0 + s * (1.0 - sg)), taps, pad.at[n])
            out_ref[n, pl.ds(a * tokens, tokens), :] = inner.astype(BF16)
            rims.append(rim)
        out_ref[n, pl.ds(base + 16, 8 * 2 * slots), :] = jnp.concatenate(rims, axis=0).astype(BF16)


def call(kernel, hid, grid, ins, outs, scratch=(), flops=0):
    def spec(shape, per):
        if per == "weights":
            return pl.BlockSpec((shape[0], HEAD), lambda i, h: (0, h[0]))
        if per is None:
            return pl.BlockSpec(shape, lambda i, h: (0,) * len(shape))
        return pl.BlockSpec((per,) + tuple(shape[1:]), lambda i, h: (i,) + (0,) * (len(shape) - 1))

    moved = sum(a.size * a.dtype.itemsize for a, _ in ins)
    moved += sum(functools.reduce(lambda x, y: x * y, s, 1) * jnp.dtype(d).itemsize for s, d, _ in outs)
    return pl.pallas_call(
        kernel,
        grid_spec=pltpu.PrefetchScalarGridSpec(
            num_scalar_prefetch=1,
            grid=grid,
            in_specs=[spec(a.shape, per) for a, per in ins],
            out_specs=[spec(s, per) for s, _, per in outs],
            scratch_shapes=list(scratch),
        ),
        out_shape=[jax.ShapeDtypeStruct(s, d) for s, d, _ in outs],
        compiler_params=pltpu.CompilerParams(
            dimension_semantics=("arbitrary",) * len(grid), vmem_limit_bytes=48 << 20
        ),
        cost_estimate=pl.CostEstimate(flops=flops, bytes_accessed=moved, transcendentals=0),
    )(hid, *[a for a, _ in ins])


def shards(
    query_in,
    key_in,
    value_in,
    beta_logit,
    query_conv,
    key_conv,
    value_conv,
    norm_gain,
    out_weight,
    grad_out,
):
    tokens, slots = key_in.shape[0], key_in.shape[1]
    width = query_in.shape[1]
    heads = width // HEAD
    shard_count = lax.axis_size("ctx")
    place = lax.axis_index("ctx")
    groups = shard_count // heads
    group_lists = [[b * heads + i for i in range(heads)] for b in range(groups)]
    rows = tokens * slots
    hid = (place % heads).astype(jnp.int32).reshape(1)

    def exchange(x):
        return lax.all_to_all(x, "ctx", 0, 0, axis_index_groups=group_lists, tiled=True)

    def by_head(x):
        return x.reshape(x.shape[0], heads, HEAD).transpose(1, 0, 2)

    tail = jnp.concatenate(
        [query_in[-RIM:].reshape(RIM, 1, width), key_in[-RIM:], value_in[-RIM:]], axis=1
    )
    tail = lax.ppermute(tail, "ctx", [(i, i + 1) for i in range(shard_count - 1)])
    tail = tail.reshape(RIM, 1 + 2 * slots, heads, HEAD).transpose(2, 1, 0, 3)
    tail = jnp.pad(tail, ((0, 0), (0, 0), (1, 0), (0, 0)))
    high = lax.reduce_precision(beta_logit, 8, 7)
    rest = beta_logit - high
    middle = lax.reduce_precision(rest, 8, 7)
    betas = jnp.stack([high, middle, rest - middle], axis=2)
    betas = betas.transpose(3, 1, 2, 0).reshape(heads, 3 * slots, tokens).astype(BF16)
    betas = jnp.pad(betas, ((0, 0), (0, 16 - 3 * slots), (0, 0)))
    kv_tail = jnp.pad(tail[:, 1:].reshape(heads, 8 * slots, HEAD), ((0, 0), (0, 16 - 8 * slots), (0, 0)))
    packed_kv = jnp.concatenate(
        [by_head(key_in[:, j]) for j in range(slots)]
        + [by_head(value_in[:, j]) for j in range(slots)]
        + [betas, kv_tail],
        axis=1,
    )
    kv = exchange(packed_kv)
    grad_normed = jnp.dot(grad_out, out_weight.T, preferred_element_type=F32).astype(BF16)
    q_tail = jnp.pad(tail[:, 0], ((0, 0), (0, 12), (0, 0)))
    qg = exchange(jnp.concatenate([by_head(query_in), by_head(grad_normed), q_tail], axis=1))

    wts = jnp.concatenate(
        [
            query_conv,
            key_conv.reshape(TAPS * slots, width),
            value_conv.reshape(TAPS * slots, width),
            norm_gain.reshape(1, width),
            jnp.zeros((-(1 + TAPS + 2 * TAPS * slots) % 8, width), F32),
        ],
        axis=0,
    )
    g = heads
    per = 2 if g % 2 == 0 else 1
    grid = (g // per,)
    unit_flops = 2 * rows * rows * rows * g
    pads = pltpu.VMEM((per * 2 * slots, tokens + 16, HEAD), F32)
    kn, wu, ti, amap, mc, end = call(
        functools.partial(keys_kernel, per, tokens, slots),
        hid,
        grid,
        [(kv, per), (wts, "weights")],
        [
            ((g, rows, HEAD), F32, per),
            ((g, rows, 2 * HEAD), F32, per),
            ((g, rows, rows), F32, per),
            ((g, HEAD, HEAD), F32, per),
            ((g, HEAD, 2 * HEAD), F32, per),
            ((HEAD, 2 * HEAD), F32, None),
        ],
        [pads, pltpu.VMEM((HEAD, 2 * HEAD), F32)],
        flops=48 * unit_flops,
    )

    def across(last, towards):
        if groups == 1:
            return jnp.zeros((HEAD, HEAD), F32)
        if groups == 2:
            moves = [(i, i + towards * heads) for i in range(shard_count) if 0 <= i + towards * heads < shard_count]
            return lax.ppermute(last[:, HEAD:], "ctx", moves)
        every = lax.all_gather(last, "ctx")
        group, head = place // heads, place % heads
        ahead = group if towards > 0 else groups - 1 - group

        def advance(i, state):
            source = i if towards > 0 else groups - 1 - i
            item = lax.dynamic_index_in_dim(every, source * heads + head, 0, False)
            return jnp.dot(item[:, :HEAD], state, precision=lax.Precision.HIGHEST) + item[:, HEAD:]

        return lax.fori_loop(0, ahead, advance, jnp.zeros((HEAD, HEAD), F32))

    start = across(end, 1)
    small_pads = pltpu.VMEM((per, tokens + 16, HEAD), F32)
    q, sc, qm, ol = call(
        functools.partial(queries_kernel, per, tokens, slots),
        hid,
        grid,
        [(qg, per), (wts, "weights"), (kn, per), (wu, per)],
        [
            ((g, tokens, HEAD), F32, per),
            ((g, tokens, rows), F32, per),
            ((g, tokens, HEAD), F32, per),
            ((g, tokens, HEAD), F32, per),
        ],
        [small_pads],
        flops=3 * unit_flops,
    )
    normed, dr, st, mb, back_end = call(
        functools.partial(outs_kernel, g, tokens, slots),
        hid,
        (1,),
        [(qg, None), (wts, "weights"), (start, None), (mc, None), (qm, None), (ol, None), (amap, None)],
        [
            ((g, tokens, HEAD), BF16, None),
            ((g, tokens, HEAD), F32, None),
            ((g, HEAD, HEAD), F32, None),
            ((g, HEAD, 2 * HEAD), F32, None),
            ((HEAD, 2 * HEAD), F32, None),
        ],
        flops=2 * unit_flops,
    )
    finish = across(back_end, -1)
    d, dk, dd, gq = call(
        functools.partial(query_grads_kernel, per, tokens, slots),
        hid,
        grid,
        [(qg, per), (wts, "weights"), (kn, per), (wu, per), (q, per), (sc, per), (dr, per), (st, per)],
        [
            ((g, rows, HEAD), F32, per),
            ((g, rows, HEAD), F32, per),
            ((g, rows, HEAD), F32, per),
            ((g, tokens + 16, HEAD), BF16, per),
        ],
        [small_pads],
        flops=4 * unit_flops,
    )
    nq = exchange(jnp.concatenate([normed, gq], axis=1))
    normed_bf = nq[:, :tokens].transpose(1, 0, 2).reshape(tokens, width)
    partial = jnp.dot(normed_bf, out_weight, preferred_element_type=F32)
    head_count = lax.axis_size("head")
    if head_count == 2:
        half = tokens // 2
        mine = lax.axis_index("head")
        pieces = partial.reshape(2, half, partial.shape[1])
        kept = lax.dynamic_index_in_dim(pieces, mine, 0, False)
        sent = lax.dynamic_index_in_dim(pieces, 1 - mine, 0, False).astype(BF16)
        layer_out = (kept + lax.ppermute(sent, "head", [(0, 1), (1, 0)]).astype(F32)).astype(BF16)
    else:
        layer_out = lax.psum_scatter(partial.astype(BF16), "head", scatter_dimension=0, tiled=True)

    block = 2 * slots * tokens + 16 + 16 * slots
    (gkv,) = call(
        functools.partial(key_grads_kernel, per, tokens, slots),
        hid,
        grid,
        [
            (kv, per), (wts, "weights"), (finish, None), (mb, per), (kn, per), (ti, per), (d, per), (dk, per),
            (dd, per), (st, per),
        ],
        [((g, block, HEAD), BF16, per)],
        [small_pads],
        flops=8 * unit_flops,
    )
    grads = exchange(gkv)

    base = 2 * slots * tokens + 16
    rims = jnp.concatenate(
        [nq[:, 2 * tokens + 8 - RIM : 2 * tokens + 8]]
        + [grads[:, base + 8 * a + 8 - RIM : base + 8 * a + 8] for a in range(2 * slots)],
        axis=1,
    )
    rims = lax.ppermute(rims, "ctx", [(i, i - 1) for i in range(1, shard_count)]).astype(F32)

    def laid(block, a):
        edge = jnp.pad(rims[:, a * RIM : (a + 1) * RIM], ((0, 0), (tokens - RIM, 0), (0, 0)))
        return (block.astype(F32) + edge).transpose(1, 0, 2).reshape(tokens, width)

    grad_query = laid(nq[:, tokens : 2 * tokens], 0)
    parts = [laid(grads[:, a * tokens : (a + 1) * tokens], 1 + a) for a in range(2 * slots)]
    grad_key = jnp.stack(parts[:slots], axis=1)
    grad_value = jnp.stack(parts[slots:], axis=1)
    marks = grads[:, 2 * slots * tokens : 2 * slots * tokens + 2 * slots].astype(F32)
    marks = marks.reshape(heads, slots, 2, tokens).sum(axis=2)
    grad_beta = marks.transpose(2, 1, 0)
    return (layer_out, grad_query, grad_key, grad_value, grad_beta)


def solution(mesh):
    placed = (
        P("ctx", "head"),
        P("ctx", None, "head"),
        P("ctx", None, "head"),
        P("ctx", None, "head"),
        P(None, "head"),
        P(None, None, "head"),
        P(None, None, "head"),
        P("head"),
        P("head", None),
        P("ctx", None),
    )
    return jax.shard_map(
        shards,
        mesh=mesh,
        in_specs=placed,
        out_specs=(
            P(("ctx", "head"), None),
            P("ctx", "head"),
            P("ctx", None, "head"),
            P("ctx", None, "head"),
            P("ctx", None, "head"),
        ),
        check_vma=False,
    )
```

time: 658 us -> 163 us (0.25); the launches traced: 648 us -> 161 us
  waiting for transfers between devices: 247 us -> 24.1 us
  other arithmetic: 200 us -> 7.11 us
  matrix products: 112 us -> 6.6 us
  Pallas kernels: 0 us -> 54.2 us
  local copies, waits for them, and re-layouts: 64 us -> 34.5 us
  starting transfers between devices: 9.45 us -> 33.8 us
  between operations: 15.2 us -> 1.16 us
    all_gather x4 -> x0, waiting for transfers between devices: 246 us -> none  [prefix_2(): gathered = jax.tree.map(lambda a: lax.all_gather(a, axis), part)]
    another operation x5 -> x4, other arithmetic: 160 us -> 2.39 us  [the longest x1 1.27 us: shards(): grad_value = jnp.stack(parts[slots:], axis=1)]
    dot_general x56 -> x2, matrix products: 103 us -> 6.6 us  [the longest x1 3.7 us: shards(): jnp.dot(grad_out, out_weight.T, preferred_element_type=F32).astype(BF16)]
    pallas_call x0 -> x5, Pallas kernels: none -> 54.2 us  [call(): pl.pallas_call(kernel, grid_spec=pltpu.PrefetchScalarGridSpec(num_scalar_...]
    all_to_all x0 -> x4, starting transfers between devices: none -> 20 us  [exchange(): lax.all_to_all(x, 'ctx', 0, 0, axis_index_groups=group_lists, tiled=True)]
    mul x13 -> x0, other arithmetic: 17.8 us -> none  [the longest x6 9.11 us: causal_conv(): kernel[offset] * padded[offset:offset + length]]
    ppermute x2 -> x5, waiting for transfers between devices: 0.01 us -> 14.1 us  [the longest x1 6.81 us: shards(): lax.ppermute(sent, 'head', [(0, 1), (1, 0)]).astype(F32)]
    while x70 -> x0, local copies, waits for them, and re-layouts: 11.7 us -> none
  transfers between devices with their start and end apart: 7 -> 9, of which waited for: 4 -> 5; matrix products, arithmetic and copies ran while one was open for 25% -> 13% of each run, Pallas kernels for 0% -> 27%
where the time goes in v1:
time: 163 us; the launch traced here: 161 us
  Pallas kernels  54.2 us (33%)
  local copies, waits for them, and re-layouts  34.5 us (21%)
  starting transfers between devices  33.8 us (21%)
  waiting for transfers between devices  24.1 us (15%)
  other arithmetic  7.11 us (4%)
  matrix products  6.6 us (4%)
    pallas_call x5, Pallas kernels, call(): pl.pallas_call(kernel, grid_spec=pltpu.PrefetchScalarGridSpec(num_scalar_...  54.2 us
    unnamed x68, local copies, waits for them, and re-layouts  21.9 us
    all_to_all x4, starting transfers between devices, exchange(): lax.all_to_all(x, 'ctx', 0, 0, axis_index_groups=group_lists, tiled=True)  20 us
    all_to_all x4, waiting for transfers between devices, exchange(): lax.all_to_all(x, 'ctx', 0, 0, axis_index_groups=group_lists, tiled=True)  10.1 us
    ppermute x1, waiting for transfers between devices, shards(): lax.ppermute(sent, 'head', [(0, 1), (1, 0)]).astype(F32)  6.81 us
    ppermute x2, waiting for transfers between devices, across(): return lax.ppermute(last[:, HEAD:], 'ctx', moves)  5.27 us
    ppermute x2, starting transfers between devices, across(): return lax.ppermute(last[:, HEAD:], 'ctx', moves)  5.2 us
    ppermute x1, starting transfers between devices, shards(): lax.ppermute(tail, 'ctx', [(i, i + 1) for i in range(shard_count - 1)])  4.54 us
  transfers between devices with their start and end apart: 9, of which 5 were waited for; matrix products, arithmetic and copies ran while one was open for 13% of the time, Pallas kernels for 27%

profile of v1, /device:TPU:1, one launch (start us, length us, event | category | flops | bytes accessed | tf_op | source)
XLA Modules:
  0.0 161.5 jit_solution(5598779043500134732)
XLA Ops:
  0.6 0.8 slice_bitcast_fusion.1
  1.5 0.8 slice.85
  3.0 4.5 %collective-permute-start = (bf16[3,5,1024]{2,1,0:T(8,128)(2,1)S(1)}, bf16[3,5,1024]{2,1,0:T(8,128)(2,1)S(1)}, u32[]{:S(2)}, u32[]{:S(2)}) collective-permute-start(bf16[3,5,1024]{2,1,0:T(8,128)(2,1)S(1)} %pad_maximum_fusion.3), channel_id=1, source_target_pairs={{0,2},{2,4},{4,6},{6,8},{8,10},{10,12},{12,14},{14,16},{16,18},{18... | collective-permute-start | bytes 92168 | tf_op jit(solution)/shard_map/ppermute | solution.py:373
  7.6 2.1 %fusion.13 = (bf16[128,1,1024]{2,1,0:T(2,128)(2,1)S(1)}, bf16[128,1,1024]{2,1,0:T(2,128)(2,1)S(1)}) fusion(bf16[128,2,1024]{2,1,0:T(2,128)(2,1)} %param.11), kind=kLoop, calls=%fused_computation.43 | loop fusion | bytes 1048576 | tf_op jit(solution)/shard_map/slice | solution.py:384
  14.6 0.8 bitcast_dynamic-update-slice_fusion.1
  17.5 4.0 %all-to-all-start.1 = ((bf16[8,544,128]{2,1,0:T(8,128)(2,1)}), bf16[8,544,128]{2,1,0:T(8,128)(2,1)S(1)}, u32[]{:S(2)}, u32[]{:S(2)}) async-start(bf16[8,544,128]{2,1,0:T(8,128)(2,1)} %constant_dynamic-update-slice_fusion), calls=%async_computation.1 | async-start | bytes 2228224 | tf_op jit(solution)/shard_map/all_to_all | solution.py:365
  21.9 3.7 %convolution_convert_fusion = bf16[128,1024]{1,0:T(8,128)(2,1)S(1)} fusion(bf16[128,2048]{1,0:T(8,128)(2,1)S(1)} %copy-done, bf16[1024,2048]{1,0:T(8,128)(2,1)} %param.18), kind=kOutput, calls=%fused_computation.2 | convolution fusion | flops 537001984 | bytes 4980736 | tf_op jit(solution)/shard_map/dot_general | solution.py:390
  26.5 0.8 fusion.3
  27.4 8.5 %all-to-all-done.1.kv_ref = bf16[8,544,128]{2,1,0:T(8,128)(2,1)S(1)} async-done(((bf16[8,544,128]{2,1,0:T(8,128)(2,1)}), bf16[8,544,128]{2,1,0:T(8,128)(2,1)S(1)}, u32[]{:S(2)}, u32[]{:S(2)}) %all-to-all-start.1) | async-done | bytes 1114144 | tf_op jit(solution)/shard_map/all_to_all | solution.py:365
  35.9 4.3 %all-to-all-start = ((bf16[8,272,128]{2,1,0:T(8,128)(2,1)}), bf16[8,272,128]{2,1,0:T(8,128)(2,1)S(1)}, u32[]{:S(2)}, u32[]{:S(2)}) async-start(bf16[8,272,128]{2,1,0:T(8,128)(2,1)} %fusion.3), calls=%async_computation | async-start | bytes 1114112 | tf_op jit(solution)/shard_map/all_to_all | solution.py:365
  40.2 26.0 %shard_map.137 = (f32[8,256,128]{2,1,0:T(8,128)S(1)}, f32[8,256,256]{2,1,0:T(8,128)S(1)}, f32[8,256,256]{2,1,0:T(8,128)}, f32[8,128,128]{2,1,0:T(8,128)S(1)}, f3...) custom-call(s32[1]{0:T(128)} %bitcast.hid, bf16[8,544,128]{2,1,0:T(8,128)(2,1)S(1)} %all-to-all-done.1.kv_ref, ...), custom_call_target="tpu_custom_call" | custom-call | flops 12884901888 | bytes 8159232 | tf_op jit(solution)/shard_map/pallas_call | solution.py:325
  66.2 1.3 copy-done.3
  67.5 1.0 copy-done.14
  68.5 0.8 copy-done.16
  69.3 3.9 %collective-permute-start.1 = (f32[128,128]{1,0:T(8,128)S(1)}, f32[128,128]{1,0:T(8,128)S(1)}, u32[]{:S(2)}, u32[]{:S(2)}) collective-permute-start(f32[128,128]{1,0:T(8,128)S(1)} %slice.93), channel_id=1, source_target_pairs={{0,16},{2,18},{4,20},{6,22},{8,24},{10,26},{12,28},{14,30},{1,17},... | collective-permute-start | bytes 196616 | tf_op jit(solution)/shard_map/ppermute | solution.py:431
  73.2 4.2 %shard_map.138 = (f32[8,128,128]{2,1,0:T(8,128)S(1)}, f32[8,128,256]{2,1,0:T(8,128)S(1)}, f32[8,128,128]{2,1,0:T(8,128)S(1)}, f32[8,128,128]{2,1,0:T(8,128)S(1)}) custom-call(s32[1]{0:T(128)} %bitcast.hid, bf16[8,272,128]{2,1,0:T(8,128)(2,1)S(1)} %all-to-all-done.qg_ref, f32[24,1024]{1,0:T(8,128)S(1)} %concatenate.20.wts_ref, ...), custom_call_target="tpu_custom_call" | custom-call | flops 805306368 | bytes 6422528 | tf_op jit(solution)/shard_map/pallas_call | solution.py:325
  77.5 1.0 copy-done.13
  78.4 2.8 %shard_map.139 = (bf16[8,128,128]{2,1,0:T(8,128)(2,1)S(1)}, f32[8,128,128]{2,1,0:T(8,128)S(1)}, f32[8,128,128]{2,1,0:T(8,128)S(1)}, f32[8,128,256]{2,1,0:T(8,128)S(1)}, f32[128,256]{1,0:T(8,128)S(1)}) custom-call(s32[1]{0:T(128)} %bitcast.hid, bf16[8,272,128]{2,1,0:T(8,128)(2,1)S(1)} %all-to-all-done.qg_ref, f32[24,1024]{1,0:T(8,128)S(1)} %concatenate.20.wts_ref, ...), custom_call_target="tpu_custom_call" | custom-call | flops 536870912 | bytes 5832704 | tf_op jit(solution)/shard_map/pallas_call | solution.py:325
  81.3 7.4 %shard_map.140 = (f32[8,256,128]{2,1,0:T(8,128)S(1)}, f32[8,256,128]{2,1,0:T(8,128)S(1)}, f32[8,256,128]{2,1,0:T(8,128)S(1)}, bf16[8,144,128]{2,1,0:T(8,128)(2,1)S(1)}) custom-call(s32[1]{0:T(128)} %bitcast.hid, bf16[8,272,128]{2,1,0:T(8,128)(2,1)S(1)} %all-to-all-done.qg_ref, f32[24,1024]{1,0:T(8,128)S(1)} %concatenate.20.wts_ref, ...), custom_call_target="tpu_custom_call" | custom-call | flops 1073741824 | bytes 9863168 | tf_op jit(solution)/shard_map/pallas_call | solution.py:325
  88.8 1.0 copy-done.7
  89.7 1.0 copy-done.9
  90.7 1.0 copy-done.11
  91.7 0.8 pad_maximum_fusion.2
  92.5 4.5 %all-to-all-start.2 = ((bf16[8,272,128]{2,1,0:T(8,128)(2,1)}), bf16[8,272,128]{2,1,0:T(8,128)(2,1)S(1)}, u32[]{:S(2)}, u32[]{:S(2)}) async-start(bf16[8,272,128]{2,1,0:T(8,128)(2,1)} %pad_maximum_fusion.2), calls=%async_computation.2 | async-start | bytes 1114112 | tf_op jit(solution)/shard_map/all_to_all | solution.py:365
  97.0 1.3 collective-permute-start.3
  98.3 5.3 %collective-permute-done.3.end_ref = f32[128,128]{1,0:T(8,128)S(1)} collective-permute-done((f32[128,128]{1,0:T(8,128)S(1)}, f32[128,128]{1,0:T(8,128)S(1)}, u32[]{:S(2)}, u32[]{:S(2)}) %collective-permute-start.3) | collective-permute-done | bytes 65568 | tf_op jit(solution)/shard_map/ppermute | solution.py:431
  103.6 1.2 copy-done.6
  104.8 1.2 copy-done.8
  106.0 1.2 copy-done.10
  107.3 1.2 copy-done.12
  108.5 13.7 %shard_map.141 = bf16[8,560,128]{2,1,0:T(8,128)(2,1)} custom-call(s32[1]{0:T(128)} %bitcast.hid, bf16[8,544,128]{2,1,0:T(8,128)(2,1)} %copy-done.4, f32[24,1024]{1,0:T(8,128)S(1)} %concatenate.20.wts_ref, f32[128,128]{1,0:T(8,128)S(1)} %collective-permute-done.3.end_ref, f32[8,128,256]{2,1,0:T(8,128)S(1)} %copy-done.6, f32[8,256,128]{2,1,0:T(8,128)S(1)} %copy-done.2, ...), custom_call_target="tpu_custom_call" | custom-call | flops 2147483648 | bytes 10289152 | tf_op jit(solution)/shard_map/pallas_call | solution.py:325
  122.2 7.2 %all-to-all-start.3 = ((bf16[8,560,128]{2,1,0:T(8,128)(2,1)}), bf16[8,560,128]{2,1,0:T(8,128)(2,1)S(1)}, u32[]{:S(2)}, u32[]{:S(2)}) async-start(bf16[8,560,128]{2,1,0:T(8,128)(2,1)} %shard_map.141), calls=%async_computation.3 | async-start | bytes 2293760 | tf_op jit(solution)/shard_map/all_to_all | solution.py:365
  129.7 2.9 %fusion = f32[2,64,2048]{2,1,0:T(8,128)S(1)} fusion(bf16[2,64,1024]{2,1,0:T(8,128)(2,1)S(1)} %dot_general.9, bf16[1024,2048]{1,0:T(8,128)(2,1)} %param.18), kind=kOutput, calls=%fused_computation | convolution fusion | flops 536870912 | bytes 5505024 | tf_op jit(solution)/shard_map/dot_general | solution.py:490
  132.7 1.3 collective-permute-start.2
  134.0 6.8 %collective-permute-done.2 = bf16[64,2048]{1,0:T(8,128)(2,1)} collective-permute-done((bf16[64,2048]{1,0:T(8,128)(2,1)S(1)}, bf16[64,2048]{1,0:T(8,128)(2,1)}, u32[]{:S(2)}, u32[]{:S(2)}) %collective-permute-start.2) | collective-permute-done | bytes 262176 | tf_op jit(solution)/shard_map/ppermute | solution.py:498
  140.8 1.7 %fusion.4 = bf16[64,2048]{1,0:T(8,128)(2,1)} fusion(bf16[64,2048]{1,0:T(8,128)(2,1)} %collective-permute-done.2, f32[2,64,2048]{2,1,0:T(8,128)S(1)} %fusion, s32[]{:T(128)S(6)} %select_n.15), kind=kLoop, calls=%fused_computation.10 | loop fusion | flops 393216 | bytes 1048580 | tf_op jit(solution)/shard_map/convert_element_type | solution.py:498
  142.5 1.6 all-to-all-done.3
  144.3 2.8 %collective-permute-start.4 = (bf16[8,15,128]{2,1,0:T(8,128)(2,1)S(1)}, bf16[8,15,128]{2,1,0:T(8,128)(2,1)S(1)}, u32[]{:S(2)}, u32[]{:S(2)}) collective-permute-start(bf16[8,15,128]{2,1,0:T(8,128)(2,1)S(1)} %concatenate.23), channel_id=1, source_target_pairs={{2,0},{4,2},{6,4},{8,6},{10,8},{12,10},{14,12},{16,14},{18,16},{20... | collective-permute-start | bytes 92168 | tf_op jit(solution)/shard_map/ppermute | solution.py:523
  147.7 2.0 %collective-permute-done.4 = bf16[8,15,128]{2,1,0:T(8,128)(2,1)S(1)} collective-permute-done((bf16[8,15,128]{2,1,0:T(8,128)(2,1)S(1)}, bf16[8,15,128]{2,1,0:T(8,128)(2,1)S(1)}, u32[]{:S(2)}, u32[]{:S(2)}) %collective-permute-start.4) | collective-permute-done | bytes 30752 | tf_op jit(solution)/shard_map/ppermute | solution.py:523
  149.7 1.3 add_bitcast_fusion.1
  151.0 2.1 %copy.68 = f32[128,8,128]{0,2,1:T(8,128)} copy(f32[128,8,128]{2,0,1:T(8,128)} %get-tuple-element.53) | data formatting | bytes 1048576 | tf_op jit(solution)/shard_map/transpose | solution.py:527
  153.1 1.0 copy.69
  154.1 1.3 pad_maximum_fusion.1
  155.4 1.3 copy.72
  156.9 1.0 copy.67
  157.9 1.1 pad_maximum_fusion
  159.0 1.3 copy.71
  160.5 1.0 copy.70
  (95 shorter events, 10.5 us)
Async XLA Ops:
  0.6 21.2 %copy-start = (bf16[128,2048]{1,0:T(8,128)(2,1)S(1)}, bf16[128,2048]{1,0:T(8,128)(2,1)}, u32[]{:S(2)}) copy-start(bf16[128,2048]{1,0:T(8,128)(2,1)} %param.19) | copy-start | bytes 1572868
  1.4 8.3 %copy-start.18 = (bf16[128,2,1024]{2,1,0:T(2,128)(2,1)S(1)}, bf16[128,2,1024]{2,1,0:T(2,128)(2,1)}, u32[]{:S(2)}) copy-start(bf16[128,2,1024]{2,1,0:T(2,128)(2,1)} %param.12) | copy-start | bytes 1572868
  3.0 13.7 %collective-permute-start = (bf16[3,5,1024]{2,1,0:T(8,128)(2,1)S(1)}, bf16[3,5,1024]{2,1,0:T(8,128)(2,1)S(1)}, u32[]{:S(2)}, u32[]{:S(2)}) collective-permute-start(bf16[3,5,1024]{2,1,0:T(8,128)(2,1)S(1)} %pad_maximum_fusion.3), channel_id=1, source_target_pairs={{0,2},{2,4},{4,6},{6,8},{8,10},{10,12},{12,14},{14,16},{16,18},{18... | collective-permute-start | bytes 92168 | tf_op jit(solution)/shard_map/ppermute | solution.py:373
  9.7 0.8 copy-start.25
  17.5 4.1 %copy-start.21 = (bf16[128,1024]{1,0:T(8,128)(2,1)S(1)}, bf16[128,1024]{1,0:T(8,128)(2,1)}, u32[]{:S(2)}) copy-start(bf16[128,1024]{1,0:T(8,128)(2,1)} %param.10) | copy-start | bytes 786436
  17.5 4.2 %copy-start.22 = (f32[4,2,1024]{2,1,0:T(2,128)S(1)}, f32[4,2,1024]{2,1,0:T(2,128)}, u32[]{:S(2)}) copy-start(f32[4,2,1024]{2,1,0:T(2,128)} %param.15) | copy-start | bytes 98308
  17.5 4.3 %copy-start.23 = (f32[4,2,1024]{2,1,0:T(2,128)S(1)}, f32[4,2,1024]{2,1,0:T(2,128)}, u32[]{:S(2)}) copy-start(f32[4,2,1024]{2,1,0:T(2,128)} %param.16) | copy-start | bytes 98308
  17.5 18.3 %all-to-all-start.1 = ((bf16[8,544,128]{2,1,0:T(8,128)(2,1)}), bf16[8,544,128]{2,1,0:T(8,128)(2,1)S(1)}, u32[]{:S(2)}, u32[]{:S(2)}) async-start(bf16[8,544,128]{2,1,0:T(8,128)(2,1)} %constant_dynamic-update-slice_fusion), calls=%async_computation.1 | async-start | bytes 2228224 | tf_op jit(solution)/shard_map/all_to_all | solution.py:365
  25.6 0.7 copy-start.24
  25.6 0.7 copy-start.26
  35.9 30.3 %copy-start.4 = (bf16[8,544,128]{2,1,0:T(8,128)(2,1)}, bf16[8,544,128]{2,1,0:T(8,128)(2,1)S(1)}, u32[]{:S(2)}) copy-start(bf16[8,544,128]{2,1,0:T(8,128)(2,1)S(1)} %all-to-all-done.1.kv_ref) | copy-start | bytes 3342340
  35.9 37.3 %all-to-all-start = ((bf16[8,272,128]{2,1,0:T(8,128)(2,1)}), bf16[8,272,128]{2,1,0:T(8,128)(2,1)S(1)}, u32[]{:S(2)}, u32[]{:S(2)}) async-start(bf16[8,272,128]{2,1,0:T(8,128)(2,1)} %fusion.3), calls=%async_computation | async-start | bytes 1114112 | tf_op jit(solution)/shard_map/all_to_all | solution.py:365
  66.2 1.3 copy-start.3
  67.5 1.0 copy-start.14
  68.5 0.8 copy-start.16
  69.3 8.2 %copy-start.1 = (f32[8,256,128]{2,1,0:T(8,128)}, f32[8,256,128]{2,1,0:T(8,128)S(1)}, u32[]{:S(2)}) copy-start(f32[8,256,128]{2,1,0:T(8,128)S(1)} %get-tuple-element.26.kn_ref) | copy-start | bytes 3145732
  69.3 9.2 %collective-permute-start.1 = (f32[128,128]{1,0:T(8,128)S(1)}, f32[128,128]{1,0:T(8,128)S(1)}, u32[]{:S(2)}, u32[]{:S(2)}) collective-permute-start(f32[128,128]{1,0:T(8,128)S(1)} %slice.93), channel_id=1, source_target_pairs={{0,16},{2,18},{4,20},{6,22},{8,24},{10,26},{12,28},{14,30},{1,17},... | collective-permute-start | bytes 196616 | tf_op jit(solution)/shard_map/ppermute | solution.py:431
  73.2 5.2 %copy-start.15 = (f32[8,128,256]{2,1,0:T(8,128)S(1)}, f32[8,128,256]{2,1,0:T(8,128)}, u32[]{:S(2)}) copy-start(f32[8,128,256]{2,1,0:T(8,128)} %copy-done.14) | copy-start | bytes 3145732
  73.2 5.2 %copy-start.17 = (f32[8,128,128]{2,1,0:T(8,128)S(1)}, f32[8,128,128]{2,1,0:T(8,128)}, u32[]{:S(2)}) copy-start(f32[8,128,128]{2,1,0:T(8,128)} %copy-done.16) | copy-start | bytes 1572868
  77.5 1.0 copy-start.13
  81.3 7.5 %copy-start.5 = (f32[8,128,256]{2,1,0:T(8,128)}, f32[8,128,256]{2,1,0:T(8,128)S(1)}, u32[]{:S(2)}) copy-start(f32[8,128,256]{2,1,0:T(8,128)S(1)} %get-tuple-element.38.mb_ref) | copy-start | bytes 3145732
  88.7 1.0 copy-start.7
  89.7 1.0 copy-start.9
  90.7 1.0 copy-start.11
  91.7 11.9 %copy-start.2 = (f32[8,256,128]{2,1,0:T(8,128)S(1)}, f32[8,256,128]{2,1,0:T(8,128)}, u32[]{:S(2)}) copy-start(f32[8,256,128]{2,1,0:T(8,128)} %copy-done.1) | copy-start | bytes 3145732
  92.5 29.7 %all-to-all-start.2 = ((bf16[8,272,128]{2,1,0:T(8,128)(2,1)}), bf16[8,272,128]{2,1,0:T(8,128)(2,1)S(1)}, u32[]{:S(2)}, u32[]{:S(2)}) async-start(bf16[8,272,128]{2,1,0:T(8,128)(2,1)} %pad_maximum_fusion.2), calls=%async_computation.2 | async-start | bytes 1114112 | tf_op jit(solution)/shard_map/all_to_all | solution.py:365
  97.0 6.6 %collective-permute-start.3 = (f32[128,128]{1,0:T(8,128)S(1)}, f32[128,128]{1,0:T(8,128)S(1)}, u32[]{:S(2)}, u32[]{:S(2)}) collective-permute-start(f32[128,128]{1,0:T(8,128)S(1)} %slice.97), channel_id=1, source_target_pairs={{16,0},{18,2},{20,4},{22,6},{24,8},{26,10},{28,12},{30,14},{17,1},... | collective-permute-start | bytes 196616 | tf_op jit(solution)/shard_map/ppermute | solution.py:431
  103.6 1.2 copy-start.6
  104.8 1.2 copy-start.8
  106.0 1.2 copy-start.10
  107.3 1.2 copy-start.12
  122.2 21.8 %all-to-all-start.3 = ((bf16[8,560,128]{2,1,0:T(8,128)(2,1)}), bf16[8,560,128]{2,1,0:T(8,128)(2,1)S(1)}, u32[]{:S(2)}, u32[]{:S(2)}) async-start(bf16[8,560,128]{2,1,0:T(8,128)(2,1)} %shard_map.141), calls=%async_computation.3 | async-start | bytes 2293760 | tf_op jit(solution)/shard_map/all_to_all | solution.py:365
  132.7 8.1 %collective-permute-start.2 = (bf16[64,2048]{1,0:T(8,128)(2,1)S(1)}, bf16[64,2048]{1,0:T(8,128)(2,1)}, u32[]{:S(2)}, u32[]{:S(2)}) collective-permute-start(bf16[64,2048]{1,0:T(8,128)(2,1)S(1)} %fusion.5), channel_id=1, source_target_pairs={{0,1},{1,0},{2,3},{3,2},{4,5},{5,4},{6,7},{7,6},{8,9},{9,8},{10,11... | collective-permute-start | bytes 786440 | tf_op jit(solution)/shard_map/ppermute | solution.py:498
  144.3 5.4 %collective-permute-start.4 = (bf16[8,15,128]{2,1,0:T(8,128)(2,1)S(1)}, bf16[8,15,128]{2,1,0:T(8,128)(2,1)S(1)}, u32[]{:S(2)}, u32[]{:S(2)}) collective-permute-start(bf16[8,15,128]{2,1,0:T(8,128)(2,1)S(1)} %concatenate.23), channel_id=1, source_target_pairs={{2,0},{4,2},{6,4},{8,6},{10,8},{12,10},{14,12},{16,14},{18,16},{20... | collective-permute-start | bytes 92168 | tf_op jit(solution)/shard_map/ppermute | solution.py:523
  151.0 2.1 %copy-start.20 = (f32[128,8,128]{2,0,1:T(8,128)S(1)}, f32[128,8,128]{2,0,1:T(8,128)}, u32[]{:S(2)}) copy-start(f32[128,8,128]{2,0,1:T(8,128)} %get-tuple-element.54) | copy-start | bytes 1572868
  155.4 1.3 copy-start.19

commit v2 on v1

v2 whole, which is shorter than its diff:
```python
import functools

import jax
import jax.numpy as jnp
from jax import lax
from jax.experimental import pallas as pl
from jax.experimental.pallas import tpu as pltpu
from jax.sharding import PartitionSpec as P

HEAD = 128
TAPS = 4
RIM = TAPS - 1
EDGE = 16
EPS = 1e-06
F32 = jnp.float32
BF16 = jnp.bfloat16

ROWS_COLS = (((1,), (0,)), ((), ()))
ROWS_ROWS = (((1,), (1,)), ((), ()))
COLS_COLS = (((0,), (0,)), ((), ()))


def two(x):
    high = x.astype(BF16)
    return high, (x - high.astype(F32)).astype(BF16)


def dot(a, b, dims):
    return lax.dot_general(a, b, dims, preferred_element_type=F32)


def mm(left, right, dims=ROWS_COLS):
    (ah, al), (bh, bl) = left, right
    ka, kb = dims[0][0][0], dims[0][1][0]
    nb = 1 - kb
    depth, cols = ah.shape[ka], bh.shape[nb]
    if depth <= HEAD:
        a = jnp.concatenate([ah, al], axis=ka)
        high, low = jnp.concatenate([bh, bh], axis=kb), jnp.concatenate([bl, bl], axis=kb)
        if cols <= HEAD:
            out = dot(a, jnp.concatenate([high, low], axis=nb), dims)
            return out[:, :cols] + out[:, cols:]
        return dot(a, high, dims) + dot(a, low, dims)
    if cols <= HEAD:
        out = dot(ah, jnp.concatenate([bh, bl], axis=nb), dims)
        return out[:, :cols] + out[:, cols:] + dot(al, bh, dims)
    return dot(ah, bh, dims) + dot(ah, bl, dims) + dot(al, bh, dims)


def grid_of(rows, cols):
    return lax.broadcasted_iota(jnp.int32, (rows, cols), 0), lax.broadcasted_iota(jnp.int32, (rows, cols), 1)


def before(rows):
    r, c = grid_of(rows, rows)
    return c < r


def level_pairs(rows, level):
    r, c = grid_of(rows, rows)
    return ((r >> (level + 1)) == (c >> (level + 1))) & (((r >> level) & 1) == 1) & (((c >> level) & 1) == 0)


def visible(tokens, slots):
    t, c = grid_of(tokens, tokens * slots)
    return c < slots * (t + 1)


def times(pattern, x):
    if pattern.shape[0] == 1:
        return pattern * x
    return (x.reshape(-1, 8, HEAD) * pattern[None]).reshape(x.shape)


def conv_rows(x, edge, taps, pad, stride):
    rows = x.shape[0]
    pad[pl.ds(0, EDGE), :] = edge
    pad[pl.ds(EDGE, rows), :] = x
    total = None
    for i in range(TAPS):
        part = times(taps[i], pad[pl.ds(EDGE - stride * (RIM - i), rows), :])
        total = part if total is None else total + part
    return total


def conv_back(grad, taps, pad, stride):
    rows = grad.shape[0]
    pad[pl.ds(8, 8), :] = jnp.zeros((8, HEAD), F32)
    pad[pl.ds(EDGE, rows), :] = grad
    pad[pl.ds(EDGE + rows, 8), :] = jnp.zeros((8, HEAD), F32)
    inner, rim = None, None
    for i in range(TAPS):
        part = times(taps[i], pad[pl.ds(EDGE + stride * (RIM - i), rows), :])
        edge = times(taps[i], pad[pl.ds(8 + stride * (RIM - i), 8), :])
        inner = part if inner is None else inner + part
        rim = edge if rim is None else rim + edge
    return inner, rim


def sigmoid(x):
    return 1.0 / (1.0 + jnp.exp(-x))


def unit(values):
    scale = lax.rsqrt(jnp.sum(values * values, axis=-1, keepdims=True) + EPS)
    return values * scale, scale


def beta_rows(tile, slots):
    return [tile[3 * j : 3 * j + 1] + tile[3 * j + 1 : 3 * j + 2] + tile[3 * j + 2 : 3 * j + 3] for j in range(slots)]


def places(tokens, slots, j):
    r, t = grid_of(tokens * slots, tokens)
    return r == slots * t + j


def column(rows, tokens, slots):
    spread = jnp.zeros((tokens * slots, tokens), F32)
    for j in range(slots):
        spread = jnp.where(places(tokens, slots, j), rows[j], spread)
    return jnp.sum(spread, axis=1, keepdims=True)


def slot_taps(wts, kind):
    return [wts[8 * (TAPS * kind + i) : 8 * (TAPS * kind + i + 1)] for i in range(TAPS)]


def query_taps(wts):
    return [wts[16 * TAPS + i : 16 * TAPS + i + 1] for i in range(TAPS)]


def gain_row(wts):
    return wts[17 * TAPS : 17 * TAPS + 1]


def edges(ref, first, rows, per, tail, halo):
    @pl.when(pl.program_id(0) == 0)
    def _():
        halo[...] = tail

    found = [halo[...]] + [ref[n, pl.ds(first + rows - EDGE, EDGE), :].astype(F32) for n in range(per - 1)]
    halo[...] = ref[per - 1, pl.ds(first + rows - EDGE, EDGE), :].astype(F32)
    return found


def inverse_kernel(per, tokens, slots, hid, kb_ref, tail_ref, wts_ref, kn_ref, ti_ref, pad, halo):
    rows = tokens * slots
    taps = slot_taps(wts_ref[...], 0)
    tops = edges(kb_ref, 0, rows, per, tail_ref[pl.ds(0, EDGE), :].astype(F32), halo)
    order = before(rows)
    blocks = rows // HEAD
    grams = []
    for n in range(per):
        s = conv_rows(kb_ref[n, pl.ds(0, rows), :].astype(F32), tops[n], taps, pad.at[n], slots)
        k = unit(s * sigmoid(s))[0]
        kn_ref[n] = k
        betas = beta_rows(kb_ref[n, pl.ds(rows, EDGE), :].astype(F32), slots)
        strength = 2.0 * sigmoid(column(betas, tokens, slots))
        k2 = two(k)
        grams.append(jnp.where(order, mm(k2, k2, ROWS_ROWS) * strength, 0.0))
    r, c = grid_of(HEAD, HEAD)
    eye = (r == c).astype(F32)
    zero = jnp.zeros((HEAD, HEAD), BF16)
    diagonal = [
        gram[b * HEAD : (b + 1) * HEAD, b * HEAD : (b + 1) * HEAD] for gram in grams for b in range(blocks)
    ]
    systems = [two(x) for x in diagonal]
    pairs = level_pairs(HEAD, 0)
    inverse = [eye - jnp.where(pairs, x, 0.0) for x in diagonal]
    level = 1
    while (1 << level) < HEAD:
        pairs = level_pairs(HEAD, level)
        split = [two(x) for x in inverse]
        crossed = [mm(tuple(jnp.where(pairs, p, zero) for p in s), x) for s, x in zip(systems, split)]
        inverse = [x - mm(s, two(y)) for x, s, y in zip(inverse, split, crossed)]
        level += 1
    for n in range(per):
        done = inverse[n * blocks : (n + 1) * blocks]
        size = HEAD
        while len(done) > 1:
            merged = []
            for b in range(0, len(done), 2):
                top, low = done[b], done[b + 1]
                cross = grams[n][(b + 1) * size : (b + 2) * size, b * size : (b + 1) * size]
                cross = mm(two(low), two(mm(two(cross), two(top))))
                merged.append(
                    jnp.concatenate(
                        [
                            jnp.concatenate([top, jnp.zeros_like(top)], axis=1),
                            jnp.concatenate([-cross, low], axis=1),
                        ],
                        axis=0,
                    )
                )
            done = merged
            size *= 2
        ti_ref[n] = done[0]


def maps_kernel(
    per, tokens, slots, hid, vq_ref, beta_ref, tail_ref, wts_ref, kn_ref, ti_ref,
    wu_ref, a_ref, mc_ref, end_ref, pad, halo, carry,
):
    rows = tokens * slots
    taps = slot_taps(wts_ref[...], 1)
    ir, ic = grid_of(HEAD, 2 * HEAD)

    @pl.when(pl.program_id(0) == 0)
    def _():
        carry[...] = (ir == ic).astype(F32)

    tops = edges(vq_ref, 0, rows, per, tail_ref[pl.ds(EDGE, EDGE), :].astype(F32), halo)
    maps = []
    for n in range(per):
        s = conv_rows(vq_ref[n, pl.ds(0, rows), :].astype(F32), tops[n], taps, pad.at[n], slots)
        v = s * sigmoid(s)
        betas = beta_rows(beta_ref[n].astype(F32), slots)
        strength = 2.0 * sigmoid(column(betas, tokens, slots))
        k = kn_ref[n]
        wu = mm(two(ti_ref[n]), two(strength * jnp.concatenate([k, v], axis=1)))
        wu_ref[n] = wu
        maps.append(mm(two(k), two(wu), COLS_COLS))
    state = carry[...]
    for n in range(per):
        mc_ref[n] = state
        a = (ir == ic)[:, :HEAD].astype(F32) - maps[n][:, :HEAD]
        a_ref[n] = a
        moved = mm(two(a), two(state))
        state = jnp.where(ic < HEAD, moved, moved + maps[n])
    carry[...] = state
    end_ref[...] = state


def queries_kernel(
    per, tokens, slots, hid, vq_ref, tail_ref, wts_ref, kn_ref, wu_ref, q_ref, sc_ref, qm_ref, ol_ref, pad, halo
):
    rows = tokens * slots
    taps = query_taps(wts_ref[...])
    tops = edges(vq_ref, rows, tokens, per, tail_ref[pl.ds(2 * EDGE, EDGE), :].astype(F32), halo)
    seen = visible(tokens, slots)
    for n in range(per):
        s = conv_rows(vq_ref[n, pl.ds(rows, tokens), :].astype(F32), tops[n], taps, pad.at[n], 1)
        q = unit(s * sigmoid(s))[0]
        scores = jnp.where(seen, mm(two(q), two(kn_ref[n]), ROWS_ROWS), 0.0)
        mapped = mm(two(scores), two(wu_ref[n]))
        q_ref[n] = q
        sc_ref[n] = scores
        qm_ref[n] = q - mapped[:, :HEAD]
        ol_ref[n] = mapped[:, HEAD:]


def outs_kernel(
    count, tokens, slots, hid, vq_ref, wts_ref, start_ref, mc_ref, qm_ref, ol_ref, a_ref,
    nm_ref, dr_ref, st_ref, mb_ref, end_ref,
):
    rows = tokens * slots
    gain = gain_row(wts_ref[...])
    start = two(start_ref[...])
    states = [
        mm(two(mc_ref[n, :, pl.ds(0, HEAD)]), start) + mc_ref[n, :, pl.ds(HEAD, HEAD)] for n in range(count)
    ]
    mapped = [two(qm_ref[n]) for n in range(count)]
    raws = [mm(mapped[n], two(states[n])) + ol_ref[n] for n in range(count)]
    local = []
    for n in range(count):
        st_ref[n] = states[n]
        raw = raws[n]
        scale = lax.rsqrt(jnp.mean(raw * raw, axis=-1, keepdims=True) + EPS)
        hat = raw * scale
        nm_ref[n] = (hat * gain).astype(BF16)
        dn = vq_ref[n, pl.ds(rows + tokens, tokens), :].astype(F32) * gain
        dr = scale * (dn - hat * jnp.mean(dn * hat, axis=-1, keepdims=True))
        dr_ref[n] = dr
        local.append(mm(mapped[n], two(dr), COLS_COLS))
    ir, ic = grid_of(HEAD, 2 * HEAD)
    state = (ir == ic).astype(F32)
    for n in range(count - 1, -1, -1):
        mb_ref[n] = state
        moved = mm(two(a_ref[n]), two(state), COLS_COLS)
        state = moved + jnp.concatenate([jnp.zeros((HEAD, HEAD), F32), local[n]], axis=1)
    end_ref[...] = state


def query_grads_kernel(
    per, tokens, slots, hid, vq_ref, tail_ref, wts_ref, kn_ref, wu_ref, q_ref, sc_ref, dr_ref, st_ref,
    d_ref, dk_ref, dd_ref, gq_ref, pad, halo,
):
    rows = tokens * slots
    taps = query_taps(wts_ref[...])
    tops = edges(vq_ref, rows, tokens, per, tail_ref[pl.ds(2 * EDGE, EDGE), :].astype(F32), halo)
    seen = visible(tokens, slots)
    for n in range(per):
        state, dr, k2 = two(st_ref[n]), two(dr_ref[n]), two(kn_ref[n])
        d = wu_ref[n, :, pl.ds(HEAD, HEAD)] - mm(two(wu_ref[n, :, pl.ds(0, HEAD)]), state)
        d_ref[n] = d
        ds = two(jnp.where(seen, mm(dr, two(d), ROWS_ROWS), 0.0))
        dq = mm(dr, state, ROWS_ROWS) + mm(ds, k2)
        dk_ref[n] = mm(ds, two(q_ref[n]), COLS_COLS)
        dd_ref[n] = mm(two(sc_ref[n]), dr, COLS_COLS)
        s = conv_rows(vq_ref[n, pl.ds(rows, tokens), :].astype(F32), tops[n], taps, pad.at[n], 1)
        sg = sigmoid(s)
        q, scale = unit(s * sg)
        dc = scale * (dq - q * jnp.sum(q * dq, axis=-1, keepdims=True))
        inner, rim = conv_back(dc * sg * (1.0 + s * (1.0 - sg)), taps, pad.at[n], 1)
        gq_ref[n, pl.ds(0, tokens), :] = inner.astype(BF16)
        gq_ref[n, pl.ds(tokens, EDGE), :] = jnp.concatenate([rim, jnp.zeros((8, HEAD), F32)], axis=0).astype(BF16)


def value_grads_kernel(
    per, tokens, slots, hid, vq_ref, beta_ref, tail_ref, wts_ref, end_ref, mb_ref, kn_ref, ti_ref, d_ref, dd_ref,
    g_ref, de_ref, gv_ref, pad, halo,
):
    rows = tokens * slots
    taps = slot_taps(wts_ref[...], 1)
    tops = edges(vq_ref, 0, rows, per, tail_ref[pl.ds(EDGE, EDGE), :].astype(F32), halo)
    end = two(end_ref[...])
    for n in range(per):
        g = mm(two(mb_ref[n, :, pl.ds(0, HEAD)]), end) + mb_ref[n, :, pl.ds(HEAD, HEAD)]
        g_ref[n] = g
        dd = dd_ref[n] + mm(two(kn_ref[n]), two(g))
        y = mm(two(ti_ref[n]), two(dd), COLS_COLS)
        betas = beta_rows(beta_ref[n].astype(F32), slots)
        de = 2.0 * sigmoid(column(betas, tokens, slots)) * y
        de_ref[n] = de
        along = jnp.sum(y * d_ref[n], axis=1, keepdims=True)
        marks = []
        for j in range(slots):
            gb = jnp.sum(jnp.where(places(tokens, slots, j), along, 0.0), axis=0, keepdims=True) * sigmoid(-betas[j])
            high = gb.astype(BF16).astype(F32)
            marks += [high, gb - high]
        marks.append(jnp.zeros((EDGE - 2 * slots, tokens), F32))
        s = conv_rows(vq_ref[n, pl.ds(0, rows), :].astype(F32), tops[n], taps, pad.at[n], slots)
        sg = sigmoid(s)
        inner, rim = conv_back(de * sg * (1.0 + s * (1.0 - sg)), taps, pad.at[n], slots)
        gv_ref[n, pl.ds(0, rows), :] = inner.astype(BF16)
        gv_ref[n, pl.ds(rows, EDGE), :] = jnp.concatenate(marks, axis=0).astype(BF16)
        gv_ref[n, pl.ds(rows + EDGE, EDGE), :] = jnp.concatenate([rim, jnp.zeros((8, HEAD), F32)], axis=0).astype(BF16)


def key_grads_kernel(
    per, tokens, slots, hid, kb_ref, tail_ref, wts_ref, kn_ref, d_ref, dk_ref, de_ref, st_ref, g_ref,
    gk_ref, pad, halo,
):
    rows = tokens * slots
    taps = slot_taps(wts_ref[...], 0)
    tops = edges(kb_ref, 0, rows, per, tail_ref[pl.ds(0, EDGE), :].astype(F32), halo)
    order = before(rows)
    for n in range(per):
        k = kn_ref[n]
        k2, d2, de2 = two(k), two(d_ref[n]), two(de_ref[n])
        dgram = jnp.where(order, mm(de2, d2, ROWS_ROWS), 0.0)
        dk = dk_ref[n] + mm(d2, two(g_ref[n]), ROWS_ROWS) - mm(de2, two(st_ref[n]), ROWS_ROWS)
        dk = dk - mm(two(dgram + dgram.T), k2)
        s = conv_rows(kb_ref[n, pl.ds(0, rows), :].astype(F32), tops[n], taps, pad.at[n], slots)
        sg = sigmoid(s)
        scale = unit(s * sg)[1]
        dc = scale * (dk - k * jnp.sum(k * dk, axis=-1, keepdims=True))
        inner, rim = conv_back(dc * sg * (1.0 + s * (1.0 - sg)), taps, pad.at[n], slots)
        gk_ref[n, pl.ds(0, rows), :] = inner.astype(BF16)
        gk_ref[n, pl.ds(rows, EDGE), :] = jnp.concatenate([rim, jnp.zeros((8, HEAD), F32)], axis=0).astype(BF16)


def call(kernel, hid, steps, ins, outs, scratch=(), us=1.0):
    def spec(shape, per):
        if per == "weights":
            return pl.BlockSpec((shape[0], HEAD), lambda i, h: (0, h[0]))
        if per is None:
            return pl.BlockSpec(shape, lambda i, h: (0,) * len(shape))
        if isinstance(per, tuple):
            count, first = per
            return pl.BlockSpec((count, EDGE, HEAD), lambda i, h: (i, first // EDGE, 0))
        return pl.BlockSpec((per,) + tuple(shape[1:]), lambda i, h: (i,) + (0,) * (len(shape) - 1))

    return pl.pallas_call(
        kernel,
        grid_spec=pltpu.PrefetchScalarGridSpec(
            num_scalar_prefetch=1,
            grid=(steps,),
            in_specs=[spec(a.shape, per) for a, per in ins],
            out_specs=[spec(s, per) for s, _, per in outs],
            scratch_shapes=list(scratch),
        ),
        out_shape=[jax.ShapeDtypeStruct(s, d) for s, d, _ in outs],
        compiler_params=pltpu.CompilerParams(dimension_semantics=("arbitrary",), vmem_limit_bytes=24 << 20),
        cost_estimate=pl.CostEstimate(flops=int(us * 1.1e9), bytes_accessed=1 << 16, transcendentals=0),
    )(hid, *[a for a, _ in ins])


def shards(
    query_in,
    key_in,
    value_in,
    beta_logit,
    query_conv,
    key_conv,
    value_conv,
    norm_gain,
    out_weight,
    grad_out,
):
    tokens, slots = key_in.shape[0], key_in.shape[1]
    width = query_in.shape[1]
    heads = width // HEAD
    shard_count = lax.axis_size("ctx")
    place = lax.axis_index("ctx")
    groups = shard_count // heads
    group_lists = [[b * heads + i for i in range(heads)] for b in range(groups)]
    rows = tokens * slots
    g = heads
    hid = (place % heads).astype(jnp.int32).reshape(1)

    def exchange(x):
        return lax.all_to_all(x, "ctx", 0, 0, axis_index_groups=group_lists, tiled=True)

    def by_head(x):
        return x.reshape(x.shape[0], heads, HEAD).transpose(1, 0, 2)

    def slots_by_head(x):
        return x.reshape(x.shape[0], slots, heads, HEAD).transpose(2, 0, 1, 3).reshape(heads, -1, HEAD)

    high = lax.reduce_precision(beta_logit, 8, 7)
    rest = beta_logit - high
    middle = lax.reduce_precision(rest, 8, 7)
    betas = jnp.stack([high, middle, rest - middle], axis=2)
    betas = betas.transpose(3, 1, 2, 0).reshape(heads, 3 * slots, tokens).astype(BF16)
    betas = jnp.pad(betas, ((0, 0), (0, EDGE - 3 * slots), (0, 0)))
    kb = exchange(jnp.concatenate([slots_by_head(key_in), betas], axis=1))

    last = EDGE // slots
    tail = jnp.concatenate(
        [slots_by_head(key_in[-last:]), slots_by_head(value_in[-last:]), by_head(query_in[-EDGE:])], axis=1
    )
    tail = jnp.concatenate([tail] * groups, axis=0)
    tail = lax.all_to_all(tail, "ctx", 0, 0, tiled=True)
    group = place // heads
    tail = lax.dynamic_index_in_dim(tail, jnp.maximum(group * heads - 1, 0), 0, False)
    tail = jnp.where(group > 0, tail, jnp.zeros_like(tail))

    grad_normed = jnp.dot(grad_out, out_weight.T, preferred_element_type=F32).astype(BF16)
    vq = exchange(
        jnp.concatenate([slots_by_head(value_in), by_head(query_in), by_head(grad_normed)], axis=1)
    )

    wts = jnp.concatenate(
        [
            jnp.tile(key_conv, (1, 8 // slots, 1)).reshape(8 * TAPS, width),
            jnp.tile(value_conv, (1, 8 // slots, 1)).reshape(8 * TAPS, width),
            query_conv,
            norm_gain.reshape(1, width),
            jnp.zeros((3, width), F32),
        ],
        axis=0,
    )
    per = 2 if g % 2 == 0 else 1
    steps = g // per

    def pad(n):
        return [pltpu.VMEM((per, n + EDGE + 8, HEAD), F32), pltpu.VMEM((EDGE, HEAD), F32)]

    kn, ti = call(
        functools.partial(inverse_kernel, per, tokens, slots),
        hid,
        steps,
        [(kb, per), (tail, None), (wts, "weights")],
        [((g, rows, HEAD), F32, per), ((g, rows, rows), F32, per)],
        pad(rows),
        us=16.0,
    )
    beta = (kb, (per, rows))
    wu, amap, mc, end = call(
        functools.partial(maps_kernel, per, tokens, slots),
        hid,
        steps,
        [(vq, per), beta, (tail, None), (wts, "weights"), (kn, per), (ti, per)],
        [
            ((g, rows, 2 * HEAD), F32, per),
            ((g, HEAD, HEAD), F32, per),
            ((g, HEAD, 2 * HEAD), F32, per),
            ((HEAD, 2 * HEAD), F32, None),
        ],
        pad(rows) + [pltpu.VMEM((HEAD, 2 * HEAD), F32)],
        us=8.0,
    )

    def across(last, towards):
        if groups == 1:
            return jnp.zeros((HEAD, HEAD), F32)
        if groups == 2:
            moves = [(i, i + towards * heads) for i in range(shard_count) if 0 <= i + towards * heads < shard_count]
            return lax.ppermute(last[:, HEAD:], "ctx", moves)
        every = lax.all_gather(last, "ctx")
        head = place % heads
        ahead = group if towards > 0 else groups - 1 - group

        def advance(i, state):
            source = i if towards > 0 else groups - 1 - i
            item = lax.dynamic_index_in_dim(every, source * heads + head, 0, False)
            return jnp.dot(item[:, :HEAD], state, precision=lax.Precision.HIGHEST) + item[:, HEAD:]

        return lax.fori_loop(0, ahead, advance, jnp.zeros((HEAD, HEAD), F32))

    start = across(end, 1)
    q, sc, qm, ol = call(
        functools.partial(queries_kernel, per, tokens, slots),
        hid,
        steps,
        [(vq, per), (tail, None), (wts, "weights"), (kn, per), (wu, per)],
        [
            ((g, tokens, HEAD), F32, per),
            ((g, tokens, rows), F32, per),
            ((g, tokens, HEAD), F32, per),
            ((g, tokens, HEAD), F32, per),
        ],
        pad(tokens),
        us=8.0,
    )
    normed, dr, st, mb, back_end = call(
        functools.partial(outs_kernel, g, tokens, slots),
        hid,
        1,
        [(vq, None), (wts, "weights"), (start, None), (mc, None), (qm, None), (ol, None), (amap, None)],
        [
            ((g, tokens, HEAD), BF16, None),
            ((g, tokens, HEAD), F32, None),
            ((g, HEAD, HEAD), F32, None),
            ((g, HEAD, 2 * HEAD), F32, None),
            ((HEAD, 2 * HEAD), F32, None),
        ],
        us=4.0,
    )
    finish = across(back_end, -1)
    d, dk, dd, gq = call(
        functools.partial(query_grads_kernel, per, tokens, slots),
        hid,
        steps,
        [
            (vq, per), (tail, None), (wts, "weights"), (kn, per), (wu, per), (q, per), (sc, per), (dr, per), (st, per),
        ],
        [
            ((g, rows, HEAD), F32, per),
            ((g, rows, HEAD), F32, per),
            ((g, rows, HEAD), F32, per),
            ((g, tokens + EDGE, HEAD), BF16, per),
        ],
        pad(tokens),
        us=20.0,
    )
    nq = exchange(jnp.concatenate([normed, gq], axis=1))
    gs, de, gv = call(
        functools.partial(value_grads_kernel, per, tokens, slots),
        hid,
        steps,
        [
            (vq, per), beta, (tail, None), (wts, "weights"), (finish, None), (mb, per), (kn, per), (ti, per),
            (d, per), (dd, per),
        ],
        [
            ((g, HEAD, HEAD), F32, per),
            ((g, rows, HEAD), F32, per),
            ((g, rows + 2 * EDGE, HEAD), BF16, per),
        ],
        pad(rows),
        us=8.0,
    )
    gv = exchange(gv)
    (gk,) = call(
        functools.partial(key_grads_kernel, per, tokens, slots),
        hid,
        steps,
        [
            (kb, per), (tail, None), (wts, "weights"), (kn, per), (d, per), (dk, per), (de, per), (st, per), (gs, per),
        ],
        [((g, rows + EDGE, HEAD), BF16, per)],
        pad(rows),
        us=12.0,
    )
    gk = exchange(gk)

    normed_bf = nq[:, :tokens].transpose(1, 0, 2).reshape(tokens, width)
    partial = jnp.dot(normed_bf, out_weight, preferred_element_type=F32)
    if lax.axis_size("head") == 2:
        half = tokens // 2
        mine = lax.axis_index("head")
        pieces = partial.reshape(2, half, partial.shape[1])
        kept = lax.dynamic_index_in_dim(pieces, mine, 0, False)
        sent = lax.dynamic_index_in_dim(pieces, 1 - mine, 0, False).astype(BF16)
        layer_out = (kept + lax.ppermute(sent, "head", [(0, 1), (1, 0)]).astype(F32)).astype(BF16)
    else:
        layer_out = lax.psum_scatter(partial.astype(BF16), "head", scatter_dimension=0, tiled=True)

    edge = RIM * slots
    rims = jnp.concatenate(
        [
            gk[:, rows + 8 - edge : rows + 8],
            gv[:, rows + EDGE + 8 - edge : rows + EDGE + 8],
            nq[:, 2 * tokens + 8 - RIM : 2 * tokens + 8],
        ],
        axis=1,
    )
    rims = lax.ppermute(rims, "ctx", [(i, i - 1) for i in range(1, shard_count)]).astype(F32)

    def slots_back(block, rim):
        block = block.reshape(heads, tokens, slots, HEAD).astype(F32)
        rim = jnp.pad(rim.reshape(heads, RIM, slots, HEAD), ((0, 0), (tokens - RIM, 0), (0, 0), (0, 0)))
        return (block + rim).transpose(1, 2, 0, 3).reshape(tokens, slots, width)

    grad_key = slots_back(gk[:, :rows], rims[:, :edge])
    grad_value = slots_back(gv[:, :rows], rims[:, edge : 2 * edge])
    rim_query = jnp.pad(rims[:, 2 * edge :], ((0, 0), (tokens - RIM, 0), (0, 0)))
    grad_query = (nq[:, tokens : 2 * tokens].astype(F32) + rim_query).transpose(1, 0, 2).reshape(tokens, width)
    marks = gv[:, rows : rows + 2 * slots].astype(F32)
    grad_beta = marks.reshape(heads, slots, 2, tokens).sum(axis=2).transpose(2, 1, 0)
    return (layer_out, grad_query, grad_key, grad_value, grad_beta)


def solution(mesh):
    placed = (
        P("ctx", "head"),
        P("ctx", None, "head"),
        P("ctx", None, "head"),
        P("ctx", None, "head"),
        P(None, "head"),
        P(None, None, "head"),
        P(None, None, "head"),
        P("head"),
        P("head", None),
        P("ctx", None),
    )
    return jax.shard_map(
        shards,
        mesh=mesh,
        in_specs=placed,
        out_specs=(
            P(("ctx", "head"), None),
            P("ctx", "head"),
            P("ctx", None, "head"),
            P("ctx", None, "head"),
            P("ctx", None, "head"),
        ),
        check_vma=False,
    )
```

time: 163 us -> 140 us (0.86)
  Pallas kernels: 54.2 us -> 40.9 us
  local copies, waits for them, and re-layouts: 34.5 us -> 24.3 us
  waiting for transfers between devices: 24.1 us -> 20.3 us
  starting transfers between devices: 33.8 us -> 36.8 us
    pallas_call x5 -> x7, Pallas kernels: 54.2 us -> 40.9 us  [call(): pl.pallas_call(kernel, grid_spec=pltpu.PrefetchScalarGridSpec(num_scalar_...]
    unnamed x68 -> x53, local copies, waits for them, and re-layouts: 21.9 us -> 13.3 us
    all_to_all x0 -> x1, starting transfers between devices: none -> 7.35 us  [shards(): tail = lax.all_to_all(tail, 'ctx', 0, 0, tiled=True)]
    ppermute x1, waiting for transfers between devices: 6.81 us -> 0.01 us  [shards(): lax.ppermute(sent, 'head', [(0, 1), (1, 0)]).astype(F32)]
    reshape x6, local copies, waits for them, and re-layouts: 0.92 us -> 6.41 us  [the longest x4 3.44 us: slots_by_head(): x.reshape(x.shape[0], slots, heads, HEAD).transpose(2, 0, 1, 3)]
    all_to_all x0 -> x1, waiting for transfers between devices: none -> 5.34 us  [shards(): tail = lax.all_to_all(tail, 'ctx', 0, 0, tiled=True)]
    ppermute x2, waiting for transfers between devices: 5.27 us -> 0.01 us  [across(): return lax.ppermute(last[:, HEAD:], 'ctx', moves)]
    ppermute x1 -> x0, starting transfers between devices: 4.54 us -> none  [shards(): lax.ppermute(tail, 'ctx', [(i, i + 1) for i in range(shard_count - 1)])]
  transfers between devices with their start and end apart: 9 -> 10, of which waited for: 5 -> 5; matrix products, arithmetic and copies ran while one was open for 13% -> 17% of each run, Pallas kernels for 27% -> 23%
where the time goes in v2:
time: 140 us; the launch traced here: 138 us
  Pallas kernels  40.9 us (29%)
  starting transfers between devices  36.8 us (26%)
  local copies, waits for them, and re-layouts  24.3 us (17%)
  waiting for transfers between devices  20.3 us (14%)
  other arithmetic  8.31 us (6%)
  matrix products  6.66 us (5%)
    pallas_call x7, Pallas kernels, call(): pl.pallas_call(kernel, grid_spec=pltpu.PrefetchScalarGridSpec(num_scalar_...  40.9 us
    all_to_all x5, starting transfers between devices, exchange(): lax.all_to_all(x, 'ctx', 0, 0, axis_index_groups=group_lists, tiled=True)  21.7 us
    unnamed x53, local copies, waits for them, and re-layouts  13.3 us
    all_to_all x5, waiting for transfers between devices, exchange(): lax.all_to_all(x, 'ctx', 0, 0, axis_index_groups=group_lists, tiled=True)  13 us
    all_to_all x1, starting transfers between devices, shards(): tail = lax.all_to_all(tail, 'ctx', 0, 0, tiled=True)  7.35 us
    all_to_all x1, waiting for transfers between devices, shards(): tail = lax.all_to_all(tail, 'ctx', 0, 0, tiled=True)  5.34 us
    dot_general x1, matrix products, shards(): jnp.dot(grad_out, out_weight.T, preferred_element_type=F32).astype(BF16)  3.76 us
    ppermute x2, starting transfers between devices, across(): return lax.ppermute(last[:, HEAD:], 'ctx', moves)  3.62 us
  transfers between devices with their start and end apart: 10, of which 5 were waited for; matrix products, arithmetic and copies ran while one was open for 17% of the time, Pallas kernels for 23%

profile of v2, /device:TPU:1, one launch (start us, length us, event | category | flops | bytes accessed | tf_op | source)
XLA Modules:
  0.0 138.4 jit_solution(9182097305176931278)
XLA Ops:
  0.6 0.8 copy_bitcast_fusion.3
  1.5 0.8 copy_bitcast_fusion.2
  2.3 0.8 bitcast_bitcast_fusion
  3.8 7.3 %all-to-all-start.2 = ((bf16[16,48,128]{2,1,0:T(8,128)(2,1)}), bf16[16,48,128]{2,1,0:T(8,128)(2,1)S(1)}, u32[]{:S(2)}, u32[]{:S(2)}) async-start(bf16[16,48,128]{2,1,0:T(8,128)(2,1)} %maximum_maximum_fusion), calls=%async_computation.2 | async-start | bytes 393216 | tf_op jit(solution)/shard_map/all_to_all | solution.py:435
  11.9 1.4 %copy_bitcast_fusion = bf16[128,2,8,128]{3,1,0,2:T(2,128)(2,1)S(1)} fusion(bf16[128,2,1024]{2,1,0:T(2,128)(2,1)} %param.11), kind=kLoop, calls=%fused_computation.12 | loop fusion | bytes 1048576 | tf_op jit(solution)/shard_map/reshape | solution.py:420
  13.3 0.8 fusion.5
  14.1 5.3 %all-to-all-done.2 = bf16[16,48,128]{2,1,0:T(8,128)(2,1)S(1)} async-done(((bf16[16,48,128]{2,1,0:T(8,128)(2,1)}), bf16[16,48,128]{2,1,0:T(8,128)(2,1)S(1)}, u32[]{:S(2)}, u32[]{:S(2)}) %all-to-all-start.2) | async-done | bytes 196640 | tf_op jit(solution)/shard_map/all_to_all | solution.py:435
  19.5 4.2 %all-to-all-start.1 = ((bf16[8,272,128]{2,1,0:T(8,128)(2,1)}), bf16[8,272,128]{2,1,0:T(8,128)(2,1)S(1)}, u32[]{:S(2)}, u32[]{:S(2)}) async-start(bf16[8,272,128]{2,1,0:T(8,128)(2,1)} %fusion.5), calls=%async_computation.1 | async-start | bytes 1114112 | tf_op jit(solution)/shard_map/all_to_all | solution.py:414
  23.9 3.8 %convolution_convert_fusion = bf16[128,1024]{1,0:T(8,128)(2,1)S(1)} fusion(bf16[128,2048]{1,0:T(8,128)(2,1)S(1)} %copy-done, bf16[1024,2048]{1,0:T(8,128)(2,1)} %param.18), kind=kOutput, calls=%fused_computation.2 | convolution fusion | flops 537001984 | bytes 4980736 | tf_op jit(solution)/shard_map/dot_general | solution.py:440
  28.6 1.0 pad_maximum_fusion
  29.7 2.4 %all-to-all-done.1.kb_ref.beta_ref = bf16[8,272,128]{2,1,0:T(8,128)(2,1)S(1)} async-done(((bf16[8,272,128]{2,1,0:T(8,128)(2,1)}), bf16[8,272,128]{2,1,0:T(8,128)(2,1)S(1)}, u32[]{:S(2)}, u32[]{:S(2)}) %all-to-all-start.1) | async-done | bytes 557088 | tf_op jit(solution)/shard_map/all_to_all | solution.py:414
  32.0 4.3 %all-to-all-start = ((bf16[8,512,128]{2,1,0:T(8,128)(2,1)}), bf16[8,512,128]{2,1,0:T(8,128)(2,1)S(1)}, u32[]{:S(2)}, u32[]{:S(2)}) async-start(bf16[8,512,128]{2,1,0:T(8,128)(2,1)} %pad_maximum_fusion), calls=%async_computation | async-start | bytes 2097152 | tf_op jit(solution)/shard_map/all_to_all | solution.py:414
  36.8 12.2 %shard_map.137 = (f32[8,256,128]{2,1,0:T(8,128)S(1)}, f32[8,256,256]{2,1,0:T(8,128)S(1)}) custom-call(s32[1]{0:T(128)} %bitcast.hid, bf16[8,272,128]{2,1,0:T(8,128)(2,1)S(1)} %all-to-all-done.1.kb_ref.beta_ref, bf16[48,128]{1,0:T(8,128)(2,1)S(1)} %select_bitcast_fusion.tail_ref, f32[72,1024]{1,0:T(8,128)S(1)} %concatenate.22.wts_ref), custom_call_target="tpu_custom_call" | custom-call | flops 17600000000 | bytes 65536 | tf_op jit(solution)/shard_map/pallas_call | solution.py:375
  49.0 1.3 copy-done.1
  50.4 2.0 %copy-done.2 = f32[8,256,256]{2,1,0:T(8,128)S(1)} copy-done((f32[8,256,256]{2,1,0:T(8,128)S(1)}, f32[8,256,256]{2,1,0:T(8,128)}, u32[]{:S(2)}) %copy-start.2) | copy-done | bytes 2097176
  52.3 6.0 %shard_map.138 = (f32[8,256,256]{2,1,0:T(8,128)S(1)}, f32[8,128,128]{2,1,0:T(8,128)S(1)}, f32[8,128,256]{2,1,0:T(8,128)S(1)}, f32[128,256]{1,0:T(8,128)S(1)}) custom-call(s32[1]{0:T(128)} %bitcast.hid, bf16[8,512,128]{2,1,0:T(8,128)(2,1)S(1)} %all-to-all-done.vq_ref, bf16[8,272,128]{2,1,0:T(8,128)(2,1)S(1)} %all-to-all-done.1.kb_ref.beta_ref, ...), custom_call_target="tpu_custom_call" | custom-call | flops 8800000000 | bytes 65536 | tf_op jit(solution)/shard_map/pallas_call | solution.py:375
  58.3 2.3 %collective-permute-start = (f32[128,128]{1,0:T(8,128)S(1)}, f32[128,128]{1,0:T(8,128)S(1)}, u32[]{:S(2)}, u32[]{:S(2)}) collective-permute-start(f32[128,128]{1,0:T(8,128)S(1)} %slice.51), channel_id=1, source_target_pairs={{0,16},{2,18},{4,20},{6,22},{8,24},{10,26},{12,28},{14,30},{1,17},... | collective-permute-start | bytes 196616 | tf_op jit(solution)/shard_map/ppermute | solution.py:491
  60.7 3.6 %shard_map.139 = (f32[8,128,128]{2,1,0:T(8,128)S(1)}, f32[8,128,256]{2,1,0:T(8,128)S(1)}, f32[8,128,128]{2,1,0:T(8,128)S(1)}, f32[8,128,128]{2,1,0:T(8,128)S(1)}) custom-call(s32[1]{0:T(128)} %bitcast.hid, bf16[8,512,128]{2,1,0:T(8,128)(2,1)S(1)} %all-to-all-done.vq_ref, bf16[48,128]{1,0:T(8,128)(2,1)S(1)} %select_bitcast_fusion.tail_ref, ...), custom_call_target="tpu_custom_call" | custom-call | flops 8800000000 | bytes 65536 | tf_op jit(solution)/shard_map/pallas_call | solution.py:375
  64.3 2.5 %shard_map.140 = (bf16[8,128,128]{2,1,0:T(8,128)(2,1)S(1)}, f32[8,128,128]{2,1,0:T(8,128)S(1)}, f32[8,128,128]{2,1,0:T(8,128)S(1)}, f32[8,128,256]{2,1,0:T(8,128)S(1)}, f32[128,256]{1,0:T(8,128)S(1)}) custom-call(s32[1]{0:T(128)} %bitcast.hid, bf16[8,512,128]{2,1,0:T(8,128)(2,1)S(1)} %all-to-all-done.vq_ref, f32[72,1024]{1,0:T(8,128)S(1)} %concatenate.22.wts_ref, ...), custom_call_target="tpu_custom_call" | custom-call | flops 4400000000 | bytes 65536 | tf_op jit(solution)/shard_map/pallas_call | solution.py:375
  67.5 1.3 collective-permute-start.2
  68.8 5.4 %shard_map.141 = (f32[8,256,128]{2,1,0:T(8,128)S(1)}, f32[8,256,128]{2,1,0:T(8,128)S(1)}, f32[8,256,128]{2,1,0:T(8,128)S(1)}, bf16[8,144,128]{2,1,0:T(8,128)(2,1)S(1)}) custom-call(s32[1]{0:T(128)} %bitcast.hid, bf16[8,512,128]{2,1,0:T(8,128)(2,1)S(1)} %all-to-all-done.vq_ref, bf16[48,128]{1,0:T(8,128)(2,1)S(1)} %select_bitcast_fusion.tail_ref, ...), custom_call_target="tpu_custom_call" | custom-call | flops 22000001024 | bytes 65536 | tf_op jit(solution)/shard_map/pallas_call | solution.py:375
  74.2 1.0 copy-done.9
  75.1 1.0 copy-done.12
  76.1 1.0 copy-done.14
  77.1 0.9 pad_maximum_fusion.1
  78.0 4.5 %all-to-all-start.3 = ((bf16[8,272,128]{2,1,0:T(8,128)(2,1)}), bf16[8,272,128]{2,1,0:T(8,128)(2,1)}, u32[]{:S(2)}, u32[]{:S(2)}) async-start(bf16[8,272,128]{2,1,0:T(8,128)(2,1)} %pad_maximum_fusion.1), calls=%async_computation.3 | async-start | bytes 1114112 | tf_op jit(solution)/shard_map/all_to_all | solution.py:414
  82.5 1.6 %copy-done.3 = f32[8,256,256]{2,1,0:T(8,128)S(1)} copy-done((f32[8,256,256]{2,1,0:T(8,128)S(1)}, f32[8,256,256]{2,1,0:T(8,128)}, u32[]{:S(2)}) %copy-start.3) | copy-done | bytes 2097176
  84.1 1.2 copy-done.8
  85.3 1.2 copy-done.10
  86.5 1.2 copy-done.13
  87.8 5.9 %shard_map.142 = (f32[8,128,128]{2,1,0:T(8,128)S(1)}, f32[8,256,128]{2,1,0:T(8,128)S(1)}, bf16[8,288,128]{2,1,0:T(8,128)(2,1)}) custom-call(s32[1]{0:T(128)} %bitcast.hid, bf16[8,512,128]{2,1,0:T(8,128)(2,1)S(1)} %all-to-all-done.vq_ref, bf16[8,272,128]{2,1,0:T(8,128)(2,1)S(1)} %all-to-all-done.1.kb_ref.beta_ref, ...), custom_call_target="tpu_custom_call" | custom-call | flops 8800000000 | bytes 65536 | tf_op jit(solution)/shard_map/pallas_call | solution.py:375
  93.6 5.4 %shard_map.143 = bf16[8,272,128]{2,1,0:T(8,128)(2,1)} custom-call(s32[1]{0:T(128)} %bitcast.hid, bf16[8,272,128]{2,1,0:T(8,128)(2,1)S(1)} %all-to-all-done.1.kb_ref.beta_ref, bf16[48,128]{1,0:T(8,128)(2,1)S(1)} %select_bitcast_fusion.tail_ref, f32[72,1024]{1,0:T(8,128)S(1)} %concatenate.22.wts_ref, f32[8,256,128]{2,1,0:T(8,128)S(1)} %copy-done.8, ...), custom_call_target="tpu_custom_call" | custom-call | flops 13200000000 | bytes 65536 | tf_op jit(solution)/shard_map/pallas_call | solution.py:375
  99.1 4.3 %all-to-all-start.4 = ((bf16[8,272,128]{2,1,0:T(8,128)(2,1)}), bf16[8,272,128]{2,1,0:T(8,128)(2,1)S(1)}, u32[]{:S(2)}, u32[]{:S(2)}) async-start(bf16[8,272,128]{2,1,0:T(8,128)(2,1)} %shard_map.143), calls=%async_computation.4 | async-start | bytes 1114112 | tf_op jit(solution)/shard_map/all_to_all | solution.py:414
  103.4 8.3 %all-to-all-done.4 = bf16[8,272,128]{2,1,0:T(8,128)(2,1)S(1)} async-done(((bf16[8,272,128]{2,1,0:T(8,128)(2,1)}), bf16[8,272,128]{2,1,0:T(8,128)(2,1)S(1)}, u32[]{:S(2)}, u32[]{:S(2)}) %all-to-all-start.4) | async-done | bytes 557088 | tf_op jit(solution)/shard_map/all_to_all | solution.py:414
  111.7 4.3 %all-to-all-start.5 = ((bf16[8,288,128]{2,1,0:T(8,128)(2,1)}), bf16[8,288,128]{2,1,0:T(8,128)(2,1)S(1)}, u32[]{:S(2)}, u32[]{:S(2)}) async-start(bf16[8,288,128]{2,1,0:T(8,128)(2,1)} %get-tuple-element.48), calls=%async_computation.5 | async-start | bytes 1179648 | tf_op jit(solution)/shard_map/all_to_all | solution.py:414
  116.0 1.0 slice_bitcast_fusion
  117.3 2.9 %fusion = f32[2,64,2048]{2,1,0:T(8,128)S(1)} fusion(bf16[2,64,1024]{2,1,0:T(8,128)(2,1)S(1)} %dot_general.9, bf16[1024,2048]{1,0:T(8,128)(2,1)} %param.18), kind=kOutput, calls=%fused_computation | convolution fusion | flops 536870912 | bytes 5505024 | tf_op jit(solution)/shard_map/dot_general | solution.py:581
  120.3 1.3 collective-permute-start.1
  121.6 0.7 slice.68
  122.4 2.3 %all-to-all-done.5 = bf16[8,288,128]{2,1,0:T(8,128)(2,1)S(1)} async-done(((bf16[8,288,128]{2,1,0:T(8,128)(2,1)}), bf16[8,288,128]{2,1,0:T(8,128)(2,1)S(1)}, u32[]{:S(2)}, u32[]{:S(2)}) %all-to-all-start.5) | async-done | bytes 589856 | tf_op jit(solution)/shard_map/all_to_all | solution.py:414
  124.8 2.8 %collective-permute-start.3 = (bf16[8,15,128]{2,1,0:T(8,128)(2,1)S(1)}, bf16[8,15,128]{2,1,0:T(8,128)(2,1)S(1)}, u32[]{:S(2)}, u32[]{:S(2)}) collective-permute-start(bf16[8,15,128]{2,1,0:T(8,128)(2,1)S(1)} %pad_maximum_fusion.2), channel_id=1, source_target_pairs={{2,0},{4,2},{6,4},{8,6},{10,8},{12,10},{14,12},{16,14},{18,16},{20... | collective-permute-start | bytes 92168 | tf_op jit(solution)/shard_map/ppermute | solution.py:601
  128.3 1.9 %collective-permute-done.3 = bf16[8,15,128]{2,1,0:T(8,128)(2,1)S(1)} collective-permute-done((bf16[8,15,128]{2,1,0:T(8,128)(2,1)S(1)}, bf16[8,15,128]{2,1,0:T(8,128)(2,1)S(1)}, u32[]{:S(2)}, u32[]{:S(2)}) %collective-permute-start.3) | collective-permute-done | bytes 30752 | tf_op jit(solution)/shard_map/ppermute | solution.py:601
  130.9 1.6 %fusion.4 = f32[128,2,8,128]{3,2,1,0:T(8,128)} fusion(f32[8,128,2,128]{3,2,1,0:T(2,128)S(1)} %bitcast.96, f32[8,3,2,128]{3,0,2,1:T(8,128)S(1)} %bitcast.108), kind=kLoop, calls=%fused_computation.9 | loop fusion | flops 262144 | bytes 2121728 | tf_op jit(solution)/shard_map/transpose | solution.py:606
  132.5 1.5 %reshape.111 = f32[128,2,1024]{2,1,0:T(2,128)} reshape(f32[128,2,8,128]{3,2,1,0:T(8,128)S(1)} %fusion.3) | data formatting | bytes 2097152 | tf_op jit(solution)/shard_map/reshape | solution.py:606
  134.0 1.5 %reshape.109 = f32[128,2,1024]{2,1,0:T(2,128)} reshape(f32[128,2,8,128]{3,2,1,0:T(8,128)S(1)} %copy-done.16) | data formatting | bytes 2097152 | tf_op jit(solution)/shard_map/reshape | solution.py:606
  135.5 1.0 add_bitcast_fusion
  136.7 1.0 copy.59
  137.7 0.7 fusion.6
  (81 shorter events, 5.6 us)
Async XLA Ops:
  0.6 23.2 %copy-start = (bf16[128,2048]{1,0:T(8,128)(2,1)S(1)}, bf16[128,2048]{1,0:T(8,128)(2,1)}, u32[]{:S(2)}) copy-start(bf16[128,2048]{1,0:T(8,128)(2,1)} %param.19) | copy-start | bytes 1572868
  1.5 22.2 %copy-start.20 = (bf16[128,1024]{1,0:T(8,128)(2,1)S(1)}, bf16[128,1024]{1,0:T(8,128)(2,1)}, u32[]{:S(2)}) copy-start(bf16[128,1024]{1,0:T(8,128)(2,1)} %param.10) | copy-start | bytes 786436
  3.8 15.7 %all-to-all-start.2 = ((bf16[16,48,128]{2,1,0:T(8,128)(2,1)}), bf16[16,48,128]{2,1,0:T(8,128)(2,1)S(1)}, u32[]{:S(2)}, u32[]{:S(2)}) async-start(bf16[16,48,128]{2,1,0:T(8,128)(2,1)} %maximum_maximum_fusion), calls=%async_computation.2 | async-start | bytes 393216 | tf_op jit(solution)/shard_map/all_to_all | solution.py:435
  19.5 12.6 %all-to-all-start.1 = ((bf16[8,272,128]{2,1,0:T(8,128)(2,1)}), bf16[8,272,128]{2,1,0:T(8,128)(2,1)S(1)}, u32[]{:S(2)}, u32[]{:S(2)}) async-start(bf16[8,272,128]{2,1,0:T(8,128)(2,1)} %fusion.5), calls=%async_computation.1 | async-start | bytes 1114112 | tf_op jit(solution)/shard_map/all_to_all | solution.py:414
  23.9 4.3 %copy-start.19 = (bf16[128,2,1024]{2,1,0:T(2,128)(2,1)S(1)}, bf16[128,2,1024]{2,1,0:T(2,128)(2,1)}, u32[]{:S(2)}) copy-start(bf16[128,2,1024]{2,1,0:T(2,128)(2,1)} %param.12) | copy-start | bytes 1572868
  28.6 7.8 %copy-start.21 = (f32[4,2,1024]{2,1,0:T(2,128)S(1)}, f32[4,2,1024]{2,1,0:T(2,128)}, u32[]{:S(2)}) copy-start(f32[4,2,1024]{2,1,0:T(2,128)} %param.15) | copy-start | bytes 98308
  28.6 7.9 %copy-start.22 = (f32[4,2,1024]{2,1,0:T(2,128)S(1)}, f32[4,2,1024]{2,1,0:T(2,128)}, u32[]{:S(2)}) copy-start(f32[4,2,1024]{2,1,0:T(2,128)} %param.16) | copy-start | bytes 98308
  28.6 8.1 %copy-start.23 = (f32[4,1024]{1,0:T(4,128)S(1)}, f32[4,1024]{1,0:T(4,128)}, u32[]{:S(2)}) copy-start(f32[4,1024]{1,0:T(4,128)} %param.14) | copy-start | bytes 49156
  28.6 8.1 %copy-start.24 = (f32[1024]{0:T(1024)S(1)}, f32[1024]{0:T(1024)}, u32[]{:S(2)}) copy-start(f32[1024]{0:T(1024)} %param.17) | copy-start | bytes 12292
  32.0 18.3 %all-to-all-start = ((bf16[8,512,128]{2,1,0:T(8,128)(2,1)}), bf16[8,512,128]{2,1,0:T(8,128)(2,1)S(1)}, u32[]{:S(2)}, u32[]{:S(2)}) async-start(bf16[8,512,128]{2,1,0:T(8,128)(2,1)} %pad_maximum_fusion), calls=%async_computation | async-start | bytes 2097152 | tf_op jit(solution)/shard_map/all_to_all | solution.py:414
  49.0 1.3 copy-start.1
  50.4 10.3 %copy-start.6 = (f32[8,256,128]{2,1,0:T(8,128)}, f32[8,256,128]{2,1,0:T(8,128)S(1)}, u32[]{:S(2)}) copy-start(f32[8,256,128]{2,1,0:T(8,128)S(1)} %get-tuple-element.27.kn_ref) | copy-start | bytes 3145732
  50.4 2.0 %copy-start.2 = (f32[8,256,256]{2,1,0:T(8,128)S(1)}, f32[8,256,256]{2,1,0:T(8,128)}, u32[]{:S(2)}) copy-start(f32[8,256,256]{2,1,0:T(8,128)} %copy-done.1) | copy-start | bytes 6291460
  58.3 5.9 %collective-permute-start = (f32[128,128]{1,0:T(8,128)S(1)}, f32[128,128]{1,0:T(8,128)S(1)}, u32[]{:S(2)}, u32[]{:S(2)}) collective-permute-start(f32[128,128]{1,0:T(8,128)S(1)} %slice.51), channel_id=1, source_target_pairs={{0,16},{2,18},{4,20},{6,22},{8,24},{10,26},{12,28},{14,30},{1,17},... | collective-permute-start | bytes 196616 | tf_op jit(solution)/shard_map/ppermute | solution.py:491
  64.3 4.5 %copy-start.7 = (f32[8,256,128]{2,1,0:T(8,128)S(1)}, f32[8,256,128]{2,1,0:T(8,128)}, u32[]{:S(2)}) copy-start(f32[8,256,128]{2,1,0:T(8,128)} %copy-done.6) | copy-start | bytes 3145732
  66.8 7.4 %copy-start.4 = (f32[8,128,128]{2,1,0:T(8,128)}, f32[8,128,128]{2,1,0:T(8,128)S(1)}, u32[]{:S(2)}) copy-start(f32[8,128,128]{2,1,0:T(8,128)S(1)} %get-tuple-element.39.st_ref) | copy-start | bytes 1572868
  67.5 15.0 %collective-permute-start.2 = (f32[128,128]{1,0:T(8,128)}, f32[128,128]{1,0:T(8,128)S(1)}, u32[]{:S(2)}, u32[]{:S(2)}) collective-permute-start(f32[128,128]{1,0:T(8,128)} %slice.54), channel_id=1, source_target_pairs={{16,0},{18,2},{20,4},{22,6},{24,8},{26,10},{28,12},{30,14},{17,1},... | collective-permute-start | bytes 196616 | tf_op jit(solution)/shard_map/ppermute | solution.py:491
  74.2 1.0 copy-start.9
  75.1 1.0 copy-start.12
  76.1 1.0 copy-start.14
  78.0 21.1 %all-to-all-start.3 = ((bf16[8,272,128]{2,1,0:T(8,128)(2,1)}), bf16[8,272,128]{2,1,0:T(8,128)(2,1)}, u32[]{:S(2)}, u32[]{:S(2)}) async-start(bf16[8,272,128]{2,1,0:T(8,128)(2,1)} %pad_maximum_fusion.1), calls=%async_computation.3 | async-start | bytes 1114112 | tf_op jit(solution)/shard_map/all_to_all | solution.py:414
  82.5 1.6 %copy-start.3 = (f32[8,256,256]{2,1,0:T(8,128)S(1)}, f32[8,256,256]{2,1,0:T(8,128)}, u32[]{:S(2)}) copy-start(f32[8,256,256]{2,1,0:T(8,128)} %copy-done.1) | copy-start | bytes 6291460
  84.1 1.2 copy-start.8
  85.3 1.2 copy-start.10
  86.5 1.2 copy-start.13
  87.8 5.9 %copy-start.5 = (f32[8,128,128]{2,1,0:T(8,128)S(1)}, f32[8,128,128]{2,1,0:T(8,128)}, u32[]{:S(2)}) copy-start(f32[8,128,128]{2,1,0:T(8,128)} %copy-done.4) | copy-start | bytes 1572868
  87.8 5.9 %copy-start.11 = (f32[8,256,128]{2,1,0:T(8,128)S(1)}, f32[8,256,128]{2,1,0:T(8,128)}, u32[]{:S(2)}) copy-start(f32[8,256,128]{2,1,0:T(8,128)} %copy-done.9) | copy-start | bytes 3145732
  87.8 5.9 %copy-start.15 = (f32[8,256,128]{2,1,0:T(8,128)S(1)}, f32[8,256,128]{2,1,0:T(8,128)}, u32[]{:S(2)}) copy-start(f32[8,256,128]{2,1,0:T(8,128)} %copy-done.14) | copy-start | bytes 3145732
  99.1 12.7 %all-to-all-start.4 = ((bf16[8,272,128]{2,1,0:T(8,128)(2,1)}), bf16[8,272,128]{2,1,0:T(8,128)(2,1)S(1)}, u32[]{:S(2)}, u32[]{:S(2)}) async-start(bf16[8,272,128]{2,1,0:T(8,128)(2,1)} %shard_map.143), calls=%async_computation.4 | async-start | bytes 1114112 | tf_op jit(solution)/shard_map/all_to_all | solution.py:414
  111.7 13.0 %all-to-all-start.5 = ((bf16[8,288,128]{2,1,0:T(8,128)(2,1)}), bf16[8,288,128]{2,1,0:T(8,128)(2,1)S(1)}, u32[]{:S(2)}, u32[]{:S(2)}) async-start(bf16[8,288,128]{2,1,0:T(8,128)(2,1)} %get-tuple-element.48), calls=%async_computation.5 | async-start | bytes 1179648 | tf_op jit(solution)/shard_map/all_to_all | solution.py:414
  120.2 2.1 %copy-start.17 = (f32[2,64,2048]{2,1,0:T(8,128)}, f32[2,64,2048]{2,1,0:T(8,128)S(1)}, u32[]{:S(2)}) copy-start(f32[2,64,2048]{2,1,0:T(8,128)S(1)} %fusion) | copy-start | bytes 3145732
  120.3 17.4 %collective-permute-start.1 = (bf16[64,2048]{1,0:T(8,128)(2,1)S(1)}, bf16[64,2048]{1,0:T(8,128)(2,1)S(1)}, u32[]{:S(2)}, u32[]{:S(2)}) collective-permute-start(bf16[64,2048]{1,0:T(8,128)(2,1)S(1)} %fusion.7), channel_id=1, source_target_pairs={{0,1},{1,0},{2,3},{3,2},{4,5},{5,4},{6,7},{7,6},{8,9},{9,8},{10,11... | collective-permute-start | bytes 786440 | tf_op jit(solution)/shard_map/ppermute | solution.py:588
  124.8 5.5 %collective-permute-start.3 = (bf16[8,15,128]{2,1,0:T(8,128)(2,1)S(1)}, bf16[8,15,128]{2,1,0:T(8,128)(2,1)S(1)}, u32[]{:S(2)}, u32[]{:S(2)}) collective-permute-start(bf16[8,15,128]{2,1,0:T(8,128)(2,1)S(1)} %pad_maximum_fusion.2), channel_id=1, source_target_pairs={{2,0},{4,2},{6,4},{8,6},{10,8},{12,10},{14,12},{16,14},{18,16},{20... | collective-permute-start | bytes 92168 | tf_op jit(solution)/shard_map/ppermute | solution.py:601
  132.5 1.5 %copy-start.16 = (f32[128,2,8,128]{3,2,1,0:T(8,128)S(1)}, f32[128,2,8,128]{3,2,1,0:T(8,128)}, u32[]{:S(2)}) copy-start(f32[128,2,8,128]{3,2,1,0:T(8,128)} %fusion.4) | copy-start | bytes 3145732
  134.0 3.7 %copy-start.18 = (f32[2,64,2048]{2,1,0:T(8,128)S(1)}, f32[2,64,2048]{2,1,0:T(8,128)}, u32[]{:S(2)}) copy-start(f32[2,64,2048]{2,1,0:T(8,128)} %copy-done.17) | copy-start | bytes 3145732

commit v3 on v2

--- a/solution.py
+++ b/solution.py
@@ -101,6 +101,11 @@
     return 1.0 / (1.0 + jnp.exp(-x))
 
 
+def silu(s):
+    sg = sigmoid(s)
+    return s * sg, sg * (1.0 + s * (1.0 - sg))
+
+
 def unit(values):
     scale = lax.rsqrt(jnp.sum(values * values, axis=-1, keepdims=True) + EPS)
     return values * scale, scale
@@ -144,7 +149,7 @@
     return found
 
 
-def inverse_kernel(per, tokens, slots, hid, kb_ref, tail_ref, wts_ref, kn_ref, ti_ref, pad, halo):
+def inverse_kernel(per, tokens, slots, hid, kb_ref, tail_ref, wts_ref, kn_ref, ti_ref, fk_ref, pad, halo):
     rows = tokens * slots
     taps = slot_taps(wts_ref[...], 0)
     tops = edges(kb_ref, 0, rows, per, tail_ref[pl.ds(0, EDGE), :].astype(F32), halo)
@@ -153,8 +158,10 @@
     grams = []
     for n in range(per):
         s = conv_rows(kb_ref[n, pl.ds(0, rows), :].astype(F32), tops[n], taps, pad.at[n], slots)
-        k = unit(s * sigmoid(s))[0]
+        c, slope = silu(s)
+        k, scale = unit(c)
         kn_ref[n] = k
+        fk_ref[n] = scale * slope
         betas = beta_rows(kb_ref[n, pl.ds(rows, EDGE), :].astype(F32), slots)
         strength = 2.0 * sigmoid(column(betas, tokens, slots))
         k2 = two(k)
@@ -200,7 +207,7 @@
 
 def maps_kernel(
     per, tokens, slots, hid, vq_ref, beta_ref, tail_ref, wts_ref, kn_ref, ti_ref,
-    wu_ref, a_ref, mc_ref, end_ref, pad, halo, carry,
+    wu_ref, a_ref, mc_ref, end_ref, fv_ref, pad, halo, carry,
 ):
     rows = tokens * slots
     taps = slot_taps(wts_ref[...], 1)
@@ -214,7 +221,7 @@
     maps = []
     for n in range(per):
         s = conv_rows(vq_ref[n, pl.ds(0, rows), :].astype(F32), tops[n], taps, pad.at[n], slots)
-        v = s * sigmoid(s)
+        v, fv_ref[n] = silu(s)
         betas = beta_rows(beta_ref[n].astype(F32), slots)
         strength = 2.0 * sigmoid(column(betas, tokens, slots))
         k = kn_ref[n]
@@ -233,7 +240,7 @@
 
 
 def queries_kernel(
-    per, tokens, slots, hid, vq_ref, tail_ref, wts_ref, kn_ref, wu_ref, q_ref, sc_ref, qm_ref, ol_ref, pad, halo
+    per, tokens, slots, hid, vq_ref, tail_ref, wts_ref, kn_ref, wu_ref, q_ref, sc_ref, qm_ref, ol_ref, fq_ref, pad, halo
 ):
     rows = tokens * slots
     taps = query_taps(wts_ref[...])
@@ -241,7 +248,9 @@
     seen = visible(tokens, slots)
     for n in range(per):
         s = conv_rows(vq_ref[n, pl.ds(rows, tokens), :].astype(F32), tops[n], taps, pad.at[n], 1)
-        q = unit(s * sigmoid(s))[0]
+        c, slope = silu(s)
+        q, scale = unit(c)
+        fq_ref[n] = scale * slope
         scores = jnp.where(seen, mm(two(q), two(kn_ref[n]), ROWS_ROWS), 0.0)
         mapped = mm(two(scores), two(wu_ref[n]))
         q_ref[n] = q
@@ -283,85 +292,76 @@
 
 
 def query_grads_kernel(
-    per, tokens, slots, hid, vq_ref, tail_ref, wts_ref, kn_ref, wu_ref, q_ref, sc_ref, dr_ref, st_ref,
-    d_ref, dk_ref, dd_ref, gq_ref, pad, halo,
+    per, tokens, slots, hid, wts_ref, kn_ref, wu_ref, q_ref, sc_ref, dr_ref, st_ref, fq_ref, nm_ref,
+    d_ref, dk_ref, dd_ref, nq_ref, pad,
 ):
-    rows = tokens * slots
     taps = query_taps(wts_ref[...])
-    tops = edges(vq_ref, rows, tokens, per, tail_ref[pl.ds(2 * EDGE, EDGE), :].astype(F32), halo)
     seen = visible(tokens, slots)
     for n in range(per):
+        q = q_ref[n]
         state, dr, k2 = two(st_ref[n]), two(dr_ref[n]), two(kn_ref[n])
         d = wu_ref[n, :, pl.ds(HEAD, HEAD)] - mm(two(wu_ref[n, :, pl.ds(0, HEAD)]), state)
         d_ref[n] = d
         ds = two(jnp.where(seen, mm(dr, two(d), ROWS_ROWS), 0.0))
         dq = mm(dr, state, ROWS_ROWS) + mm(ds, k2)
-        dk_ref[n] = mm(ds, two(q_ref[n]), COLS_COLS)
+        dk_ref[n] = mm(ds, two(q), COLS_COLS)
         dd_ref[n] = mm(two(sc_ref[n]), dr, COLS_COLS)
-        s = conv_rows(vq_ref[n, pl.ds(rows, tokens), :].astype(F32), tops[n], taps, pad.at[n], 1)
-        sg = sigmoid(s)
-        q, scale = unit(s * sg)
-        dc = scale * (dq - q * jnp.sum(q * dq, axis=-1, keepdims=True))
-        inner, rim = conv_back(dc * sg * (1.0 + s * (1.0 - sg)), taps, pad.at[n], 1)
-        gq_ref[n, pl.ds(0, tokens), :] = inner.astype(BF16)
-        gq_ref[n, pl.ds(tokens, EDGE), :] = jnp.concatenate([rim, jnp.zeros((8, HEAD), F32)], axis=0).astype(BF16)
-
-
-def value_grads_kernel(
-    per, tokens, slots, hid, vq_ref, beta_ref, tail_ref, wts_ref, end_ref, mb_ref, kn_ref, ti_ref, d_ref, dd_ref,
-    g_ref, de_ref, gv_ref, pad, halo,
+        inner, rim = conv_back(fq_ref[n] * (dq - q * jnp.sum(q * dq, axis=-1, keepdims=True)), taps, pad.at[n], 1)
+        nq_ref[n, pl.ds(0, tokens), :] = nm_ref[n]
+        nq_ref[n, pl.ds(tokens, tokens), :] = inner.astype(BF16)
+        nq_ref[n, pl.ds(2 * tokens, EDGE), :] = jnp.concatenate([rim, jnp.zeros((8, HEAD), F32)], axis=0).astype(BF16)
+
+
+def grads_kernel(
+    per, tokens, slots, hid, beta_ref, wts_ref, end_ref, mb_ref, kn_ref, ti_ref, d_ref, dk_ref, dd_ref, st_ref,
+    fk_ref, fv_ref, out_ref, pad,
 ):
     rows = tokens * slots
-    taps = slot_taps(wts_ref[...], 1)
-    tops = edges(vq_ref, 0, rows, per, tail_ref[pl.ds(EDGE, EDGE), :].astype(F32), halo)
+    wts = wts_ref[...]
+    order = before(rows)
     end = two(end_ref[...])
     for n in range(per):
-        g = mm(two(mb_ref[n, :, pl.ds(0, HEAD)]), end) + mb_ref[n, :, pl.ds(HEAD, HEAD)]
-        g_ref[n] = g
-        dd = dd_ref[n] + mm(two(kn_ref[n]), two(g))
-        y = mm(two(ti_ref[n]), two(dd), COLS_COLS)
+        k, d = kn_ref[n], d_ref[n]
+        k2, d2 = two(k), two(d)
+        g2 = two(mm(two(mb_ref[n, :, pl.ds(0, HEAD)]), end) + mb_ref[n, :, pl.ds(HEAD, HEAD)])
+        y = mm(two(ti_ref[n]), two(dd_ref[n] + mm(k2, g2)), COLS_COLS)
         betas = beta_rows(beta_ref[n].astype(F32), slots)
         de = 2.0 * sigmoid(column(betas, tokens, slots)) * y
-        de_ref[n] = de
-        along = jnp.sum(y * d_ref[n], axis=1, keepdims=True)
+        de2 = two(de)
+        dgram = jnp.where(order, mm(de2, d2, ROWS_ROWS), 0.0)
+        dk = dk_ref[n] + mm(d2, g2, ROWS_ROWS) - mm(de2, two(st_ref[n]), ROWS_ROWS)
+        dk = dk - mm(two(dgram + dgram.T), k2)
+        along = jnp.sum(y * d, axis=1, keepdims=True)
         marks = []
         for j in range(slots):
             gb = jnp.sum(jnp.where(places(tokens, slots, j), along, 0.0), axis=0, keepdims=True) * sigmoid(-betas[j])
             high = gb.astype(BF16).astype(F32)
             marks += [high, gb - high]
         marks.append(jnp.zeros((EDGE - 2 * slots, tokens), F32))
-        s = conv_rows(vq_ref[n, pl.ds(0, rows), :].astype(F32), tops[n], taps, pad.at[n], slots)
-        sg = sigmoid(s)
-        inner, rim = conv_back(de * sg * (1.0 + s * (1.0 - sg)), taps, pad.at[n], slots)
-        gv_ref[n, pl.ds(0, rows), :] = inner.astype(BF16)
-        gv_ref[n, pl.ds(rows, EDGE), :] = jnp.concatenate(marks, axis=0).astype(BF16)
-        gv_ref[n, pl.ds(rows + EDGE, EDGE), :] = jnp.concatenate([rim, jnp.zeros((8, HEAD), F32)], axis=0).astype(BF16)
-
-
-def key_grads_kernel(
-    per, tokens, slots, hid, kb_ref, tail_ref, wts_ref, kn_ref, d_ref, dk_ref, de_ref, st_ref, g_ref,
-    gk_ref, pad, halo,
-):
+        value, value_rim = conv_back(fv_ref[n] * de, slot_taps(wts, 1), pad.at[2 * n], slots)
+        part = fk_ref[n] * (dk - k * jnp.sum(k * dk, axis=-1, keepdims=True))
+        key, key_rim = conv_back(part, slot_taps(wts, 0), pad.at[2 * n + 1], slots)
+        out_ref[n, pl.ds(0, rows), :] = key.astype(BF16)
+        out_ref[n, pl.ds(rows, rows), :] = value.astype(BF16)
+        out_ref[n, pl.ds(2 * rows, EDGE), :] = jnp.concatenate(marks, axis=0).astype(BF16)
+        out_ref[n, pl.ds(2 * rows + EDGE, EDGE), :] = jnp.concatenate([key_rim, value_rim], axis=0).astype(BF16)
+
+
+def unpack_kernel(tokens, slots, got_ref, rim_ref, gk_ref, gv_ref):
     rows = tokens * slots
-    taps = slot_taps(wts_ref[...], 0)
-    tops = edges(kb_ref, 0, rows, per, tail_ref[pl.ds(0, EDGE), :].astype(F32), halo)
-    order = before(rows)
-    for n in range(per):
-        k = kn_ref[n]
-        k2, d2, de2 = two(k), two(d_ref[n]), two(de_ref[n])
-        dgram = jnp.where(order, mm(de2, d2, ROWS_ROWS), 0.0)
-        dk = dk_ref[n] + mm(d2, two(g_ref[n]), ROWS_ROWS) - mm(de2, two(st_ref[n]), ROWS_ROWS)
-        dk = dk - mm(two(dgram + dgram.T), k2)
-        s = conv_rows(kb_ref[n, pl.ds(0, rows), :].astype(F32), tops[n], taps, pad.at[n], slots)
-        sg = sigmoid(s)
-        scale = unit(s * sg)[1]
-        dc = scale * (dk - k * jnp.sum(k * dk, axis=-1, keepdims=True))
-        inner, rim = conv_back(dc * sg * (1.0 + s * (1.0 - sg)), taps, pad.at[n], slots)
-        gk_ref[n, pl.ds(0, rows), :] = inner.astype(BF16)
-        gk_ref[n, pl.ds(rows, EDGE), :] = jnp.concatenate([rim, jnp.zeros((8, HEAD), F32)], axis=0).astype(BF16)
-
-
-def call(kernel, hid, steps, ins, outs, scratch=(), us=1.0):
+    for a, out_ref in enumerate((gk_ref, gv_ref)):
+        main = got_ref[0, pl.ds(a * rows, rows), :].astype(F32)
+        last = main[rows - 8 :] + rim_ref[0, pl.ds(8 * a, 8), :].astype(F32)
+        out_ref[...] = jnp.concatenate([main[: rows - 8], last], axis=0).reshape(tokens, slots, HEAD)
+
+
+def unpack_query_kernel(tokens, got_ref, rim_ref, gq_ref):
+    main = got_ref[0, pl.ds(tokens, tokens), :].astype(F32)
+    last = main[tokens - 8 :] + rim_ref[0, pl.ds(0, 8), :].astype(F32)
+    gq_ref[...] = jnp.concatenate([main[: tokens - 8], last], axis=0)
+
+
+def call(kernel, hid, steps, ins, outs, scratch=(), us=1.0, grant=24):
     def spec(shape, per):
         if per == "weights":
             return pl.BlockSpec((shape[0], HEAD), lambda i, h: (0, h[0]))
@@ -381,10 +381,10 @@
             out_specs=[spec(s, per) for s, _, per in outs],
             scratch_shapes=list(scratch),
         ),
-        out_shape=[jax.ShapeDtypeStruct(s, d) for s, d, _ in outs],
-        compiler_params=pltpu.CompilerParams(dimension_semantics=("arbitrary",), vmem_limit_bytes=24 << 20),
+        out_shape=[pltpu.HBM(s, d) if len(s) == 3 else jax.ShapeDtypeStruct(s, d) for s, d, _ in outs],
+        compiler_params=pltpu.CompilerParams(dimension_semantics=("arbitrary",), vmem_limit_bytes=grant << 20),
         cost_estimate=pl.CostEstimate(flops=int(us * 1.1e9), bytes_accessed=1 << 16, transcendentals=0),
-    )(hid, *[a for a, _ in ins])
+    )(hid, *[pltpu.with_memory_space_constraint(a, pltpu.HBM) if a.dtype == F32 and a.ndim == 3 else a for a, _ in ins])
 
 
 def shards(
@@ -425,17 +425,16 @@
     betas = jnp.stack([high, middle, rest - middle], axis=2)
     betas = betas.transpose(3, 1, 2, 0).reshape(heads, 3 * slots, tokens).astype(BF16)
     betas = jnp.pad(betas, ((0, 0), (0, EDGE - 3 * slots), (0, 0)))
-    kb = exchange(jnp.concatenate([slots_by_head(key_in), betas], axis=1))
-
     last = EDGE // slots
-    tail = jnp.concatenate(
-        [slots_by_head(key_in[-last:]), slots_by_head(value_in[-last:]), by_head(query_in[-EDGE:])], axis=1
-    )
-    tail = jnp.concatenate([tail] * groups, axis=0)
-    tail = lax.all_to_all(tail, "ctx", 0, 0, tiled=True)
+    kb = exchange(
+        jnp.concatenate(
+            [slots_by_head(key_in), betas, slots_by_head(value_in[-last:]), by_head(query_in[-EDGE:])], axis=1
+        )
+    )
+
     group = place // heads
-    tail = lax.dynamic_index_in_dim(tail, jnp.maximum(group * heads - 1, 0), 0, False)
-    tail = jnp.where(group > 0, tail, jnp.zeros_like(tail))
+    tail = jnp.concatenate([kb[g - 1, rows - EDGE : rows], kb[g - 1, rows + EDGE :]], axis=0)
+    tail = lax.ppermute(tail, "ctx", [(i, i + heads) for i in range(shard_count - heads)])
 
     grad_normed = jnp.dot(grad_out, out_weight.T, preferred_element_type=F32).astype(BF16)
     vq = exchange(
@@ -458,17 +457,17 @@
     def pad(n):
         return [pltpu.VMEM((per, n + EDGE + 8, HEAD), F32), pltpu.VMEM((EDGE, HEAD), F32)]
 
-    kn, ti = call(
+    kn, ti, fk = call(
         functools.partial(inverse_kernel, per, tokens, slots),
         hid,
         steps,
         [(kb, per), (tail, None), (wts, "weights")],
-        [((g, rows, HEAD), F32, per), ((g, rows, rows), F32, per)],
+        [((g, rows, HEAD), F32, per), ((g, rows, rows), F32, per), ((g, rows, HEAD), F32, per)],
         pad(rows),
-        us=16.0,
+        us=12.0,
     )
     beta = (kb, (per, rows))
-    wu, amap, mc, end = call(
+    wu, amap, mc, end, fv = call(
         functools.partial(maps_kernel, per, tokens, slots),
         hid,
         steps,
@@ -478,6 +477,7 @@
             ((g, HEAD, HEAD), F32, per),
             ((g, HEAD, 2 * HEAD), F32, per),
             ((HEAD, 2 * HEAD), F32, None),
+            ((g, rows, HEAD), F32, per),
         ],
         pad(rows) + [pltpu.VMEM((HEAD, 2 * HEAD), F32)],
         us=8.0,
@@ -501,7 +501,7 @@
         return lax.fori_loop(0, ahead, advance, jnp.zeros((HEAD, HEAD), F32))
 
     start = across(end, 1)
-    q, sc, qm, ol = call(
+    q, sc, qm, ol, fq = call(
         functools.partial(queries_kernel, per, tokens, slots),
         hid,
         steps,
@@ -509,6 +509,7 @@
         [
             ((g, tokens, HEAD), F32, per),
             ((g, tokens, rows), F32, per),
+            ((g, tokens, HEAD), F32, per),
             ((g, tokens, HEAD), F32, per),
             ((g, tokens, HEAD), F32, per),
         ],
@@ -530,52 +531,36 @@
         us=4.0,
     )
     finish = across(back_end, -1)
-    d, dk, dd, gq = call(
+    d, dk, dd, nq = call(
         functools.partial(query_grads_kernel, per, tokens, slots),
         hid,
         steps,
         [
-            (vq, per), (tail, None), (wts, "weights"), (kn, per), (wu, per), (q, per), (sc, per), (dr, per), (st, per),
+            (wts, "weights"), (kn, per), (wu, per), (q, per), (sc, per), (dr, per), (st, per), (fq, per), (normed, per),
         ],
         [
             ((g, rows, HEAD), F32, per),
             ((g, rows, HEAD), F32, per),
             ((g, rows, HEAD), F32, per),
-            ((g, tokens + EDGE, HEAD), BF16, per),
+            ((g, 2 * tokens + EDGE, HEAD), BF16, per),
         ],
-        pad(tokens),
+        pad(tokens)[:1],
         us=20.0,
     )
-    nq = exchange(jnp.concatenate([normed, gq], axis=1))
-    gs, de, gv = call(
-        functools.partial(value_grads_kernel, per, tokens, slots),
+    nq = exchange(nq)
+    (grads,) = call(
+        functools.partial(grads_kernel, per, tokens, slots),
         hid,
         steps,
         [
-            (vq, per), beta, (tail, None), (wts, "weights"), (finish, None), (mb, per), (kn, per), (ti, per),
-            (d, per), (dd, per),
+            beta, (wts, "weights"), (finish, None), (mb, per), (kn, per), (ti, per), (d, per), (dk, per), (dd, per),
+            (st, per), (fk, per), (fv, per),
         ],
-        [
-            ((g, HEAD, HEAD), F32, per),
-            ((g, rows, HEAD), F32, per),
-            ((g, rows + 2 * EDGE, HEAD), BF16, per),
-        ],
-        pad(rows),
-        us=8.0,
-    )
-    gv = exchange(gv)
-    (gk,) = call(
-        functools.partial(key_grads_kernel, per, tokens, slots),
-        hid,
-        steps,
-        [
-            (kb, per), (tail, None), (wts, "weights"), (kn, per), (d, per), (dk, per), (de, per), (st, per), (gs, per),
-        ],
-        [((g, rows + EDGE, HEAD), BF16, per)],
-        pad(rows),
-        us=12.0,
-    )
-    gk = exchange(gk)
+        [((g, 2 * rows + 2 * EDGE, HEAD), BF16, per)],
+        [pltpu.VMEM((2 * per, rows + EDGE + 8, HEAD), F32)],
+        us=20.0,
+    )
+    grads = exchange(grads)
 
     normed_bf = nq[:, :tokens].transpose(1, 0, 2).reshape(tokens, width)
     partial = jnp.dot(normed_bf, out_weight, preferred_element_type=F32)
@@ -589,27 +574,27 @@
     else:
         layer_out = lax.psum_scatter(partial.astype(BF16), "head", scatter_dimension=0, tiled=True)
 
-    edge = RIM * slots
-    rims = jnp.concatenate(
-        [
-            gk[:, rows + 8 - edge : rows + 8],
-            gv[:, rows + EDGE + 8 - edge : rows + EDGE + 8],
-            nq[:, 2 * tokens + 8 - RIM : 2 * tokens + 8],
-        ],
-        axis=1,
-    )
-    rims = lax.ppermute(rims, "ctx", [(i, i - 1) for i in range(1, shard_count)]).astype(F32)
-
-    def slots_back(block, rim):
-        block = block.reshape(heads, tokens, slots, HEAD).astype(F32)
-        rim = jnp.pad(rim.reshape(heads, RIM, slots, HEAD), ((0, 0), (tokens - RIM, 0), (0, 0), (0, 0)))
-        return (block + rim).transpose(1, 2, 0, 3).reshape(tokens, slots, width)
-
-    grad_key = slots_back(gk[:, :rows], rims[:, :edge])
-    grad_value = slots_back(gv[:, :rows], rims[:, edge : 2 * edge])
-    rim_query = jnp.pad(rims[:, 2 * edge :], ((0, 0), (tokens - RIM, 0), (0, 0)))
-    grad_query = (nq[:, tokens : 2 * tokens].astype(F32) + rim_query).transpose(1, 0, 2).reshape(tokens, width)
-    marks = gv[:, rows : rows + 2 * slots].astype(F32)
+    back = [(i, i - 1) for i in range(1, shard_count)]
+    query_rim = lax.ppermute(nq[:, 2 * tokens :], "ctx", back)
+    rim = lax.ppermute(grads[:, 2 * rows + EDGE :], "ctx", back)
+    part = lambda x: pl.BlockSpec((1,) + x.shape[1:], lambda h: (h, 0, 0))
+    grad_query = pl.pallas_call(
+        functools.partial(unpack_query_kernel, tokens),
+        grid=(heads,),
+        in_specs=[part(nq), part(query_rim)],
+        out_specs=pl.BlockSpec((tokens, HEAD), lambda h: (0, h)),
+        out_shape=jax.ShapeDtypeStruct((tokens, width), F32),
+        compiler_params=pltpu.CompilerParams(vmem_limit_bytes=8 << 20),
+    )(nq, query_rim)
+    grad_key, grad_value = pl.pallas_call(
+        functools.partial(unpack_kernel, tokens, slots),
+        grid=(heads,),
+        in_specs=[part(grads), part(rim)],
+        out_specs=[pl.BlockSpec((tokens, slots, HEAD), lambda h: (0, 0, h))] * 2,
+        out_shape=[jax.ShapeDtypeStruct((tokens, slots, width), F32)] * 2,
+        compiler_params=pltpu.CompilerParams(vmem_limit_bytes=8 << 20),
+    )(grads, rim)
+    marks = grads[:, 2 * rows : 2 * rows + 2 * slots].astype(F32)
     grad_beta = marks.reshape(heads, slots, 2, tokens).sum(axis=2).transpose(2, 1, 0)
     return (layer_out, grad_query, grad_key, grad_value, grad_beta)
 

time: 140 us -> 131 us (0.936)
  local copies, waits for them, and re-layouts: 24.3 us -> 5.51 us
  Pallas kernels: 40.9 us -> 56.4 us
  other arithmetic: 8.31 us -> 4.54 us
  starting transfers between devices: 36.8 us -> 34.1 us
    ppermute x1 -> x3, waiting for transfers between devices: 1.94 us -> 18.1 us  [the longest x1 8.07 us: shards(): query_rim = lax.ppermute(nq[:, 2 * tokens:], 'ctx', back)]
    unnamed x53 -> x22, local copies, waits for them, and re-layouts: 13.3 us -> 2.01 us
    all_to_all x5 -> x4, waiting for transfers between devices: 13 us -> 3.03 us  [exchange(): lax.all_to_all(x, 'ctx', 0, 0, axis_index_groups=group_lists, tiled=True)]
    pallas_call x7 -> x6, Pallas kernels: 40.9 us -> 50.7 us  [call(): pl.pallas_call(kernel, grid_spec=pltpu.PrefetchScalarGridSpec(num_scalar_...]
    all_to_all x1 -> x0, starting transfers between devices: 7.35 us -> none  [shards(): tail = lax.all_to_all(tail, 'ctx', 0, 0, tiled=True)]
    pallas_call x0 -> x2, Pallas kernels: none -> 5.61 us  [the longest x1 3.06 us: shards(): pl.pallas_call(functools.partial(unpack_kernel, tokens, slots), grid=(hea...]
    ppermute x1 -> x3, starting transfers between devices: 2.78 us -> 8.3 us  [the longest x1 4.21 us: shards(): lax.ppermute(tail, 'ctx', [(i, i + heads) for i in range(shard_count - he...]
    all_to_all x1 -> x0, waiting for transfers between devices: 5.34 us -> none  [shards(): tail = lax.all_to_all(tail, 'ctx', 0, 0, tiled=True)]
  transfers between devices with their start and end apart: 10 -> 10, of which waited for: 5 -> 4; matrix products, arithmetic and copies ran while one was open for 17% -> 9% of each run, Pallas kernels for 23% -> 31%
where the time goes in v3:
time: 131 us; the launch traced here: 129 us
  Pallas kernels  56.4 us (43%)
  starting transfers between devices  34.1 us (26%)
  waiting for transfers between devices  21.1 us (16%)
  matrix products  6.66 us (5%)
  local copies, waits for them, and re-layouts  5.51 us (4%)
  other arithmetic  4.54 us (3%)
    pallas_call x6, Pallas kernels, call(): pl.pallas_call(kernel, grid_spec=pltpu.PrefetchScalarGridSpec(num_scalar_...  50.7 us
    all_to_all x4, starting transfers between devices, exchange(): lax.all_to_all(x, 'ctx', 0, 0, axis_index_groups=group_lists, tiled=True)  18.5 us
    ppermute x1, waiting for transfers between devices, shards(): query_rim = lax.ppermute(nq[:, 2 * tokens:], 'ctx', back)  8.07 us
    ppermute x1, waiting for transfers between devices, shards(): lax.ppermute(tail, 'ctx', [(i, i + heads) for i in range(shard_count - he...  7.38 us
    ppermute x2, starting transfers between devices, across(): return lax.ppermute(last[:, HEAD:], 'ctx', moves)  6 us
    ppermute x1, starting transfers between devices, shards(): lax.ppermute(tail, 'ctx', [(i, i + heads) for i in range(shard_count - he...  4.21 us
    dot_general x1, matrix products, shards(): jnp.dot(grad_out, out_weight.T, preferred_element_type=F32).astype(BF16)  3.76 us
    pallas_call x1, Pallas kernels, shards(): pl.pallas_call(functools.partial(unpack_kernel, tokens, slots), grid=(hea...  3.06 us
  transfers between devices with their start and end apart: 10, of which 4 were waited for; matrix products, arithmetic and copies ran while one was open for 9% of the time, Pallas kernels for 31%

profile of v3, /device:TPU:1, one launch (start us, length us, event | category | flops | bytes accessed | tf_op | source)
XLA Modules:
  0.0 129.3 jit_solution(7507874952601476631)
XLA Ops:
  0.6 0.0 copy-start
  0.6 0.0 copy-start.5
  0.7 0.8 fusion.11
  1.5 0.2 copy-done
  1.7 0.4 copy_bitcast_fusion.1
  2.1 0.8 copy_bitcast_fusion.2
  2.9 0.8 bitcast_bitcast_fusion
  3.6 0.9 fusion.6
  4.5 5.3 %all-to-all-start = ((bf16[8,304,128]{2,1,0:T(8,128)(2,1)}), bf16[8,304,128]{2,1,0:T(8,128)(2,1)S(1)}, u32[]{:S(2)}, u32[]{:S(2)}) async-start(bf16[8,304,128]{2,1,0:T(8,128)(2,1)} %fusion.6), calls=%async_computation | async-start | bytes 1245184 | tf_op jit(solution)/shard_map/all_to_all | solution.py:414
  9.8 0.2 copy.38
  10.0 3.8 %convolution_convert_fusion = bf16[128,1024]{1,0:T(8,128)(2,1)S(1)} fusion(bf16[128,2048]{1,0:T(8,128)(2,1)S(1)} %copy-done.4, bf16[1024,2048]{1,0:T(8,128)(2,1)} %param.18), kind=kOutput, calls=%fused_computation.6 | convolution fusion | flops 537001984 | bytes 4980736 | tf_op jit(solution)/shard_map/dot_general | solution.py:439
  13.8 0.2 copy.40
  13.9 0.2 copy.41
  14.1 0.2 copy.39
  14.3 0.4 copy_bitcast_fusion
  14.7 0.0 copy-start.8
  14.7 0.0 copy-start.9
  14.7 1.1 pad_maximum_fusion
  15.8 3.0 %all-to-all-done.kb_ref.beta_ref = bf16[8,304,128]{2,1,0:T(8,128)(2,1)S(1)} async-done(((bf16[8,304,128]{2,1,0:T(8,128)(2,1)}), bf16[8,304,128]{2,1,0:T(8,128)(2,1)S(1)}, u32[]{:S(2)}, u32[]{:S(2)}) %all-to-all-start) | async-done | bytes 622624 | tf_op jit(solution)/shard_map/all_to_all | solution.py:414
  18.8 4.3 %all-to-all-start.1 = ((bf16[8,512,128]{2,1,0:T(8,128)(2,1)}), bf16[8,512,128]{2,1,0:T(8,128)(2,1)S(1)}, u32[]{:S(2)}, u32[]{:S(2)}) async-start(bf16[8,512,128]{2,1,0:T(8,128)(2,1)} %pad_maximum_fusion), calls=%async_computation.1 | async-start | bytes 2097152 | tf_op jit(solution)/shard_map/all_to_all | solution.py:414
  23.2 4.2 %collective-permute-start = (bf16[48,128]{1,0:T(8,128)(2,1)S(1)}, bf16[48,128]{1,0:T(8,128)(2,1)S(1)}, u32[]{:S(2)}, u32[]{:S(2)}) collective-permute-start(bf16[48,128]{1,0:T(8,128)(2,1)S(1)} %pad_maximum_fusion.2), channel_id=1, source_target_pairs={{0,16},{2,18},{4,20},{6,22},{8,24},{10,26},{12,28},{14,30},{1,17},... | collective-permute-start | bytes 36872 | tf_op jit(solution)/shard_map/ppermute | solution.py:437
  27.5 0.1 tile.17
  27.6 0.1 tile.19
  27.7 0.1 concatenate.12.wts_ref
  27.8 7.4 %collective-permute-done.tail_ref = bf16[48,128]{1,0:T(8,128)(2,1)S(1)} collective-permute-done((bf16[48,128]{1,0:T(8,128)(2,1)S(1)}, bf16[48,128]{1,0:T(8,128)(2,1)S(1)}, u32[]{:S(2)}, u32[]{:S(2)}) %collective-permute-start) | collective-permute-done | bytes 12320 | tf_op jit(solution)/shard_map/ppermute | solution.py:437
  35.2 13.2 %shard_map.137 = (f32[8,256,128]{2,1,0:T(8,128)}, f32[8,256,256]{2,1,0:T(8,128)}, f32[8,256,128]{2,1,0:T(8,128)}) custom-call(s32[1]{0:T(128)} %bitcast.hid, bf16[8,304,128]{2,1,0:T(8,128)(2,1)S(1)} %all-to-all-done.kb_ref.beta_ref, bf16[48,128]{1,0:T(8,128)(2,1)S(1)} %collective-permute-done.tail_ref, f32[72,1024]{1,0:T(8,128)S(1)} %concatenate.12.wts_ref), custom_call_target="tpu_custom_call" | custom-call | flops 13200000000 | bytes 65536 | tf_op jit(solution)/shard_map/pallas_call | solution.py:375
  48.4 8.0 %shard_map.138 = (f32[8,256,256]{2,1,0:T(8,128)}, f32[8,128,128]{2,1,0:T(8,128)}, f32[8,128,256]{2,1,0:T(8,128)}, f32[128,256]{1,0:T(8,128)S(1)}, f32[8,256,128]{2,1,0:T(8,128)}) custom-call(s32[1]{0:T(128)} %bitcast.hid, bf16[8,512,128]{2,1,0:T(8,128)(2,1)S(1)} %all-to-all-done.1.vq_ref, bf16[8,304,128]{2,1,0:T(8,128)(2,1)S(1)} %all-to-all-done.kb_ref.beta_ref, ...), custom_call_target="tpu_custom_call" | custom-call | flops 8800000000 | bytes 65536 | tf_op jit(solution)/shard_map/pallas_call | solution.py:375
  56.3 4.7 %collective-permute-start.1 = (f32[128,128]{1,0:T(8,128)S(1)}, f32[128,128]{1,0:T(8,128)S(1)}, u32[]{:S(2)}, u32[]{:S(2)}) collective-permute-start(f32[128,128]{1,0:T(8,128)S(1)} %slice.34), channel_id=1, source_target_pairs={{0,16},{2,18},{4,20},{6,22},{8,24},{10,26},{12,28},{14,30},{1,17},... | collective-permute-start | bytes 196616 | tf_op jit(solution)/shard_map/ppermute | solution.py:491
  61.0 5.9 %shard_map.139 = (f32[8,128,128]{2,1,0:T(8,128)}, f32[8,128,256]{2,1,0:T(8,128)}, f32[8,128,128]{2,1,0:T(8,128)}, f32[8,128,128]{2,1,0:T(8,128)}, f32[8,128,128]{2,1,0:T(8,128)}) custom-call(s32[1]{0:T(128)} %bitcast.hid, bf16[8,512,128]{2,1,0:T(8,128)(2,1)S(1)} %all-to-all-done.1.vq_ref, bf16[48,128]{1,0:T(8,128)(2,1)S(1)} %collective-permute-done.tail_ref, ...), custom_call_target="tpu_custom_call" | custom-call | flops 8800000000 | bytes 65536 | tf_op jit(solution)/shard_map/pallas_call | solution.py:375
  67.0 5.0 %shard_map.140 = (bf16[8,128,128]{2,1,0:T(8,128)(2,1)}, f32[8,128,128]{2,1,0:T(8,128)}, f32[8,128,128]{2,1,0:T(8,128)}, f32[8,128,256]{2,1,0:T(8,128)}, f32[128,256]{1,0:T(8,128)S(1)}) custom-call(s32[1]{0:T(128)} %bitcast.hid, bf16[8,512,128]{2,1,0:T(8,128)(2,1)S(1)} %all-to-all-done.1.vq_ref, f32[72,1024]{1,0:T(8,128)S(1)} %concatenate.12.wts_ref, ...), custom_call_target="tpu_custom_call" | custom-call | flops 4400000000 | bytes 65536 | tf_op jit(solution)/shard_map/pallas_call | solution.py:375
  71.9 1.3 collective-permute-start.4
  73.2 0.9 copy-done.1
  74.2 7.6 %shard_map.141 = (f32[8,256,128]{2,1,0:T(8,128)}, f32[8,256,128]{2,1,0:T(8,128)}, f32[8,256,128]{2,1,0:T(8,128)}, bf16[8,272,128]{2,1,0:T(8,128)(2,1)}) custom-call(s32[1]{0:T(128)} %bitcast.hid, f32[72,1024]{1,0:T(8,128)S(1)} %concatenate.12.wts_ref, f32[8,256,128]{2,1,0:T(8,128)} %get-tuple-element.29.kn_ref, f32[8,256,256]{2,1,0:T(8,128)} %get-tuple-element.31.wu_ref, ...), custom_call_target="tpu_custom_call" | custom-call | flops 22000001024 | bytes 65536 | tf_op jit(solution)/shard_map/pallas_call | solution.py:375
  81.8 4.6 %all-to-all-start.2 = ((bf16[8,272,128]{2,1,0:T(8,128)(2,1)}), bf16[8,272,128]{2,1,0:T(8,128)(2,1)S(1)}, u32[]{:S(2)}, u32[]{:S(2)}) async-start(bf16[8,272,128]{2,1,0:T(8,128)(2,1)} %get-tuple-element.43), calls=%async_computation.2 | async-start | bytes 1114112 | tf_op jit(solution)/shard_map/all_to_all | solution.py:414
  86.4 11.1 %shard_map.143 = bf16[8,544,128]{2,1,0:T(8,128)(2,1)} custom-call(s32[1]{0:T(128)} %bitcast.hid, bf16[8,304,128]{2,1,0:T(8,128)(2,1)S(1)} %all-to-all-done.kb_ref.beta_ref, f32[72,1024]{1,0:T(8,128)S(1)} %concatenate.12.wts_ref, f32[128,128]{1,0:T(8,128)S(1)} %collective-permute-done.4.end_ref, f32[8,128,256]{2,1,0:T(8,128)} %get-tuple-element.45.mb_ref, ...), custom_call_target="tpu_custom_call" | custom-call | flops 22000001024 | bytes 65536 | tf_op jit(solution)/shard_map/pallas_call | solution.py:375
  97.6 4.2 %all-to-all-start.3 = ((bf16[8,544,128]{2,1,0:T(8,128)(2,1)}), bf16[8,544,128]{2,1,0:T(8,128)(2,1)S(1)}, u32[]{:S(2)}, u32[]{:S(2)}) async-start(bf16[8,544,128]{2,1,0:T(8,128)(2,1)} %shard_map.143), calls=%async_computation.3 | async-start | bytes 2228224 | tf_op jit(solution)/shard_map/all_to_all | solution.py:414
  101.8 0.2 copy.42
  102.0 0.1 dot_general.9
  102.1 2.9 %fusion = f32[2,64,2048]{2,1,0:T(8,128)S(1)} fusion(bf16[2,64,1024]{2,1,0:T(8,128)(2,1)S(1)} %dot_general.9, bf16[1024,2048]{1,0:T(8,128)(2,1)} %param.18), kind=kOutput, calls=%fused_computation | convolution fusion | flops 536870912 | bytes 5505024 | tf_op jit(solution)/shard_map/dot_general | solution.py:566
  105.1 1.3 collective-permute-start.2
  106.4 2.2 %collective-permute-start.3 = (bf16[8,16,128]{2,1,0:T(8,128)(2,1)S(1)}, bf16[8,16,128]{2,1,0:T(8,128)(2,1)S(1)}, u32[]{:S(2)}, u32[]{:S(2)}) collective-permute-start(bf16[8,16,128]{2,1,0:T(8,128)(2,1)S(1)} %slice.43), channel_id=1, source_target_pairs={{2,0},{4,2},{6,4},{8,6},{10,8},{12,10},{14,12},{16,14},{18,16},{20... | collective-permute-start | bytes 98312 | tf_op jit(solution)/shard_map/ppermute | solution.py:578
  108.6 8.1 %collective-permute-done.3.rim_ref = bf16[8,16,128]{2,1,0:T(8,128)(2,1)S(1)} collective-permute-done((bf16[8,16,128]{2,1,0:T(8,128)(2,1)S(1)}, bf16[8,16,128]{2,1,0:T(8,128)(2,1)S(1)}, u32[]{:S(2)}, u32[]{:S(2)}) %collective-permute-start.3) | collective-permute-done | bytes 32800 | tf_op jit(solution)/shard_map/ppermute | solution.py:578
  116.6 2.6 %shard_map.142 = f32[128,1024]{1,0:T(8,128)} custom-call(bf16[8,272,128]{2,1,0:T(8,128)(2,1)S(1)} %all-to-all-done.2.got_ref, bf16[8,16,128]{2,1,0:T(8,128)(2,1)S(1)} %collective-permute-done.3.rim_ref), custom_call_target="tpu_custom_call" | custom-call | tf_op jit(solution)/shard_map/pallas_call | solution.py:581
  119.2 1.8 %fusion.7 = bf16[64,2048]{1,0:T(8,128)(2,1)} fusion(bf16[64,2048]{1,0:T(8,128)(2,1)S(1)} %collective-permute-done.2, f32[2,64,2048]{2,1,0:T(8,128)} %copy-done.2, s32[]{:T(128)S(6)} %select_n.15), kind=kLoop, calls=%fused_computation.14 | loop fusion | flops 393216 | bytes 1048580 | tf_op jit(solution)/shard_map/convert_element_type | solution.py:573
  121.0 1.9 %collective-permute-start.5 = (bf16[8,16,128]{2,1,0:T(8,128)(2,1)S(1)}, bf16[8,16,128]{2,1,0:T(8,128)(2,1)S(1)}, u32[]{:S(2)}, u32[]{:S(2)}) collective-permute-start(bf16[8,16,128]{2,1,0:T(8,128)(2,1)S(1)} %slice.44), channel_id=1, source_target_pairs={{2,0},{4,2},{6,4},{8,6},{10,8},{12,10},{14,12},{16,14},{18,16},{20... | collective-permute-start | bytes 98312 | tf_op jit(solution)/shard_map/ppermute | solution.py:579
  123.0 0.6 copy.43
  123.6 2.7 %collective-permute-done.5.rim_ref = bf16[8,16,128]{2,1,0:T(8,128)(2,1)S(1)} collective-permute-done((bf16[8,16,128]{2,1,0:T(8,128)(2,1)S(1)}, bf16[8,16,128]{2,1,0:T(8,128)(2,1)S(1)}, u32[]{:S(2)}, u32[]{:S(2)}) %collective-permute-start.5) | collective-permute-done | bytes 32800 | tf_op jit(solution)/shard_map/ppermute | solution.py:579
  126.2 3.1 %shard_map.144 = (f32[128,2,1024]{2,1,0:T(2,128)}, f32[128,2,1024]{2,1,0:T(2,128)}) custom-call(bf16[8,544,128]{2,1,0:T(8,128)(2,1)S(1)} %all-to-all-done.3.got_ref, bf16[8,16,128]{2,1,0:T(8,128)(2,1)S(1)} %collective-permute-done.5.rim_ref), custom_call_target="tpu_custom_call" | custom-call | tf_op jit(solution)/shard_map/pallas_call | solution.py:589
  (36 shorter events, 0.3 us)
Async XLA Ops:
  0.6 1.1 copy-start
  0.6 9.2 %copy-start.5 = (bf16[128,1024]{1,0:T(8,128)(2,1)S(1)}, bf16[128,1024]{1,0:T(8,128)(2,1)}, u32[]{:S(2)}) copy-start(bf16[128,1024]{1,0:T(8,128)(2,1)} %param.10) | copy-start | bytes 786436
  1.7 8.3 %copy-start.4 = (bf16[128,2048]{1,0:T(8,128)(2,1)S(1)}, bf16[128,2048]{1,0:T(8,128)(2,1)}, u32[]{:S(2)}) copy-start(bf16[128,2048]{1,0:T(8,128)(2,1)} %param.19) | copy-start | bytes 1572868
  4.5 14.3 %all-to-all-start = ((bf16[8,304,128]{2,1,0:T(8,128)(2,1)}), bf16[8,304,128]{2,1,0:T(8,128)(2,1)S(1)}, u32[]{:S(2)}, u32[]{:S(2)}) async-start(bf16[8,304,128]{2,1,0:T(8,128)(2,1)} %fusion.6), calls=%async_computation | async-start | bytes 1245184 | tf_op jit(solution)/shard_map/all_to_all | solution.py:414
  10.0 4.3 %copy-start.3 = (bf16[128,2,1024]{2,1,0:T(2,128)(2,1)S(1)}, bf16[128,2,1024]{2,1,0:T(2,128)(2,1)}, u32[]{:S(2)}) copy-start(bf16[128,2,1024]{2,1,0:T(2,128)(2,1)} %param.12) | copy-start | bytes 1572868
  14.7 12.7 %copy-start.6 = (f32[4,2,1024]{2,1,0:T(2,128)S(1)}, f32[4,2,1024]{2,1,0:T(2,128)}, u32[]{:S(2)}) copy-start(f32[4,2,1024]{2,1,0:T(2,128)} %param.15) | copy-start | bytes 98308
  14.7 12.9 %copy-start.7 = (f32[4,2,1024]{2,1,0:T(2,128)S(1)}, f32[4,2,1024]{2,1,0:T(2,128)}, u32[]{:S(2)}) copy-start(f32[4,2,1024]{2,1,0:T(2,128)} %param.16) | copy-start | bytes 98308
  14.7 13.0 %copy-start.8 = (f32[4,1024]{1,0:T(4,128)S(1)}, f32[4,1024]{1,0:T(4,128)}, u32[]{:S(2)}) copy-start(f32[4,1024]{1,0:T(4,128)} %param.14) | copy-start | bytes 49156
  14.7 13.0 %copy-start.9 = (f32[1024]{0:T(1024)S(1)}, f32[1024]{0:T(1024)}, u32[]{:S(2)}) copy-start(f32[1024]{0:T(1024)} %param.17) | copy-start | bytes 12292
  18.8 29.5 %all-to-all-start.1 = ((bf16[8,512,128]{2,1,0:T(8,128)(2,1)}), bf16[8,512,128]{2,1,0:T(8,128)(2,1)S(1)}, u32[]{:S(2)}, u32[]{:S(2)}) async-start(bf16[8,512,128]{2,1,0:T(8,128)(2,1)} %pad_maximum_fusion), calls=%async_computation.1 | async-start | bytes 2097152 | tf_op jit(solution)/shard_map/all_to_all | solution.py:414
  23.2 12.0 %collective-permute-start = (bf16[48,128]{1,0:T(8,128)(2,1)S(1)}, bf16[48,128]{1,0:T(8,128)(2,1)S(1)}, u32[]{:S(2)}, u32[]{:S(2)}) collective-permute-start(bf16[48,128]{1,0:T(8,128)(2,1)S(1)} %pad_maximum_fusion.2), channel_id=1, source_target_pairs={{0,16},{2,18},{4,20},{6,22},{8,24},{10,26},{12,28},{14,30},{1,17},... | collective-permute-start | bytes 36872 | tf_op jit(solution)/shard_map/ppermute | solution.py:437
  56.3 10.6 %collective-permute-start.1 = (f32[128,128]{1,0:T(8,128)S(1)}, f32[128,128]{1,0:T(8,128)S(1)}, u32[]{:S(2)}, u32[]{:S(2)}) collective-permute-start(f32[128,128]{1,0:T(8,128)S(1)} %slice.34), channel_id=1, source_target_pairs={{0,16},{2,18},{4,20},{6,22},{8,24},{10,26},{12,28},{14,30},{1,17},... | collective-permute-start | bytes 196616 | tf_op jit(solution)/shard_map/ppermute | solution.py:491
  71.9 14.5 %collective-permute-start.4 = (f32[128,128]{1,0:T(8,128)S(1)}, f32[128,128]{1,0:T(8,128)S(1)}, u32[]{:S(2)}, u32[]{:S(2)}) collective-permute-start(f32[128,128]{1,0:T(8,128)S(1)} %slice.37), channel_id=1, source_target_pairs={{16,0},{18,2},{20,4},{22,6},{24,8},{26,10},{28,12},{30,14},{17,1},... | collective-permute-start | bytes 196616 | tf_op jit(solution)/shard_map/ppermute | solution.py:491
  73.2 1.0 copy-start.1
  81.8 15.8 %all-to-all-start.2 = ((bf16[8,272,128]{2,1,0:T(8,128)(2,1)}), bf16[8,272,128]{2,1,0:T(8,128)(2,1)S(1)}, u32[]{:S(2)}, u32[]{:S(2)}) async-start(bf16[8,272,128]{2,1,0:T(8,128)(2,1)} %get-tuple-element.43), calls=%async_computation.2 | async-start | bytes 1114112 | tf_op jit(solution)/shard_map/all_to_all | solution.py:414
  97.6 23.4 %all-to-all-start.3 = ((bf16[8,544,128]{2,1,0:T(8,128)(2,1)}), bf16[8,544,128]{2,1,0:T(8,128)(2,1)S(1)}, u32[]{:S(2)}, u32[]{:S(2)}) async-start(bf16[8,544,128]{2,1,0:T(8,128)(2,1)} %shard_map.143), calls=%async_computation.3 | async-start | bytes 2228224 | tf_op jit(solution)/shard_map/all_to_all | solution.py:414
  105.1 1.3 %copy-start.2 = (f32[2,64,2048]{2,1,0:T(8,128)}, f32[2,64,2048]{2,1,0:T(8,128)S(1)}, u32[]{:S(2)}) copy-start(f32[2,64,2048]{2,1,0:T(8,128)S(1)} %fusion) | copy-start | bytes 3145732
  105.1 14.1 %collective-permute-start.2 = (bf16[64,2048]{1,0:T(8,128)(2,1)S(1)}, bf16[64,2048]{1,0:T(8,128)(2,1)S(1)}, u32[]{:S(2)}, u32[]{:S(2)}) collective-permute-start(bf16[64,2048]{1,0:T(8,128)(2,1)S(1)} %fusion.8), channel_id=1, source_target_pairs={{0,1},{1,0},{2,3},{3,2},{4,5},{5,4},{6,7},{7,6},{8,9},{9,8},{10,11... | collective-permute-start | bytes 786440 | tf_op jit(solution)/shard_map/ppermute | solution.py:573
  106.4 10.3 %collective-permute-start.3 = (bf16[8,16,128]{2,1,0:T(8,128)(2,1)S(1)}, bf16[8,16,128]{2,1,0:T(8,128)(2,1)S(1)}, u32[]{:S(2)}, u32[]{:S(2)}) collective-permute-start(bf16[8,16,128]{2,1,0:T(8,128)(2,1)S(1)} %slice.43), channel_id=1, source_target_pairs={{2,0},{4,2},{6,4},{8,6},{10,8},{12,10},{14,12},{16,14},{18,16},{20... | collective-permute-start | bytes 98312 | tf_op jit(solution)/shard_map/ppermute | solution.py:578
  121.0 5.2 %collective-permute-start.5 = (bf16[8,16,128]{2,1,0:T(8,128)(2,1)S(1)}, bf16[8,16,128]{2,1,0:T(8,128)(2,1)S(1)}, u32[]{:S(2)}, u32[]{:S(2)}) collective-permute-start(bf16[8,16,128]{2,1,0:T(8,128)(2,1)S(1)} %slice.44), channel_id=1, source_target_pairs={{2,0},{4,2},{6,4},{8,6},{10,8},{12,10},{14,12},{16,14},{18,16},{20... | collective-permute-start | bytes 98312 | tf_op jit(solution)/shard_map/ppermute | solution.py:579

commit v4 on v3

--- a/solution.py
+++ b/solution.py
@@ -139,20 +139,15 @@
     return wts[17 * TAPS : 17 * TAPS + 1]
 
 
-def edges(ref, first, rows, per, tail, halo):
-    @pl.when(pl.program_id(0) == 0)
-    def _():
-        halo[...] = tail
-
-    found = [halo[...]] + [ref[n, pl.ds(first + rows - EDGE, EDGE), :].astype(F32) for n in range(per - 1)]
-    halo[...] = ref[per - 1, pl.ds(first + rows - EDGE, EDGE), :].astype(F32)
-    return found
-
-
-def inverse_kernel(per, tokens, slots, hid, kb_ref, tail_ref, wts_ref, kn_ref, ti_ref, fk_ref, pad, halo):
+def edges(ref, first, rows, per, tail, prev_ref):
+    prev = jnp.where(pl.program_id(0) == 0, tail, prev_ref[0].astype(F32))
+    return [prev] + [ref[n, pl.ds(first + rows - EDGE, EDGE), :].astype(F32) for n in range(per - 1)]
+
+
+def inverse_kernel(per, tokens, slots, hid, kb_ref, prev_ref, tail_ref, wts_ref, kn_ref, ti_ref, fk_ref, pad):
     rows = tokens * slots
     taps = slot_taps(wts_ref[...], 0)
-    tops = edges(kb_ref, 0, rows, per, tail_ref[pl.ds(0, EDGE), :].astype(F32), halo)
+    tops = edges(kb_ref, 0, rows, per, tail_ref[pl.ds(0, EDGE), :].astype(F32), prev_ref)
     order = before(rows)
     blocks = rows // HEAD
     grams = []
@@ -206,8 +201,8 @@
 
 
 def maps_kernel(
-    per, tokens, slots, hid, vq_ref, beta_ref, tail_ref, wts_ref, kn_ref, ti_ref,
-    wu_ref, a_ref, mc_ref, end_ref, fv_ref, pad, halo, carry,
+    per, tokens, slots, hid, vq_ref, prev_ref, beta_ref, tail_ref, wts_ref, kn_ref, ti_ref,
+    wu_ref, a_ref, mc_ref, fv_ref, end_ref, pad, carry,
 ):
     rows = tokens * slots
     taps = slot_taps(wts_ref[...], 1)
@@ -217,7 +212,8 @@
     def _():
         carry[...] = (ir == ic).astype(F32)
 
-    tops = edges(vq_ref, 0, rows, per, tail_ref[pl.ds(EDGE, EDGE), :].astype(F32), halo)
+    tail = tail_ref[pl.ds(EDGE, EDGE), :].astype(F32)
+    tops = edges(vq_ref, 0, rows, per, tail, prev_ref)
     maps = []
     for n in range(per):
         s = conv_rows(vq_ref[n, pl.ds(0, rows), :].astype(F32), tops[n], taps, pad.at[n], slots)
@@ -240,11 +236,13 @@
 
 
 def queries_kernel(
-    per, tokens, slots, hid, vq_ref, tail_ref, wts_ref, kn_ref, wu_ref, q_ref, sc_ref, qm_ref, ol_ref, fq_ref, pad, halo
+    per, tokens, slots, hid, vq_ref, prev_ref, tail_ref, wts_ref, kn_ref, wu_ref,
+    q_ref, sc_ref, qm_ref, ol_ref, fq_ref, pad,
 ):
     rows = tokens * slots
     taps = query_taps(wts_ref[...])
-    tops = edges(vq_ref, rows, tokens, per, tail_ref[pl.ds(2 * EDGE, EDGE), :].astype(F32), halo)
+    tail = tail_ref[pl.ds(2 * EDGE, EDGE), :].astype(F32)
+    tops = edges(vq_ref, rows, tokens, per, tail, prev_ref)
     seen = visible(tokens, slots)
     for n in range(per):
         s = conv_rows(vq_ref[n, pl.ds(rows, tokens), :].astype(F32), tops[n], taps, pad.at[n], 1)
@@ -260,46 +258,30 @@
 
 
 def outs_kernel(
-    count, tokens, slots, hid, vq_ref, wts_ref, start_ref, mc_ref, qm_ref, ol_ref, a_ref,
-    nm_ref, dr_ref, st_ref, mb_ref, end_ref,
+    per, count, tokens, slots, hid, vq_ref, wts_ref, start_ref, kn_ref, mc_ref, qm_ref, ol_ref, a_ref, wu_ref, q_ref,
+    sc_ref, fq_ref, st_ref, mb_ref, d_ref, dk_ref, dd_ref, nq_ref, end_ref, pad, local,
 ):
+    step = pl.program_id(0)
     rows = tokens * slots
-    gain = gain_row(wts_ref[...])
+    wts = wts_ref[...]
+    gain = gain_row(wts)
+    taps = query_taps(wts)
+    seen = visible(tokens, slots)
     start = two(start_ref[...])
-    states = [
-        mm(two(mc_ref[n, :, pl.ds(0, HEAD)]), start) + mc_ref[n, :, pl.ds(HEAD, HEAD)] for n in range(count)
-    ]
-    mapped = [two(qm_ref[n]) for n in range(count)]
-    raws = [mm(mapped[n], two(states[n])) + ol_ref[n] for n in range(count)]
-    local = []
-    for n in range(count):
+    states = [mm(two(mc_ref[n, :, pl.ds(0, HEAD)]), start) + mc_ref[n, :, pl.ds(HEAD, HEAD)] for n in range(per)]
+    halves = [two(x) for x in states]
+    mapped = [two(qm_ref[n]) for n in range(per)]
+    raws = [mm(mapped[n], halves[n]) + ol_ref[n] for n in range(per)]
+    for n in range(per):
         st_ref[n] = states[n]
-        raw = raws[n]
+        raw, state = raws[n], halves[n]
         scale = lax.rsqrt(jnp.mean(raw * raw, axis=-1, keepdims=True) + EPS)
         hat = raw * scale
-        nm_ref[n] = (hat * gain).astype(BF16)
+        nq_ref[n, pl.ds(0, tokens), :] = (hat * gain).astype(BF16)
         dn = vq_ref[n, pl.ds(rows + tokens, tokens), :].astype(F32) * gain
-        dr = scale * (dn - hat * jnp.mean(dn * hat, axis=-1, keepdims=True))
-        dr_ref[n] = dr
-        local.append(mm(mapped[n], two(dr), COLS_COLS))
-    ir, ic = grid_of(HEAD, 2 * HEAD)
-    state = (ir == ic).astype(F32)
-    for n in range(count - 1, -1, -1):
-        mb_ref[n] = state
-        moved = mm(two(a_ref[n]), two(state), COLS_COLS)
-        state = moved + jnp.concatenate([jnp.zeros((HEAD, HEAD), F32), local[n]], axis=1)
-    end_ref[...] = state
-
-
-def query_grads_kernel(
-    per, tokens, slots, hid, wts_ref, kn_ref, wu_ref, q_ref, sc_ref, dr_ref, st_ref, fq_ref, nm_ref,
-    d_ref, dk_ref, dd_ref, nq_ref, pad,
-):
-    taps = query_taps(wts_ref[...])
-    seen = visible(tokens, slots)
-    for n in range(per):
-        q = q_ref[n]
-        state, dr, k2 = two(st_ref[n]), two(dr_ref[n]), two(kn_ref[n])
+        dr = two(scale * (dn - hat * jnp.mean(dn * hat, axis=-1, keepdims=True)))
+        local[step * per + n] = mm(mapped[n], dr, COLS_COLS)
+        q, k2 = q_ref[n], two(kn_ref[n])
         d = wu_ref[n, :, pl.ds(HEAD, HEAD)] - mm(two(wu_ref[n, :, pl.ds(0, HEAD)]), state)
         d_ref[n] = d
         ds = two(jnp.where(seen, mm(dr, two(d), ROWS_ROWS), 0.0))
@@ -307,9 +289,18 @@
         dk_ref[n] = mm(ds, two(q), COLS_COLS)
         dd_ref[n] = mm(two(sc_ref[n]), dr, COLS_COLS)
         inner, rim = conv_back(fq_ref[n] * (dq - q * jnp.sum(q * dq, axis=-1, keepdims=True)), taps, pad.at[n], 1)
-        nq_ref[n, pl.ds(0, tokens), :] = nm_ref[n]
         nq_ref[n, pl.ds(tokens, tokens), :] = inner.astype(BF16)
         nq_ref[n, pl.ds(2 * tokens, EDGE), :] = jnp.concatenate([rim, jnp.zeros((8, HEAD), F32)], axis=0).astype(BF16)
+
+    @pl.when(step == pl.num_programs(0) - 1)
+    def _():
+        ir, ic = grid_of(HEAD, 2 * HEAD)
+        state = (ir == ic).astype(F32)
+        for n in range(count - 1, -1, -1):
+            mb_ref[n] = state
+            moved = mm(two(a_ref[n]), two(state), COLS_COLS)
+            state = moved + jnp.concatenate([jnp.zeros((HEAD, HEAD), F32), local[n]], axis=1)
+        end_ref[...] = state
 
 
 def grads_kernel(
@@ -361,30 +352,48 @@
     gq_ref[...] = jnp.concatenate([main[: tokens - 8], last], axis=0)
 
 
-def call(kernel, hid, steps, ins, outs, scratch=(), us=1.0, grant=24):
-    def spec(shape, per):
-        if per == "weights":
+FAR = ("kn", "ti", "fk", "fv", "st", "mb", "d", "dk", "dd")
+
+
+def call(kernel, hid, steps, live, ins, reads, outs, scratch=(), us=1.0, grant=24):
+    def spec(shape, how):
+        if how == "weights":
             return pl.BlockSpec((shape[0], HEAD), lambda i, h: (0, h[0]))
-        if per is None:
+        if how is None:
             return pl.BlockSpec(shape, lambda i, h: (0,) * len(shape))
-        if isinstance(per, tuple):
-            count, first = per
-            return pl.BlockSpec((count, EDGE, HEAD), lambda i, h: (i, first // EDGE, 0))
-        return pl.BlockSpec((per,) + tuple(shape[1:]), lambda i, h: (i,) + (0,) * (len(shape) - 1))
-
-    return pl.pallas_call(
+        if isinstance(how, tuple):
+            kind, count, row = how
+            if kind == "prev":
+                return pl.BlockSpec((1, EDGE, HEAD), lambda i, h: (jnp.maximum(i * count - 1, 0), row // EDGE, 0))
+            return pl.BlockSpec((count, EDGE, HEAD), lambda i, h: (i, row // EDGE, 0))
+        return pl.BlockSpec((how,) + tuple(shape[1:]), lambda i, h: (i,) + (0,) * (len(shape) - 1))
+
+    def home(name):
+        return pltpu.HBM if name in FAR else pltpu.VMEM
+
+    operands = [a for a, _ in ins]
+    operands += [pltpu.with_memory_space_constraint(live[name], home(name)) for name, _ in reads]
+    hows = [how for _, how in ins + reads]
+    results = pl.pallas_call(
         kernel,
         grid_spec=pltpu.PrefetchScalarGridSpec(
             num_scalar_prefetch=1,
             grid=(steps,),
-            in_specs=[spec(a.shape, per) for a, per in ins],
-            out_specs=[spec(s, per) for s, _, per in outs],
+            in_specs=[spec(a.shape, how) for a, how in zip(operands, hows)],
+            out_specs=[spec(shape, how) for _, shape, _, how in outs],
             scratch_shapes=list(scratch),
         ),
-        out_shape=[pltpu.HBM(s, d) if len(s) == 3 else jax.ShapeDtypeStruct(s, d) for s, d, _ in outs],
+        out_shape=[
+            jax.ShapeDtypeStruct(shape, dtype) if name is None else home(name)(shape, dtype)
+            for name, shape, dtype, _ in outs
+        ],
         compiler_params=pltpu.CompilerParams(dimension_semantics=("arbitrary",), vmem_limit_bytes=grant << 20),
         cost_estimate=pl.CostEstimate(flops=int(us * 1.1e9), bytes_accessed=1 << 16, transcendentals=0),
-    )(hid, *[pltpu.with_memory_space_constraint(a, pltpu.HBM) if a.dtype == F32 and a.ndim == 3 else a for a, _ in ins])
+    )(hid, *operands)
+    for (name, _, _, _), result in zip(outs, results):
+        if name is not None:
+            live[name] = result
+    return [r for (name, _, _, _), r in zip(outs, results) if name is None]
 
 
 def shards(
@@ -437,9 +446,9 @@
     tail = lax.ppermute(tail, "ctx", [(i, i + heads) for i in range(shard_count - heads)])
 
     grad_normed = jnp.dot(grad_out, out_weight.T, preferred_element_type=F32).astype(BF16)
-    vq = exchange(
-        jnp.concatenate([slots_by_head(value_in), by_head(query_in), by_head(grad_normed)], axis=1)
-    )
+    vq = jnp.concatenate([slots_by_head(value_in), by_head(query_in), by_head(grad_normed)], axis=1)
+    vq, tail = lax.optimization_barrier((vq, tail))
+    vq = exchange(vq)
 
     wts = jnp.concatenate(
         [
@@ -455,31 +464,38 @@
     steps = g // per
 
     def pad(n):
-        return [pltpu.VMEM((per, n + EDGE + 8, HEAD), F32), pltpu.VMEM((EDGE, HEAD), F32)]
-
-    kn, ti, fk = call(
-        functools.partial(inverse_kernel, per, tokens, slots),
+        return [pltpu.VMEM((per, n + EDGE + 8, HEAD), F32)]
+
+    def big(name, *shape, per=per):
+        return (name, (g,) + shape, F32, per)
+
+    live = {}
+    wide = 4 if g % 4 == 0 else per
+    call(
+        functools.partial(inverse_kernel, wide, tokens, slots),
         hid,
-        steps,
-        [(kb, per), (tail, None), (wts, "weights")],
-        [((g, rows, HEAD), F32, per), ((g, rows, rows), F32, per), ((g, rows, HEAD), F32, per)],
-        pad(rows),
-        us=12.0,
-    )
-    beta = (kb, (per, rows))
-    wu, amap, mc, end, fv = call(
+        g // wide,
+        live,
+        [(kb, wide), (kb, ("prev", wide, rows - EDGE)), (tail, None), (wts, "weights")],
+        [],
+        [big("kn", rows, HEAD, per=wide), big("ti", rows, rows, per=wide), big("fk", rows, HEAD, per=wide)],
+        scratch=[pltpu.VMEM((wide, rows + EDGE + 8, HEAD), F32)],
+        us=9.0,
+        grant=40,
+    )
+    beta = (kb, ("rows", per, rows))
+    (end,) = call(
         functools.partial(maps_kernel, per, tokens, slots),
         hid,
         steps,
-        [(vq, per), beta, (tail, None), (wts, "weights"), (kn, per), (ti, per)],
+        live,
+        [(vq, per), (vq, ("prev", per, rows - EDGE)), beta, (tail, None), (wts, "weights")],
+        [("kn", per), ("ti", per)],
         [
-            ((g, rows, 2 * HEAD), F32, per),
-            ((g, HEAD, HEAD), F32, per),
-            ((g, HEAD, 2 * HEAD), F32, per),
-            ((HEAD, 2 * HEAD), F32, None),
-            ((g, rows, HEAD), F32, per),
+            big("wu", rows, 2 * HEAD), big("a", HEAD, HEAD), big("mc", HEAD, 2 * HEAD), big("fv", rows, HEAD),
+            (None, (HEAD, 2 * HEAD), F32, None),
         ],
-        pad(rows) + [pltpu.VMEM((HEAD, 2 * HEAD), F32)],
+        scratch=pad(rows) + [pltpu.VMEM((HEAD, 2 * HEAD), F32)],
         us=8.0,
     )
 
@@ -501,63 +517,48 @@
         return lax.fori_loop(0, ahead, advance, jnp.zeros((HEAD, HEAD), F32))
 
     start = across(end, 1)
-    q, sc, qm, ol, fq = call(
+    call(
         functools.partial(queries_kernel, per, tokens, slots),
         hid,
         steps,
-        [(vq, per), (tail, None), (wts, "weights"), (kn, per), (wu, per)],
+        live,
+        [(vq, per), (vq, ("prev", per, rows + tokens - EDGE)), (tail, None), (wts, "weights")],
+        [("kn", per), ("wu", per)],
         [
-            ((g, tokens, HEAD), F32, per),
-            ((g, tokens, rows), F32, per),
-            ((g, tokens, HEAD), F32, per),
-            ((g, tokens, HEAD), F32, per),
-            ((g, tokens, HEAD), F32, per),
+            big("q", tokens, HEAD), big("sc", tokens, rows), big("qm", tokens, HEAD), big("ol", tokens, HEAD),
+            big("fq", tokens, HEAD),
         ],
-        pad(tokens),
+        scratch=pad(tokens),
         us=8.0,
     )
-    normed, dr, st, mb, back_end = call(
-        functools.partial(outs_kernel, g, tokens, slots),
-        hid,
-        1,
-        [(vq, None), (wts, "weights"), (start, None), (mc, None), (qm, None), (ol, None), (amap, None)],
-        [
-            ((g, tokens, HEAD), BF16, None),
-            ((g, tokens, HEAD), F32, None),
-            ((g, HEAD, HEAD), F32, None),
-            ((g, HEAD, 2 * HEAD), F32, None),
-            ((HEAD, 2 * HEAD), F32, None),
-        ],
-        us=4.0,
-    )
-    finish = across(back_end, -1)
-    d, dk, dd, nq = call(
-        functools.partial(query_grads_kernel, per, tokens, slots),
+    nq, back_end = call(
+        functools.partial(outs_kernel, per, g, tokens, slots),
         hid,
         steps,
+        live,
+        [(vq, per), (wts, "weights"), (start, None)],
         [
-            (wts, "weights"), (kn, per), (wu, per), (q, per), (sc, per), (dr, per), (st, per), (fq, per), (normed, per),
+            ("kn", per), ("mc", per), ("qm", per), ("ol", per), ("a", None), ("wu", per), ("q", per), ("sc", per),
+            ("fq", per),
         ],
         [
-            ((g, rows, HEAD), F32, per),
-            ((g, rows, HEAD), F32, per),
-            ((g, rows, HEAD), F32, per),
-            ((g, 2 * tokens + EDGE, HEAD), BF16, per),
+            big("st", HEAD, HEAD), big("mb", HEAD, 2 * HEAD, per=None), big("d", rows, HEAD), big("dk", rows, HEAD),
+            big("dd", rows, HEAD), (None, (g, 2 * tokens + EDGE, HEAD), BF16, per), (None, (HEAD, 2 * HEAD), F32, None),
         ],
-        pad(tokens)[:1],
-        us=20.0,
-    )
+        scratch=pad(tokens) + [pltpu.VMEM((g, HEAD, HEAD), F32)],
+        us=10.0,
+    )
+    finish = across(back_end, -1)
     nq = exchange(nq)
     (grads,) = call(
         functools.partial(grads_kernel, per, tokens, slots),
         hid,
         steps,
-        [
-            beta, (wts, "weights"), (finish, None), (mb, per), (kn, per), (ti, per), (d, per), (dk, per), (dd, per),
-            (st, per), (fk, per), (fv, per),
-        ],
-        [((g, 2 * rows + 2 * EDGE, HEAD), BF16, per)],
-        [pltpu.VMEM((2 * per, rows + EDGE + 8, HEAD), F32)],
+        live,
+        [beta, (wts, "weights"), (finish, None)],
+        [(name, per) for name in ("mb", "kn", "ti", "d", "dk", "dd", "st", "fk", "fv")],
+        [(None, (g, 2 * rows + 2 * EDGE, HEAD), BF16, per)],
+        scratch=[pltpu.VMEM((2 * per, rows + EDGE + 8, HEAD), F32)],
         us=20.0,
     )
     grads = exchange(grads)

time: 131 us -> 122 us (0.931)
  Pallas kernels: 56.4 us -> 48.1 us
  starting transfers between devices: 34.1 us -> 35.7 us
    pallas_call x6 -> x5, Pallas kernels: 50.7 us -> 42.5 us  [call(): pl.pallas_call(kernel, grid_spec=pltpu.PrefetchScalarGridSpec(num_scalar_...]
    ppermute x1, waiting for transfers between devices: 7.38 us -> 0.01 us  [shards(): lax.ppermute(tail, 'ctx', [(i, i + heads) for i in range(shard_count - he...]
    all_to_all x4, waiting for transfers between devices: 3.03 us -> 9 us  [exchange(): lax.all_to_all(x, 'ctx', 0, 0, axis_index_groups=group_lists, tiled=True)]
    all_to_all x4, starting transfers between devices: 18.5 us -> 19.9 us  [exchange(): lax.all_to_all(x, 'ctx', 0, 0, axis_index_groups=group_lists, tiled=True)]
  transfers between devices with their start and end apart: 10 -> 10, of which waited for: 4 -> 5; matrix products, arithmetic and copies ran while one was open for 9% -> 10% of each run, Pallas kernels for 31% -> 22%
where the time goes in v4:
time: 122 us; the launch traced here: 121 us
  Pallas kernels  48.1 us (39%)
  starting transfers between devices  35.7 us (29%)
  waiting for transfers between devices  20.3 us (17%)
  matrix products  6.66 us (5%)
  local copies, waits for them, and re-layouts  4.56 us (4%)
  other arithmetic  4.52 us (4%)
    pallas_call x5, Pallas kernels, call(): pl.pallas_call(kernel, grid_spec=pltpu.PrefetchScalarGridSpec(num_scalar_...  42.5 us
    all_to_all x4, starting transfers between devices, exchange(): lax.all_to_all(x, 'ctx', 0, 0, axis_index_groups=group_lists, tiled=True)  19.9 us
    all_to_all x4, waiting for transfers between devices, exchange(): lax.all_to_all(x, 'ctx', 0, 0, axis_index_groups=group_lists, tiled=True)  9 us
    ppermute x1, waiting for transfers between devices, shards(): query_rim = lax.ppermute(nq[:, 2 * tokens:], 'ctx', back)  7.92 us
    ppermute x2, starting transfers between devices, across(): return lax.ppermute(last[:, HEAD:], 'ctx', moves)  6.12 us
    ppermute x1, starting transfers between devices, shards(): lax.ppermute(tail, 'ctx', [(i, i + heads) for i in range(shard_count - he...  4.2 us
    dot_general x1, matrix products, shards(): jnp.dot(grad_out, out_weight.T, preferred_element_type=F32).astype(BF16)  3.76 us
    pallas_call x1, Pallas kernels, shards(): pl.pallas_call(functools.partial(unpack_kernel, tokens, slots), grid=(hea...  3.06 us
  transfers between devices with their start and end apart: 10, of which 5 were waited for; matrix products, arithmetic and copies ran while one was open for 10% of the time, Pallas kernels for 22%

profile of v4, /device:TPU:1, one launch (start us, length us, event | category | flops | bytes accessed | tf_op | source)
XLA Modules:
  0.0 120.8 jit_solution(11702572177847373926)
XLA Ops:
  0.6 0.0 copy-start
  0.6 0.0 copy-start.4
  0.7 0.8 fusion.11
  1.5 0.2 copy-done
  1.7 0.4 copy_bitcast_fusion
  2.1 0.8 copy_bitcast_fusion.2
  2.9 0.8 bitcast_bitcast_fusion
  3.6 0.9 fusion.6
  4.5 5.3 %all-to-all-start = ((bf16[8,304,128]{2,1,0:T(8,128)(2,1)}), bf16[8,304,128]{2,1,0:T(8,128)(2,1)S(1)}, u32[]{:S(2)}, u32[]{:S(2)}) async-start(bf16[8,304,128]{2,1,0:T(8,128)(2,1)} %fusion.6), calls=%async_computation | async-start | bytes 1245184 | tf_op jit(solution)/shard_map/all_to_all | solution.py:423
  9.8 0.2 copy.32
  10.0 0.0 copy-start.2
  10.0 3.8 %convolution_convert_fusion = bf16[128,1024]{1,0:T(8,128)(2,1)S(1)} fusion(bf16[128,2048]{1,0:T(8,128)(2,1)S(1)} %copy-done.3, bf16[1024,2048]{1,0:T(8,128)(2,1)} %param.18), kind=kOutput, calls=%fused_computation.6 | convolution fusion | flops 537001984 | bytes 4980736 | tf_op jit(solution)/shard_map/dot_general | solution.py:448
  13.8 0.2 copy.34
  13.9 0.2 copy.35
  14.1 0.2 copy.33
  14.3 0.4 copy_bitcast_fusion.1
  14.7 4.1 %all-to-all-done.kb_ref.prev_ref.beta_ref = bf16[8,304,128]{2,1,0:T(8,128)(2,1)S(1)} async-done(((bf16[8,304,128]{2,1,0:T(8,128)(2,1)}), bf16[8,304,128]{2,1,0:T(8,128)(2,1)S(1)}, u32[]{:S(2)}, u32[]{:S(2)}) %all-to-all-start) | async-done | bytes 622624 | tf_op jit(solution)/shard_map/all_to_all | solution.py:423
  18.8 4.2 %collective-permute-start = (bf16[48,128]{1,0:T(8,128)(2,1)S(1)}, bf16[48,128]{1,0:T(8,128)(2,1)S(1)}, u32[]{:S(2)}, u32[]{:S(2)}) collective-permute-start(bf16[48,128]{1,0:T(8,128)(2,1)S(1)} %pad_maximum_fusion.2), channel_id=1, source_target_pairs={{0,16},{2,18},{4,20},{6,22},{8,24},{10,26},{12,28},{14,30},{1,17},... | collective-permute-start | bytes 36872 | tf_op jit(solution)/shard_map/ppermute | solution.py:446
  23.0 0.0 copy-start.5
  23.1 0.0 copy-start.6
  23.1 1.0 pad_maximum_fusion
  24.1 4.9 %all-to-all-start.1 = ((bf16[8,512,128]{2,1,0:T(8,128)(2,1)}), bf16[8,512,128]{2,1,0:T(8,128)(2,1)S(1)}, u32[]{:S(2)}, u32[]{:S(2)}) async-start(bf16[8,512,128]{2,1,0:T(8,128)(2,1)} %pad_maximum_fusion), calls=%async_computation.1 | async-start | bytes 2097152 | tf_op jit(solution)/shard_map/all_to_all | solution.py:423
  29.1 0.1 tile.17
  29.2 0.1 tile.19
  29.4 8.4 %shard_map.137 = (f32[8,256,128]{2,1,0:T(8,128)}, f32[8,256,256]{2,1,0:T(8,128)}, f32[8,256,128]{2,1,0:T(8,128)}) custom-call(s32[1]{0:T(128)} %bitcast.hid, bf16[8,304,128]{2,1,0:T(8,128)(2,1)S(1)} %all-to-all-done.kb_ref.prev_ref.beta_ref, bf16[8,304,128]{2,1,0:T(8,128)(2,1)S(1)} %all-to-all-done.kb_ref.prev_ref.beta_ref, ...), custom_call_target="tpu_custom_call" | custom-call | flops 9900000256 | bytes 65536 | tf_op jit(solution)/shard_map/pallas_call | solution.py:377
  37.8 4.9 %all-to-all-done.1.vq_ref.prev_ref = bf16[8,512,128]{2,1,0:T(8,128)(2,1)S(1)} async-done(((bf16[8,512,128]{2,1,0:T(8,128)(2,1)}), bf16[8,512,128]{2,1,0:T(8,128)(2,1)S(1)}, u32[]{:S(2)}, u32[]{:S(2)}) %all-to-all-start.1) | async-done | bytes 1048608 | tf_op jit(solution)/shard_map/all_to_all | solution.py:423
  42.7 7.7 %shard_map.138 = (f32[8,256,256]{2,1,0:T(8,128)S(1)}, f32[8,128,128]{2,1,0:T(8,128)S(1)}, f32[8,128,256]{2,1,0:T(8,128)S(1)}, f32[8,256,128]{2,1,0:T(8,128)}, f32[128,256]{1,0:T(8,128)S(1)}) custom-call(s32[1]{0:T(128)} %bitcast.hid, bf16[8,512,128]{2,1,0:T(8,128)(2,1)S(1)} %all-to-all-done.1.vq_ref.prev_ref, ...), custom_call_target="tpu_custom_call" | custom-call | flops 8800000000 | bytes 65536 | tf_op jit(solution)/shard_map/pallas_call | solution.py:377
  50.4 4.8 %collective-permute-start.1 = (f32[128,128]{1,0:T(8,128)S(1)}, f32[128,128]{1,0:T(8,128)S(1)}, u32[]{:S(2)}, u32[]{:S(2)}) collective-permute-start(f32[128,128]{1,0:T(8,128)S(1)} %slice.34), channel_id=1, source_target_pairs={{0,16},{2,18},{4,20},{6,22},{8,24},{10,26},{12,28},{14,30},{1,17},... | collective-permute-start | bytes 196616 | tf_op jit(solution)/shard_map/ppermute | solution.py:507
  55.2 4.6 %shard_map.139 = (f32[8,128,128]{2,1,0:T(8,128)S(1)}, f32[8,128,256]{2,1,0:T(8,128)S(1)}, f32[8,128,128]{2,1,0:T(8,128)S(1)}, f32[8,128,128]{2,1,0:T(8,128)S(1)}, f32[8,128,128]{2,1,0:T(8,128)S(1)}) custom-call(s32[1]{0:T(128)} %bitcast.hid, bf16[8,512,128]{2,1,0:T(8,128)(2,1)S(1)} %all-to-all-done.1.vq_ref.prev_ref, ...), custom_call_target="tpu_custom_call" | custom-call | flops 8800000000 | bytes 65536 | tf_op jit(solution)/shard_map/pallas_call | solution.py:377
  59.8 10.7 %shard_map.140 = (f32[8,128,128]{2,1,0:T(8,128)}, f32[8,128,256]{2,1,0:T(8,128)}, f32[8,256,128]{2,1,0:T(8,128)}, f32[8,256,128]{2,1,0:T(8,128)}, f32[8,256,128]...) custom-call(s32[1]{0:T(128)} %bitcast.hid, ...), custom_call_target="tpu_custom_call" | custom-call | flops 11000000512 | bytes 65536 | tf_op jit(solution)/shard_map/pallas_call | solution.py:377
  70.5 1.3 %collective-permute-start.4 = (f32[128,128]{1,0:T(8,128)S(1)}, f32[128,128]{1,0:T(8,128)S(1)}, u32[]{:S(2)}, u32[]{:S(2)}) collective-permute-start(f32[128,128]{1,0:T(8,128)S(1)} %slice.37), channel_id=1, source_target_pairs={{16,0},{18,2},{20,4},{22,6},{24,8},{26,10},{28,12},{30,14},{17,1},... | collective-permute-start | bytes 196616 | tf_op jit(solution)/shard_map/ppermute | solution.py:507
  71.8 4.6 %all-to-all-start.2 = ((bf16[8,272,128]{2,1,0:T(8,128)(2,1)}), bf16[8,272,128]{2,1,0:T(8,128)(2,1)S(1)}, u32[]{:S(2)}, u32[]{:S(2)}) async-start(bf16[8,272,128]{2,1,0:T(8,128)(2,1)} %get-tuple-element.42), calls=%async_computation.2 | async-start | bytes 1114112 | tf_op jit(solution)/shard_map/all_to_all | solution.py:423
  76.4 0.7 collective-permute-done.4.end_ref
  77.2 11.1 %shard_map.142 = bf16[8,544,128]{2,1,0:T(8,128)(2,1)} custom-call(s32[1]{0:T(128)} %bitcast.hid, bf16[8,304,128]{2,1,0:T(8,128)(2,1)S(1)} %all-to-all-done.kb_ref.prev_ref.beta_ref, f32[72,1024]{1,0:T(8,128)S(1)} %concatenate.15.wts_ref, f32[128,128]{1,0:T(8,128)S(1)} %collective-permute-done.4.end_ref, f32[8,128,256]{2,1,0:T(8,128)} %get-tuple-element.44.mb_ref, ...), custom_call_target="tpu_custom_call" | custom-call | flops 22000001024 | bytes 65536 | tf_op jit(solution)/shard_map/pallas_call | solution.py:377
  88.3 5.1 %all-to-all-start.3 = ((bf16[8,544,128]{2,1,0:T(8,128)(2,1)}), bf16[8,544,128]{2,1,0:T(8,128)(2,1)S(1)}, u32[]{:S(2)}, u32[]{:S(2)}) async-start(bf16[8,544,128]{2,1,0:T(8,128)(2,1)} %shard_map.142), calls=%async_computation.3 | async-start | bytes 2228224 | tf_op jit(solution)/shard_map/all_to_all | solution.py:423
  93.4 0.2 copy.42
  93.5 0.1 dot_general.9
  93.7 2.9 %fusion = f32[2,64,2048]{2,1,0:T(8,128)S(1)} fusion(bf16[2,64,1024]{2,1,0:T(8,128)(2,1)S(1)} %dot_general.9, bf16[1024,2048]{1,0:T(8,128)(2,1)} %param.18), kind=kOutput, calls=%fused_computation | convolution fusion | flops 536870912 | bytes 5505024 | tf_op jit(solution)/shard_map/dot_general | solution.py:567
  96.6 0.0 copy-start.1
  96.6 1.3 %collective-permute-start.2 = (bf16[64,2048]{1,0:T(8,128)(2,1)S(1)}, bf16[64,2048]{1,0:T(8,128)(2,1)S(1)}, u32[]{:S(2)}, u32[]{:S(2)}) collective-permute-start(bf16[64,2048]{1,0:T(8,128)(2,1)S(1)} %fusion.8), channel_id=1, source_target_pairs={{0,1},{1,0},{2,3},{3,2},{4,5},{5,4},{6,7},{7,6},{8,9},{9,8},{10,11... | collective-permute-start | bytes 786440 | tf_op jit(solution)/shard_map/ppermute | solution.py:574
  97.9 2.3 %collective-permute-start.3 = (bf16[8,16,128]{2,1,0:T(8,128)(2,1)S(1)}, bf16[8,16,128]{2,1,0:T(8,128)(2,1)S(1)}, u32[]{:S(2)}, u32[]{:S(2)}) collective-permute-start(bf16[8,16,128]{2,1,0:T(8,128)(2,1)S(1)} %slice.43), channel_id=1, source_target_pairs={{2,0},{4,2},{6,4},{8,6},{10,8},{12,10},{14,12},{16,14},{18,16},{20... | collective-permute-start | bytes 98312 | tf_op jit(solution)/shard_map/ppermute | solution.py:579
  100.2 7.9 %collective-permute-done.3.rim_ref = bf16[8,16,128]{2,1,0:T(8,128)(2,1)S(1)} collective-permute-done((bf16[8,16,128]{2,1,0:T(8,128)(2,1)S(1)}, bf16[8,16,128]{2,1,0:T(8,128)(2,1)S(1)}, u32[]{:S(2)}, u32[]{:S(2)}) %collective-permute-start.3) | collective-permute-done | bytes 32800 | tf_op jit(solution)/shard_map/ppermute | solution.py:579
  108.2 2.6 %shard_map.141 = f32[128,1024]{1,0:T(8,128)} custom-call(bf16[8,272,128]{2,1,0:T(8,128)(2,1)S(1)} %all-to-all-done.2.got_ref, bf16[8,16,128]{2,1,0:T(8,128)(2,1)S(1)} %collective-permute-done.3.rim_ref), custom_call_target="tpu_custom_call" | custom-call | tf_op jit(solution)/shard_map/pallas_call | solution.py:582
  110.7 1.8 %fusion.7 = bf16[64,2048]{1,0:T(8,128)(2,1)} fusion(bf16[64,2048]{1,0:T(8,128)(2,1)S(1)} %collective-permute-done.2, f32[2,64,2048]{2,1,0:T(8,128)} %copy-done.1, s32[]{:T(128)S(6)} %select_n.15), kind=kLoop, calls=%fused_computation.14 | loop fusion | flops 393216 | bytes 1048580 | tf_op jit(solution)/shard_map/convert_element_type | solution.py:574
  112.5 1.9 %collective-permute-start.5 = (bf16[8,16,128]{2,1,0:T(8,128)(2,1)S(1)}, bf16[8,16,128]{2,1,0:T(8,128)(2,1)S(1)}, u32[]{:S(2)}, u32[]{:S(2)}) collective-permute-start(bf16[8,16,128]{2,1,0:T(8,128)(2,1)S(1)} %slice.44), channel_id=1, source_target_pairs={{2,0},{4,2},{6,4},{8,6},{10,8},{12,10},{14,12},{16,14},{18,16},{20... | collective-permute-start | bytes 98312 | tf_op jit(solution)/shard_map/ppermute | solution.py:580
  114.5 0.6 copy.43
  115.1 2.7 %collective-permute-done.5.rim_ref = bf16[8,16,128]{2,1,0:T(8,128)(2,1)S(1)} collective-permute-done((bf16[8,16,128]{2,1,0:T(8,128)(2,1)S(1)}, bf16[8,16,128]{2,1,0:T(8,128)(2,1)S(1)}, u32[]{:S(2)}, u32[]{:S(2)}) %collective-permute-start.5) | collective-permute-done | bytes 32800 | tf_op jit(solution)/shard_map/ppermute | solution.py:580
  117.8 3.1 %shard_map.143 = (f32[128,2,1024]{2,1,0:T(2,128)}, f32[128,2,1024]{2,1,0:T(2,128)}) custom-call(bf16[8,544,128]{2,1,0:T(8,128)(2,1)S(1)} %all-to-all-done.3.got_ref, bf16[8,16,128]{2,1,0:T(8,128)(2,1)S(1)} %collective-permute-done.5.rim_ref), custom_call_target="tpu_custom_call" | custom-call | tf_op jit(solution)/shard_map/pallas_call | solution.py:590
  (33 shorter events, 0.3 us)
Async XLA Ops:
  0.6 1.1 copy-start
  0.6 9.2 %copy-start.4 = (bf16[128,1024]{1,0:T(8,128)(2,1)S(1)}, bf16[128,1024]{1,0:T(8,128)(2,1)}, u32[]{:S(2)}) copy-start(bf16[128,1024]{1,0:T(8,128)(2,1)} %param.10) | copy-start | bytes 786436
  1.7 8.3 %copy-start.3 = (bf16[128,2048]{1,0:T(8,128)(2,1)S(1)}, bf16[128,2048]{1,0:T(8,128)(2,1)}, u32[]{:S(2)}) copy-start(bf16[128,2048]{1,0:T(8,128)(2,1)} %param.19) | copy-start | bytes 1572868
  4.5 14.3 %all-to-all-start = ((bf16[8,304,128]{2,1,0:T(8,128)(2,1)}), bf16[8,304,128]{2,1,0:T(8,128)(2,1)S(1)}, u32[]{:S(2)}, u32[]{:S(2)}) async-start(bf16[8,304,128]{2,1,0:T(8,128)(2,1)} %fusion.6), calls=%async_computation | async-start | bytes 1245184 | tf_op jit(solution)/shard_map/all_to_all | solution.py:423
  10.0 4.3 %copy-start.2 = (bf16[128,2,1024]{2,1,0:T(2,128)(2,1)S(1)}, bf16[128,2,1024]{2,1,0:T(2,128)(2,1)}, u32[]{:S(2)}) copy-start(bf16[128,2,1024]{2,1,0:T(2,128)(2,1)} %param.12) | copy-start | bytes 1572868
  18.8 5.3 %collective-permute-start = (bf16[48,128]{1,0:T(8,128)(2,1)S(1)}, bf16[48,128]{1,0:T(8,128)(2,1)S(1)}, u32[]{:S(2)}, u32[]{:S(2)}) collective-permute-start(bf16[48,128]{1,0:T(8,128)(2,1)S(1)} %pad_maximum_fusion.2), channel_id=1, source_target_pairs={{0,16},{2,18},{4,20},{6,22},{8,24},{10,26},{12,28},{14,30},{1,17},... | collective-permute-start | bytes 36872 | tf_op jit(solution)/shard_map/ppermute | solution.py:446
  23.0 6.0 %copy-start.5 = (f32[4,2,1024]{2,1,0:T(2,128)S(1)}, f32[4,2,1024]{2,1,0:T(2,128)}, u32[]{:S(2)}) copy-start(f32[4,2,1024]{2,1,0:T(2,128)} %param.15) | copy-start | bytes 98308
  23.1 6.1 %copy-start.6 = (f32[4,2,1024]{2,1,0:T(2,128)S(1)}, f32[4,2,1024]{2,1,0:T(2,128)}, u32[]{:S(2)}) copy-start(f32[4,2,1024]{2,1,0:T(2,128)} %param.16) | copy-start | bytes 98308
  23.1 6.3 %copy-start.7 = (f32[4,1024]{1,0:T(4,128)S(1)}, f32[4,1024]{1,0:T(4,128)}, u32[]{:S(2)}) copy-start(f32[4,1024]{1,0:T(4,128)} %param.14) | copy-start | bytes 49156
  23.1 6.3 %copy-start.8 = (f32[1024]{0:T(1024)S(1)}, f32[1024]{0:T(1024)}, u32[]{:S(2)}) copy-start(f32[1024]{0:T(1024)} %param.17) | copy-start | bytes 12292
  24.1 18.5 %all-to-all-start.1 = ((bf16[8,512,128]{2,1,0:T(8,128)(2,1)}), bf16[8,512,128]{2,1,0:T(8,128)(2,1)S(1)}, u32[]{:S(2)}, u32[]{:S(2)}) async-start(bf16[8,512,128]{2,1,0:T(8,128)(2,1)} %pad_maximum_fusion), calls=%async_computation.1 | async-start | bytes 2097152 | tf_op jit(solution)/shard_map/all_to_all | solution.py:423
  50.4 9.5 %collective-permute-start.1 = (f32[128,128]{1,0:T(8,128)S(1)}, f32[128,128]{1,0:T(8,128)S(1)}, u32[]{:S(2)}, u32[]{:S(2)}) collective-permute-start(f32[128,128]{1,0:T(8,128)S(1)} %slice.34), channel_id=1, source_target_pairs={{0,16},{2,18},{4,20},{6,22},{8,24},{10,26},{12,28},{14,30},{1,17},... | collective-permute-start | bytes 196616 | tf_op jit(solution)/shard_map/ppermute | solution.py:507
  70.5 6.6 %collective-permute-start.4 = (f32[128,128]{1,0:T(8,128)S(1)}, f32[128,128]{1,0:T(8,128)S(1)}, u32[]{:S(2)}, u32[]{:S(2)}) collective-permute-start(f32[128,128]{1,0:T(8,128)S(1)} %slice.37), channel_id=1, source_target_pairs={{16,0},{18,2},{20,4},{22,6},{24,8},{26,10},{28,12},{30,14},{17,1},... | collective-permute-start | bytes 196616 | tf_op jit(solution)/shard_map/ppermute | solution.py:507
  71.8 16.4 %all-to-all-start.2 = ((bf16[8,272,128]{2,1,0:T(8,128)(2,1)}), bf16[8,272,128]{2,1,0:T(8,128)(2,1)S(1)}, u32[]{:S(2)}, u32[]{:S(2)}) async-start(bf16[8,272,128]{2,1,0:T(8,128)(2,1)} %get-tuple-element.42), calls=%async_computation.2 | async-start | bytes 1114112 | tf_op jit(solution)/shard_map/all_to_all | solution.py:423
  88.3 24.3 %all-to-all-start.3 = ((bf16[8,544,128]{2,1,0:T(8,128)(2,1)}), bf16[8,544,128]{2,1,0:T(8,128)(2,1)S(1)}, u32[]{:S(2)}, u32[]{:S(2)}) async-start(bf16[8,544,128]{2,1,0:T(8,128)(2,1)} %shard_map.142), calls=%async_computation.3 | async-start | bytes 2228224 | tf_op jit(solution)/shard_map/all_to_all | solution.py:423
  96.6 1.3 %copy-start.1 = (f32[2,64,2048]{2,1,0:T(8,128)}, f32[2,64,2048]{2,1,0:T(8,128)S(1)}, u32[]{:S(2)}) copy-start(f32[2,64,2048]{2,1,0:T(8,128)S(1)} %fusion) | copy-start | bytes 3145732
  96.6 14.1 %collective-permute-start.2 = (bf16[64,2048]{1,0:T(8,128)(2,1)S(1)}, bf16[64,2048]{1,0:T(8,128)(2,1)S(1)}, u32[]{:S(2)}, u32[]{:S(2)}) collective-permute-start(bf16[64,2048]{1,0:T(8,128)(2,1)S(1)} %fusion.8), channel_id=1, source_target_pairs={{0,1},{1,0},{2,3},{3,2},{4,5},{5,4},{6,7},{7,6},{8,9},{9,8},{10,11... | collective-permute-start | bytes 786440 | tf_op jit(solution)/shard_map/ppermute | solution.py:574
  97.9 10.3 %collective-permute-start.3 = (bf16[8,16,128]{2,1,0:T(8,128)(2,1)S(1)}, bf16[8,16,128]{2,1,0:T(8,128)(2,1)S(1)}, u32[]{:S(2)}, u32[]{:S(2)}) collective-permute-start(bf16[8,16,128]{2,1,0:T(8,128)(2,1)S(1)} %slice.43), channel_id=1, source_target_pairs={{2,0},{4,2},{6,4},{8,6},{10,8},{12,10},{14,12},{16,14},{18,16},{20... | collective-permute-start | bytes 98312 | tf_op jit(solution)/shard_map/ppermute | solution.py:579
  112.5 5.2 %collective-permute-start.5 = (bf16[8,16,128]{2,1,0:T(8,128)(2,1)S(1)}, bf16[8,16,128]{2,1,0:T(8,128)(2,1)S(1)}, u32[]{:S(2)}, u32[]{:S(2)}) collective-permute-start(bf16[8,16,128]{2,1,0:T(8,128)(2,1)S(1)} %slice.44), channel_id=1, source_target_pairs={{2,0},{4,2},{6,4},{8,6},{10,8},{12,10},{14,12},{16,14},{18,16},{20... | collective-permute-start | bytes 98312 | tf_op jit(solution)/shard_map/ppermute | solution.py:580

commit v5 on v4

--- a/solution.py
+++ b/solution.py
@@ -47,6 +47,12 @@
     return dot(ah, bh, dims) + dot(ah, bl, dims) + dot(al, bh, dims)
 
 
+def mm_half(left, right, dims=ROWS_COLS):
+    (ah, al), (bh, _) = left, right
+    ka, kb = dims[0][0][0], dims[0][1][0]
+    return dot(jnp.concatenate([ah, al], axis=ka), jnp.concatenate([bh, bh], axis=kb), dims)
+
+
 def grid_of(rows, cols):
     return lax.broadcasted_iota(jnp.int32, (rows, cols), 0), lax.broadcasted_iota(jnp.int32, (rows, cols), 1)
 
@@ -144,25 +150,36 @@
     return [prev] + [ref[n, pl.ds(first + rows - EDGE, EDGE), :].astype(F32) for n in range(per - 1)]
 
 
-def inverse_kernel(per, tokens, slots, hid, kb_ref, prev_ref, tail_ref, wts_ref, kn_ref, ti_ref, fk_ref, pad):
+def inverse_kernel(
+    per, tokens, slots, hid, kb_ref, prev_ref, tail_ref, wts_ref,
+    kh_ref, kl_ref, xh_ref, xl_ref, th_ref, tl_ref, wh_ref, wl_ref, fk_ref, a_ref, m_ref, end_ref, pad, carry,
+):
     rows = tokens * slots
+    step = pl.program_id(0)
     taps = slot_taps(wts_ref[...], 0)
     tops = edges(kb_ref, 0, rows, per, tail_ref[pl.ds(0, EDGE), :].astype(F32), prev_ref)
     order = before(rows)
     blocks = rows // HEAD
-    grams = []
+    ir, ic = grid_of(HEAD, HEAD)
+
+    @pl.when(step == 0)
+    def _():
+        carry[...] = (ir == ic).astype(F32)
+
+    grams, keys, scaled = [], [], []
     for n in range(per):
         s = conv_rows(kb_ref[n, pl.ds(0, rows), :].astype(F32), tops[n], taps, pad.at[n], slots)
         c, slope = silu(s)
         k, scale = unit(c)
-        kn_ref[n] = k
         fk_ref[n] = scale * slope
         betas = beta_rows(kb_ref[n, pl.ds(rows, EDGE), :].astype(F32), slots)
         strength = 2.0 * sigmoid(column(betas, tokens, slots))
         k2 = two(k)
+        kh_ref[n], kl_ref[n] = k2
+        keys.append(k2)
+        scaled.append(two(strength * k))
         grams.append(jnp.where(order, mm(k2, k2, ROWS_ROWS) * strength, 0.0))
-    r, c = grid_of(HEAD, HEAD)
-    eye = (r == c).astype(F32)
+    eye = (ir == ic).astype(F32)
     zero = jnp.zeros((HEAD, HEAD), BF16)
     diagonal = [
         gram[b * HEAD : (b + 1) * HEAD, b * HEAD : (b + 1) * HEAD] for gram in grams for b in range(blocks)
@@ -197,20 +214,31 @@
                 )
             done = merged
             size *= 2
-        ti_ref[n] = done[0]
+        x2 = two(done[0])
+        xh_ref[n], xl_ref[n] = x2
+        th_ref[n], tl_ref[n] = x2[0].T, x2[1].T
+        w2 = two(mm(x2, scaled[n]))
+        wh_ref[n], wl_ref[n] = w2
+        a_ref[n] = eye - mm(keys[n], w2, COLS_COLS)
+    state = carry[...]
+    for n in range(per):
+        m_ref[n] = state
+        state = mm(two(a_ref[n]), two(state))
+    carry[...] = state
+    end_ref[...] = state
 
 
 def maps_kernel(
-    per, tokens, slots, hid, vq_ref, prev_ref, beta_ref, tail_ref, wts_ref, kn_ref, ti_ref,
-    wu_ref, a_ref, mc_ref, fv_ref, end_ref, pad, carry,
+    per, tokens, slots, hid, vq_ref, prev_ref, beta_ref, tail_ref, wts_ref, kh_ref, kl_ref, xh_ref, xl_ref, a_ref,
+    m_ref,
+    u_ref, c_ref, an_ref, mn_ref, fv_ref, end_ref, pad, carry,
 ):
     rows = tokens * slots
     taps = slot_taps(wts_ref[...], 1)
-    ir, ic = grid_of(HEAD, 2 * HEAD)
 
     @pl.when(pl.program_id(0) == 0)
     def _():
-        carry[...] = (ir == ic).astype(F32)
+        carry[...] = jnp.zeros((HEAD, HEAD), F32)
 
     tail = tail_ref[pl.ds(EDGE, EDGE), :].astype(F32)
     tops = edges(vq_ref, 0, rows, per, tail, prev_ref)
@@ -220,23 +248,20 @@
         v, fv_ref[n] = silu(s)
         betas = beta_rows(beta_ref[n].astype(F32), slots)
         strength = 2.0 * sigmoid(column(betas, tokens, slots))
-        k = kn_ref[n]
-        wu = mm(two(ti_ref[n]), two(strength * jnp.concatenate([k, v], axis=1)))
-        wu_ref[n] = wu
-        maps.append(mm(two(k), two(wu), COLS_COLS))
+        u = mm((xh_ref[n], xl_ref[n]), two(strength * v))
+        u_ref[n] = u
+        maps.append(mm((kh_ref[n], kl_ref[n]), two(u), COLS_COLS))
     state = carry[...]
     for n in range(per):
-        mc_ref[n] = state
-        a = (ir == ic)[:, :HEAD].astype(F32) - maps[n][:, :HEAD]
-        a_ref[n] = a
-        moved = mm(two(a), two(state))
-        state = jnp.where(ic < HEAD, moved, moved + maps[n])
+        c_ref[n] = state
+        an_ref[n], mn_ref[n] = a_ref[n], m_ref[n]
+        state = mm(two(a_ref[n]), two(state)) + maps[n]
     carry[...] = state
     end_ref[...] = state
 
 
 def queries_kernel(
-    per, tokens, slots, hid, vq_ref, prev_ref, tail_ref, wts_ref, kn_ref, wu_ref,
+    per, tokens, slots, hid, vq_ref, prev_ref, tail_ref, wts_ref, kh_ref, kl_ref, wh_ref, wl_ref, u_ref,
     q_ref, sc_ref, qm_ref, ol_ref, fq_ref, pad,
 ):
     rows = tokens * slots
@@ -249,8 +274,10 @@
         c, slope = silu(s)
         q, scale = unit(c)
         fq_ref[n] = scale * slope
-        scores = jnp.where(seen, mm(two(q), two(kn_ref[n]), ROWS_ROWS), 0.0)
-        mapped = mm(two(scores), two(wu_ref[n]))
+        scores = jnp.where(seen, mm(two(q), (kh_ref[n], kl_ref[n]), ROWS_ROWS), 0.0)
+        uh, ul = two(u_ref[n])
+        both = jnp.concatenate([wh_ref[n], uh], axis=1), jnp.concatenate([wl_ref[n], ul], axis=1)
+        mapped = mm(two(scores), both)
         q_ref[n] = q
         sc_ref[n] = scores
         qm_ref[n] = q - mapped[:, :HEAD]
@@ -258,68 +285,75 @@
 
 
 def outs_kernel(
-    per, count, tokens, slots, hid, vq_ref, wts_ref, start_ref, kn_ref, mc_ref, qm_ref, ol_ref, a_ref, wu_ref, q_ref,
-    sc_ref, fq_ref, st_ref, mb_ref, d_ref, dk_ref, dd_ref, nq_ref, end_ref, pad, local,
+    per, tokens, slots, hid, vq_ref, wts_ref, start_ref, m_ref, c_ref, qm_ref, ol_ref, a_ref,
+    st_ref, dr_ref, mb_ref, nm_ref, end_ref,
 ):
-    step = pl.program_id(0)
     rows = tokens * slots
-    wts = wts_ref[...]
-    gain = gain_row(wts)
-    taps = query_taps(wts)
-    seen = visible(tokens, slots)
+    gain = gain_row(wts_ref[...])
     start = two(start_ref[...])
-    states = [mm(two(mc_ref[n, :, pl.ds(0, HEAD)]), start) + mc_ref[n, :, pl.ds(HEAD, HEAD)] for n in range(per)]
-    halves = [two(x) for x in states]
+    states = [mm(two(m_ref[n]), start) + c_ref[n] for n in range(per)]
     mapped = [two(qm_ref[n]) for n in range(per)]
-    raws = [mm(mapped[n], halves[n]) + ol_ref[n] for n in range(per)]
+    raws = [mm(mapped[n], two(states[n])) + ol_ref[n] for n in range(per)]
+    local = []
     for n in range(per):
         st_ref[n] = states[n]
-        raw, state = raws[n], halves[n]
+        raw = raws[n]
         scale = lax.rsqrt(jnp.mean(raw * raw, axis=-1, keepdims=True) + EPS)
         hat = raw * scale
-        nq_ref[n, pl.ds(0, tokens), :] = (hat * gain).astype(BF16)
+        nm_ref[n] = (hat * gain).astype(BF16)
         dn = vq_ref[n, pl.ds(rows + tokens, tokens), :].astype(F32) * gain
-        dr = two(scale * (dn - hat * jnp.mean(dn * hat, axis=-1, keepdims=True)))
-        local[step * per + n] = mm(mapped[n], dr, COLS_COLS)
-        q, k2 = q_ref[n], two(kn_ref[n])
-        d = wu_ref[n, :, pl.ds(HEAD, HEAD)] - mm(two(wu_ref[n, :, pl.ds(0, HEAD)]), state)
+        dr = scale * (dn - hat * jnp.mean(dn * hat, axis=-1, keepdims=True))
+        dr_ref[n] = dr
+        local.append(mm(mapped[n], two(dr), COLS_COLS))
+    ir, ic = grid_of(HEAD, 2 * HEAD)
+    state = (ir == ic).astype(F32)
+    for n in range(per - 1, -1, -1):
+        mb_ref[n] = state
+        moved = mm(two(a_ref[n]), two(state), COLS_COLS)
+        state = moved + jnp.concatenate([jnp.zeros((HEAD, HEAD), F32), local[n]], axis=1)
+    end_ref[...] = state
+
+
+def query_grads_kernel(
+    per, tokens, slots, hid, wts_ref, nm_ref, kh_ref, kl_ref, wh_ref, wl_ref, u_ref, q_ref, sc_ref, dr_ref, st_ref,
+    fq_ref, mb_ref, d_ref, dk_ref, dd_ref, stf_ref, mbf_ref, nq_ref, pad,
+):
+    taps = query_taps(wts_ref[...])
+    seen = visible(tokens, slots)
+    for n in range(per):
+        q, k2 = q_ref[n], (kh_ref[n], kl_ref[n])
+        stf_ref[n], mbf_ref[n] = st_ref[n], mb_ref[n]
+        state, dr = two(st_ref[n]), two(dr_ref[n])
+        d = u_ref[n] - mm((wh_ref[n], wl_ref[n]), state)
         d_ref[n] = d
         ds = two(jnp.where(seen, mm(dr, two(d), ROWS_ROWS), 0.0))
         dq = mm(dr, state, ROWS_ROWS) + mm(ds, k2)
         dk_ref[n] = mm(ds, two(q), COLS_COLS)
         dd_ref[n] = mm(two(sc_ref[n]), dr, COLS_COLS)
         inner, rim = conv_back(fq_ref[n] * (dq - q * jnp.sum(q * dq, axis=-1, keepdims=True)), taps, pad.at[n], 1)
+        nq_ref[n, pl.ds(0, tokens), :] = nm_ref[n]
         nq_ref[n, pl.ds(tokens, tokens), :] = inner.astype(BF16)
         nq_ref[n, pl.ds(2 * tokens, EDGE), :] = jnp.concatenate([rim, jnp.zeros((8, HEAD), F32)], axis=0).astype(BF16)
 
-    @pl.when(step == pl.num_programs(0) - 1)
-    def _():
-        ir, ic = grid_of(HEAD, 2 * HEAD)
-        state = (ir == ic).astype(F32)
-        for n in range(count - 1, -1, -1):
-            mb_ref[n] = state
-            moved = mm(two(a_ref[n]), two(state), COLS_COLS)
-            state = moved + jnp.concatenate([jnp.zeros((HEAD, HEAD), F32), local[n]], axis=1)
-        end_ref[...] = state
-
 
 def grads_kernel(
-    per, tokens, slots, hid, beta_ref, wts_ref, end_ref, mb_ref, kn_ref, ti_ref, d_ref, dk_ref, dd_ref, st_ref,
-    fk_ref, fv_ref, out_ref, pad,
+    per, tokens, slots, hid, beta_ref, wts_ref, end_ref, mb_ref, kh_ref, kl_ref, th_ref, tl_ref, d_ref, dk_ref, dd_ref,
+    st_ref, fk_ref, fv_ref, out_ref, pad,
 ):
     rows = tokens * slots
     wts = wts_ref[...]
     order = before(rows)
     end = two(end_ref[...])
     for n in range(per):
-        k, d = kn_ref[n], d_ref[n]
-        k2, d2 = two(k), two(d)
+        d, k2 = d_ref[n], (kh_ref[n], kl_ref[n])
+        d2 = two(d)
+        k = k2[0].astype(F32) + k2[1].astype(F32)
         g2 = two(mm(two(mb_ref[n, :, pl.ds(0, HEAD)]), end) + mb_ref[n, :, pl.ds(HEAD, HEAD)])
-        y = mm(two(ti_ref[n]), two(dd_ref[n] + mm(k2, g2)), COLS_COLS)
+        y = mm((th_ref[n], tl_ref[n]), two(dd_ref[n] + mm(k2, g2)))
         betas = beta_rows(beta_ref[n].astype(F32), slots)
         de = 2.0 * sigmoid(column(betas, tokens, slots)) * y
         de2 = two(de)
-        dgram = jnp.where(order, mm(de2, d2, ROWS_ROWS), 0.0)
+        dgram = jnp.where(order, mm_half(de2, d2, ROWS_ROWS), 0.0)
         dk = dk_ref[n] + mm(d2, g2, ROWS_ROWS) - mm(de2, two(st_ref[n]), ROWS_ROWS)
         dk = dk - mm(two(dgram + dgram.T), k2)
         along = jnp.sum(y * d, axis=1, keepdims=True)
@@ -338,21 +372,26 @@
         out_ref[n, pl.ds(2 * rows + EDGE, EDGE), :] = jnp.concatenate([key_rim, value_rim], axis=0).astype(BF16)
 
 
-def unpack_kernel(tokens, slots, got_ref, rim_ref, gk_ref, gv_ref):
+def unpack_kernel(tokens, slots, got_ref, gk_ref, gv_ref):
     rows = tokens * slots
     for a, out_ref in enumerate((gk_ref, gv_ref)):
-        main = got_ref[0, pl.ds(a * rows, rows), :].astype(F32)
-        last = main[rows - 8 :] + rim_ref[0, pl.ds(8 * a, 8), :].astype(F32)
-        out_ref[...] = jnp.concatenate([main[: rows - 8], last], axis=0).reshape(tokens, slots, HEAD)
-
-
-def unpack_query_kernel(tokens, got_ref, rim_ref, gq_ref):
-    main = got_ref[0, pl.ds(tokens, tokens), :].astype(F32)
-    last = main[tokens - 8 :] + rim_ref[0, pl.ds(0, 8), :].astype(F32)
-    gq_ref[...] = jnp.concatenate([main[: tokens - 8], last], axis=0)
-
-
-FAR = ("kn", "ti", "fk", "fv", "st", "mb", "d", "dk", "dd")
+        out_ref[...] = got_ref[0, pl.ds(a * rows, rows), :].astype(F32).reshape(tokens, slots, HEAD)
+
+
+def unpack_query_kernel(tokens, got_ref, gq_ref):
+    gq_ref[...] = got_ref[0, pl.ds(tokens, tokens), :].astype(F32)
+
+
+def rims_kernel(heads, slots, rim_ref, gq_ref, gk_ref, gv_ref, nq_ref, nk_ref, nv_ref):
+    for h in range(heads):
+        part = pl.ds(h * HEAD, HEAD)
+        rim = rim_ref[h].astype(F32)
+        nq_ref[:, part] = gq_ref[:, part] + rim[:8]
+        nk_ref[:, :, part] = gk_ref[:, :, part] + rim[8:16].reshape(8 // slots, slots, HEAD)
+        nv_ref[:, :, part] = gv_ref[:, :, part] + rim[16:].reshape(8 // slots, slots, HEAD)
+
+
+FAR = ("kh", "kl", "xh", "xl", "th", "tl", "wh", "wl", "a", "m", "fk", "fv", "stf", "mbf", "d", "dk", "dd")
 
 
 def call(kernel, hid, steps, live, ins, reads, outs, scratch=(), us=1.0, grant=24):
@@ -466,37 +505,43 @@
     def pad(n):
         return [pltpu.VMEM((per, n + EDGE + 8, HEAD), F32)]
 
-    def big(name, *shape, per=per):
-        return (name, (g,) + shape, F32, per)
+    def big(name, *shape, per=per, kind=F32):
+        return (name, (g,) + shape, kind, per)
 
     live = {}
     wide = 4 if g % 4 == 0 else per
-    call(
+    (m_end,) = call(
         functools.partial(inverse_kernel, wide, tokens, slots),
         hid,
         g // wide,
         live,
         [(kb, wide), (kb, ("prev", wide, rows - EDGE)), (tail, None), (wts, "weights")],
         [],
-        [big("kn", rows, HEAD, per=wide), big("ti", rows, rows, per=wide), big("fk", rows, HEAD, per=wide)],
-        scratch=[pltpu.VMEM((wide, rows + EDGE + 8, HEAD), F32)],
-        us=9.0,
+        [big(name, rows, HEAD, per=wide, kind=BF16) for name in ("kh", "kl")]
+        + [big(name, rows, rows, per=wide, kind=BF16) for name in ("xh", "xl", "th", "tl")]
+        + [big(name, rows, HEAD, per=wide, kind=BF16) for name in ("wh", "wl")]
+        + [
+            big("fk", rows, HEAD, per=wide), big("a", HEAD, HEAD, per=wide), big("m", HEAD, HEAD, per=wide),
+            (None, (HEAD, HEAD), F32, None),
+        ],
+        scratch=[pltpu.VMEM((wide, rows + EDGE + 8, HEAD), F32), pltpu.VMEM((HEAD, HEAD), F32)],
+        us=11.0,
         grant=40,
     )
     beta = (kb, ("rows", per, rows))
-    (end,) = call(
+    (c_end,) = call(
         functools.partial(maps_kernel, per, tokens, slots),
         hid,
         steps,
         live,
         [(vq, per), (vq, ("prev", per, rows - EDGE)), beta, (tail, None), (wts, "weights")],
-        [("kn", per), ("ti", per)],
+        [(name, per) for name in ("kh", "kl", "xh", "xl", "a", "m")],
         [
-            big("wu", rows, 2 * HEAD), big("a", HEAD, HEAD), big("mc", HEAD, 2 * HEAD), big("fv", rows, HEAD),
-            (None, (HEAD, 2 * HEAD), F32, None),
+            big("u", rows, HEAD), big("c", HEAD, HEAD), big("an", HEAD, HEAD), big("mn", HEAD, HEAD),
+            big("fv", rows, HEAD), (None, (HEAD, HEAD), F32, None),
         ],
-        scratch=pad(rows) + [pltpu.VMEM((HEAD, 2 * HEAD), F32)],
-        us=8.0,
+        scratch=pad(rows) + [pltpu.VMEM((HEAD, HEAD), F32)],
+        us=6.0,
     )
 
     def across(last, towards):
@@ -504,8 +549,8 @@
             return jnp.zeros((HEAD, HEAD), F32)
         if groups == 2:
             moves = [(i, i + towards * heads) for i in range(shard_count) if 0 <= i + towards * heads < shard_count]
-            return lax.ppermute(last[:, HEAD:], "ctx", moves)
-        every = lax.all_gather(last, "ctx")
+            return lax.ppermute(last[1], "ctx", moves)
+        every = lax.all_gather(jnp.concatenate(last, axis=1), "ctx")
         head = place % heads
         ahead = group if towards > 0 else groups - 1 - group
 
@@ -516,14 +561,14 @@
 
         return lax.fori_loop(0, ahead, advance, jnp.zeros((HEAD, HEAD), F32))
 
-    start = across(end, 1)
+    start = across((m_end, c_end), 1)
     call(
         functools.partial(queries_kernel, per, tokens, slots),
         hid,
         steps,
         live,
         [(vq, per), (vq, ("prev", per, rows + tokens - EDGE)), (tail, None), (wts, "weights")],
-        [("kn", per), ("wu", per)],
+        [(name, per) for name in ("kh", "kl", "wh", "wl", "u")],
         [
             big("q", tokens, HEAD), big("sc", tokens, rows), big("qm", tokens, HEAD), big("ol", tokens, HEAD),
             big("fq", tokens, HEAD),
@@ -531,24 +576,34 @@
         scratch=pad(tokens),
         us=8.0,
     )
-    nq, back_end = call(
-        functools.partial(outs_kernel, per, g, tokens, slots),
+    normed, back_end = call(
+        functools.partial(outs_kernel, g, tokens, slots),
+        hid,
+        1,
+        live,
+        [(vq, g), (wts, "weights"), (start, None)],
+        [(name, g) for name in ("mn", "c", "qm", "ol", "an")],
+        [
+            big("st", HEAD, HEAD, per=g), big("dr", tokens, HEAD, per=g), big("mb", HEAD, 2 * HEAD, per=g),
+            (None, (g, tokens, HEAD), BF16, g), (None, (HEAD, 2 * HEAD), F32, None),
+        ],
+        us=4.0,
+    )
+    finish = across((back_end[:, :HEAD], back_end[:, HEAD:]), -1)
+    (nq,) = call(
+        functools.partial(query_grads_kernel, per, tokens, slots),
         hid,
         steps,
         live,
-        [(vq, per), (wts, "weights"), (start, None)],
+        [(wts, "weights"), (normed, per)],
+        [(name, per) for name in ("kh", "kl", "wh", "wl", "u", "q", "sc", "dr", "st", "fq", "mb")],
         [
-            ("kn", per), ("mc", per), ("qm", per), ("ol", per), ("a", None), ("wu", per), ("q", per), ("sc", per),
-            ("fq", per),
+            big("d", rows, HEAD), big("dk", rows, HEAD), big("dd", rows, HEAD), big("stf", HEAD, HEAD),
+            big("mbf", HEAD, 2 * HEAD), (None, (g, 2 * tokens + EDGE, HEAD), BF16, per),
         ],
-        [
-            big("st", HEAD, HEAD), big("mb", HEAD, 2 * HEAD, per=None), big("d", rows, HEAD), big("dk", rows, HEAD),
-            big("dd", rows, HEAD), (None, (g, 2 * tokens + EDGE, HEAD), BF16, per), (None, (HEAD, 2 * HEAD), F32, None),
-        ],
-        scratch=pad(tokens) + [pltpu.VMEM((g, HEAD, HEAD), F32)],
-        us=10.0,
-    )
-    finish = across(back_end, -1)
+        scratch=pad(tokens),
+        us=20.0,
+    )
     nq = exchange(nq)
     (grads,) = call(
         functools.partial(grads_kernel, per, tokens, slots),
@@ -556,7 +611,7 @@
         steps,
         live,
         [beta, (wts, "weights"), (finish, None)],
-        [(name, per) for name in ("mb", "kn", "ti", "d", "dk", "dd", "st", "fk", "fv")],
+        [(name, per) for name in ("mbf", "kh", "kl", "th", "tl", "d", "dk", "dd", "stf", "fk", "fv")],
         [(None, (g, 2 * rows + 2 * EDGE, HEAD), BF16, per)],
         scratch=[pltpu.VMEM((2 * per, rows + EDGE + 8, HEAD), F32)],
         us=20.0,
@@ -575,26 +630,40 @@
     else:
         layer_out = lax.psum_scatter(partial.astype(BF16), "head", scatter_dimension=0, tiled=True)
 
-    back = [(i, i - 1) for i in range(1, shard_count)]
-    query_rim = lax.ppermute(nq[:, 2 * tokens :], "ctx", back)
-    rim = lax.ppermute(grads[:, 2 * rows + EDGE :], "ctx", back)
+    rim = jnp.concatenate([nq[:, 2 * tokens : 2 * tokens + 8], grads[:, 2 * rows + EDGE :]], axis=1)
+    rim = lax.ppermute(rim, "ctx", [(i, i - 1) for i in range(1, shard_count)])
     part = lambda x: pl.BlockSpec((1,) + x.shape[1:], lambda h: (h, 0, 0))
+    small = pltpu.CompilerParams(vmem_limit_bytes=8 << 20)
+    cost = lambda us: pl.CostEstimate(flops=int(us * 1.1e9), bytes_accessed=1 << 16, transcendentals=0)
     grad_query = pl.pallas_call(
         functools.partial(unpack_query_kernel, tokens),
         grid=(heads,),
-        in_specs=[part(nq), part(query_rim)],
+        in_specs=[part(nq)],
         out_specs=pl.BlockSpec((tokens, HEAD), lambda h: (0, h)),
         out_shape=jax.ShapeDtypeStruct((tokens, width), F32),
-        compiler_params=pltpu.CompilerParams(vmem_limit_bytes=8 << 20),
-    )(nq, query_rim)
+        compiler_params=small,
+        cost_estimate=cost(2.0),
+    )(nq)
     grad_key, grad_value = pl.pallas_call(
         functools.partial(unpack_kernel, tokens, slots),
         grid=(heads,),
-        in_specs=[part(grads), part(rim)],
+        in_specs=[part(grads)],
         out_specs=[pl.BlockSpec((tokens, slots, HEAD), lambda h: (0, 0, h))] * 2,
         out_shape=[jax.ShapeDtypeStruct((tokens, slots, width), F32)] * 2,
-        compiler_params=pltpu.CompilerParams(vmem_limit_bytes=8 << 20),
-    )(grads, rim)
+        compiler_params=small,
+        cost_estimate=cost(10.0),
+    )(grads)
+    flat = pl.BlockSpec((8, width), lambda i: (tokens // 8 - 1, 0))
+    deep = pl.BlockSpec((8 // slots, slots, width), lambda i: (tokens * slots // 8 - 1, 0, 0))
+    grad_query, grad_key, grad_value = pl.pallas_call(
+        functools.partial(rims_kernel, heads, slots),
+        grid=(1,),
+        in_specs=[pl.BlockSpec(rim.shape, lambda i: (0, 0, 0)), flat, deep, deep],
+        out_specs=[flat, deep, deep],
+        out_shape=[jax.ShapeDtypeStruct(x.shape, F32) for x in (grad_query, grad_key, grad_value)],
+        input_output_aliases={1: 0, 2: 1, 3: 2},
+        compiler_params=small,
+    )(rim, grad_query, grad_key, grad_value)
     marks = grads[:, 2 * rows : 2 * rows + 2 * slots].astype(F32)
     grad_beta = marks.reshape(heads, slots, 2, tokens).sum(axis=2).transpose(2, 1, 0)
     return (layer_out, grad_query, grad_key, grad_value, grad_beta)

time: 122 us -> 113 us (0.926)
  waiting for transfers between devices: 20.3 us -> 9.19 us
  Pallas kernels: 48.1 us -> 52.4 us
  starting transfers between devices: 35.7 us -> 33.5 us
  local copies, waits for them, and re-layouts: 4.56 us -> 6 us
    ppermute x4 -> x3, waiting for transfers between devices: 11.3 us -> 0.01 us  [the longest x2 0.01 us: across(): return lax.ppermute(last[1], 'ctx', moves)]
    ppermute x1, waiting for transfers between devices: 0.01 us -> 4.17 us  [shards(): lax.ppermute(sent, 'head', [(0, 1), (1, 0)]).astype(F32)]
    all_to_all x4, waiting for transfers between devices: 9 us -> 5.02 us  [exchange(): lax.all_to_all(x, 'ctx', 0, 0, axis_index_groups=group_lists, tiled=True)]
    pallas_call x5 -> x6, Pallas kernels: 42.5 us -> 45.3 us  [call(): pl.pallas_call(kernel, grid_spec=pltpu.PrefetchScalarGridSpec(num_scalar_...]
    unnamed x20 -> x22, local copies, waits for them, and re-layouts: 1.06 us -> 2.52 us
    pallas_call x0 -> x1, Pallas kernels: none -> 1.45 us  [shards(): pl.pallas_call(functools.partial(rims_kernel, heads, slots), grid=(1,), i...]
    ppermute x4 -> x3, starting transfers between devices: 10.4 us -> 9.07 us  [the longest x2 6.29 us: across(): return lax.ppermute(last[1], 'ctx', moves)]
  transfers between devices with their start and end apart: 10 -> 9, of which waited for: 5 -> 3; matrix products, arithmetic and copies ran while one was open for 10% -> 10% of each run, Pallas kernels for 22% -> 38%
where the time goes in v5:
time: 113 us; the launch traced here: 112 us
  Pallas kernels  52.4 us (46%)
  starting transfers between devices  33.5 us (30%)
  waiting for transfers between devices  9.19 us (8%)
  matrix products  6.6 us (6%)
  local copies, waits for them, and re-layouts  6 us (5%)
  other arithmetic  3.49 us (3%)
    pallas_call x6, Pallas kernels, call(): pl.pallas_call(kernel, grid_spec=pltpu.PrefetchScalarGridSpec(num_scalar_...  45.3 us
    all_to_all x4, starting transfers between devices, exchange(): lax.all_to_all(x, 'ctx', 0, 0, axis_index_groups=group_lists, tiled=True)  19 us
    ppermute x2, starting transfers between devices, across(): return lax.ppermute(last[1], 'ctx', moves)  6.29 us
    all_to_all x4, waiting for transfers between devices, exchange(): lax.all_to_all(x, 'ctx', 0, 0, axis_index_groups=group_lists, tiled=True)  5.02 us
    ppermute x1, starting transfers between devices, shards(): lax.ppermute(tail, 'ctx', [(i, i + heads) for i in range(shard_count - he...  4.2 us
    ppermute x1, waiting for transfers between devices, shards(): lax.ppermute(sent, 'head', [(0, 1), (1, 0)]).astype(F32)  4.17 us
    dot_general x1, matrix products, shards(): jnp.dot(grad_out, out_weight.T, preferred_element_type=F32).astype(BF16)  3.7 us
    pallas_call x1, Pallas kernels, shards(): pl.pallas_call(functools.partial(unpack_kernel, tokens, slots), grid=(hea...  3.08 us
  transfers between devices with their start and end apart: 9, of which 3 were waited for; matrix products, arithmetic and copies ran while one was open for 10% of the time, Pallas kernels for 38%

profile of v5, /device:TPU:1, one launch (start us, length us, event | category | flops | bytes accessed | tf_op | source)
XLA Modules:
  0.0 112.2 jit_solution(9876831927249968687)
XLA Ops:
  0.6 0.0 copy-start
  0.6 0.8 fusion.11
  1.4 0.3 copy-done
  1.7 0.4 copy_bitcast_fusion
  2.1 0.8 copy_bitcast_fusion.2
  2.8 0.8 bitcast_bitcast_fusion
  3.6 0.9 fusion.6
  4.5 5.3 %all-to-all-start = ((bf16[8,304,128]{2,1,0:T(8,128)(2,1)}), bf16[8,304,128]{2,1,0:T(8,128)(2,1)S(1)}, u32[]{:S(2)}, u32[]{:S(2)}) async-start(bf16[8,304,128]{2,1,0:T(8,128)(2,1)} %fusion.6), calls=%async_computation | async-start | bytes 1245184 | tf_op jit(solution)/shard_map/all_to_all | solution.py:462
  9.8 0.2 copy.35
  10.0 3.7 %convolution_convert_fusion = bf16[128,1024]{1,0:T(8,128)(2,1)S(1)} fusion(bf16[128,2048]{1,0:T(8,128)(2,1)S(1)} %copy-done.4, bf16[1024,2048]{1,0:T(8,128)(2,1)} %param.18), kind=kOutput, calls=%fused_computation.6 | convolution fusion | flops 537001984 | bytes 4980736 | tf_op jit(solution)/shard_map/dot_general | solution.py:487
  13.7 0.0 copy-start.3
  13.7 0.2 copy.37
  13.9 0.2 copy.38
  14.1 0.2 copy.36
  14.3 0.5 copy-done.3
  14.7 0.4 copy_bitcast_fusion.1
  15.1 3.7 %all-to-all-done.kb_ref.prev_ref.beta_ref = bf16[8,304,128]{2,1,0:T(8,128)(2,1)S(1)} async-done(((bf16[8,304,128]{2,1,0:T(8,128)(2,1)}), bf16[8,304,128]{2,1,0:T(8,128)(2,1)S(1)}, u32[]{:S(2)}, u32[]{:S(2)}) %all-to-all-start) | async-done | bytes 622624 | tf_op jit(solution)/shard_map/all_to_all | solution.py:462
  18.8 4.2 %collective-permute-start = (bf16[48,128]{1,0:T(8,128)(2,1)S(1)}, bf16[48,128]{1,0:T(8,128)(2,1)S(1)}, u32[]{:S(2)}, u32[]{:S(2)}) collective-permute-start(bf16[48,128]{1,0:T(8,128)(2,1)S(1)} %pad_maximum_fusion.3), channel_id=1, source_target_pairs={{0,16},{2,18},{4,20},{6,22},{8,24},{10,26},{12,28},{14,30},{1,17},... | collective-permute-start | bytes 36872 | tf_op jit(solution)/shard_map/ppermute | solution.py:485
  23.1 1.0 pad_maximum_fusion
  24.1 0.0 collective-permute-done.tail_ref
  24.1 4.9 %all-to-all-start.1 = ((bf16[8,512,128]{2,1,0:T(8,128)(2,1)}), bf16[8,512,128]{2,1,0:T(8,128)(2,1)S(1)}, u32[]{:S(2)}, u32[]{:S(2)}) async-start(bf16[8,512,128]{2,1,0:T(8,128)(2,1)} %pad_maximum_fusion), calls=%async_computation.1 | async-start | bytes 2097152 | tf_op jit(solution)/shard_map/all_to_all | solution.py:462
  29.1 0.1 tile.17
  29.3 0.1 tile.19
  29.4 13.6 %shard_map.137 = (bf16[8,256,128]{2,1,0:T(8,128)(2,1)}, bf16[8,256,128]{2,1,0:T(8,128)(2,1)}, bf16[8,256,256]{2,1,0:T(8,128)(2,1)}, bf16[8,256,256]{2,1,0:T(8,12...) custom-call(s32[1]{0:T(128)} %bitcast.hid, ...), custom_call_target="tpu_custom_call" | custom-call | flops 12099999744 | bytes 65536 | tf_op jit(solution)/shard_map/pallas_call | solution.py:416
  43.1 0.0 all-to-all-done.1.vq_ref.prev_ref
  43.1 6.0 %shard_map.138 = (f32[8,256,128]{2,1,0:T(8,128)S(1)}, f32[8,128,128]{2,1,0:T(8,128)S(1)}, f32[8,128,128]{2,1,0:T(8,128)S(1)}, f32[8,128,128]{2,1,0:T(8,128)S(1)}...) custom-call(s32[1]{0:T(128)} %bitcast.hid, bf16[8,512,128]{2,1,0:T(8,128)(2,1)S(1)} %all-to-all-done.1.vq_ref.prev_ref, ...), custom_call_target="tpu_custom_call" | custom-call | flops 6600000000 | bytes 65536 | tf_op jit(solution)/shard_map/pallas_call | solution.py:416
  49.1 4.8 %collective-permute-start.1 = (f32[128,128]{1,0:T(8,128)S(1)}, f32[128,128]{1,0:T(8,128)S(1)}, u32[]{:S(2)}, u32[]{:S(2)}) collective-permute-start(f32[128,128]{1,0:T(8,128)S(1)} %get-tuple-element.53), channel_id=1, source_target_pairs={{0,16},{2,18},{4,20},{6,22},{8,24},{10,26},{12,28},{14,30},{1,17},... | collective-permute-start | bytes 196616 | tf_op jit(solution)/shard_map/ppermute | solution.py:552
  54.0 4.9 %shard_map.139 = (f32[8,128,128]{2,1,0:T(8,128)S(1)}, f32[8,128,256]{2,1,0:T(8,128)S(1)}, f32[8,128,128]{2,1,0:T(8,128)S(1)}, f32[8,128,128]{2,1,0:T(8,128)S(1)}, f32[8,128,128]{2,1,0:T(8,128)S(1)}) custom-call(s32[1]{0:T(128)} %bitcast.hid, bf16[8,512,128]{2,1,0:T(8,128)(2,1)S(1)} %all-to-all-done.1.vq_ref.prev_ref, ...), custom_call_target="tpu_custom_call" | custom-call | flops 8800000000 | bytes 65536 | tf_op jit(solution)/shard_map/pallas_call | solution.py:416
  58.9 2.5 %shard_map.140 = (f32[8,128,128]{2,1,0:T(8,128)S(1)}, f32[8,128,128]{2,1,0:T(8,128)S(1)}, f32[8,128,256]{2,1,0:T(8,128)S(1)}, bf16[8,128,128]{2,1,0:T(8,128)(2,1)S(1)}, f32[128,256]{1,0:T(8,128)S(1)}) custom-call(s32[1]{0:T(128)} %bitcast.hid, bf16[8,512,128]{2,1,0:T(8,128)(2,1)S(1)} %all-to-all-done.1.vq_ref.prev_ref, f32[72,1024]{1,0:T(8,128)S(1)} %concatenate.15.wts_ref, ...), custom_call_target="tpu_custom_call" | custom-call | flops 4400000000 | bytes 65536 | tf_op jit(solution)/shard_map/pallas_call | solution.py:416
  61.4 1.5 %collective-permute-start.3 = (f32[128,128]{1,0:T(8,128)S(1)}, f32[128,128]{1,0:T(8,128)S(1)}, u32[]{:S(2)}, u32[]{:S(2)}) collective-permute-start(f32[128,128]{1,0:T(8,128)S(1)} %slice.33), channel_id=1, source_target_pairs={{16,0},{18,2},{20,4},{22,6},{24,8},{26,10},{28,12},{30,14},{17,1},... | collective-permute-start | bytes 196616 | tf_op jit(solution)/shard_map/ppermute | solution.py:552
  62.9 7.4 %shard_map.141 = (f32[8,256,128]{2,1,0:T(8,128)}, f32[8,256,128]{2,1,0:T(8,128)}, f32[8,256,128]{2,1,0:T(8,128)}, f32[8,128,128]{2,1,0:T(8,128)}, f32[8,128,256]{2,1,0:T(8,128)}, /*index=5*/bf16[8,272,128]{2,1,0:T(8,128)(2,1)}) custom-call(s32[1]{0:T(128)} %bitcast.hid, f32[72,1024]{1,0:T(8,128)S(1)} %concatenate.15.wts_ref, ...), custom_call_target="tpu_custom_call" | custom-call | flops 22000001024 | bytes 65536 | tf_op jit(solution)/shard_map/pallas_call | solution.py:416
  70.3 4.5 %all-to-all-start.2 = ((bf16[8,272,128]{2,1,0:T(8,128)(2,1)}), bf16[8,272,128]{2,1,0:T(8,128)(2,1)S(1)}, u32[]{:S(2)}, u32[]{:S(2)}) async-start(bf16[8,272,128]{2,1,0:T(8,128)(2,1)} %get-tuple-element.69), calls=%async_computation.2 | async-start | bytes 1114112 | tf_op jit(solution)/shard_map/all_to_all | solution.py:462
  74.9 10.8 %shard_map.142 = bf16[8,544,128]{2,1,0:T(8,128)(2,1)} custom-call(s32[1]{0:T(128)} %bitcast.hid, bf16[8,304,128]{2,1,0:T(8,128)(2,1)S(1)} %all-to-all-done.kb_ref.prev_ref.beta_ref, f32[72,1024]{1,0:T(8,128)S(1)} %concatenate.15.wts_ref, f32[128,128]{1,0:T(8,128)S(1)} %collective-permute-done.3.end_ref, f32[8,128,256]{2,1,0:T(8,128)} %get-tuple-element.71.mb_ref, ...), custom_call_target="tpu_custom_call" | custom-call | flops 22000001024 | bytes 65536 | tf_op jit(solution)/shard_map/pallas_call | solution.py:416
  85.7 4.2 %all-to-all-start.3 = ((bf16[8,544,128]{2,1,0:T(8,128)(2,1)}), bf16[8,544,128]{2,1,0:T(8,128)(2,1)S(1)}, u32[]{:S(2)}, u32[]{:S(2)}) async-start(bf16[8,544,128]{2,1,0:T(8,128)(2,1)} %shard_map.142), calls=%async_computation.3 | async-start | bytes 2228224 | tf_op jit(solution)/shard_map/all_to_all | solution.py:462
  89.9 0.2 copy.45
  90.1 0.1 dot_general.9
  90.2 2.9 %fusion = f32[2,64,2048]{2,1,0:T(8,128)S(1)} fusion(bf16[2,64,1024]{2,1,0:T(8,128)(2,1)S(1)} %dot_general.9, bf16[1024,2048]{1,0:T(8,128)(2,1)} %param.18), kind=kOutput, calls=%fused_computation | convolution fusion | flops 536870912 | bytes 5505024 | tf_op jit(solution)/shard_map/dot_general | solution.py:622
  93.1 0.0 copy-start.1
  93.1 1.0 copy-done.1
  94.1 1.3 %collective-permute-start.2 = (bf16[64,2048]{1,0:T(8,128)(2,1)S(1)}, bf16[64,2048]{1,0:T(8,128)(2,1)S(1)}, u32[]{:S(2)}, u32[]{:S(2)}) collective-permute-start(bf16[64,2048]{1,0:T(8,128)(2,1)S(1)} %fusion.8), channel_id=1, source_target_pairs={{0,1},{1,0},{2,3},{3,2},{4,5},{5,4},{6,7},{7,6},{8,9},{9,8},{10,11... | collective-permute-start | bytes 786440 | tf_op jit(solution)/shard_map/ppermute | solution.py:629
  95.4 2.6 %shard_map.143.gq_ref = f32[128,1024]{1,0:T(8,128)} custom-call(bf16[8,272,128]{2,1,0:T(8,128)(2,1)S(1)} %all-to-all-done.2.got_ref), custom_call_target="tpu_custom_call" | custom-call | flops 2200000000 | bytes 65536 | tf_op jit(solution)/shard_map/pallas_call | solution.py:638
  98.0 4.2 %collective-permute-done.2 = bf16[64,2048]{1,0:T(8,128)(2,1)S(1)} collective-permute-done((bf16[64,2048]{1,0:T(8,128)(2,1)S(1)}, bf16[64,2048]{1,0:T(8,128)(2,1)S(1)}, u32[]{:S(2)}, u32[]{:S(2)}) %collective-permute-start.2) | collective-permute-done | bytes 262176 | tf_op jit(solution)/shard_map/ppermute | solution.py:629
  102.1 0.8 fusion.7
  102.9 1.3 %all-to-all-done.3.got_ref = bf16[8,544,128]{2,1,0:T(8,128)(2,1)S(1)} async-done(((bf16[8,544,128]{2,1,0:T(8,128)(2,1)}), bf16[8,544,128]{2,1,0:T(8,128)(2,1)S(1)}, u32[]{:S(2)}, u32[]{:S(2)}) %all-to-all-start.3) | async-done | bytes 1114144 | tf_op jit(solution)/shard_map/all_to_all | solution.py:462
  104.2 2.8 %collective-permute-start.4 = (bf16[8,24,128]{2,1,0:T(8,128)(2,1)S(1)}, bf16[8,24,128]{2,1,0:T(8,128)(2,1)S(1)}, u32[]{:S(2)}, u32[]{:S(2)}) collective-permute-start(bf16[8,24,128]{2,1,0:T(8,128)(2,1)S(1)} %pad_maximum_fusion.1), channel_id=1, source_target_pairs={{2,0},{4,2},{6,4},{8,6},{10,8},{12,10},{14,12},{16,14},{18,16},{20... | collective-permute-start | bytes 147464 | tf_op jit(solution)/shard_map/ppermute | solution.py:634
  107.0 3.1 %shard_map.144 = (f32[128,2,1024]{2,1,0:T(2,128)}, f32[128,2,1024]{2,1,0:T(2,128)}) custom-call(bf16[8,544,128]{2,1,0:T(8,128)(2,1)S(1)} %all-to-all-done.3.got_ref), custom_call_target="tpu_custom_call" | custom-call | flops 11000000512 | bytes 65536 | tf_op jit(solution)/shard_map/pallas_call | solution.py:647
  110.1 0.6 copy.46
  110.7 1.4 %shard_map.145 = (f32[128,1024]{1,0:T(8,128)}, f32[128,2,1024]{2,1,0:T(2,128)}, f32[128,2,1024]{2,1,0:T(2,128)}) custom-call(bf16[8,24,128]{2,1,0:T(8,128)(2,1)S(1)} %collective-permute-done.4.rim_ref, f32[128,1024]{1,0:T(8,128)} %shard_map.143.gq_ref, ...), custom_call_target="tpu_custom_call", output_to_operand_aliasing={{0}: (1, {}), {1}: (2, {}), {2}: (3, {})} | custom-call | tf_op jit(solution)/shard_map/pallas_call | solution.py:658
  (35 shorter events, 0.3 us)
Async XLA Ops:
  0.6 1.1 copy-start
  3.6 6.2 %copy-start.5 = (bf16[128,1024]{1,0:T(8,128)(2,1)S(1)}, bf16[128,1024]{1,0:T(8,128)(2,1)}, u32[]{:S(2)}) copy-start(bf16[128,1024]{1,0:T(8,128)(2,1)} %param.10) | copy-start | bytes 786436
  3.6 6.4 %copy-start.4 = (bf16[128,2048]{1,0:T(8,128)(2,1)S(1)}, bf16[128,2048]{1,0:T(8,128)(2,1)}, u32[]{:S(2)}) copy-start(bf16[128,2048]{1,0:T(8,128)(2,1)} %param.19) | copy-start | bytes 1572868
  4.5 14.3 %all-to-all-start = ((bf16[8,304,128]{2,1,0:T(8,128)(2,1)}), bf16[8,304,128]{2,1,0:T(8,128)(2,1)S(1)}, u32[]{:S(2)}, u32[]{:S(2)}) async-start(bf16[8,304,128]{2,1,0:T(8,128)(2,1)} %fusion.6), calls=%async_computation | async-start | bytes 1245184 | tf_op jit(solution)/shard_map/all_to_all | solution.py:462
  13.7 1.0 copy-start.3
  18.8 5.3 %collective-permute-start = (bf16[48,128]{1,0:T(8,128)(2,1)S(1)}, bf16[48,128]{1,0:T(8,128)(2,1)S(1)}, u32[]{:S(2)}, u32[]{:S(2)}) collective-permute-start(bf16[48,128]{1,0:T(8,128)(2,1)S(1)} %pad_maximum_fusion.3), channel_id=1, source_target_pairs={{0,16},{2,18},{4,20},{6,22},{8,24},{10,26},{12,28},{14,30},{1,17},... | collective-permute-start | bytes 36872 | tf_op jit(solution)/shard_map/ppermute | solution.py:485
  24.1 5.0 %copy-start.6 = (f32[4,2,1024]{2,1,0:T(2,128)S(1)}, f32[4,2,1024]{2,1,0:T(2,128)}, u32[]{:S(2)}) copy-start(f32[4,2,1024]{2,1,0:T(2,128)} %param.15) | copy-start | bytes 98308
  24.1 5.1 %copy-start.7 = (f32[4,2,1024]{2,1,0:T(2,128)S(1)}, f32[4,2,1024]{2,1,0:T(2,128)}, u32[]{:S(2)}) copy-start(f32[4,2,1024]{2,1,0:T(2,128)} %param.16) | copy-start | bytes 98308
  24.1 5.3 %copy-start.8 = (f32[4,1024]{1,0:T(4,128)S(1)}, f32[4,1024]{1,0:T(4,128)}, u32[]{:S(2)}) copy-start(f32[4,1024]{1,0:T(4,128)} %param.14) | copy-start | bytes 49156
  24.1 5.3 %copy-start.9 = (f32[1024]{0:T(1024)S(1)}, f32[1024]{0:T(1024)}, u32[]{:S(2)}) copy-start(f32[1024]{0:T(1024)} %param.17) | copy-start | bytes 12292
  24.1 19.0 %all-to-all-start.1 = ((bf16[8,512,128]{2,1,0:T(8,128)(2,1)}), bf16[8,512,128]{2,1,0:T(8,128)(2,1)S(1)}, u32[]{:S(2)}, u32[]{:S(2)}) async-start(bf16[8,512,128]{2,1,0:T(8,128)(2,1)} %pad_maximum_fusion), calls=%async_computation.1 | async-start | bytes 2097152 | tf_op jit(solution)/shard_map/all_to_all | solution.py:462
  49.1 9.7 %collective-permute-start.1 = (f32[128,128]{1,0:T(8,128)S(1)}, f32[128,128]{1,0:T(8,128)S(1)}, u32[]{:S(2)}, u32[]{:S(2)}) collective-permute-start(f32[128,128]{1,0:T(8,128)S(1)} %get-tuple-element.53), channel_id=1, source_target_pairs={{0,16},{2,18},{4,20},{6,22},{8,24},{10,26},{12,28},{14,30},{1,17},... | collective-permute-start | bytes 196616 | tf_op jit(solution)/shard_map/ppermute | solution.py:552
  61.4 13.4 %collective-permute-start.3 = (f32[128,128]{1,0:T(8,128)S(1)}, f32[128,128]{1,0:T(8,128)S(1)}, u32[]{:S(2)}, u32[]{:S(2)}) collective-permute-start(f32[128,128]{1,0:T(8,128)S(1)} %slice.33), channel_id=1, source_target_pairs={{16,0},{18,2},{20,4},{22,6},{24,8},{26,10},{28,12},{30,14},{17,1},... | collective-permute-start | bytes 196616 | tf_op jit(solution)/shard_map/ppermute | solution.py:552
  70.3 15.3 %all-to-all-start.2 = ((bf16[8,272,128]{2,1,0:T(8,128)(2,1)}), bf16[8,272,128]{2,1,0:T(8,128)(2,1)S(1)}, u32[]{:S(2)}, u32[]{:S(2)}) async-start(bf16[8,272,128]{2,1,0:T(8,128)(2,1)} %get-tuple-element.69), calls=%async_computation.2 | async-start | bytes 1114112 | tf_op jit(solution)/shard_map/all_to_all | solution.py:462
  85.7 18.5 %all-to-all-start.3 = ((bf16[8,544,128]{2,1,0:T(8,128)(2,1)}), bf16[8,544,128]{2,1,0:T(8,128)(2,1)S(1)}, u32[]{:S(2)}, u32[]{:S(2)}) async-start(bf16[8,544,128]{2,1,0:T(8,128)(2,1)} %shard_map.142), calls=%async_computation.3 | async-start | bytes 2228224 | tf_op jit(solution)/shard_map/all_to_all | solution.py:462
  93.1 1.0 copy-start.1
  94.1 8.0 %collective-permute-start.2 = (bf16[64,2048]{1,0:T(8,128)(2,1)S(1)}, bf16[64,2048]{1,0:T(8,128)(2,1)S(1)}, u32[]{:S(2)}, u32[]{:S(2)}) collective-permute-start(bf16[64,2048]{1,0:T(8,128)(2,1)S(1)} %fusion.8), channel_id=1, source_target_pairs={{0,1},{1,0},{2,3},{3,2},{4,5},{5,4},{6,7},{7,6},{8,9},{9,8},{10,11... | collective-permute-start | bytes 786440 | tf_op jit(solution)/shard_map/ppermute | solution.py:629
  95.4 6.7 %copy-start.2 = (f32[2,64,2048]{2,1,0:T(8,128)S(1)}, f32[2,64,2048]{2,1,0:T(8,128)}, u32[]{:S(2)}) copy-start(f32[2,64,2048]{2,1,0:T(8,128)} %copy-done.1) | copy-start | bytes 3145732
  104.2 6.5 %collective-permute-start.4 = (bf16[8,24,128]{2,1,0:T(8,128)(2,1)S(1)}, bf16[8,24,128]{2,1,0:T(8,128)(2,1)S(1)}, u32[]{:S(2)}, u32[]{:S(2)}) collective-permute-start(bf16[8,24,128]{2,1,0:T(8,128)(2,1)S(1)} %pad_maximum_fusion.1), channel_id=1, source_target_pairs={{2,0},{4,2},{6,4},{8,6},{10,8},{12,10},{14,12},{16,14},{18,16},{20... | collective-permute-start | bytes 147464 | tf_op jit(solution)/shard_map/ppermute | solution.py:634

commit v6 on v5

--- a/solution.py
+++ b/solution.py
@@ -12,6 +12,8 @@
 RIM = TAPS - 1
 EDGE = 16
 EPS = 1e-06
+BEFORE = 1 << 16
+AFTER = 1 << 17
 F32 = jnp.float32
 BF16 = jnp.bfloat16
 
@@ -47,6 +49,18 @@
     return dot(ah, bh, dims) + dot(ah, bl, dims) + dot(al, bh, dims)
 
 
+def piece(x, row, col=None):
+    cols = slice(None) if col is None else slice(col * HEAD, (col + 1) * HEAD)
+    return tuple(p[row * HEAD : (row + 1) * HEAD, cols] for p in x)
+
+
+def lower_times(x, b):
+    count = x[0].shape[0] // HEAD
+    return jnp.concatenate(
+        [sum(mm(piece(x, i, j), piece(b, j)) for j in range(i + 1)) for i in range(count)], axis=0
+    )
+
+
 def mm_half(left, right, dims=ROWS_COLS):
     (ah, al), (bh, _) = left, right
     ka, kb = dims[0][0][0], dims[0][1][0]
@@ -145,7 +159,8 @@
     return wts[17 * TAPS : 17 * TAPS + 1]
 
 
-def edges(ref, first, rows, per, tail, prev_ref):
+def edges(hid, ref, first, rows, per, tail, prev_ref):
+    tail = jnp.where((hid[0] & BEFORE) > 0, tail, 0.0)
     prev = jnp.where(pl.program_id(0) == 0, tail, prev_ref[0].astype(F32))
     return [prev] + [ref[n, pl.ds(first + rows - EDGE, EDGE), :].astype(F32) for n in range(per - 1)]
 
@@ -157,8 +172,8 @@
     rows = tokens * slots
     step = pl.program_id(0)
     taps = slot_taps(wts_ref[...], 0)
-    tops = edges(kb_ref, 0, rows, per, tail_ref[pl.ds(0, EDGE), :].astype(F32), prev_ref)
-    order = before(rows)
+    tops = edges(hid, kb_ref, 0, rows, per, tail_ref[pl.ds(0, EDGE), :].astype(F32), prev_ref)
+    order = before(HEAD)
     blocks = rows // HEAD
     ir, ic = grid_of(HEAD, HEAD)
 
@@ -178,12 +193,15 @@
         kh_ref[n], kl_ref[n] = k2
         keys.append(k2)
         scaled.append(two(strength * k))
-        grams.append(jnp.where(order, mm(k2, k2, ROWS_ROWS) * strength, 0.0))
+        gram = {}
+        for i in range(blocks):
+            for j in range(i + 1):
+                part = mm(piece(k2, i), piece(k2, j), ROWS_ROWS) * strength[i * HEAD : (i + 1) * HEAD]
+                gram[i, j] = jnp.where(order, part, 0.0) if i == j else part
+        grams.append(gram)
     eye = (ir == ic).astype(F32)
     zero = jnp.zeros((HEAD, HEAD), BF16)
-    diagonal = [
-        gram[b * HEAD : (b + 1) * HEAD, b * HEAD : (b + 1) * HEAD] for gram in grams for b in range(blocks)
-    ]
+    diagonal = [gram[b, b] for gram in grams for b in range(blocks)]
     systems = [two(x) for x in diagonal]
     pairs = level_pairs(HEAD, 0)
     inverse = [eye - jnp.where(pairs, x, 0.0) for x in diagonal]
@@ -195,29 +213,27 @@
         inverse = [x - mm(s, two(y)) for x, s, y in zip(inverse, split, crossed)]
         level += 1
     for n in range(per):
-        done = inverse[n * blocks : (n + 1) * blocks]
-        size = HEAD
-        while len(done) > 1:
-            merged = []
-            for b in range(0, len(done), 2):
-                top, low = done[b], done[b + 1]
-                cross = grams[n][(b + 1) * size : (b + 2) * size, b * size : (b + 1) * size]
-                cross = mm(two(low), two(mm(two(cross), two(top))))
-                merged.append(
-                    jnp.concatenate(
-                        [
-                            jnp.concatenate([top, jnp.zeros_like(top)], axis=1),
-                            jnp.concatenate([-cross, low], axis=1),
-                        ],
-                        axis=0,
-                    )
-                )
-            done = merged
-            size *= 2
-        x2 = two(done[0])
+        done = {(b, b): inverse[n * blocks + b] for b in range(blocks)}
+        halves = {(b, b): two(done[b, b]) for b in range(blocks)}
+        for j in range(blocks):
+            for i in range(j + 1, blocks):
+                cross = sum(mm(two(grams[n][i, m]), halves[m, j]) for m in range(j, i))
+                done[i, j] = -mm(halves[i, i], two(cross))
+                halves[i, j] = two(done[i, j])
+        nothing = jnp.zeros((HEAD, HEAD), BF16)
+        x2 = tuple(
+            jnp.concatenate(
+                [
+                    jnp.concatenate([halves[i, j][p] if j <= i else nothing for j in range(blocks)], axis=1)
+                    for i in range(blocks)
+                ],
+                axis=0,
+            )
+            for p in range(2)
+        )
         xh_ref[n], xl_ref[n] = x2
         th_ref[n], tl_ref[n] = x2[0].T, x2[1].T
-        w2 = two(mm(x2, scaled[n]))
+        w2 = two(lower_times(x2, scaled[n]))
         wh_ref[n], wl_ref[n] = w2
         a_ref[n] = eye - mm(keys[n], w2, COLS_COLS)
     state = carry[...]
@@ -241,14 +257,14 @@
         carry[...] = jnp.zeros((HEAD, HEAD), F32)
 
     tail = tail_ref[pl.ds(EDGE, EDGE), :].astype(F32)
-    tops = edges(vq_ref, 0, rows, per, tail, prev_ref)
+    tops = edges(hid, vq_ref, 0, rows, per, tail, prev_ref)
     maps = []
     for n in range(per):
         s = conv_rows(vq_ref[n, pl.ds(0, rows), :].astype(F32), tops[n], taps, pad.at[n], slots)
         v, fv_ref[n] = silu(s)
         betas = beta_rows(beta_ref[n].astype(F32), slots)
         strength = 2.0 * sigmoid(column(betas, tokens, slots))
-        u = mm((xh_ref[n], xl_ref[n]), two(strength * v))
+        u = lower_times((xh_ref[n], xl_ref[n]), two(strength * v))
         u_ref[n] = u
         maps.append(mm((kh_ref[n], kl_ref[n]), two(u), COLS_COLS))
     state = carry[...]
@@ -267,7 +283,7 @@
     rows = tokens * slots
     taps = query_taps(wts_ref[...])
     tail = tail_ref[pl.ds(2 * EDGE, EDGE), :].astype(F32)
-    tops = edges(vq_ref, rows, tokens, per, tail, prev_ref)
+    tops = edges(hid, vq_ref, rows, tokens, per, tail, prev_ref)
     seen = visible(tokens, slots)
     for n in range(per):
         s = conv_rows(vq_ref[n, pl.ds(rows, tokens), :].astype(F32), tops[n], taps, pad.at[n], 1)
@@ -290,7 +306,7 @@
 ):
     rows = tokens * slots
     gain = gain_row(wts_ref[...])
-    start = two(start_ref[...])
+    start = two(jnp.where((hid[0] & BEFORE) > 0, start_ref[...], 0.0))
     states = [mm(two(m_ref[n]), start) + c_ref[n] for n in range(per)]
     mapped = [two(qm_ref[n]) for n in range(per)]
     raws = [mm(mapped[n], two(states[n])) + ol_ref[n] for n in range(per)]
@@ -343,7 +359,7 @@
     rows = tokens * slots
     wts = wts_ref[...]
     order = before(rows)
-    end = two(end_ref[...])
+    end = two(jnp.where((hid[0] & AFTER) > 0, end_ref[...], 0.0))
     for n in range(per):
         d, k2 = d_ref[n], (kh_ref[n], kl_ref[n])
         d2 = two(d)
@@ -353,8 +369,8 @@
         betas = beta_rows(beta_ref[n].astype(F32), slots)
         de = 2.0 * sigmoid(column(betas, tokens, slots)) * y
         de2 = two(de)
+        dk = dk_ref[n] + mm(d2, g2, ROWS_ROWS) - mm(de2, two(st_ref[n]), ROWS_ROWS)
         dgram = jnp.where(order, mm_half(de2, d2, ROWS_ROWS), 0.0)
-        dk = dk_ref[n] + mm(d2, g2, ROWS_ROWS) - mm(de2, two(st_ref[n]), ROWS_ROWS)
         dk = dk - mm(two(dgram + dgram.T), k2)
         along = jnp.sum(y * d, axis=1, keepdims=True)
         marks = []
@@ -372,23 +388,28 @@
         out_ref[n, pl.ds(2 * rows + EDGE, EDGE), :] = jnp.concatenate([key_rim, value_rim], axis=0).astype(BF16)
 
 
-def unpack_kernel(tokens, slots, got_ref, gk_ref, gv_ref):
+def unpack_kernel(per, tokens, slots, got_ref, gk_ref, gv_ref):
     rows = tokens * slots
-    for a, out_ref in enumerate((gk_ref, gv_ref)):
-        out_ref[...] = got_ref[0, pl.ds(a * rows, rows), :].astype(F32).reshape(tokens, slots, HEAD)
+    for n in range(per):
+        for a, out_ref in enumerate((gk_ref, gv_ref)):
+            main = got_ref[n, pl.ds(a * rows, rows), :].astype(F32)
+            out_ref[:, :, pl.ds(n * HEAD, HEAD)] = main.reshape(tokens, slots, HEAD)
 
 
 def unpack_query_kernel(tokens, got_ref, gq_ref):
     gq_ref[...] = got_ref[0, pl.ds(tokens, tokens), :].astype(F32)
 
 
-def rims_kernel(heads, slots, rim_ref, gq_ref, gk_ref, gv_ref, nq_ref, nk_ref, nv_ref):
+def rims_kernel(heads, slots, rim_ref, gq_ref, gk_ref, gv_ref, mark_ref, nq_ref, nk_ref, nv_ref, gb_ref):
     for h in range(heads):
         part = pl.ds(h * HEAD, HEAD)
         rim = rim_ref[h].astype(F32)
         nq_ref[:, part] = gq_ref[:, part] + rim[:8]
         nk_ref[:, :, part] = gk_ref[:, :, part] + rim[8:16].reshape(8 // slots, slots, HEAD)
         nv_ref[:, :, part] = gv_ref[:, :, part] + rim[16:].reshape(8 // slots, slots, HEAD)
+        mark = mark_ref[h].astype(F32)
+        for j in range(slots):
+            gb_ref[j, pl.ds(h, 1), :] = mark[2 * j : 2 * j + 1] + mark[2 * j + 1 : 2 * j + 2]
 
 
 FAR = ("kh", "kl", "xh", "xl", "th", "tl", "wh", "wl", "a", "m", "fk", "fv", "stf", "mbf", "d", "dk", "dd")
@@ -397,7 +418,7 @@
 def call(kernel, hid, steps, live, ins, reads, outs, scratch=(), us=1.0, grant=24):
     def spec(shape, how):
         if how == "weights":
-            return pl.BlockSpec((shape[0], HEAD), lambda i, h: (0, h[0]))
+            return pl.BlockSpec((shape[0], HEAD), lambda i, h: (0, h[0] & (BEFORE - 1)))
         if how is None:
             return pl.BlockSpec(shape, lambda i, h: (0,) * len(shape))
         if isinstance(how, tuple):
@@ -456,7 +477,8 @@
     group_lists = [[b * heads + i for i in range(heads)] for b in range(groups)]
     rows = tokens * slots
     g = heads
-    hid = (place % heads).astype(jnp.int32).reshape(1)
+    first, final = place < heads, place >= shard_count - heads
+    hid = (place % heads + jnp.where(first, 0, BEFORE) + jnp.where(final, 0, AFTER)).astype(jnp.int32).reshape(1)
 
     def exchange(x):
         return lax.all_to_all(x, "ctx", 0, 0, axis_index_groups=group_lists, tiled=True)
@@ -482,10 +504,11 @@
 
     group = place // heads
     tail = jnp.concatenate([kb[g - 1, rows - EDGE : rows], kb[g - 1, rows + EDGE :]], axis=0)
-    tail = lax.ppermute(tail, "ctx", [(i, i + heads) for i in range(shard_count - heads)])
 
     grad_normed = jnp.dot(grad_out, out_weight.T, preferred_element_type=F32).astype(BF16)
     vq = jnp.concatenate([slots_by_head(value_in), by_head(query_in), by_head(grad_normed)], axis=1)
+    vq, tail = lax.optimization_barrier((vq, tail))
+    tail = lax.ppermute(tail, "ctx", [(i, (i + heads) % shard_count) for i in range(shard_count)])
     vq, tail = lax.optimization_barrier((vq, tail))
     vq = exchange(vq)
 
@@ -548,7 +571,7 @@
         if groups == 1:
             return jnp.zeros((HEAD, HEAD), F32)
         if groups == 2:
-            moves = [(i, i + towards * heads) for i in range(shard_count) if 0 <= i + towards * heads < shard_count]
+            moves = [(i, (i + towards * heads) % shard_count) for i in range(shard_count)]
             return lax.ppermute(last[1], "ctx", moves)
         every = lax.all_gather(jnp.concatenate(last, axis=1), "ctx")
         head = place % heads
@@ -645,27 +668,29 @@
         cost_estimate=cost(2.0),
     )(nq)
     grad_key, grad_value = pl.pallas_call(
-        functools.partial(unpack_kernel, tokens, slots),
-        grid=(heads,),
-        in_specs=[part(grads)],
-        out_specs=[pl.BlockSpec((tokens, slots, HEAD), lambda h: (0, 0, h))] * 2,
+        functools.partial(unpack_kernel, per, tokens, slots),
+        grid=(steps,),
+        in_specs=[pl.BlockSpec((per,) + grads.shape[1:], lambda h: (h, 0, 0))],
+        out_specs=[pl.BlockSpec((tokens, slots, per * HEAD), lambda h: (0, 0, h))] * 2,
         out_shape=[jax.ShapeDtypeStruct((tokens, slots, width), F32)] * 2,
         compiler_params=small,
         cost_estimate=cost(10.0),
     )(grads)
     flat = pl.BlockSpec((8, width), lambda i: (tokens // 8 - 1, 0))
     deep = pl.BlockSpec((8 // slots, slots, width), lambda i: (tokens * slots // 8 - 1, 0, 0))
-    grad_query, grad_key, grad_value = pl.pallas_call(
+    mark = pl.BlockSpec((heads, EDGE, tokens), lambda i: (0, 2 * rows // EDGE, 0))
+    beta_spec = pl.BlockSpec((slots, heads, tokens), lambda i: (0, 0, 0))
+    grad_query, grad_key, grad_value, grad_beta = pl.pallas_call(
         functools.partial(rims_kernel, heads, slots),
         grid=(1,),
-        in_specs=[pl.BlockSpec(rim.shape, lambda i: (0, 0, 0)), flat, deep, deep],
-        out_specs=[flat, deep, deep],
-        out_shape=[jax.ShapeDtypeStruct(x.shape, F32) for x in (grad_query, grad_key, grad_value)],
+        in_specs=[pl.BlockSpec(rim.shape, lambda i: (0, 0, 0)), flat, deep, deep, mark],
+        out_specs=[flat, deep, deep, beta_spec],
+        out_shape=[jax.ShapeDtypeStruct(x.shape, F32) for x in (grad_query, grad_key, grad_value)]
+        + [jax.ShapeDtypeStruct((slots, heads, tokens), F32)],
         input_output_aliases={1: 0, 2: 1, 3: 2},
         compiler_params=small,
-    )(rim, grad_query, grad_key, grad_value)
-    marks = grads[:, 2 * rows : 2 * rows + 2 * slots].astype(F32)
-    grad_beta = marks.reshape(heads, slots, 2, tokens).sum(axis=2).transpose(2, 1, 0)
+    )(rim, grad_query, grad_key, grad_value, grads)
+    grad_beta = grad_beta.transpose(2, 0, 1)
     return (layer_out, grad_query, grad_key, grad_value, grad_beta)
 
 

time: 113 us -> 109 us (0.965)
  starting transfers between devices: 33.5 us -> 29.9 us
    ppermute x2, starting transfers between devices: 6.29 us -> 2.43 us  [across(): return lax.ppermute(last[1], 'ctx', moves)]
    all_to_all x4, starting transfers between devices: 19 us -> 21 us  [exchange(): lax.all_to_all(x, 'ctx', 0, 0, axis_index_groups=group_lists, tiled=True)]
    ppermute x1, starting transfers between devices: 4.2 us -> 2.37 us  [shards(): lax.ppermute(tail, 'ctx', [(i, (i + heads) % shard_count) for i in range(...]
    ppermute x1, waiting for transfers between devices: 0.01 us -> 1.14 us  [shards(): lax.ppermute(tail, 'ctx', [(i, (i + heads) % shard_count) for i in range(...]
    unnamed x22 -> x21, local copies, waits for them, and re-layouts: 2.52 us -> 1.92 us
  transfers between devices with their start and end apart: 9 -> 9, of which waited for: 3 -> 5; matrix products, arithmetic and copies ran while one was open for 10% -> 9% of each run, Pallas kernels for 38% -> 38%
where the time goes in v6:
time: 109 us; the launch traced here: 108 us
  Pallas kernels  51.3 us (47%)
  starting transfers between devices  29.9 us (27%)
  waiting for transfers between devices  10.1 us (9%)
  matrix products  6.6 us (6%)
  local copies, waits for them, and re-layouts  5.4 us (5%)
  other arithmetic  3.46 us (3%)
    pallas_call x6, Pallas kernels, call(): pl.pallas_call(kernel, grid_spec=pltpu.PrefetchScalarGridSpec(num_scalar_...  45.3 us
    all_to_all x4, starting transfers between devices, exchange(): lax.all_to_all(x, 'ctx', 0, 0, axis_index_groups=group_lists, tiled=True)  21 us
    ppermute x1, waiting for transfers between devices, shards(): lax.ppermute(sent, 'head', [(0, 1), (1, 0)]).astype(F32)  4.17 us
    all_to_all x4, waiting for transfers between devices, exchange(): lax.all_to_all(x, 'ctx', 0, 0, axis_index_groups=group_lists, tiled=True)  3.97 us
    dot_general x1, matrix products, shards(): jnp.dot(grad_out, out_weight.T, preferred_element_type=F32).astype(BF16)  3.7 us
    dot_general x1, matrix products, shards(): partial = jnp.dot(normed_bf, out_weight, preferred_element_type=F32)  2.9 us
    ppermute x1, starting transfers between devices, shards(): rim = lax.ppermute(rim, 'ctx', [(i, i - 1) for i in range(1, shard_count)])  2.78 us
    pallas_call x1, Pallas kernels, shards(): pl.pallas_call(functools.partial(unpack_query_kernel, tokens), grid=(head...  2.56 us
  transfers between devices with their start and end apart: 9, of which 5 were waited for; matrix products, arithmetic and copies ran while one was open for 9% of the time, Pallas kernels for 38%

profile of v6, /device:TPU:1, one launch (start us, length us, event | category | flops | bytes accessed | tf_op | source)
XLA Modules:
  0.0 107.6 jit_solution(3611890136819714917)
XLA Ops:
  0.6 0.0 copy-start
  0.6 0.8 fusion.11
  1.4 0.3 copy-done
  1.7 0.4 copy_bitcast_fusion
  2.1 0.8 copy_bitcast_fusion.2
  2.8 0.8 bitcast_bitcast_fusion
  3.6 0.9 fusion.6
  4.5 5.3 %all-to-all-start = ((bf16[8,304,128]{2,1,0:T(8,128)(2,1)}), bf16[8,304,128]{2,1,0:T(8,128)(2,1)S(1)}, u32[]{:S(2)}, u32[]{:S(2)}) async-start(bf16[8,304,128]{2,1,0:T(8,128)(2,1)} %fusion.6), calls=%async_computation | async-start | bytes 1245184 | tf_op jit(solution)/shard_map/all_to_all | solution.py:484
  9.8 0.2 copy.23
  10.0 3.7 %convolution_convert_fusion = bf16[128,1024]{1,0:T(8,128)(2,1)S(1)} fusion(bf16[128,2048]{1,0:T(8,128)(2,1)S(1)} %copy-done.4, bf16[1024,2048]{1,0:T(8,128)(2,1)} %param.18), kind=kOutput, calls=%fused_computation.6 | convolution fusion | flops 537001984 | bytes 4980736 | tf_op jit(solution)/shard_map/dot_general | solution.py:508
  13.7 0.0 copy-start.3
  13.7 0.2 copy.25
  13.9 0.2 copy.26
  14.1 0.2 copy.24
  14.3 0.5 copy-done.3
  14.7 0.4 copy_bitcast_fusion.1
  15.1 1.0 pad_maximum_fusion
  16.2 2.7 %all-to-all-done.kb_ref.prev_ref.beta_ref = bf16[8,304,128]{2,1,0:T(8,128)(2,1)S(1)} async-done(((bf16[8,304,128]{2,1,0:T(8,128)(2,1)}), bf16[8,304,128]{2,1,0:T(8,128)(2,1)S(1)}, u32[]{:S(2)}, u32[]{:S(2)}) %all-to-all-start) | async-done | bytes 622624 | tf_op jit(solution)/shard_map/all_to_all | solution.py:484
  18.9 0.0 copy-start.8
  18.9 0.0 copy-start.9
  18.9 2.4 %collective-permute-start = (bf16[48,128]{1,0:T(8,128)(2,1)S(1)}, bf16[48,128]{1,0:T(8,128)(2,1)S(1)}, u32[]{:S(2)}, u32[]{:S(2)}) collective-permute-start(bf16[48,128]{1,0:T(8,128)(2,1)S(1)} %pad_maximum_fusion.3), channel_id=1, source_target_pairs={{0,16},{2,18},{4,20},{6,22},{8,24},{10,26},{12,28},{14,30},{16,0},... | collective-permute-start | bytes 36872 | tf_op jit(solution)/shard_map/ppermute | solution.py:511
  21.2 1.1 %collective-permute-done.tail_ref = bf16[48,128]{1,0:T(8,128)(2,1)S(1)} collective-permute-done((bf16[48,128]{1,0:T(8,128)(2,1)S(1)}, bf16[48,128]{1,0:T(8,128)(2,1)S(1)}, u32[]{:S(2)}, u32[]{:S(2)}) %collective-permute-start) | collective-permute-done | bytes 12320 | tf_op jit(solution)/shard_map/ppermute | solution.py:511
  22.4 5.5 %all-to-all-start.1 = ((bf16[8,512,128]{2,1,0:T(8,128)(2,1)}), bf16[8,512,128]{2,1,0:T(8,128)(2,1)S(1)}, u32[]{:S(2)}, u32[]{:S(2)}) async-start(bf16[8,512,128]{2,1,0:T(8,128)(2,1)} %pad_maximum_fusion), calls=%async_computation.1 | async-start | bytes 2097152 | tf_op jit(solution)/shard_map/all_to_all | solution.py:484
  27.9 0.1 tile.17
  28.1 0.1 tile.19
  28.3 13.7 %shard_map.137 = (bf16[8,256,128]{2,1,0:T(8,128)(2,1)}, bf16[8,256,128]{2,1,0:T(8,128)(2,1)}, bf16[8,256,256]{2,1,0:T(8,128)(2,1)}, bf16[8,256,256]{2,1,0:T(8,12...) custom-call(s32[1]{0:T(128)} %bitcast.hid, ...), custom_call_target="tpu_custom_call" | custom-call | flops 12099999744 | bytes 65536 | tf_op jit(solution)/shard_map/pallas_call | solution.py:437
  42.0 6.0 %shard_map.138 = (f32[8,256,128]{2,1,0:T(8,128)S(1)}, f32[8,128,128]{2,1,0:T(8,128)S(1)}, f32[8,128,128]{2,1,0:T(8,128)S(1)}, f32[8,128,128]{2,1,0:T(8,128)S(1)}...) custom-call(s32[1]{0:T(128)} %bitcast.hid, bf16[8,512,128]{2,1,0:T(8,128)(2,1)S(1)} %all-to-all-done.1.vq_ref.prev_ref, ...), custom_call_target="tpu_custom_call" | custom-call | flops 6600000000 | bytes 65536 | tf_op jit(solution)/shard_map/pallas_call | solution.py:437
  47.9 2.3 %collective-permute-start.1 = (f32[128,128]{1,0:T(8,128)S(1)}, f32[128,128]{1,0:T(8,128)S(1)}, u32[]{:S(2)}, u32[]{:S(2)}) collective-permute-start(f32[128,128]{1,0:T(8,128)S(1)} %get-tuple-element.58), channel_id=1, source_target_pairs={{0,16},{2,18},{4,20},{6,22},{8,24},{10,26},{12,28},{14,30},{16,0},... | collective-permute-start | bytes 196616 | tf_op jit(solution)/shard_map/ppermute | solution.py:575
  50.2 4.9 %shard_map.139 = (f32[8,128,128]{2,1,0:T(8,128)S(1)}, f32[8,128,256]{2,1,0:T(8,128)S(1)}, f32[8,128,128]{2,1,0:T(8,128)S(1)}, f32[8,128,128]{2,1,0:T(8,128)S(1)}, f32[8,128,128]{2,1,0:T(8,128)S(1)}) custom-call(s32[1]{0:T(128)} %bitcast.hid, bf16[8,512,128]{2,1,0:T(8,128)(2,1)S(1)} %all-to-all-done.1.vq_ref.prev_ref, ...), custom_call_target="tpu_custom_call" | custom-call | flops 8800000000 | bytes 65536 | tf_op jit(solution)/shard_map/pallas_call | solution.py:437
  55.1 2.5 %shard_map.140 = (f32[8,128,128]{2,1,0:T(8,128)S(1)}, f32[8,128,128]{2,1,0:T(8,128)S(1)}, f32[8,128,256]{2,1,0:T(8,128)S(1)}, bf16[8,128,128]{2,1,0:T(8,128)(2,1)S(1)}, f32[128,256]{1,0:T(8,128)S(1)}) custom-call(s32[1]{0:T(128)} %bitcast.hid, bf16[8,512,128]{2,1,0:T(8,128)(2,1)S(1)} %all-to-all-done.1.vq_ref.prev_ref, f32[72,1024]{1,0:T(8,128)S(1)} %concatenate.15.wts_ref, ...), custom_call_target="tpu_custom_call" | custom-call | flops 4400000000 | bytes 65536 | tf_op jit(solution)/shard_map/pallas_call | solution.py:437
  57.6 0.1 collective-permute-start.3
  57.8 7.4 %shard_map.141 = (f32[8,256,128]{2,1,0:T(8,128)}, f32[8,256,128]{2,1,0:T(8,128)}, f32[8,256,128]{2,1,0:T(8,128)}, f32[8,128,128]{2,1,0:T(8,128)}, f32[8,128,256]{2,1,0:T(8,128)}, /*index=5*/bf16[8,272,128]{2,1,0:T(8,128)(2,1)}) custom-call(s32[1]{0:T(128)} %bitcast.hid, f32[72,1024]{1,0:T(8,128)S(1)} %concatenate.15.wts_ref, ...), custom_call_target="tpu_custom_call" | custom-call | flops 22000001024 | bytes 65536 | tf_op jit(solution)/shard_map/pallas_call | solution.py:437
  65.2 6.0 %all-to-all-start.2 = ((bf16[8,272,128]{2,1,0:T(8,128)(2,1)}), bf16[8,272,128]{2,1,0:T(8,128)(2,1)S(1)}, u32[]{:S(2)}, u32[]{:S(2)}) async-start(bf16[8,272,128]{2,1,0:T(8,128)(2,1)} %get-tuple-element.74), calls=%async_computation.2 | async-start | bytes 1114112 | tf_op jit(solution)/shard_map/all_to_all | solution.py:484
  71.2 10.8 %shard_map.142 = bf16[8,544,128]{2,1,0:T(8,128)(2,1)} custom-call(s32[1]{0:T(128)} %bitcast.hid, bf16[8,304,128]{2,1,0:T(8,128)(2,1)S(1)} %all-to-all-done.kb_ref.prev_ref.beta_ref, f32[72,1024]{1,0:T(8,128)S(1)} %concatenate.15.wts_ref, f32[128,128]{1,0:T(8,128)S(1)} %collective-permute-done.3.end_ref, f32[8,128,256]{2,1,0:T(8,128)} %get-tuple-element.76.mb_ref, ...), custom_call_target="tpu_custom_call" | custom-call | flops 22000001024 | bytes 65536 | tf_op jit(solution)/shard_map/pallas_call | solution.py:437
  82.0 4.2 %all-to-all-start.3 = ((bf16[8,544,128]{2,1,0:T(8,128)(2,1)}), bf16[8,544,128]{2,1,0:T(8,128)(2,1)S(1)}, u32[]{:S(2)}, u32[]{:S(2)}) async-start(bf16[8,544,128]{2,1,0:T(8,128)(2,1)} %shard_map.142), calls=%async_computation.3 | async-start | bytes 2228224 | tf_op jit(solution)/shard_map/all_to_all | solution.py:484
  86.3 0.2 copy.33
  86.4 0.1 dot_general.9
  86.6 2.9 %fusion = f32[2,64,2048]{2,1,0:T(8,128)S(1)} fusion(bf16[2,64,1024]{2,1,0:T(8,128)(2,1)S(1)} %dot_general.9, bf16[1024,2048]{1,0:T(8,128)(2,1)} %param.18), kind=kOutput, calls=%fused_computation | convolution fusion | flops 536870912 | bytes 5505024 | tf_op jit(solution)/shard_map/dot_general | solution.py:645
  89.5 1.0 copy-done.1
  90.5 1.3 %collective-permute-start.2 = (bf16[64,2048]{1,0:T(8,128)(2,1)S(1)}, bf16[64,2048]{1,0:T(8,128)(2,1)S(1)}, u32[]{:S(2)}, u32[]{:S(2)}) collective-permute-start(bf16[64,2048]{1,0:T(8,128)(2,1)S(1)} %fusion.8), channel_id=1, source_target_pairs={{0,1},{1,0},{2,3},{3,2},{4,5},{5,4},{6,7},{7,6},{8,9},{9,8},{10,11... | collective-permute-start | bytes 786440 | tf_op jit(solution)/shard_map/ppermute | solution.py:652
  91.8 2.6 %shard_map.143.gq_ref = f32[128,1024]{1,0:T(8,128)} custom-call(bf16[8,272,128]{2,1,0:T(8,128)(2,1)S(1)} %all-to-all-done.2.got_ref), custom_call_target="tpu_custom_call" | custom-call | flops 2200000000 | bytes 65536 | tf_op jit(solution)/shard_map/pallas_call | solution.py:661
  94.3 4.2 %collective-permute-done.2 = bf16[64,2048]{1,0:T(8,128)(2,1)S(1)} collective-permute-done((bf16[64,2048]{1,0:T(8,128)(2,1)S(1)}, bf16[64,2048]{1,0:T(8,128)(2,1)S(1)}, u32[]{:S(2)}, u32[]{:S(2)}) %collective-permute-start.2) | collective-permute-done | bytes 262176 | tf_op jit(solution)/shard_map/ppermute | solution.py:652
  98.5 0.8 fusion.7
  99.2 1.3 %all-to-all-done.3.got_ref.mark_ref = bf16[8,544,128]{2,1,0:T(8,128)(2,1)S(1)} async-done(((bf16[8,544,128]{2,1,0:T(8,128)(2,1)}), bf16[8,544,128]{2,1,0:T(8,128)(2,1)S(1)}, u32[]{:S(2)}, u32[]{:S(2)}) %all-to-all-start.3) | async-done | bytes 1114144 | tf_op jit(solution)/shard_map/all_to_all | solution.py:484
  100.5 2.8 %collective-permute-start.4 = (bf16[8,24,128]{2,1,0:T(8,128)(2,1)S(1)}, bf16[8,24,128]{2,1,0:T(8,128)(2,1)S(1)}, u32[]{:S(2)}, u32[]{:S(2)}) collective-permute-start(bf16[8,24,128]{2,1,0:T(8,128)(2,1)S(1)} %pad_maximum_fusion.1), channel_id=1, source_target_pairs={{2,0},{4,2},{6,4},{8,6},{10,8},{12,10},{14,12},{16,14},{18,16},{20... | collective-permute-start | bytes 147464 | tf_op jit(solution)/shard_map/ppermute | solution.py:657
  103.3 2.0 %shard_map.144 = (f32[128,2,1024]{2,1,0:T(2,128)}, f32[128,2,1024]{2,1,0:T(2,128)}) custom-call(bf16[8,544,128]{2,1,0:T(8,128)(2,1)S(1)} %all-to-all-done.3.got_ref.mark_ref), custom_call_target="tpu_custom_call" | custom-call | flops 11000000512 | bytes 65536 | tf_op jit(solution)/shard_map/pallas_call | solution.py:670
  105.3 0.8 collective-permute-done.4.rim_ref
  106.2 1.5 %shard_map.145 = (f32[128,1024]{1,0:T(8,128)}, f32[128,2,1024]{2,1,0:T(2,128)}, f32[128,2,1024]{2,1,0:T(2,128)}, f32[2,8,128]{2,1,0:T(8,128)}) custom-call(bf16[8,24,128]{2,1,0:T(8,128)(2,1)S(1)} %collective-permute-done.4.rim_ref, f32[128,1024]{1,0:T(8,128)} %shard_map.143.gq_ref, ...), custom_call_target="tpu_custom_call", output_to_operand_aliasing={{0}: (1, {}), {1}: (2, {}), {2}: (3, {})} | custom-call | tf_op jit(solution)/shard_map/pallas_call | solution.py:683
  (32 shorter events, 0.3 us)
Async XLA Ops:
  0.6 1.1 copy-start
  3.6 6.2 %copy-start.5 = (bf16[128,1024]{1,0:T(8,128)(2,1)S(1)}, bf16[128,1024]{1,0:T(8,128)(2,1)}, u32[]{:S(2)}) copy-start(bf16[128,1024]{1,0:T(8,128)(2,1)} %param.10) | copy-start | bytes 786436
  3.6 6.4 %copy-start.4 = (bf16[128,2048]{1,0:T(8,128)(2,1)S(1)}, bf16[128,2048]{1,0:T(8,128)(2,1)}, u32[]{:S(2)}) copy-start(bf16[128,2048]{1,0:T(8,128)(2,1)} %param.19) | copy-start | bytes 1572868
  4.5 14.3 %all-to-all-start = ((bf16[8,304,128]{2,1,0:T(8,128)(2,1)}), bf16[8,304,128]{2,1,0:T(8,128)(2,1)S(1)}, u32[]{:S(2)}, u32[]{:S(2)}) async-start(bf16[8,304,128]{2,1,0:T(8,128)(2,1)} %fusion.6), calls=%async_computation | async-start | bytes 1245184 | tf_op jit(solution)/shard_map/all_to_all | solution.py:484
  13.7 1.0 copy-start.3
  16.2 11.7 %copy-start.6 = (f32[4,2,1024]{2,1,0:T(2,128)S(1)}, f32[4,2,1024]{2,1,0:T(2,128)}, u32[]{:S(2)}) copy-start(f32[4,2,1024]{2,1,0:T(2,128)} %param.15) | copy-start | bytes 98308
  18.8 9.2 %copy-start.7 = (f32[4,2,1024]{2,1,0:T(2,128)S(1)}, f32[4,2,1024]{2,1,0:T(2,128)}, u32[]{:S(2)}) copy-start(f32[4,2,1024]{2,1,0:T(2,128)} %param.16) | copy-start | bytes 98308
  18.9 9.3 %copy-start.8 = (f32[4,1024]{1,0:T(4,128)S(1)}, f32[4,1024]{1,0:T(4,128)}, u32[]{:S(2)}) copy-start(f32[4,1024]{1,0:T(4,128)} %param.14) | copy-start | bytes 49156
  18.9 9.3 %copy-start.9 = (f32[1024]{0:T(1024)S(1)}, f32[1024]{0:T(1024)}, u32[]{:S(2)}) copy-start(f32[1024]{0:T(1024)} %param.17) | copy-start | bytes 12292
  18.9 3.5 %collective-permute-start = (bf16[48,128]{1,0:T(8,128)(2,1)S(1)}, bf16[48,128]{1,0:T(8,128)(2,1)S(1)}, u32[]{:S(2)}, u32[]{:S(2)}) collective-permute-start(bf16[48,128]{1,0:T(8,128)(2,1)S(1)} %pad_maximum_fusion.3), channel_id=1, source_target_pairs={{0,16},{2,18},{4,20},{6,22},{8,24},{10,26},{12,28},{14,30},{16,0},... | collective-permute-start | bytes 36872 | tf_op jit(solution)/shard_map/ppermute | solution.py:511
  22.4 19.6 %all-to-all-start.1 = ((bf16[8,512,128]{2,1,0:T(8,128)(2,1)}), bf16[8,512,128]{2,1,0:T(8,128)(2,1)S(1)}, u32[]{:S(2)}, u32[]{:S(2)}) async-start(bf16[8,512,128]{2,1,0:T(8,128)(2,1)} %pad_maximum_fusion), calls=%async_computation.1 | async-start | bytes 2097152 | tf_op jit(solution)/shard_map/all_to_all | solution.py:484
  47.9 7.2 %collective-permute-start.1 = (f32[128,128]{1,0:T(8,128)S(1)}, f32[128,128]{1,0:T(8,128)S(1)}, u32[]{:S(2)}, u32[]{:S(2)}) collective-permute-start(f32[128,128]{1,0:T(8,128)S(1)} %get-tuple-element.58), channel_id=1, source_target_pairs={{0,16},{2,18},{4,20},{6,22},{8,24},{10,26},{12,28},{14,30},{16,0},... | collective-permute-start | bytes 196616 | tf_op jit(solution)/shard_map/ppermute | solution.py:575
  57.6 13.5 %collective-permute-start.3 = (f32[128,128]{1,0:T(8,128)S(1)}, f32[128,128]{1,0:T(8,128)S(1)}, u32[]{:S(2)}, u32[]{:S(2)}) collective-permute-start(f32[128,128]{1,0:T(8,128)S(1)} %slice.30), channel_id=1, source_target_pairs={{0,16},{2,18},{4,20},{6,22},{8,24},{10,26},{12,28},{14,30},{16,0},... | collective-permute-start | bytes 196616 | tf_op jit(solution)/shard_map/ppermute | solution.py:575
  65.2 16.8 %all-to-all-start.2 = ((bf16[8,272,128]{2,1,0:T(8,128)(2,1)}), bf16[8,272,128]{2,1,0:T(8,128)(2,1)S(1)}, u32[]{:S(2)}, u32[]{:S(2)}) async-start(bf16[8,272,128]{2,1,0:T(8,128)(2,1)} %get-tuple-element.74), calls=%async_computation.2 | async-start | bytes 1114112 | tf_op jit(solution)/shard_map/all_to_all | solution.py:484
  82.0 18.5 %all-to-all-start.3 = ((bf16[8,544,128]{2,1,0:T(8,128)(2,1)}), bf16[8,544,128]{2,1,0:T(8,128)(2,1)S(1)}, u32[]{:S(2)}, u32[]{:S(2)}) async-start(bf16[8,544,128]{2,1,0:T(8,128)(2,1)} %shard_map.142), calls=%async_computation.3 | async-start | bytes 2228224 | tf_op jit(solution)/shard_map/all_to_all | solution.py:484
  89.5 1.0 copy-start.1
  90.5 8.0 %collective-permute-start.2 = (bf16[64,2048]{1,0:T(8,128)(2,1)S(1)}, bf16[64,2048]{1,0:T(8,128)(2,1)S(1)}, u32[]{:S(2)}, u32[]{:S(2)}) collective-permute-start(bf16[64,2048]{1,0:T(8,128)(2,1)S(1)} %fusion.8), channel_id=1, source_target_pairs={{0,1},{1,0},{2,3},{3,2},{4,5},{5,4},{6,7},{7,6},{8,9},{9,8},{10,11... | collective-permute-start | bytes 786440 | tf_op jit(solution)/shard_map/ppermute | solution.py:652
  91.8 6.7 %copy-start.2 = (f32[2,64,2048]{2,1,0:T(8,128)S(1)}, f32[2,64,2048]{2,1,0:T(8,128)}, u32[]{:S(2)}) copy-start(f32[2,64,2048]{2,1,0:T(8,128)} %copy-done.1) | copy-start | bytes 3145732
  100.5 5.6 %collective-permute-start.4 = (bf16[8,24,128]{2,1,0:T(8,128)(2,1)S(1)}, bf16[8,24,128]{2,1,0:T(8,128)(2,1)S(1)}, u32[]{:S(2)}, u32[]{:S(2)}) collective-permute-start(bf16[8,24,128]{2,1,0:T(8,128)(2,1)S(1)} %pad_maximum_fusion.1), channel_id=1, source_target_pairs={{2,0},{4,2},{6,4},{8,6},{10,8},{12,10},{14,12},{16,14},{18,16},{20... | collective-permute-start | bytes 147464 | tf_op jit(solution)/shard_map/ppermute | solution.py:657

commit v7 on v6

--- a/solution.py
+++ b/solution.py
@@ -249,6 +249,7 @@
     m_ref,
     u_ref, c_ref, an_ref, mn_ref, fv_ref, end_ref, pad, carry,
 ):
+
     rows = tokens * slots
     taps = slot_taps(wts_ref[...], 1)
 
@@ -258,17 +259,17 @@
 
     tail = tail_ref[pl.ds(EDGE, EDGE), :].astype(F32)
     tops = edges(hid, vq_ref, 0, rows, per, tail, prev_ref)
-    maps = []
+    rights = []
     for n in range(per):
         s = conv_rows(vq_ref[n, pl.ds(0, rows), :].astype(F32), tops[n], taps, pad.at[n], slots)
         v, fv_ref[n] = silu(s)
         betas = beta_rows(beta_ref[n].astype(F32), slots)
-        strength = 2.0 * sigmoid(column(betas, tokens, slots))
-        u = lower_times((xh_ref[n], xl_ref[n]), two(strength * v))
-        u_ref[n] = u
-        maps.append(mm((kh_ref[n], kl_ref[n]), two(u), COLS_COLS))
+        rights.append(two(2.0 * sigmoid(column(betas, tokens, slots)) * v))
+    us = [lower_times((xh_ref[n], xl_ref[n]), rights[n]) for n in range(per)]
+    maps = [mm((kh_ref[n], kl_ref[n]), two(us[n]), COLS_COLS) for n in range(per)]
     state = carry[...]
     for n in range(per):
+        u_ref[n] = us[n]
         c_ref[n] = state
         an_ref[n], mn_ref[n] = a_ref[n], m_ref[n]
         state = mm(two(a_ref[n]), two(state)) + maps[n]
@@ -285,19 +286,26 @@
     tail = tail_ref[pl.ds(2 * EDGE, EDGE), :].astype(F32)
     tops = edges(hid, vq_ref, rows, tokens, per, tail, prev_ref)
     seen = visible(tokens, slots)
+    qs = []
     for n in range(per):
         s = conv_rows(vq_ref[n, pl.ds(rows, tokens), :].astype(F32), tops[n], taps, pad.at[n], 1)
         c, slope = silu(s)
         q, scale = unit(c)
         fq_ref[n] = scale * slope
-        scores = jnp.where(seen, mm(two(q), (kh_ref[n], kl_ref[n]), ROWS_ROWS), 0.0)
+        q_ref[n] = q
+        qs.append(q)
+    scores = [
+        jnp.where(seen, mm(two(qs[n]), (kh_ref[n], kl_ref[n]), ROWS_ROWS), 0.0) for n in range(per)
+    ]
+    mapped = []
+    for n in range(per):
         uh, ul = two(u_ref[n])
         both = jnp.concatenate([wh_ref[n], uh], axis=1), jnp.concatenate([wl_ref[n], ul], axis=1)
-        mapped = mm(two(scores), both)
-        q_ref[n] = q
-        sc_ref[n] = scores
-        qm_ref[n] = q - mapped[:, :HEAD]
-        ol_ref[n] = mapped[:, HEAD:]
+        mapped.append(mm(two(scores[n]), both))
+    for n in range(per):
+        sc_ref[n] = scores[n]
+        qm_ref[n] = qs[n] - mapped[n][:, :HEAD]
+        ol_ref[n] = mapped[n][:, HEAD:]
 
 
 def outs_kernel(
@@ -336,17 +344,24 @@
 ):
     taps = query_taps(wts_ref[...])
     seen = visible(tokens, slots)
-    for n in range(per):
-        q, k2 = q_ref[n], (kh_ref[n], kl_ref[n])
+    chunks = range(per)
+    for n in chunks:
         stf_ref[n], mbf_ref[n] = st_ref[n], mb_ref[n]
-        state, dr = two(st_ref[n]), two(dr_ref[n])
-        d = u_ref[n] - mm((wh_ref[n], wl_ref[n]), state)
-        d_ref[n] = d
-        ds = two(jnp.where(seen, mm(dr, two(d), ROWS_ROWS), 0.0))
-        dq = mm(dr, state, ROWS_ROWS) + mm(ds, k2)
-        dk_ref[n] = mm(ds, two(q), COLS_COLS)
-        dd_ref[n] = mm(two(sc_ref[n]), dr, COLS_COLS)
-        inner, rim = conv_back(fq_ref[n] * (dq - q * jnp.sum(q * dq, axis=-1, keepdims=True)), taps, pad.at[n], 1)
+    states = [two(st_ref[n]) for n in chunks]
+    drs = [two(dr_ref[n]) for n in chunks]
+    keys = [(kh_ref[n], kl_ref[n]) for n in chunks]
+    qs = [q_ref[n] for n in chunks]
+    found = [u_ref[n] - mm((wh_ref[n], wl_ref[n]), states[n]) for n in chunks]
+    dss = [two(jnp.where(seen, mm(drs[n], two(found[n]), ROWS_ROWS), 0.0)) for n in chunks]
+    for n in chunks:
+        d_ref[n] = found[n]
+        dd_ref[n] = mm(two(sc_ref[n]), drs[n], COLS_COLS)
+    dqs = [mm(drs[n], states[n], ROWS_ROWS) + mm(dss[n], keys[n]) for n in chunks]
+    for n in chunks:
+        dk_ref[n] = mm(dss[n], two(qs[n]), COLS_COLS)
+    for n in chunks:
+        part = fq_ref[n] * (dqs[n] - qs[n] * jnp.sum(qs[n] * dqs[n], axis=-1, keepdims=True))
+        inner, rim = conv_back(part, taps, pad.at[n], 1)
         nq_ref[n, pl.ds(0, tokens), :] = nm_ref[n]
         nq_ref[n, pl.ds(tokens, tokens), :] = inner.astype(BF16)
         nq_ref[n, pl.ds(2 * tokens, EDGE), :] = jnp.concatenate([rim, jnp.zeros((8, HEAD), F32)], axis=0).astype(BF16)
@@ -360,27 +375,32 @@
     wts = wts_ref[...]
     order = before(rows)
     end = two(jnp.where((hid[0] & AFTER) > 0, end_ref[...], 0.0))
-    for n in range(per):
-        d, k2 = d_ref[n], (kh_ref[n], kl_ref[n])
-        d2 = two(d)
-        k = k2[0].astype(F32) + k2[1].astype(F32)
-        g2 = two(mm(two(mb_ref[n, :, pl.ds(0, HEAD)]), end) + mb_ref[n, :, pl.ds(HEAD, HEAD)])
-        y = mm((th_ref[n], tl_ref[n]), two(dd_ref[n] + mm(k2, g2)))
-        betas = beta_rows(beta_ref[n].astype(F32), slots)
-        de = 2.0 * sigmoid(column(betas, tokens, slots)) * y
-        de2 = two(de)
-        dk = dk_ref[n] + mm(d2, g2, ROWS_ROWS) - mm(de2, two(st_ref[n]), ROWS_ROWS)
-        dgram = jnp.where(order, mm_half(de2, d2, ROWS_ROWS), 0.0)
-        dk = dk - mm(two(dgram + dgram.T), k2)
-        along = jnp.sum(y * d, axis=1, keepdims=True)
+    chunks = range(per)
+    keys = [(kh_ref[n], kl_ref[n]) for n in chunks]
+    gs = [two(mm(two(mb_ref[n, :, pl.ds(0, HEAD)]), end) + mb_ref[n, :, pl.ds(HEAD, HEAD)]) for n in chunks]
+    dds = [two(dd_ref[n] + mm(keys[n], gs[n])) for n in chunks]
+    ys = [mm((th_ref[n], tl_ref[n]), dds[n]) for n in chunks]
+    betas = [beta_rows(beta_ref[n].astype(F32), slots) for n in chunks]
+    des = [2.0 * sigmoid(column(betas[n], tokens, slots)) * ys[n] for n in chunks]
+    halves = [two(des[n]) for n in chunks]
+    ds = [two(d_ref[n]) for n in chunks]
+    grams = [jnp.where(order, mm_half(halves[n], ds[n], ROWS_ROWS), 0.0) for n in chunks]
+    direct = [
+        dk_ref[n] + mm(ds[n], gs[n], ROWS_ROWS) - mm(halves[n], two(st_ref[n]), ROWS_ROWS) for n in chunks
+    ]
+    dks = [direct[n] - mm(two(grams[n] + grams[n].T), keys[n]) for n in chunks]
+    for n in chunks:
+        along = jnp.sum(ys[n] * d_ref[n], axis=1, keepdims=True)
         marks = []
         for j in range(slots):
-            gb = jnp.sum(jnp.where(places(tokens, slots, j), along, 0.0), axis=0, keepdims=True) * sigmoid(-betas[j])
+            gb = jnp.sum(jnp.where(places(tokens, slots, j), along, 0.0), axis=0, keepdims=True)
+            gb = gb * sigmoid(-betas[n][j])
             high = gb.astype(BF16).astype(F32)
             marks += [high, gb - high]
         marks.append(jnp.zeros((EDGE - 2 * slots, tokens), F32))
-        value, value_rim = conv_back(fv_ref[n] * de, slot_taps(wts, 1), pad.at[2 * n], slots)
-        part = fk_ref[n] * (dk - k * jnp.sum(k * dk, axis=-1, keepdims=True))
+        value, value_rim = conv_back(fv_ref[n] * des[n], slot_taps(wts, 1), pad.at[2 * n], slots)
+        k = keys[n][0].astype(F32) + keys[n][1].astype(F32)
+        part = fk_ref[n] * (dks[n] - k * jnp.sum(k * dks[n], axis=-1, keepdims=True))
         key, key_rim = conv_back(part, slot_taps(wts, 0), pad.at[2 * n + 1], slots)
         out_ref[n, pl.ds(0, rows), :] = key.astype(BF16)
         out_ref[n, pl.ds(rows, rows), :] = value.astype(BF16)
@@ -415,7 +435,7 @@
 FAR = ("kh", "kl", "xh", "xl", "th", "tl", "wh", "wl", "a", "m", "fk", "fv", "stf", "mbf", "d", "dk", "dd")
 
 
-def call(kernel, hid, steps, live, ins, reads, outs, scratch=(), us=1.0, grant=24):
+def call(kernel, hid, steps, live, ins, reads, outs, scratch=(), us=1.0, grant=40):
     def spec(shape, how):
         if how == "weights":
             return pl.BlockSpec((shape[0], HEAD), lambda i, h: (0, h[0] & (BEFORE - 1)))
@@ -522,7 +542,7 @@
         ],
         axis=0,
     )
-    per = 2 if g % 2 == 0 else 1
+    per = 4 if g % 4 == 0 else 1
     steps = g // per
 
     def pad(n):

time: 109 us -> 103 us (0.945)
  Pallas kernels: 51.3 us -> 42.7 us
  starting transfers between devices: 29.9 us -> 32 us
  waiting for transfers between devices: 10.1 us -> 11.2 us
    pallas_call x6, Pallas kernels: 45.3 us -> 37.1 us  [call(): pl.pallas_call(kernel, grid_spec=pltpu.PrefetchScalarGridSpec(num_scalar_...]
    ppermute x2, starting transfers between devices: 2.43 us -> 3.54 us  [across(): return lax.ppermute(last[1], 'ctx', moves)]
  transfers between devices with their start and end apart: 9 -> 9, of which waited for: 5 -> 6; matrix products, arithmetic and copies ran while one was open for 9% -> 10% of each run, Pallas kernels for 38% -> 33%
where the time goes in v7:
time: 103 us; the launch traced here: 102 us
  Pallas kernels  42.7 us (41%)
  starting transfers between devices  32 us (31%)
  waiting for transfers between devices  11.2 us (11%)
  matrix products  6.6 us (6%)
  local copies, waits for them, and re-layouts  5.4 us (5%)
  other arithmetic  3.46 us (3%)
    pallas_call x6, Pallas kernels, call(): pl.pallas_call(kernel, grid_spec=pltpu.PrefetchScalarGridSpec(num_scalar_...  37.1 us
    all_to_all x4, starting transfers between devices, exchange(): lax.all_to_all(x, 'ctx', 0, 0, axis_index_groups=group_lists, tiled=True)  22 us
    all_to_all x4, waiting for transfers between devices, exchange(): lax.all_to_all(x, 'ctx', 0, 0, axis_index_groups=group_lists, tiled=True)  4.83 us
    ppermute x1, waiting for transfers between devices, shards(): lax.ppermute(sent, 'head', [(0, 1), (1, 0)]).astype(F32)  4 us
    dot_general x1, matrix products, shards(): jnp.dot(grad_out, out_weight.T, preferred_element_type=F32).astype(BF16)  3.7 us
    ppermute x2, starting transfers between devices, across(): return lax.ppermute(last[1], 'ctx', moves)  3.54 us
    dot_general x1, matrix products, shards(): partial = jnp.dot(normed_bf, out_weight, preferred_element_type=F32)  2.9 us
    ppermute x1, starting transfers between devices, shards(): rim = lax.ppermute(rim, 'ctx', [(i, i - 1) for i in range(1, shard_count)])  2.78 us
  transfers between devices with their start and end apart: 9, of which 6 were waited for; matrix products, arithmetic and copies ran while one was open for 10% of the time, Pallas kernels for 33%

profile of v7, /device:TPU:1, one launch (start us, length us, event | category | flops | bytes accessed | tf_op | source)
XLA Modules:
  0.0 102.3 jit_solution(8387193567837212288)
XLA Ops:
  0.6 0.0 copy-start
  0.6 0.8 fusion.11
  1.4 0.3 copy-done
  1.7 0.4 copy_bitcast_fusion
  2.1 0.8 copy_bitcast_fusion.2
  2.8 0.8 bitcast_bitcast_fusion
  3.6 0.9 fusion.6
  4.5 5.3 %all-to-all-start = ((bf16[8,304,128]{2,1,0:T(8,128)(2,1)}), bf16[8,304,128]{2,1,0:T(8,128)(2,1)S(1)}, u32[]{:S(2)}, u32[]{:S(2)}) async-start(bf16[8,304,128]{2,1,0:T(8,128)(2,1)} %fusion.6), calls=%async_computation | async-start | bytes 1245184 | tf_op jit(solution)/shard_map/all_to_all | solution.py:504
  9.8 0.2 copy.23
  10.0 3.7 %convolution_convert_fusion = bf16[128,1024]{1,0:T(8,128)(2,1)S(1)} fusion(bf16[128,2048]{1,0:T(8,128)(2,1)S(1)} %copy-done.4, bf16[1024,2048]{1,0:T(8,128)(2,1)} %param.18), kind=kOutput, calls=%fused_computation.6 | convolution fusion | flops 537001984 | bytes 4980736 | tf_op jit(solution)/shard_map/dot_general | solution.py:528
  13.7 0.2 copy.25
  13.9 0.2 copy.26
  14.1 0.2 copy.24
  14.3 0.5 copy-done.3
  14.7 0.4 copy_bitcast_fusion.1
  15.1 1.0 %pad_maximum_fusion = bf16[8,512,128]{2,1,0:T(8,128)(2,1)} fusion(bf16[8,128,128]{2,1,0:T(8,128)(2,1)S(1)} %bitcast.73, bf16[8,128,128]{2,1,0:T(8,128)(2,1)S(1)} %bitcast.74, bf16[8,256,128]{2,1,0:T(8,128)(2,1)S(1)} %bitcast.70), kind=kLoop, calls=%fused_computation.7 | loop fusion | flops 3145728 | bytes 2097152 | tf_op jit(solution)/shard_map/concatenate | solution.py:529
  16.2 2.7 %all-to-all-done.kb_ref.prev_ref.beta_ref = bf16[8,304,128]{2,1,0:T(8,128)(2,1)S(1)} async-done(((bf16[8,304,128]{2,1,0:T(8,128)(2,1)}), bf16[8,304,128]{2,1,0:T(8,128)(2,1)S(1)}, u32[]{:S(2)}, u32[]{:S(2)}) %all-to-all-start) | async-done | bytes 622624 | tf_op jit(solution)/shard_map/all_to_all | solution.py:504
  18.9 0.0 copy-start.8
  18.9 0.0 copy-start.9
  18.9 2.4 %collective-permute-start = (bf16[48,128]{1,0:T(8,128)(2,1)S(1)}, bf16[48,128]{1,0:T(8,128)(2,1)S(1)}, u32[]{:S(2)}, u32[]{:S(2)}) collective-permute-start(bf16[48,128]{1,0:T(8,128)(2,1)S(1)} %pad_maximum_fusion.3), channel_id=1, source_target_pairs={{0,16},{2,18},{4,20},{6,22},{8,24},{10,26},{12,28},{14,30},{16,0},... | collective-permute-start | bytes 36872 | tf_op jit(solution)/shard_map/ppermute | solution.py:531
  21.2 1.1 %collective-permute-done.tail_ref = bf16[48,128]{1,0:T(8,128)(2,1)S(1)} collective-permute-done((bf16[48,128]{1,0:T(8,128)(2,1)S(1)}, bf16[48,128]{1,0:T(8,128)(2,1)S(1)}, u32[]{:S(2)}, u32[]{:S(2)}) %collective-permute-start) | collective-permute-done | bytes 12320 | tf_op jit(solution)/shard_map/ppermute | solution.py:531
  22.4 5.5 %all-to-all-start.1 = ((bf16[8,512,128]{2,1,0:T(8,128)(2,1)}), bf16[8,512,128]{2,1,0:T(8,128)(2,1)S(1)}, u32[]{:S(2)}, u32[]{:S(2)}) async-start(bf16[8,512,128]{2,1,0:T(8,128)(2,1)} %pad_maximum_fusion), calls=%async_computation.1 | async-start | bytes 2097152 | tf_op jit(solution)/shard_map/all_to_all | solution.py:504
  27.9 0.1 tile.17
  28.1 0.1 tile.19
  28.3 13.7 %shard_map.137 = (bf16[8,256,128]{2,1,0:T(8,128)(2,1)}, bf16[8,256,128]{2,1,0:T(8,128)(2,1)}, bf16[8,256,256]{2,1,0:T(8,128)(2,1)}, bf16[8,256,256]{2,1,0:T(8,12...) custom-call(s32[1]{0:T(128)} %bitcast.hid, ...), custom_call_target="tpu_custom_call" | custom-call | flops 12099999744 | bytes 65536 | tf_op jit(solution)/shard_map/pallas_call | solution.py:457
  42.0 5.3 %shard_map.138 = (f32[8,256,128]{2,1,0:T(8,128)S(1)}, f32[8,128,128]{2,1,0:T(8,128)S(1)}, f32[8,128,128]{2,1,0:T(8,128)S(1)}, f32[8,128,128]{2,1,0:T(8,128)S(1)}...) custom-call(s32[1]{0:T(128)} %bitcast.hid, bf16[8,512,128]{2,1,0:T(8,128)(2,1)S(1)} %all-to-all-done.1.vq_ref.prev_ref, ...), custom_call_target="tpu_custom_call" | custom-call | flops 6600000000 | bytes 65536 | tf_op jit(solution)/shard_map/pallas_call | solution.py:457
  47.3 2.3 %collective-permute-start.1 = (f32[128,128]{1,0:T(8,128)S(1)}, f32[128,128]{1,0:T(8,128)S(1)}, u32[]{:S(2)}, u32[]{:S(2)}) collective-permute-start(f32[128,128]{1,0:T(8,128)S(1)} %get-tuple-element.58), channel_id=1, source_target_pairs={{0,16},{2,18},{4,20},{6,22},{8,24},{10,26},{12,28},{14,30},{16,0},... | collective-permute-start | bytes 196616 | tf_op jit(solution)/shard_map/ppermute | solution.py:595
  49.6 2.9 %shard_map.139 = (f32[8,128,128]{2,1,0:T(8,128)S(1)}, f32[8,128,256]{2,1,0:T(8,128)S(1)}, f32[8,128,128]{2,1,0:T(8,128)S(1)}, f32[8,128,128]{2,1,0:T(8,128)S(1)}, f32[8,128,128]{2,1,0:T(8,128)S(1)}) custom-call(s32[1]{0:T(128)} %bitcast.hid, bf16[8,512,128]{2,1,0:T(8,128)(2,1)S(1)} %all-to-all-done.1.vq_ref.prev_ref, ...), custom_call_target="tpu_custom_call" | custom-call | flops 8800000000 | bytes 65536 | tf_op jit(solution)/shard_map/pallas_call | solution.py:457
  52.5 2.5 %shard_map.140 = (f32[8,128,128]{2,1,0:T(8,128)S(1)}, f32[8,128,128]{2,1,0:T(8,128)S(1)}, f32[8,128,256]{2,1,0:T(8,128)S(1)}, bf16[8,128,128]{2,1,0:T(8,128)(2,1)S(1)}, f32[128,256]{1,0:T(8,128)S(1)}) custom-call(s32[1]{0:T(128)} %bitcast.hid, bf16[8,512,128]{2,1,0:T(8,128)(2,1)S(1)} %all-to-all-done.1.vq_ref.prev_ref, f32[72,1024]{1,0:T(8,128)S(1)} %concatenate.15.wts_ref, ...), custom_call_target="tpu_custom_call" | custom-call | flops 4400000000 | bytes 65536 | tf_op jit(solution)/shard_map/pallas_call | solution.py:457
  55.0 1.2 %collective-permute-start.3 = (f32[128,128]{1,0:T(8,128)S(1)}, f32[128,128]{1,0:T(8,128)S(1)}, u32[]{:S(2)}, u32[]{:S(2)}) collective-permute-start(f32[128,128]{1,0:T(8,128)S(1)} %slice.30), channel_id=1, source_target_pairs={{0,16},{2,18},{4,20},{6,22},{8,24},{10,26},{12,28},{14,30},{16,0},... | collective-permute-start | bytes 196616 | tf_op jit(solution)/shard_map/ppermute | solution.py:595
  56.3 5.1 %shard_map.141 = (f32[8,256,128]{2,1,0:T(8,128)}, f32[8,256,128]{2,1,0:T(8,128)}, f32[8,256,128]{2,1,0:T(8,128)}, f32[8,128,128]{2,1,0:T(8,128)}, f32[8,128,256]{2,1,0:T(8,128)}, /*index=5*/bf16[8,272,128]{2,1,0:T(8,128)(2,1)}) custom-call(s32[1]{0:T(128)} %bitcast.hid, f32[72,1024]{1,0:T(8,128)S(1)} %concatenate.15.wts_ref, ...), custom_call_target="tpu_custom_call" | custom-call | flops 22000001024 | bytes 65536 | tf_op jit(solution)/shard_map/pallas_call | solution.py:457
  61.3 6.9 %all-to-all-start.2 = ((bf16[8,272,128]{2,1,0:T(8,128)(2,1)}), bf16[8,272,128]{2,1,0:T(8,128)(2,1)S(1)}, u32[]{:S(2)}, u32[]{:S(2)}) async-start(bf16[8,272,128]{2,1,0:T(8,128)(2,1)} %get-tuple-element.74), calls=%async_computation.2 | async-start | bytes 1114112 | tf_op jit(solution)/shard_map/all_to_all | solution.py:504
  68.2 7.7 %shard_map.142 = bf16[8,544,128]{2,1,0:T(8,128)(2,1)} custom-call(s32[1]{0:T(128)} %bitcast.hid, bf16[8,304,128]{2,1,0:T(8,128)(2,1)S(1)} %all-to-all-done.kb_ref.prev_ref.beta_ref, f32[72,1024]{1,0:T(8,128)S(1)} %concatenate.15.wts_ref, f32[128,128]{1,0:T(8,128)S(1)} %collective-permute-done.3.end_ref, f32[8,128,256]{2,1,0:T(8,128)} %get-tuple-element.76.mb_ref, ...), custom_call_target="tpu_custom_call" | custom-call | flops 22000001024 | bytes 65536 | tf_op jit(solution)/shard_map/pallas_call | solution.py:457
  75.9 0.7 all-to-all-done.2.got_ref
  76.6 4.3 %all-to-all-start.3 = ((bf16[8,544,128]{2,1,0:T(8,128)(2,1)}), bf16[8,544,128]{2,1,0:T(8,128)(2,1)S(1)}, u32[]{:S(2)}, u32[]{:S(2)}) async-start(bf16[8,544,128]{2,1,0:T(8,128)(2,1)} %shard_map.142), calls=%async_computation.3 | async-start | bytes 2228224 | tf_op jit(solution)/shard_map/all_to_all | solution.py:504
  80.9 0.2 copy.33
  81.1 0.1 dot_general.9
  81.2 2.9 %fusion = f32[2,64,2048]{2,1,0:T(8,128)S(1)} fusion(bf16[2,64,1024]{2,1,0:T(8,128)(2,1)S(1)} %dot_general.9, bf16[1024,2048]{1,0:T(8,128)(2,1)} %param.18), kind=kOutput, calls=%fused_computation | convolution fusion | flops 536870912 | bytes 5505024 | tf_op jit(solution)/shard_map/dot_general | solution.py:665
  84.1 1.0 copy-done.1
  85.1 1.3 %collective-permute-start.2 = (bf16[64,2048]{1,0:T(8,128)(2,1)S(1)}, bf16[64,2048]{1,0:T(8,128)(2,1)S(1)}, u32[]{:S(2)}, u32[]{:S(2)}) collective-permute-start(bf16[64,2048]{1,0:T(8,128)(2,1)S(1)} %fusion.8), channel_id=1, source_target_pairs={{0,1},{1,0},{2,3},{3,2},{4,5},{5,4},{6,7},{7,6},{8,9},{9,8},{10,11... | collective-permute-start | bytes 786440 | tf_op jit(solution)/shard_map/ppermute | solution.py:672
  86.4 2.6 %shard_map.143.gq_ref = f32[128,1024]{1,0:T(8,128)} custom-call(bf16[8,272,128]{2,1,0:T(8,128)(2,1)S(1)} %all-to-all-done.2.got_ref), custom_call_target="tpu_custom_call" | custom-call | flops 2200000000 | bytes 65536 | tf_op jit(solution)/shard_map/pallas_call | solution.py:681
  89.0 4.0 %collective-permute-done.2 = bf16[64,2048]{1,0:T(8,128)(2,1)S(1)} collective-permute-done((bf16[64,2048]{1,0:T(8,128)(2,1)S(1)}, bf16[64,2048]{1,0:T(8,128)(2,1)S(1)}, u32[]{:S(2)}, u32[]{:S(2)}) %collective-permute-start.2) | collective-permute-done | bytes 262176 | tf_op jit(solution)/shard_map/ppermute | solution.py:672
  93.0 0.8 fusion.7
  93.7 1.5 %all-to-all-done.3.got_ref.mark_ref = bf16[8,544,128]{2,1,0:T(8,128)(2,1)S(1)} async-done(((bf16[8,544,128]{2,1,0:T(8,128)(2,1)}), bf16[8,544,128]{2,1,0:T(8,128)(2,1)S(1)}, u32[]{:S(2)}, u32[]{:S(2)}) %all-to-all-start.3) | async-done | bytes 1114144 | tf_op jit(solution)/shard_map/all_to_all | solution.py:504
  95.2 2.8 %collective-permute-start.4 = (bf16[8,24,128]{2,1,0:T(8,128)(2,1)S(1)}, bf16[8,24,128]{2,1,0:T(8,128)(2,1)S(1)}, u32[]{:S(2)}, u32[]{:S(2)}) collective-permute-start(bf16[8,24,128]{2,1,0:T(8,128)(2,1)S(1)} %pad_maximum_fusion.1), channel_id=1, source_target_pairs={{2,0},{4,2},{6,4},{8,6},{10,8},{12,10},{14,12},{16,14},{18,16},{20... | collective-permute-start | bytes 147464 | tf_op jit(solution)/shard_map/ppermute | solution.py:677
  98.0 1.6 %shard_map.144 = (f32[128,2,1024]{2,1,0:T(2,128)}, f32[128,2,1024]{2,1,0:T(2,128)}) custom-call(bf16[8,544,128]{2,1,0:T(8,128)(2,1)S(1)} %all-to-all-done.3.got_ref.mark_ref), custom_call_target="tpu_custom_call" | custom-call | flops 11000000512 | bytes 65536 | tf_op jit(solution)/shard_map/pallas_call | solution.py:690
  99.6 1.2 %collective-permute-done.4.rim_ref = bf16[8,24,128]{2,1,0:T(8,128)(2,1)S(1)} collective-permute-done((bf16[8,24,128]{2,1,0:T(8,128)(2,1)S(1)}, bf16[8,24,128]{2,1,0:T(8,128)(2,1)S(1)}, u32[]{:S(2)}, u32[]{:S(2)}) %collective-permute-start.4) | collective-permute-done | bytes 49184 | tf_op jit(solution)/shard_map/ppermute | solution.py:677
  100.8 1.5 %shard_map.145 = (f32[128,1024]{1,0:T(8,128)}, f32[128,2,1024]{2,1,0:T(2,128)}, f32[128,2,1024]{2,1,0:T(2,128)}, f32[2,8,128]{2,1,0:T(8,128)}) custom-call(bf16[8,24,128]{2,1,0:T(8,128)(2,1)S(1)} %collective-permute-done.4.rim_ref, f32[128,1024]{1,0:T(8,128)} %shard_map.143.gq_ref, ...), custom_call_target="tpu_custom_call", output_to_operand_aliasing={{0}: (1, {}), {1}: (2, {}), {2}: (3, {})} | custom-call | tf_op jit(solution)/shard_map/pallas_call | solution.py:703
  (32 shorter events, 0.3 us)
Async XLA Ops:
  0.6 1.1 %copy-start = (bf16[128,2,1024]{2,1,0:T(2,128)(2,1)S(1)}, bf16[128,2,1024]{2,1,0:T(2,128)(2,1)}, u32[]{:S(2)}) copy-start(bf16[128,2,1024]{2,1,0:T(2,128)(2,1)} %param.11) | copy-start | bytes 1572868
  3.6 6.2 %copy-start.5 = (bf16[128,1024]{1,0:T(8,128)(2,1)S(1)}, bf16[128,1024]{1,0:T(8,128)(2,1)}, u32[]{:S(2)}) copy-start(bf16[128,1024]{1,0:T(8,128)(2,1)} %param.10) | copy-start | bytes 786436
  3.6 6.4 %copy-start.4 = (bf16[128,2048]{1,0:T(8,128)(2,1)S(1)}, bf16[128,2048]{1,0:T(8,128)(2,1)}, u32[]{:S(2)}) copy-start(bf16[128,2048]{1,0:T(8,128)(2,1)} %param.19) | copy-start | bytes 1572868
  4.5 14.3 %all-to-all-start = ((bf16[8,304,128]{2,1,0:T(8,128)(2,1)}), bf16[8,304,128]{2,1,0:T(8,128)(2,1)S(1)}, u32[]{:S(2)}, u32[]{:S(2)}) async-start(bf16[8,304,128]{2,1,0:T(8,128)(2,1)} %fusion.6), calls=%async_computation | async-start | bytes 1245184 | tf_op jit(solution)/shard_map/all_to_all | solution.py:504
  13.7 1.0 %copy-start.3 = (bf16[128,2,1024]{2,1,0:T(2,128)(2,1)S(1)}, bf16[128,2,1024]{2,1,0:T(2,128)(2,1)}, u32[]{:S(2)}) copy-start(bf16[128,2,1024]{2,1,0:T(2,128)(2,1)} %param.12) | copy-start | bytes 1572868
  16.2 11.7 %copy-start.6 = (f32[4,2,1024]{2,1,0:T(2,128)S(1)}, f32[4,2,1024]{2,1,0:T(2,128)}, u32[]{:S(2)}) copy-start(f32[4,2,1024]{2,1,0:T(2,128)} %param.15) | copy-start | bytes 98308
  18.8 9.2 %copy-start.7 = (f32[4,2,1024]{2,1,0:T(2,128)S(1)}, f32[4,2,1024]{2,1,0:T(2,128)}, u32[]{:S(2)}) copy-start(f32[4,2,1024]{2,1,0:T(2,128)} %param.16) | copy-start | bytes 98308
  18.9 9.3 %copy-start.8 = (f32[4,1024]{1,0:T(4,128)S(1)}, f32[4,1024]{1,0:T(4,128)}, u32[]{:S(2)}) copy-start(f32[4,1024]{1,0:T(4,128)} %param.14) | copy-start | bytes 49156
  18.9 9.3 %copy-start.9 = (f32[1024]{0:T(1024)S(1)}, f32[1024]{0:T(1024)}, u32[]{:S(2)}) copy-start(f32[1024]{0:T(1024)} %param.17) | copy-start | bytes 12292
  18.9 3.5 %collective-permute-start = (bf16[48,128]{1,0:T(8,128)(2,1)S(1)}, bf16[48,128]{1,0:T(8,128)(2,1)S(1)}, u32[]{:S(2)}, u32[]{:S(2)}) collective-permute-start(bf16[48,128]{1,0:T(8,128)(2,1)S(1)} %pad_maximum_fusion.3), channel_id=1, source_target_pairs={{0,16},{2,18},{4,20},{6,22},{8,24},{10,26},{12,28},{14,30},{16,0},... | collective-permute-start | bytes 36872 | tf_op jit(solution)/shard_map/ppermute | solution.py:531
  22.4 19.6 %all-to-all-start.1 = ((bf16[8,512,128]{2,1,0:T(8,128)(2,1)}), bf16[8,512,128]{2,1,0:T(8,128)(2,1)S(1)}, u32[]{:S(2)}, u32[]{:S(2)}) async-start(bf16[8,512,128]{2,1,0:T(8,128)(2,1)} %pad_maximum_fusion), calls=%async_computation.1 | async-start | bytes 2097152 | tf_op jit(solution)/shard_map/all_to_all | solution.py:504
  47.3 5.2 %collective-permute-start.1 = (f32[128,128]{1,0:T(8,128)S(1)}, f32[128,128]{1,0:T(8,128)S(1)}, u32[]{:S(2)}, u32[]{:S(2)}) collective-permute-start(f32[128,128]{1,0:T(8,128)S(1)} %get-tuple-element.58), channel_id=1, source_target_pairs={{0,16},{2,18},{4,20},{6,22},{8,24},{10,26},{12,28},{14,30},{16,0},... | collective-permute-start | bytes 196616 | tf_op jit(solution)/shard_map/ppermute | solution.py:595
  55.0 13.2 %collective-permute-start.3 = (f32[128,128]{1,0:T(8,128)S(1)}, f32[128,128]{1,0:T(8,128)S(1)}, u32[]{:S(2)}, u32[]{:S(2)}) collective-permute-start(f32[128,128]{1,0:T(8,128)S(1)} %slice.30), channel_id=1, source_target_pairs={{0,16},{2,18},{4,20},{6,22},{8,24},{10,26},{12,28},{14,30},{16,0},... | collective-permute-start | bytes 196616 | tf_op jit(solution)/shard_map/ppermute | solution.py:595
  61.3 15.2 %all-to-all-start.2 = ((bf16[8,272,128]{2,1,0:T(8,128)(2,1)}), bf16[8,272,128]{2,1,0:T(8,128)(2,1)S(1)}, u32[]{:S(2)}, u32[]{:S(2)}) async-start(bf16[8,272,128]{2,1,0:T(8,128)(2,1)} %get-tuple-element.74), calls=%async_computation.2 | async-start | bytes 1114112 | tf_op jit(solution)/shard_map/all_to_all | solution.py:504
  76.6 18.7 %all-to-all-start.3 = ((bf16[8,544,128]{2,1,0:T(8,128)(2,1)}), bf16[8,544,128]{2,1,0:T(8,128)(2,1)S(1)}, u32[]{:S(2)}, u32[]{:S(2)}) async-start(bf16[8,544,128]{2,1,0:T(8,128)(2,1)} %shard_map.142), calls=%async_computation.3 | async-start | bytes 2228224 | tf_op jit(solution)/shard_map/all_to_all | solution.py:504
  84.1 1.0 copy-start.1
  85.1 7.8 %collective-permute-start.2 = (bf16[64,2048]{1,0:T(8,128)(2,1)S(1)}, bf16[64,2048]{1,0:T(8,128)(2,1)S(1)}, u32[]{:S(2)}, u32[]{:S(2)}) collective-permute-start(bf16[64,2048]{1,0:T(8,128)(2,1)S(1)} %fusion.8), channel_id=1, source_target_pairs={{0,1},{1,0},{2,3},{3,2},{4,5},{5,4},{6,7},{7,6},{8,9},{9,8},{10,11... | collective-permute-start | bytes 786440 | tf_op jit(solution)/shard_map/ppermute | solution.py:672
  86.4 6.6 %copy-start.2 = (f32[2,64,2048]{2,1,0:T(8,128)S(1)}, f32[2,64,2048]{2,1,0:T(8,128)}, u32[]{:S(2)}) copy-start(f32[2,64,2048]{2,1,0:T(8,128)} %copy-done.1) | copy-start | bytes 3145732
  95.2 5.6 %collective-permute-start.4 = (bf16[8,24,128]{2,1,0:T(8,128)(2,1)S(1)}, bf16[8,24,128]{2,1,0:T(8,128)(2,1)S(1)}, u32[]{:S(2)}, u32[]{:S(2)}) collective-permute-start(bf16[8,24,128]{2,1,0:T(8,128)(2,1)S(1)} %pad_maximum_fusion.1), channel_id=1, source_target_pairs={{2,0},{4,2},{6,4},{8,6},{10,8},{12,10},{14,12},{16,14},{18,16},{20... | collective-permute-start | bytes 147464 | tf_op jit(solution)/shard_map/ppermute | solution.py:677

commit v8 on v7

--- a/solution.py
+++ b/solution.py
@@ -181,7 +181,7 @@
     def _():
         carry[...] = (ir == ic).astype(F32)
 
-    grams, keys, scaled = [], [], []
+    grams, keys, scaled, strengths = [], [], [], []
     for n in range(per):
         s = conv_rows(kb_ref[n, pl.ds(0, rows), :].astype(F32), tops[n], taps, pad.at[n], slots)
         c, slope = silu(s)
@@ -193,12 +193,13 @@
         kh_ref[n], kl_ref[n] = k2
         keys.append(k2)
         scaled.append(two(strength * k))
-        gram = {}
-        for i in range(blocks):
-            for j in range(i + 1):
-                part = mm(piece(k2, i), piece(k2, j), ROWS_ROWS) * strength[i * HEAD : (i + 1) * HEAD]
-                gram[i, j] = jnp.where(order, part, 0.0) if i == j else part
-        grams.append(gram)
+        strengths.append(strength)
+        grams.append({})
+    for i in range(blocks):
+        for j in range(i + 1):
+            for n in range(per):
+                part = mm(piece(keys[n], i), piece(keys[n], j), ROWS_ROWS) * strengths[n][i * HEAD : (i + 1) * HEAD]
+                grams[n][i, j] = jnp.where(order, part, 0.0) if i == j else part
     eye = (ir == ic).astype(F32)
     zero = jnp.zeros((HEAD, HEAD), BF16)
     diagonal = [gram[b, b] for gram in grams for b in range(blocks)]
@@ -212,34 +213,40 @@
         crossed = [mm(tuple(jnp.where(pairs, p, zero) for p in s), x) for s, x in zip(systems, split)]
         inverse = [x - mm(s, two(y)) for x, s, y in zip(inverse, split, crossed)]
         level += 1
-    for n in range(per):
-        done = {(b, b): inverse[n * blocks + b] for b in range(blocks)}
-        halves = {(b, b): two(done[b, b]) for b in range(blocks)}
-        for j in range(blocks):
-            for i in range(j + 1, blocks):
-                cross = sum(mm(two(grams[n][i, m]), halves[m, j]) for m in range(j, i))
-                done[i, j] = -mm(halves[i, i], two(cross))
-                halves[i, j] = two(done[i, j])
-        nothing = jnp.zeros((HEAD, HEAD), BF16)
-        x2 = tuple(
+    halves = [{(b, b): two(inverse[n * blocks + b]) for b in range(blocks)} for n in range(per)]
+    for j in range(blocks):
+        for i in range(j + 1, blocks):
+            cross = [
+                two(sum(mm(two(grams[n][i, m]), halves[n][m, j]) for m in range(j, i))) for n in range(per)
+            ]
+            found = [two(-mm(halves[n][i, i], cross[n])) for n in range(per)]
+            for n in range(per):
+                halves[n][i, j] = found[n]
+    nothing = jnp.zeros((HEAD, HEAD), BF16)
+    whole = [
+        tuple(
             jnp.concatenate(
                 [
-                    jnp.concatenate([halves[i, j][p] if j <= i else nothing for j in range(blocks)], axis=1)
+                    jnp.concatenate([halves[n][i, j][p] if j <= i else nothing for j in range(blocks)], axis=1)
                     for i in range(blocks)
                 ],
                 axis=0,
             )
             for p in range(2)
         )
-        xh_ref[n], xl_ref[n] = x2
-        th_ref[n], tl_ref[n] = x2[0].T, x2[1].T
-        w2 = two(lower_times(x2, scaled[n]))
-        wh_ref[n], wl_ref[n] = w2
-        a_ref[n] = eye - mm(keys[n], w2, COLS_COLS)
+        for n in range(per)
+    ]
+    ws = [two(lower_times(whole[n], scaled[n])) for n in range(per)]
+    steps = [eye - mm(keys[n], ws[n], COLS_COLS) for n in range(per)]
+    for n in range(per):
+        xh_ref[n], xl_ref[n] = whole[n]
+        th_ref[n], tl_ref[n] = whole[n][0].T, whole[n][1].T
+        wh_ref[n], wl_ref[n] = ws[n]
+        a_ref[n] = steps[n]
     state = carry[...]
     for n in range(per):
         m_ref[n] = state
-        state = mm(two(a_ref[n]), two(state))
+        state = mm(two(steps[n]), two(state))
     carry[...] = state
     end_ref[...] = state
 
@@ -416,8 +423,9 @@
             out_ref[:, :, pl.ds(n * HEAD, HEAD)] = main.reshape(tokens, slots, HEAD)
 
 
-def unpack_query_kernel(tokens, got_ref, gq_ref):
-    gq_ref[...] = got_ref[0, pl.ds(tokens, tokens), :].astype(F32)
+def unpack_query_kernel(per, tokens, got_ref, gq_ref):
+    for n in range(per):
+        gq_ref[:, pl.ds(n * HEAD, HEAD)] = got_ref[n, pl.ds(tokens, tokens), :].astype(F32)
 
 
 def rims_kernel(heads, slots, rim_ref, gq_ref, gk_ref, gv_ref, mark_ref, nq_ref, nk_ref, nv_ref, gb_ref):
@@ -675,14 +683,13 @@
 
     rim = jnp.concatenate([nq[:, 2 * tokens : 2 * tokens + 8], grads[:, 2 * rows + EDGE :]], axis=1)
     rim = lax.ppermute(rim, "ctx", [(i, i - 1) for i in range(1, shard_count)])
-    part = lambda x: pl.BlockSpec((1,) + x.shape[1:], lambda h: (h, 0, 0))
     small = pltpu.CompilerParams(vmem_limit_bytes=8 << 20)
     cost = lambda us: pl.CostEstimate(flops=int(us * 1.1e9), bytes_accessed=1 << 16, transcendentals=0)
     grad_query = pl.pallas_call(
-        functools.partial(unpack_query_kernel, tokens),
-        grid=(heads,),
-        in_specs=[part(nq)],
-        out_specs=pl.BlockSpec((tokens, HEAD), lambda h: (0, h)),
+        functools.partial(unpack_query_kernel, per, tokens),
+        grid=(steps,),
+        in_specs=[pl.BlockSpec((per,) + nq.shape[1:], lambda h: (h, 0, 0))],
+        out_specs=pl.BlockSpec((tokens, per * HEAD), lambda h: (0, h)),
         out_shape=jax.ShapeDtypeStruct((tokens, width), F32),
         compiler_params=small,
         cost_estimate=cost(2.0),

time: 103 us -> 101 us (0.981)
  Pallas kernels: 42.7 us -> 38.1 us
  waiting for transfers between devices: 11.2 us -> 15.2 us
    pallas_call x6, Pallas kernels: 37.1 us -> 34.3 us  [call(): pl.pallas_call(kernel, grid_spec=pltpu.PrefetchScalarGridSpec(num_scalar_...]
    all_to_all x4, waiting for transfers between devices: 4.83 us -> 7 us  [exchange(): lax.all_to_all(x, 'ctx', 0, 0, axis_index_groups=group_lists, tiled=True)]
    ppermute x1, waiting for transfers between devices: 4 us -> 5.82 us  [shards(): lax.ppermute(sent, 'head', [(0, 1), (1, 0)]).astype(F32)]
    pallas_call x1, Pallas kernels: 2.56 us -> 0.82 us  [shards(): pl.pallas_call(functools.partial(unpack_query_kernel, per, tokens), grid=...]
  transfers between devices with their start and end apart: 9 -> 9, of which waited for: 6 -> 7; matrix products, arithmetic and copies ran while one was open for 10% -> 10% of each run, Pallas kernels for 33% -> 29%
where the time goes in v8:
time: 101 us
  Pallas kernels  38.1 us (38%)
  starting transfers between devices  31 us (31%)
  waiting for transfers between devices  15.2 us (15%)
  matrix products  6.6 us (7%)
  local copies, waits for them, and re-layouts  5.4 us (5%)
  other arithmetic  3.46 us (3%)
    pallas_call x6, Pallas kernels, call(): pl.pallas_call(kernel, grid_spec=pltpu.PrefetchScalarGridSpec(num_scalar_...  34.3 us
    all_to_all x4, starting transfers between devices, exchange(): lax.all_to_all(x, 'ctx', 0, 0, axis_index_groups=group_lists, tiled=True)  21 us
    all_to_all x4, waiting for transfers between devices, exchange(): lax.all_to_all(x, 'ctx', 0, 0, axis_index_groups=group_lists, tiled=True)  7 us
    ppermute x1, waiting for transfers between devices, shards(): lax.ppermute(sent, 'head', [(0, 1), (1, 0)]).astype(F32)  5.82 us
    dot_general x1, matrix products, shards(): jnp.dot(grad_out, out_weight.T, preferred_element_type=F32).astype(BF16)  3.7 us
    ppermute x2, starting transfers between devices, across(): return lax.ppermute(last[1], 'ctx', moves)  3.51 us
    dot_general x1, matrix products, shards(): partial = jnp.dot(normed_bf, out_weight, preferred_element_type=F32)  2.9 us
    ppermute x1, starting transfers between devices, shards(): rim = lax.ppermute(rim, 'ctx', [(i, i - 1) for i in range(1, shard_count)])  2.78 us
  transfers between devices with their start and end apart: 9, of which 7 were waited for; matrix products, arithmetic and copies ran while one was open for 10% of the time, Pallas kernels for 29%

profile of v8, /device:TPU:1, one launch (start us, length us, event | category | flops | bytes accessed | tf_op | source)
XLA Modules:
  0.0 100.7 jit_solution(15905136200256656439)
XLA Ops:
  0.6 0.0 copy-start
  0.6 0.8 fusion.11
  1.4 0.3 copy-done
  1.7 0.4 copy_bitcast_fusion
  2.1 0.8 copy_bitcast_fusion.2
  2.8 0.8 bitcast_bitcast_fusion
  3.6 0.9 fusion.6
  4.5 5.3 %all-to-all-start = ((bf16[8,304,128]{2,1,0:T(8,128)(2,1)}), bf16[8,304,128]{2,1,0:T(8,128)(2,1)S(1)}, u32[]{:S(2)}, u32[]{:S(2)}) async-start(bf16[8,304,128]{2,1,0:T(8,128)(2,1)} %fusion.6), calls=%async_computation | async-start | bytes 1245184 | tf_op jit(solution)/shard_map/all_to_all | solution.py:512
  9.8 0.2 copy.23
  10.0 3.7 %convolution_convert_fusion = bf16[128,1024]{1,0:T(8,128)(2,1)S(1)} fusion(bf16[128,2048]{1,0:T(8,128)(2,1)S(1)} %copy-done.4, bf16[1024,2048]{1,0:T(8,128)(2,1)} %param.18), kind=kOutput, calls=%fused_computation.6 | convolution fusion | flops 537001984 | bytes 4980736 | tf_op jit(solution)/shard_map/dot_general | solution.py:536
  13.7 0.2 copy.25
  13.9 0.2 copy.26
  14.1 0.2 copy.24
  14.3 0.5 copy-done.3
  14.7 0.4 copy_bitcast_fusion.1
  15.1 1.0 %pad_maximum_fusion = bf16[8,512,128]{2,1,0:T(8,128)(2,1)} fusion(bf16[8,128,128]{2,1,0:T(8,128)(2,1)S(1)} %bitcast.73, bf16[8,128,128]{2,1,0:T(8,128)(2,1)S(1)} %bitcast.74, bf16[8,256,128]{2,1,0:T(8,128)(2,1)S(1)} %bitcast.70), kind=kLoop, calls=%fused_computation.7 | loop fusion | flops 3145728 | bytes 2097152 | tf_op jit(solution)/shard_map/concatenate | solution.py:537
  16.2 2.7 %all-to-all-done.kb_ref.prev_ref.beta_ref = bf16[8,304,128]{2,1,0:T(8,128)(2,1)S(1)} async-done(((bf16[8,304,128]{2,1,0:T(8,128)(2,1)}), bf16[8,304,128]{2,1,0:T(8,128)(2,1)S(1)}, u32[]{:S(2)}, u32[]{:S(2)}) %all-to-all-start) | async-done | bytes 622624 | tf_op jit(solution)/shard_map/all_to_all | solution.py:512
  18.9 0.0 copy-start.8
  18.9 2.4 %collective-permute-start = (bf16[48,128]{1,0:T(8,128)(2,1)S(1)}, bf16[48,128]{1,0:T(8,128)(2,1)S(1)}, u32[]{:S(2)}, u32[]{:S(2)}) collective-permute-start(bf16[48,128]{1,0:T(8,128)(2,1)S(1)} %pad_maximum_fusion.3), channel_id=1, source_target_pairs={{0,16},{2,18},{4,20},{6,22},{8,24},{10,26},{12,28},{14,30},{16,0},... | collective-permute-start | bytes 36872 | tf_op jit(solution)/shard_map/ppermute | solution.py:539
  21.2 1.1 %collective-permute-done.tail_ref = bf16[48,128]{1,0:T(8,128)(2,1)S(1)} collective-permute-done((bf16[48,128]{1,0:T(8,128)(2,1)S(1)}, bf16[48,128]{1,0:T(8,128)(2,1)S(1)}, u32[]{:S(2)}, u32[]{:S(2)}) %collective-permute-start) | collective-permute-done | bytes 12320 | tf_op jit(solution)/shard_map/ppermute | solution.py:539
  22.4 5.5 %all-to-all-start.1 = ((bf16[8,512,128]{2,1,0:T(8,128)(2,1)}), bf16[8,512,128]{2,1,0:T(8,128)(2,1)S(1)}, u32[]{:S(2)}, u32[]{:S(2)}) async-start(bf16[8,512,128]{2,1,0:T(8,128)(2,1)} %pad_maximum_fusion), calls=%async_computation.1 | async-start | bytes 2097152 | tf_op jit(solution)/shard_map/all_to_all | solution.py:512
  27.9 0.1 tile.17
  28.1 0.1 tile.19
  28.3 10.9 %shard_map.137 = (bf16[8,256,128]{2,1,0:T(8,128)(2,1)}, bf16[8,256,128]{2,1,0:T(8,128)(2,1)}, bf16[8,256,256]{2,1,0:T(8,128)(2,1)}, bf16[8,256,256]{2,1,0:T(8,12...) custom-call(s32[1]{0:T(128)} %bitcast.hid, ...), custom_call_target="tpu_custom_call" | custom-call | flops 12099999744 | bytes 65536 | tf_op jit(solution)/shard_map/pallas_call | solution.py:465
  39.1 2.3 %all-to-all-done.1.vq_ref.prev_ref = bf16[8,512,128]{2,1,0:T(8,128)(2,1)S(1)} async-done(((bf16[8,512,128]{2,1,0:T(8,128)(2,1)}), bf16[8,512,128]{2,1,0:T(8,128)(2,1)S(1)}, u32[]{:S(2)}, u32[]{:S(2)}) %all-to-all-start.1) | async-done | bytes 1048608 | tf_op jit(solution)/shard_map/all_to_all | solution.py:512
  41.5 5.3 %shard_map.138 = (f32[8,256,128]{2,1,0:T(8,128)S(1)}, f32[8,128,128]{2,1,0:T(8,128)S(1)}, f32[8,128,128]{2,1,0:T(8,128)S(1)}, f32[8,128,128]{2,1,0:T(8,128)S(1)}...) custom-call(s32[1]{0:T(128)} %bitcast.hid, bf16[8,512,128]{2,1,0:T(8,128)(2,1)S(1)} %all-to-all-done.1.vq_ref.prev_ref, ...), custom_call_target="tpu_custom_call" | custom-call | flops 6600000000 | bytes 65536 | tf_op jit(solution)/shard_map/pallas_call | solution.py:465
  46.8 2.3 %collective-permute-start.1 = (f32[128,128]{1,0:T(8,128)S(1)}, f32[128,128]{1,0:T(8,128)S(1)}, u32[]{:S(2)}, u32[]{:S(2)}) collective-permute-start(f32[128,128]{1,0:T(8,128)S(1)} %get-tuple-element.58), channel_id=1, source_target_pairs={{0,16},{2,18},{4,20},{6,22},{8,24},{10,26},{12,28},{14,30},{16,0},... | collective-permute-start | bytes 196616 | tf_op jit(solution)/shard_map/ppermute | solution.py:603
  49.1 2.9 %shard_map.139 = (f32[8,128,128]{2,1,0:T(8,128)S(1)}, f32[8,128,256]{2,1,0:T(8,128)S(1)}, f32[8,128,128]{2,1,0:T(8,128)S(1)}, f32[8,128,128]{2,1,0:T(8,128)S(1)}, f32[8,128,128]{2,1,0:T(8,128)S(1)}) custom-call(s32[1]{0:T(128)} %bitcast.hid, bf16[8,512,128]{2,1,0:T(8,128)(2,1)S(1)} %all-to-all-done.1.vq_ref.prev_ref, ...), custom_call_target="tpu_custom_call" | custom-call | flops 8800000000 | bytes 65536 | tf_op jit(solution)/shard_map/pallas_call | solution.py:465
  52.0 2.5 %shard_map.140 = (f32[8,128,128]{2,1,0:T(8,128)S(1)}, f32[8,128,128]{2,1,0:T(8,128)S(1)}, f32[8,128,256]{2,1,0:T(8,128)S(1)}, bf16[8,128,128]{2,1,0:T(8,128)(2,1)S(1)}, f32[128,256]{1,0:T(8,128)S(1)}) custom-call(s32[1]{0:T(128)} %bitcast.hid, bf16[8,512,128]{2,1,0:T(8,128)(2,1)S(1)} %all-to-all-done.1.vq_ref.prev_ref, f32[72,1024]{1,0:T(8,128)S(1)} %concatenate.15.wts_ref, ...), custom_call_target="tpu_custom_call" | custom-call | flops 4400000000 | bytes 65536 | tf_op jit(solution)/shard_map/pallas_call | solution.py:465
  54.5 1.2 %collective-permute-start.3 = (f32[128,128]{1,0:T(8,128)S(1)}, f32[128,128]{1,0:T(8,128)S(1)}, u32[]{:S(2)}, u32[]{:S(2)}) collective-permute-start(f32[128,128]{1,0:T(8,128)S(1)} %slice.30), channel_id=1, source_target_pairs={{0,16},{2,18},{4,20},{6,22},{8,24},{10,26},{12,28},{14,30},{16,0},... | collective-permute-start | bytes 196616 | tf_op jit(solution)/shard_map/ppermute | solution.py:603
  55.7 5.1 %shard_map.141 = (f32[8,256,128]{2,1,0:T(8,128)}, f32[8,256,128]{2,1,0:T(8,128)}, f32[8,256,128]{2,1,0:T(8,128)}, f32[8,128,128]{2,1,0:T(8,128)}, f32[8,128,256]{2,1,0:T(8,128)}, /*index=5*/bf16[8,272,128]{2,1,0:T(8,128)(2,1)}) custom-call(s32[1]{0:T(128)} %bitcast.hid, f32[72,1024]{1,0:T(8,128)S(1)} %concatenate.15.wts_ref, ...), custom_call_target="tpu_custom_call" | custom-call | flops 22000001024 | bytes 65536 | tf_op jit(solution)/shard_map/pallas_call | solution.py:465
  60.8 5.8 %all-to-all-start.2 = ((bf16[8,272,128]{2,1,0:T(8,128)(2,1)}), bf16[8,272,128]{2,1,0:T(8,128)(2,1)S(1)}, u32[]{:S(2)}, u32[]{:S(2)}) async-start(bf16[8,272,128]{2,1,0:T(8,128)(2,1)} %get-tuple-element.74), calls=%async_computation.2 | async-start | bytes 1114112 | tf_op jit(solution)/shard_map/all_to_all | solution.py:512
  66.6 7.7 %shard_map.142 = bf16[8,544,128]{2,1,0:T(8,128)(2,1)} custom-call(s32[1]{0:T(128)} %bitcast.hid, bf16[8,304,128]{2,1,0:T(8,128)(2,1)S(1)} %all-to-all-done.kb_ref.prev_ref.beta_ref, f32[72,1024]{1,0:T(8,128)S(1)} %concatenate.15.wts_ref, f32[128,128]{1,0:T(8,128)S(1)} %collective-permute-done.3.end_ref, f32[8,128,256]{2,1,0:T(8,128)} %get-tuple-element.76.mb_ref, ...), custom_call_target="tpu_custom_call" | custom-call | flops 22000001024 | bytes 65536 | tf_op jit(solution)/shard_map/pallas_call | solution.py:465
  74.3 0.6 all-to-all-done.2.got_ref
  74.9 4.4 %all-to-all-start.3 = ((bf16[8,544,128]{2,1,0:T(8,128)(2,1)}), bf16[8,544,128]{2,1,0:T(8,128)(2,1)S(1)}, u32[]{:S(2)}, u32[]{:S(2)}) async-start(bf16[8,544,128]{2,1,0:T(8,128)(2,1)} %shard_map.142), calls=%async_computation.3 | async-start | bytes 2228224 | tf_op jit(solution)/shard_map/all_to_all | solution.py:512
  79.3 0.2 copy.33
  79.5 0.1 dot_general.9
  79.6 2.9 %fusion = f32[2,64,2048]{2,1,0:T(8,128)S(1)} fusion(bf16[2,64,1024]{2,1,0:T(8,128)(2,1)S(1)} %dot_general.9, bf16[1024,2048]{1,0:T(8,128)(2,1)} %param.18), kind=kOutput, calls=%fused_computation | convolution fusion | flops 536870912 | bytes 5505024 | tf_op jit(solution)/shard_map/dot_general | solution.py:673
  82.5 1.0 copy-done.1
  83.5 1.3 %collective-permute-start.2 = (bf16[64,2048]{1,0:T(8,128)(2,1)S(1)}, bf16[64,2048]{1,0:T(8,128)(2,1)S(1)}, u32[]{:S(2)}, u32[]{:S(2)}) collective-permute-start(bf16[64,2048]{1,0:T(8,128)(2,1)S(1)} %fusion.8), channel_id=1, source_target_pairs={{0,1},{1,0},{2,3},{3,2},{4,5},{5,4},{6,7},{7,6},{8,9},{9,8},{10,11... | collective-permute-start | bytes 786440 | tf_op jit(solution)/shard_map/ppermute | solution.py:680
  84.8 0.8 shard_map.143.gq_ref
  85.6 5.8 %collective-permute-done.2 = bf16[64,2048]{1,0:T(8,128)(2,1)S(1)} collective-permute-done((bf16[64,2048]{1,0:T(8,128)(2,1)S(1)}, bf16[64,2048]{1,0:T(8,128)(2,1)S(1)}, u32[]{:S(2)}, u32[]{:S(2)}) %collective-permute-start.2) | collective-permute-done | bytes 262176 | tf_op jit(solution)/shard_map/ppermute | solution.py:680
  91.5 0.8 fusion.7
  92.2 1.4 %all-to-all-done.3.got_ref.mark_ref = bf16[8,544,128]{2,1,0:T(8,128)(2,1)S(1)} async-done(((bf16[8,544,128]{2,1,0:T(8,128)(2,1)}), bf16[8,544,128]{2,1,0:T(8,128)(2,1)S(1)}, u32[]{:S(2)}, u32[]{:S(2)}) %all-to-all-start.3) | async-done | bytes 1114144 | tf_op jit(solution)/shard_map/all_to_all | solution.py:512
  93.6 2.8 %collective-permute-start.4 = (bf16[8,24,128]{2,1,0:T(8,128)(2,1)S(1)}, bf16[8,24,128]{2,1,0:T(8,128)(2,1)S(1)}, u32[]{:S(2)}, u32[]{:S(2)}) collective-permute-start(bf16[8,24,128]{2,1,0:T(8,128)(2,1)S(1)} %pad_maximum_fusion.1), channel_id=1, source_target_pairs={{2,0},{4,2},{6,4},{8,6},{10,8},{12,10},{14,12},{16,14},{18,16},{20... | collective-permute-start | bytes 147464 | tf_op jit(solution)/shard_map/ppermute | solution.py:685
  96.4 1.6 %shard_map.144 = (f32[128,2,1024]{2,1,0:T(2,128)}, f32[128,2,1024]{2,1,0:T(2,128)}) custom-call(bf16[8,544,128]{2,1,0:T(8,128)(2,1)S(1)} %all-to-all-done.3.got_ref.mark_ref), custom_call_target="tpu_custom_call" | custom-call | flops 11000000512 | bytes 65536 | tf_op jit(solution)/shard_map/pallas_call | solution.py:697
  98.0 1.2 %collective-permute-done.4.rim_ref = bf16[8,24,128]{2,1,0:T(8,128)(2,1)S(1)} collective-permute-done((bf16[8,24,128]{2,1,0:T(8,128)(2,1)S(1)}, bf16[8,24,128]{2,1,0:T(8,128)(2,1)S(1)}, u32[]{:S(2)}, u32[]{:S(2)}) %collective-permute-start.4) | collective-permute-done | bytes 49184 | tf_op jit(solution)/shard_map/ppermute | solution.py:685
  99.2 1.5 %shard_map.145 = (f32[128,1024]{1,0:T(8,128)}, f32[128,2,1024]{2,1,0:T(2,128)}, f32[128,2,1024]{2,1,0:T(2,128)}, f32[2,8,128]{2,1,0:T(8,128)}) custom-call(bf16[8,24,128]{2,1,0:T(8,128)(2,1)S(1)} %collective-permute-done.4.rim_ref, f32[128,1024]{1,0:T(8,128)} %shard_map.143.gq_ref, ...), custom_call_target="tpu_custom_call", output_to_operand_aliasing={{0}: (1, {}), {1}: (2, {}), {2}: (3, {})} | custom-call | tf_op jit(solution)/shard_map/pallas_call | solution.py:710
  (32 shorter events, 0.3 us)
Async XLA Ops:
  0.6 1.1 %copy-start = (bf16[128,2,1024]{2,1,0:T(2,128)(2,1)S(1)}, bf16[128,2,1024]{2,1,0:T(2,128)(2,1)}, u32[]{:S(2)}) copy-start(bf16[128,2,1024]{2,1,0:T(2,128)(2,1)} %param.11) | copy-start | bytes 1572868
  3.6 6.2 %copy-start.5 = (bf16[128,1024]{1,0:T(8,128)(2,1)S(1)}, bf16[128,1024]{1,0:T(8,128)(2,1)}, u32[]{:S(2)}) copy-start(bf16[128,1024]{1,0:T(8,128)(2,1)} %param.10) | copy-start | bytes 786436
  3.6 6.4 %copy-start.4 = (bf16[128,2048]{1,0:T(8,128)(2,1)S(1)}, bf16[128,2048]{1,0:T(8,128)(2,1)}, u32[]{:S(2)}) copy-start(bf16[128,2048]{1,0:T(8,128)(2,1)} %param.19) | copy-start | bytes 1572868
  4.5 14.3 %all-to-all-start = ((bf16[8,304,128]{2,1,0:T(8,128)(2,1)}), bf16[8,304,128]{2,1,0:T(8,128)(2,1)S(1)}, u32[]{:S(2)}, u32[]{:S(2)}) async-start(bf16[8,304,128]{2,1,0:T(8,128)(2,1)} %fusion.6), calls=%async_computation | async-start | bytes 1245184 | tf_op jit(solution)/shard_map/all_to_all | solution.py:512
  13.7 1.0 %copy-start.3 = (bf16[128,2,1024]{2,1,0:T(2,128)(2,1)S(1)}, bf16[128,2,1024]{2,1,0:T(2,128)(2,1)}, u32[]{:S(2)}) copy-start(bf16[128,2,1024]{2,1,0:T(2,128)(2,1)} %param.12) | copy-start | bytes 1572868
  16.2 11.7 %copy-start.6 = (f32[4,2,1024]{2,1,0:T(2,128)S(1)}, f32[4,2,1024]{2,1,0:T(2,128)}, u32[]{:S(2)}) copy-start(f32[4,2,1024]{2,1,0:T(2,128)} %param.15) | copy-start | bytes 98308
  18.8 9.2 %copy-start.7 = (f32[4,2,1024]{2,1,0:T(2,128)S(1)}, f32[4,2,1024]{2,1,0:T(2,128)}, u32[]{:S(2)}) copy-start(f32[4,2,1024]{2,1,0:T(2,128)} %param.16) | copy-start | bytes 98308
  18.9 9.3 %copy-start.8 = (f32[4,1024]{1,0:T(4,128)S(1)}, f32[4,1024]{1,0:T(4,128)}, u32[]{:S(2)}) copy-start(f32[4,1024]{1,0:T(4,128)} %param.14) | copy-start | bytes 49156
  18.9 9.3 %copy-start.9 = (f32[1024]{0:T(1024)S(1)}, f32[1024]{0:T(1024)}, u32[]{:S(2)}) copy-start(f32[1024]{0:T(1024)} %param.17) | copy-start | bytes 12292
  18.9 3.5 %collective-permute-start = (bf16[48,128]{1,0:T(8,128)(2,1)S(1)}, bf16[48,128]{1,0:T(8,128)(2,1)S(1)}, u32[]{:S(2)}, u32[]{:S(2)}) collective-permute-start(bf16[48,128]{1,0:T(8,128)(2,1)S(1)} %pad_maximum_fusion.3), channel_id=1, source_target_pairs={{0,16},{2,18},{4,20},{6,22},{8,24},{10,26},{12,28},{14,30},{16,0},... | collective-permute-start | bytes 36872 | tf_op jit(solution)/shard_map/ppermute | solution.py:539
  22.4 19.1 %all-to-all-start.1 = ((bf16[8,512,128]{2,1,0:T(8,128)(2,1)}), bf16[8,512,128]{2,1,0:T(8,128)(2,1)S(1)}, u32[]{:S(2)}, u32[]{:S(2)}) async-start(bf16[8,512,128]{2,1,0:T(8,128)(2,1)} %pad_maximum_fusion), calls=%async_computation.1 | async-start | bytes 2097152 | tf_op jit(solution)/shard_map/all_to_all | solution.py:512
  46.8 5.2 %collective-permute-start.1 = (f32[128,128]{1,0:T(8,128)S(1)}, f32[128,128]{1,0:T(8,128)S(1)}, u32[]{:S(2)}, u32[]{:S(2)}) collective-permute-start(f32[128,128]{1,0:T(8,128)S(1)} %get-tuple-element.58), channel_id=1, source_target_pairs={{0,16},{2,18},{4,20},{6,22},{8,24},{10,26},{12,28},{14,30},{16,0},... | collective-permute-start | bytes 196616 | tf_op jit(solution)/shard_map/ppermute | solution.py:603
  54.5 12.1 %collective-permute-start.3 = (f32[128,128]{1,0:T(8,128)S(1)}, f32[128,128]{1,0:T(8,128)S(1)}, u32[]{:S(2)}, u32[]{:S(2)}) collective-permute-start(f32[128,128]{1,0:T(8,128)S(1)} %slice.30), channel_id=1, source_target_pairs={{0,16},{2,18},{4,20},{6,22},{8,24},{10,26},{12,28},{14,30},{16,0},... | collective-permute-start | bytes 196616 | tf_op jit(solution)/shard_map/ppermute | solution.py:603
  60.8 14.1 %all-to-all-start.2 = ((bf16[8,272,128]{2,1,0:T(8,128)(2,1)}), bf16[8,272,128]{2,1,0:T(8,128)(2,1)S(1)}, u32[]{:S(2)}, u32[]{:S(2)}) async-start(bf16[8,272,128]{2,1,0:T(8,128)(2,1)} %get-tuple-element.74), calls=%async_computation.2 | async-start | bytes 1114112 | tf_op jit(solution)/shard_map/all_to_all | solution.py:512
  74.9 18.7 %all-to-all-start.3 = ((bf16[8,544,128]{2,1,0:T(8,128)(2,1)}), bf16[8,544,128]{2,1,0:T(8,128)(2,1)S(1)}, u32[]{:S(2)}, u32[]{:S(2)}) async-start(bf16[8,544,128]{2,1,0:T(8,128)(2,1)} %shard_map.142), calls=%async_computation.3 | async-start | bytes 2228224 | tf_op jit(solution)/shard_map/all_to_all | solution.py:512
  82.5 1.0 copy-start.1
  83.5 7.9 %collective-permute-start.2 = (bf16[64,2048]{1,0:T(8,128)(2,1)S(1)}, bf16[64,2048]{1,0:T(8,128)(2,1)S(1)}, u32[]{:S(2)}, u32[]{:S(2)}) collective-permute-start(bf16[64,2048]{1,0:T(8,128)(2,1)S(1)} %fusion.8), channel_id=1, source_target_pairs={{0,1},{1,0},{2,3},{3,2},{4,5},{5,4},{6,7},{7,6},{8,9},{9,8},{10,11... | collective-permute-start | bytes 786440 | tf_op jit(solution)/shard_map/ppermute | solution.py:680
  84.8 6.6 %copy-start.2 = (f32[2,64,2048]{2,1,0:T(8,128)S(1)}, f32[2,64,2048]{2,1,0:T(8,128)}, u32[]{:S(2)}) copy-start(f32[2,64,2048]{2,1,0:T(8,128)} %copy-done.1) | copy-start | bytes 3145732
  93.6 5.6 %collective-permute-start.4 = (bf16[8,24,128]{2,1,0:T(8,128)(2,1)S(1)}, bf16[8,24,128]{2,1,0:T(8,128)(2,1)S(1)}, u32[]{:S(2)}, u32[]{:S(2)}) collective-permute-start(bf16[8,24,128]{2,1,0:T(8,128)(2,1)S(1)} %pad_maximum_fusion.1), channel_id=1, source_target_pairs={{2,0},{4,2},{6,4},{8,6},{10,8},{12,10},{14,12},{16,14},{18,16},{20... | collective-permute-start | bytes 147464 | tf_op jit(solution)/shard_map/ppermute | solution.py:685

commit v9 on v8

--- a/solution.py
+++ b/solution.py
@@ -253,8 +253,7 @@
 
 def maps_kernel(
     per, tokens, slots, hid, vq_ref, prev_ref, beta_ref, tail_ref, wts_ref, kh_ref, kl_ref, xh_ref, xl_ref, a_ref,
-    m_ref,
-    u_ref, c_ref, an_ref, mn_ref, fv_ref, end_ref, pad, carry,
+    u_ref, c_ref, fv_ref, end_ref, pad, carry,
 ):
 
     rows = tokens * slots
@@ -278,7 +277,6 @@
     for n in range(per):
         u_ref[n] = us[n]
         c_ref[n] = state
-        an_ref[n], mn_ref[n] = a_ref[n], m_ref[n]
         state = mm(two(a_ref[n]), two(state)) + maps[n]
     carry[...] = state
     end_ref[...] = state
@@ -286,7 +284,7 @@
 
 def queries_kernel(
     per, tokens, slots, hid, vq_ref, prev_ref, tail_ref, wts_ref, kh_ref, kl_ref, wh_ref, wl_ref, u_ref,
-    q_ref, sc_ref, qm_ref, ol_ref, fq_ref, pad,
+    a_ref, m_ref, q_ref, sc_ref, qm_ref, ol_ref, fq_ref, an_ref, mn_ref, pad,
 ):
     rows = tokens * slots
     taps = query_taps(wts_ref[...])
@@ -310,6 +308,7 @@
         both = jnp.concatenate([wh_ref[n], uh], axis=1), jnp.concatenate([wl_ref[n], ul], axis=1)
         mapped.append(mm(two(scores[n]), both))
     for n in range(per):
+        an_ref[n], mn_ref[n] = a_ref[n], m_ref[n]
         sc_ref[n] = scores[n]
         qm_ref[n] = qs[n] - mapped[n][:, :HEAD]
         ol_ref[n] = mapped[n][:, HEAD:]
@@ -586,9 +585,9 @@
         steps,
         live,
         [(vq, per), (vq, ("prev", per, rows - EDGE)), beta, (tail, None), (wts, "weights")],
-        [(name, per) for name in ("kh", "kl", "xh", "xl", "a", "m")],
+        [(name, per) for name in ("kh", "kl", "xh", "xl", "a")],
         [
-            big("u", rows, HEAD), big("c", HEAD, HEAD), big("an", HEAD, HEAD), big("mn", HEAD, HEAD),
+            big("u", rows, HEAD), big("c", HEAD, HEAD),
             big("fv", rows, HEAD), (None, (HEAD, HEAD), F32, None),
         ],
         scratch=pad(rows) + [pltpu.VMEM((HEAD, HEAD), F32)],
@@ -619,10 +618,10 @@
         steps,
         live,
         [(vq, per), (vq, ("prev", per, rows + tokens - EDGE)), (tail, None), (wts, "weights")],
-        [(name, per) for name in ("kh", "kl", "wh", "wl", "u")],
+        [(name, per) for name in ("kh", "kl", "wh", "wl", "u", "a", "m")],
         [
             big("q", tokens, HEAD), big("sc", tokens, rows), big("qm", tokens, HEAD), big("ol", tokens, HEAD),
-            big("fq", tokens, HEAD),
+            big("fq", tokens, HEAD), big("an", HEAD, HEAD), big("mn", HEAD, HEAD),
         ],
         scratch=pad(tokens),
         us=8.0,

time: 101 us -> 101 us (level)
  no operation moved by 1% of the time
where the time goes in v9:
time: 101 us; the launch traced here: 100 us
  Pallas kernels  37.8 us (37%)
  starting transfers between devices  30.8 us (30%)
  waiting for transfers between devices  15.2 us (15%)
  matrix products  6.6 us (7%)
  local copies, waits for them, and re-layouts  5.4 us (5%)
  other arithmetic  3.46 us (3%)
    pallas_call x6, Pallas kernels, call(): pl.pallas_call(kernel, grid_spec=pltpu.PrefetchScalarGridSpec(num_scalar_...  34 us
    all_to_all x4, starting transfers between devices, exchange(): lax.all_to_all(x, 'ctx', 0, 0, axis_index_groups=group_lists, tiled=True)  21 us
    all_to_all x4, waiting for transfers between devices, exchange(): lax.all_to_all(x, 'ctx', 0, 0, axis_index_groups=group_lists, tiled=True)  7 us
    ppermute x1, waiting for transfers between devices, shards(): lax.ppermute(sent, 'head', [(0, 1), (1, 0)]).astype(F32)  5.81 us
    dot_general x1, matrix products, shards(): jnp.dot(grad_out, out_weight.T, preferred_element_type=F32).astype(BF16)  3.7 us
    ppermute x2, starting transfers between devices, across(): return lax.ppermute(last[1], 'ctx', moves)  3.36 us
    dot_general x1, matrix products, shards(): partial = jnp.dot(normed_bf, out_weight, preferred_element_type=F32)  2.9 us
    ppermute x1, starting transfers between devices, shards(): rim = lax.ppermute(rim, 'ctx', [(i, i - 1) for i in range(1, shard_count)])  2.78 us
  transfers between devices with their start and end apart: 9, of which 7 were waited for; matrix products, arithmetic and copies ran while one was open for 10% of the time, Pallas kernels for 29%

profile of v9, /device:TPU:1, one launch (start us, length us, event | category | flops | bytes accessed | tf_op | source)
XLA Modules:
  0.0 100.2 jit_solution(2332849578678494783)
XLA Ops:
  0.6 0.0 copy-start
  0.6 0.8 fusion.11
  1.4 0.3 copy-done
  1.7 0.4 copy_bitcast_fusion
  2.1 0.8 copy_bitcast_fusion.2
  2.8 0.8 bitcast_bitcast_fusion
  3.6 0.9 fusion.6
  4.5 5.3 %all-to-all-start = ((bf16[8,304,128]{2,1,0:T(8,128)(2,1)}), bf16[8,304,128]{2,1,0:T(8,128)(2,1)S(1)}, u32[]{:S(2)}, u32[]{:S(2)}) async-start(bf16[8,304,128]{2,1,0:T(8,128)(2,1)} %fusion.6), calls=%async_computation | async-start | bytes 1245184 | tf_op jit(solution)/shard_map/all_to_all | solution.py:511
  9.8 0.2 copy.23
  10.0 3.7 %convolution_convert_fusion = bf16[128,1024]{1,0:T(8,128)(2,1)S(1)} fusion(bf16[128,2048]{1,0:T(8,128)(2,1)S(1)} %copy-done.4, bf16[1024,2048]{1,0:T(8,128)(2,1)} %param.18), kind=kOutput, calls=%fused_computation.6 | convolution fusion | flops 537001984 | bytes 4980736 | tf_op jit(solution)/shard_map/dot_general | solution.py:535
  13.7 0.2 copy.25
  13.9 0.2 copy.26
  14.1 0.2 copy.24
  14.3 0.5 copy-done.3
  14.7 0.4 copy_bitcast_fusion.1
  15.1 1.0 %pad_maximum_fusion = bf16[8,512,128]{2,1,0:T(8,128)(2,1)} fusion(bf16[8,128,128]{2,1,0:T(8,128)(2,1)S(1)} %bitcast.73, bf16[8,128,128]{2,1,0:T(8,128)(2,1)S(1)} %bitcast.74, bf16[8,256,128]{2,1,0:T(8,128)(2,1)S(1)} %bitcast.70), kind=kLoop, calls=%fused_computation.7 | loop fusion | flops 3145728 | bytes 2097152 | tf_op jit(solution)/shard_map/concatenate | solution.py:536
  16.2 2.7 %all-to-all-done.kb_ref.prev_ref.beta_ref = bf16[8,304,128]{2,1,0:T(8,128)(2,1)S(1)} async-done(((bf16[8,304,128]{2,1,0:T(8,128)(2,1)}), bf16[8,304,128]{2,1,0:T(8,128)(2,1)S(1)}, u32[]{:S(2)}, u32[]{:S(2)}) %all-to-all-start) | async-done | bytes 622624 | tf_op jit(solution)/shard_map/all_to_all | solution.py:511
  18.9 0.0 copy-start.8
  18.9 2.4 %collective-permute-start = (bf16[48,128]{1,0:T(8,128)(2,1)S(1)}, bf16[48,128]{1,0:T(8,128)(2,1)S(1)}, u32[]{:S(2)}, u32[]{:S(2)}) collective-permute-start(bf16[48,128]{1,0:T(8,128)(2,1)S(1)} %pad_maximum_fusion.3), channel_id=1, source_target_pairs={{0,16},{2,18},{4,20},{6,22},{8,24},{10,26},{12,28},{14,30},{16,0},... | collective-permute-start | bytes 36872 | tf_op jit(solution)/shard_map/ppermute | solution.py:538
  21.2 1.1 %collective-permute-done.tail_ref = bf16[48,128]{1,0:T(8,128)(2,1)S(1)} collective-permute-done((bf16[48,128]{1,0:T(8,128)(2,1)S(1)}, bf16[48,128]{1,0:T(8,128)(2,1)S(1)}, u32[]{:S(2)}, u32[]{:S(2)}) %collective-permute-start) | collective-permute-done | bytes 12320 | tf_op jit(solution)/shard_map/ppermute | solution.py:538
  22.4 5.5 %all-to-all-start.1 = ((bf16[8,512,128]{2,1,0:T(8,128)(2,1)}), bf16[8,512,128]{2,1,0:T(8,128)(2,1)S(1)}, u32[]{:S(2)}, u32[]{:S(2)}) async-start(bf16[8,512,128]{2,1,0:T(8,128)(2,1)} %pad_maximum_fusion), calls=%async_computation.1 | async-start | bytes 2097152 | tf_op jit(solution)/shard_map/all_to_all | solution.py:511
  27.9 0.1 tile.17
  28.1 0.1 tile.19
  28.3 10.9 %shard_map.137 = (bf16[8,256,128]{2,1,0:T(8,128)(2,1)}, bf16[8,256,128]{2,1,0:T(8,128)(2,1)}, bf16[8,256,256]{2,1,0:T(8,128)(2,1)}, bf16[8,256,256]{2,1,0:T(8,12...) custom-call(s32[1]{0:T(128)} %bitcast.hid, ...), custom_call_target="tpu_custom_call" | custom-call | flops 12099999744 | bytes 65536 | tf_op jit(solution)/shard_map/pallas_call | solution.py:464
  39.1 2.3 %all-to-all-done.1.vq_ref.prev_ref = bf16[8,512,128]{2,1,0:T(8,128)(2,1)S(1)} async-done(((bf16[8,512,128]{2,1,0:T(8,128)(2,1)}), bf16[8,512,128]{2,1,0:T(8,128)(2,1)S(1)}, u32[]{:S(2)}, u32[]{:S(2)}) %all-to-all-start.1) | async-done | bytes 1048608 | tf_op jit(solution)/shard_map/all_to_all | solution.py:511
  41.5 4.8 %shard_map.138 = (f32[8,256,128]{2,1,0:T(8,128)S(1)}, f32[8,128,128]{2,1,0:T(8,128)S(1)}, f32[8,256,128]{2,1,0:T(8,128)}, f32[128,128]{1,0:T(8,128)S(1)}) custom-call(s32[1]{0:T(128)} %bitcast.hid, bf16[8,512,128]{2,1,0:T(8,128)(2,1)S(1)} %all-to-all-done.1.vq_ref.prev_ref, bf16[8,512,128]{2,1,0:T(8,128)(2,1)S(1)} %all-to-all-done.1.vq_ref.prev_ref, ...), custom_call_target="tpu_custom_call" | custom-call | flops 6600000000 | bytes 65536 | tf_op jit(solution)/shard_map/pallas_call | solution.py:464
  46.3 2.3 %collective-permute-start.1 = (f32[128,128]{1,0:T(8,128)S(1)}, f32[128,128]{1,0:T(8,128)S(1)}, u32[]{:S(2)}, u32[]{:S(2)}) collective-permute-start(f32[128,128]{1,0:T(8,128)S(1)} %get-tuple-element.57), channel_id=1, source_target_pairs={{0,16},{2,18},{4,20},{6,22},{8,24},{10,26},{12,28},{14,30},{16,0},... | collective-permute-start | bytes 196616 | tf_op jit(solution)/shard_map/ppermute | solution.py:602
  48.6 3.0 %shard_map.139 = (f32[8,128,128]{2,1,0:T(8,128)S(1)}, f32[8,128,256]{2,1,0:T(8,128)S(1)}, f32[8,128,128]{2,1,0:T(8,128)S(1)}, f32[8,128,128]{2,1,0:T(8,128)S(1)}...) custom-call(s32[1]{0:T(128)} %bitcast.hid, ...), custom_call_target="tpu_custom_call" | custom-call | flops 8800000000 | bytes 65536 | tf_op jit(solution)/shard_map/pallas_call | solution.py:464
  51.7 2.5 %shard_map.140 = (f32[8,128,128]{2,1,0:T(8,128)S(1)}, f32[8,128,128]{2,1,0:T(8,128)S(1)}, f32[8,128,256]{2,1,0:T(8,128)S(1)}, bf16[8,128,128]{2,1,0:T(8,128)(2,1)S(1)}, f32[128,256]{1,0:T(8,128)S(1)}) custom-call(s32[1]{0:T(128)} %bitcast.hid, bf16[8,512,128]{2,1,0:T(8,128)(2,1)S(1)} %all-to-all-done.1.vq_ref.prev_ref, f32[72,1024]{1,0:T(8,128)S(1)} %concatenate.15.wts_ref, ...), custom_call_target="tpu_custom_call" | custom-call | flops 4400000000 | bytes 65536 | tf_op jit(solution)/shard_map/pallas_call | solution.py:464
  54.2 1.0 %collective-permute-start.3 = (f32[128,128]{1,0:T(8,128)S(1)}, f32[128,128]{1,0:T(8,128)S(1)}, u32[]{:S(2)}, u32[]{:S(2)}) collective-permute-start(f32[128,128]{1,0:T(8,128)S(1)} %slice.30), channel_id=1, source_target_pairs={{0,16},{2,18},{4,20},{6,22},{8,24},{10,26},{12,28},{14,30},{16,0},... | collective-permute-start | bytes 196616 | tf_op jit(solution)/shard_map/ppermute | solution.py:602
  55.2 5.1 %shard_map.141 = (f32[8,256,128]{2,1,0:T(8,128)}, f32[8,256,128]{2,1,0:T(8,128)}, f32[8,256,128]{2,1,0:T(8,128)}, f32[8,128,128]{2,1,0:T(8,128)}, f32[8,128,256]{2,1,0:T(8,128)}, /*index=5*/bf16[8,272,128]{2,1,0:T(8,128)(2,1)}) custom-call(s32[1]{0:T(128)} %bitcast.hid, f32[72,1024]{1,0:T(8,128)S(1)} %concatenate.15.wts_ref, ...), custom_call_target="tpu_custom_call" | custom-call | flops 22000001024 | bytes 65536 | tf_op jit(solution)/shard_map/pallas_call | solution.py:464
  60.3 5.8 %all-to-all-start.2 = ((bf16[8,272,128]{2,1,0:T(8,128)(2,1)}), bf16[8,272,128]{2,1,0:T(8,128)(2,1)S(1)}, u32[]{:S(2)}, u32[]{:S(2)}) async-start(bf16[8,272,128]{2,1,0:T(8,128)(2,1)} %get-tuple-element.74), calls=%async_computation.2 | async-start | bytes 1114112 | tf_op jit(solution)/shard_map/all_to_all | solution.py:511
  66.1 7.7 %shard_map.142 = bf16[8,544,128]{2,1,0:T(8,128)(2,1)} custom-call(s32[1]{0:T(128)} %bitcast.hid, bf16[8,304,128]{2,1,0:T(8,128)(2,1)S(1)} %all-to-all-done.kb_ref.prev_ref.beta_ref, f32[72,1024]{1,0:T(8,128)S(1)} %concatenate.15.wts_ref, f32[128,128]{1,0:T(8,128)S(1)} %collective-permute-done.3.end_ref, f32[8,128,256]{2,1,0:T(8,128)} %get-tuple-element.76.mb_ref, ...), custom_call_target="tpu_custom_call" | custom-call | flops 22000001024 | bytes 65536 | tf_op jit(solution)/shard_map/pallas_call | solution.py:464
  73.8 0.6 all-to-all-done.2.got_ref
  74.4 4.4 %all-to-all-start.3 = ((bf16[8,544,128]{2,1,0:T(8,128)(2,1)}), bf16[8,544,128]{2,1,0:T(8,128)(2,1)S(1)}, u32[]{:S(2)}, u32[]{:S(2)}) async-start(bf16[8,544,128]{2,1,0:T(8,128)(2,1)} %shard_map.142), calls=%async_computation.3 | async-start | bytes 2228224 | tf_op jit(solution)/shard_map/all_to_all | solution.py:511
  78.8 0.2 copy.33
  79.0 0.1 dot_general.9
  79.1 2.9 %fusion = f32[2,64,2048]{2,1,0:T(8,128)S(1)} fusion(bf16[2,64,1024]{2,1,0:T(8,128)(2,1)S(1)} %dot_general.9, bf16[1024,2048]{1,0:T(8,128)(2,1)} %param.18), kind=kOutput, calls=%fused_computation | convolution fusion | flops 536870912 | bytes 5505024 | tf_op jit(solution)/shard_map/dot_general | solution.py:672
  82.1 1.0 copy-done.1
  83.1 1.3 %collective-permute-start.2 = (bf16[64,2048]{1,0:T(8,128)(2,1)S(1)}, bf16[64,2048]{1,0:T(8,128)(2,1)S(1)}, u32[]{:S(2)}, u32[]{:S(2)}) collective-permute-start(bf16[64,2048]{1,0:T(8,128)(2,1)S(1)} %fusion.8), channel_id=1, source_target_pairs={{0,1},{1,0},{2,3},{3,2},{4,5},{5,4},{6,7},{7,6},{8,9},{9,8},{10,11... | collective-permute-start | bytes 786440 | tf_op jit(solution)/shard_map/ppermute | solution.py:679
  84.4 0.8 shard_map.143.gq_ref
  85.2 5.8 %collective-permute-done.2 = bf16[64,2048]{1,0:T(8,128)(2,1)S(1)} collective-permute-done((bf16[64,2048]{1,0:T(8,128)(2,1)S(1)}, bf16[64,2048]{1,0:T(8,128)(2,1)S(1)}, u32[]{:S(2)}, u32[]{:S(2)}) %collective-permute-start.2) | collective-permute-done | bytes 262176 | tf_op jit(solution)/shard_map/ppermute | solution.py:679
  91.0 0.8 fusion.7
  91.8 1.4 %all-to-all-done.3.got_ref.mark_ref = bf16[8,544,128]{2,1,0:T(8,128)(2,1)S(1)} async-done(((bf16[8,544,128]{2,1,0:T(8,128)(2,1)}), bf16[8,544,128]{2,1,0:T(8,128)(2,1)S(1)}, u32[]{:S(2)}, u32[]{:S(2)}) %all-to-all-start.3) | async-done | bytes 1114144 | tf_op jit(solution)/shard_map/all_to_all | solution.py:511
  93.1 2.8 %collective-permute-start.4 = (bf16[8,24,128]{2,1,0:T(8,128)(2,1)S(1)}, bf16[8,24,128]{2,1,0:T(8,128)(2,1)S(1)}, u32[]{:S(2)}, u32[]{:S(2)}) collective-permute-start(bf16[8,24,128]{2,1,0:T(8,128)(2,1)S(1)} %pad_maximum_fusion.1), channel_id=1, source_target_pairs={{2,0},{4,2},{6,4},{8,6},{10,8},{12,10},{14,12},{16,14},{18,16},{20... | collective-permute-start | bytes 147464 | tf_op jit(solution)/shard_map/ppermute | solution.py:684
  95.9 1.6 %shard_map.144 = (f32[128,2,1024]{2,1,0:T(2,128)}, f32[128,2,1024]{2,1,0:T(2,128)}) custom-call(bf16[8,544,128]{2,1,0:T(8,128)(2,1)S(1)} %all-to-all-done.3.got_ref.mark_ref), custom_call_target="tpu_custom_call" | custom-call | flops 11000000512 | bytes 65536 | tf_op jit(solution)/shard_map/pallas_call | solution.py:696
  97.5 1.2 %collective-permute-done.4.rim_ref = bf16[8,24,128]{2,1,0:T(8,128)(2,1)S(1)} collective-permute-done((bf16[8,24,128]{2,1,0:T(8,128)(2,1)S(1)}, bf16[8,24,128]{2,1,0:T(8,128)(2,1)S(1)}, u32[]{:S(2)}, u32[]{:S(2)}) %collective-permute-start.4) | collective-permute-done | bytes 49184 | tf_op jit(solution)/shard_map/ppermute | solution.py:684
  98.8 1.5 %shard_map.145 = (f32[128,1024]{1,0:T(8,128)}, f32[128,2,1024]{2,1,0:T(2,128)}, f32[128,2,1024]{2,1,0:T(2,128)}, f32[2,8,128]{2,1,0:T(8,128)}) custom-call(bf16[8,24,128]{2,1,0:T(8,128)(2,1)S(1)} %collective-permute-done.4.rim_ref, f32[128,1024]{1,0:T(8,128)} %shard_map.143.gq_ref, ...), custom_call_target="tpu_custom_call", output_to_operand_aliasing={{0}: (1, {}), {1}: (2, {}), {2}: (3, {})} | custom-call | tf_op jit(solution)/shard_map/pallas_call | solution.py:709
  (32 shorter events, 0.3 us)
Async XLA Ops:
  0.6 1.1 %copy-start = (bf16[128,2,1024]{2,1,0:T(2,128)(2,1)S(1)}, bf16[128,2,1024]{2,1,0:T(2,128)(2,1)}, u32[]{:S(2)}) copy-start(bf16[128,2,1024]{2,1,0:T(2,128)(2,1)} %param.11) | copy-start | bytes 1572868
  3.6 6.2 %copy-start.5 = (bf16[128,1024]{1,0:T(8,128)(2,1)S(1)}, bf16[128,1024]{1,0:T(8,128)(2,1)}, u32[]{:S(2)}) copy-start(bf16[128,1024]{1,0:T(8,128)(2,1)} %param.10) | copy-start | bytes 786436
  3.6 6.4 %copy-start.4 = (bf16[128,2048]{1,0:T(8,128)(2,1)S(1)}, bf16[128,2048]{1,0:T(8,128)(2,1)}, u32[]{:S(2)}) copy-start(bf16[128,2048]{1,0:T(8,128)(2,1)} %param.19) | copy-start | bytes 1572868
  4.5 14.3 %all-to-all-start = ((bf16[8,304,128]{2,1,0:T(8,128)(2,1)}), bf16[8,304,128]{2,1,0:T(8,128)(2,1)S(1)}, u32[]{:S(2)}, u32[]{:S(2)}) async-start(bf16[8,304,128]{2,1,0:T(8,128)(2,1)} %fusion.6), calls=%async_computation | async-start | bytes 1245184 | tf_op jit(solution)/shard_map/all_to_all | solution.py:511
  13.7 1.0 %copy-start.3 = (bf16[128,2,1024]{2,1,0:T(2,128)(2,1)S(1)}, bf16[128,2,1024]{2,1,0:T(2,128)(2,1)}, u32[]{:S(2)}) copy-start(bf16[128,2,1024]{2,1,0:T(2,128)(2,1)} %param.12) | copy-start | bytes 1572868
  16.2 11.7 %copy-start.6 = (f32[4,2,1024]{2,1,0:T(2,128)S(1)}, f32[4,2,1024]{2,1,0:T(2,128)}, u32[]{:S(2)}) copy-start(f32[4,2,1024]{2,1,0:T(2,128)} %param.15) | copy-start | bytes 98308
  18.8 9.2 %copy-start.7 = (f32[4,2,1024]{2,1,0:T(2,128)S(1)}, f32[4,2,1024]{2,1,0:T(2,128)}, u32[]{:S(2)}) copy-start(f32[4,2,1024]{2,1,0:T(2,128)} %param.16) | copy-start | bytes 98308
  18.9 9.3 %copy-start.8 = (f32[4,1024]{1,0:T(4,128)S(1)}, f32[4,1024]{1,0:T(4,128)}, u32[]{:S(2)}) copy-start(f32[4,1024]{1,0:T(4,128)} %param.14) | copy-start | bytes 49156
  18.9 9.3 %copy-start.9 = (f32[1024]{0:T(1024)S(1)}, f32[1024]{0:T(1024)}, u32[]{:S(2)}) copy-start(f32[1024]{0:T(1024)} %param.17) | copy-start | bytes 12292
  18.9 3.5 %collective-permute-start = (bf16[48,128]{1,0:T(8,128)(2,1)S(1)}, bf16[48,128]{1,0:T(8,128)(2,1)S(1)}, u32[]{:S(2)}, u32[]{:S(2)}) collective-permute-start(bf16[48,128]{1,0:T(8,128)(2,1)S(1)} %pad_maximum_fusion.3), channel_id=1, source_target_pairs={{0,16},{2,18},{4,20},{6,22},{8,24},{10,26},{12,28},{14,30},{16,0},... | collective-permute-start | bytes 36872 | tf_op jit(solution)/shard_map/ppermute | solution.py:538
  22.4 19.1 %all-to-all-start.1 = ((bf16[8,512,128]{2,1,0:T(8,128)(2,1)}), bf16[8,512,128]{2,1,0:T(8,128)(2,1)S(1)}, u32[]{:S(2)}, u32[]{:S(2)}) async-start(bf16[8,512,128]{2,1,0:T(8,128)(2,1)} %pad_maximum_fusion), calls=%async_computation.1 | async-start | bytes 2097152 | tf_op jit(solution)/shard_map/all_to_all | solution.py:511
  46.3 5.4 %collective-permute-start.1 = (f32[128,128]{1,0:T(8,128)S(1)}, f32[128,128]{1,0:T(8,128)S(1)}, u32[]{:S(2)}, u32[]{:S(2)}) collective-permute-start(f32[128,128]{1,0:T(8,128)S(1)} %get-tuple-element.57), channel_id=1, source_target_pairs={{0,16},{2,18},{4,20},{6,22},{8,24},{10,26},{12,28},{14,30},{16,0},... | collective-permute-start | bytes 196616 | tf_op jit(solution)/shard_map/ppermute | solution.py:602
  54.2 11.9 %collective-permute-start.3 = (f32[128,128]{1,0:T(8,128)S(1)}, f32[128,128]{1,0:T(8,128)S(1)}, u32[]{:S(2)}, u32[]{:S(2)}) collective-permute-start(f32[128,128]{1,0:T(8,128)S(1)} %slice.30), channel_id=1, source_target_pairs={{0,16},{2,18},{4,20},{6,22},{8,24},{10,26},{12,28},{14,30},{16,0},... | collective-permute-start | bytes 196616 | tf_op jit(solution)/shard_map/ppermute | solution.py:602
  60.3 14.1 %all-to-all-start.2 = ((bf16[8,272,128]{2,1,0:T(8,128)(2,1)}), bf16[8,272,128]{2,1,0:T(8,128)(2,1)S(1)}, u32[]{:S(2)}, u32[]{:S(2)}) async-start(bf16[8,272,128]{2,1,0:T(8,128)(2,1)} %get-tuple-element.74), calls=%async_computation.2 | async-start | bytes 1114112 | tf_op jit(solution)/shard_map/all_to_all | solution.py:511
  74.4 18.7 %all-to-all-start.3 = ((bf16[8,544,128]{2,1,0:T(8,128)(2,1)}), bf16[8,544,128]{2,1,0:T(8,128)(2,1)S(1)}, u32[]{:S(2)}, u32[]{:S(2)}) async-start(bf16[8,544,128]{2,1,0:T(8,128)(2,1)} %shard_map.142), calls=%async_computation.3 | async-start | bytes 2228224 | tf_op jit(solution)/shard_map/all_to_all | solution.py:511
  82.0 1.0 copy-start.1
  83.1 7.9 %collective-permute-start.2 = (bf16[64,2048]{1,0:T(8,128)(2,1)S(1)}, bf16[64,2048]{1,0:T(8,128)(2,1)S(1)}, u32[]{:S(2)}, u32[]{:S(2)}) collective-permute-start(bf16[64,2048]{1,0:T(8,128)(2,1)S(1)} %fusion.8), channel_id=1, source_target_pairs={{0,1},{1,0},{2,3},{3,2},{4,5},{5,4},{6,7},{7,6},{8,9},{9,8},{10,11... | collective-permute-start | bytes 786440 | tf_op jit(solution)/shard_map/ppermute | solution.py:679
  84.4 6.6 %copy-start.2 = (f32[2,64,2048]{2,1,0:T(8,128)S(1)}, f32[2,64,2048]{2,1,0:T(8,128)}, u32[]{:S(2)}) copy-start(f32[2,64,2048]{2,1,0:T(8,128)} %copy-done.1) | copy-start | bytes 3145732
  93.1 5.6 %collective-permute-start.4 = (bf16[8,24,128]{2,1,0:T(8,128)(2,1)S(1)}, bf16[8,24,128]{2,1,0:T(8,128)(2,1)S(1)}, u32[]{:S(2)}, u32[]{:S(2)}) collective-permute-start(bf16[8,24,128]{2,1,0:T(8,128)(2,1)S(1)} %pad_maximum_fusion.1), channel_id=1, source_target_pairs={{2,0},{4,2},{6,4},{8,6},{10,8},{12,10},{14,12},{16,14},{18,16},{20... | collective-permute-start | bytes 147464 | tf_op jit(solution)/shard_map/ppermute | solution.py:684
